TPU v7x, 512 devices: a whole 4x4x16 slice. The times are simulated.
512 devices in a mesh: pts: 16 (over x, z_hi, core), ctr: 32 (over z_lo, y).
Axes of the slice: x: 4, y: 4, z: 16 (z_hi: 2, z_lo: 8; z = z_hi * 8 + z_lo), core: 2. Of those that a mesh axis runs over, the one named last changes fastest.
Arguments:
- points: float32 [8192, 256], P('pts'), may hold values from -6 to 6
- labels: bfloat16 [8192, 256], P('pts'), may hold values from -6 to 6
- centres: float32 [2, 4096, 256], P(None, 'ctr'), may hold values from -6 to 6
- coeffs: float32 [2, 4096, 256], P(None, 'pts'), may hold values from -6 to 6
- diag_inverse: float32 [2, 4096, 4096], P(None, 'ctr', 'pts'), may hold values from -0.09375 to 0.09375
- off_block: float32 [4096, 4096], P('pts', 'ctr'), may hold values from -0.09375 to 0.09375
Outputs:
- transposed: float32 [2, 4096, 256], P(None, 'ctr', 'pts')
All inputs are finite; a program needn't handle non-finite values.
Results may differ from a plain program's by a relative error of at most 0.0003.
Values sent between devices are 32-bit elements; how exact they have to be, the bound alone decides.
No kernel may reach another device: no remote copies, remote signals or barrier semaphores. Data moves between devices by JAX's collectives and lax.ppermute only.
A program may use at most 64 MiB of HBM per device.

v0:
```python
import math

import jax
import jax.numpy as jnp
from jax import lax
from jax.sharding import PartitionSpec as P


def kernel_tile(points, flat_centres):
    score = lax.dot_general(
        points,
        flat_centres,
        (((1,), (1,)), ((), ())),
        precision=lax.Precision.HIGHEST,
        preferred_element_type=jnp.float32,
    ) / math.sqrt(points.shape[1])
    return score + score * score * score / 3.0


def local(points, labels, centres, coeffs, diag_inverse, off_block):
    high = lax.Precision.HIGHEST
    panels = centres.shape[0]
    local_rows = centres.shape[1]
    flat_centres = centres.reshape(panels * local_rows, centres.shape[2])
    kernel = kernel_tile(points, flat_centres)
    second = lax.psum(
        jnp.dot(diag_inverse[1], coeffs[1], precision=high, preferred_element_type=jnp.float32),
        "pts",
    )
    carried = lax.psum(
        jnp.dot(off_block, second, precision=high, preferred_element_type=jnp.float32), "ctr"
    )
    rest = coeffs[0] - carried
    first = lax.psum(
        jnp.dot(diag_inverse[0], rest, precision=high, preferred_element_type=jnp.float32), "pts"
    )
    solved = jnp.concatenate([first, second], axis=0)
    total_centres = panels * local_rows * lax.axis_size("ctr")
    pred_scale = 1.0 / (2.0 * math.sqrt(total_centres))
    partial_pred = jnp.dot(kernel, solved, precision=high, preferred_element_type=jnp.float32)
    pred = lax.psum(partial_pred, "ctr")
    weights = jnp.tanh(pred * pred_scale - labels.astype(jnp.float32))
    total_points = points.shape[0] * lax.axis_size("pts")
    term = lax.dot_general(
        kernel,
        weights,
        (((0,), (0,)), ((), ())),
        precision=high,
        preferred_element_type=jnp.float32,
    )
    term = term.reshape(panels, local_rows, weights.shape[1])
    summed = lax.psum_scatter(term, "pts", scatter_dimension=2, tiled=True)
    return summed / (2.0 * math.sqrt(total_points))


def solution(mesh):
    return jax.shard_map(
        local,
        mesh=mesh,
        in_specs=(
            P("pts", None),
            P("pts", None),
            P(None, "ctr", None),
            P(None, "pts", None),
            P(None, "ctr", "pts"),
            P("pts", "ctr"),
        ),
        out_specs=P(None, "ctr", "pts"),
        check_vma=False,
    )
```

profile of v0, /device:TPU:1, one launch (start us, length us, event | category | flops | bytes accessed | tf_op | source)
XLA Modules:
  0.0 1539.9 jit_solution(7603430247279964926)
XLA Ops:
  6.5 0.0 copy-start
  6.5 0.0 all-reduce.5.cloned.1.call-start
  6.5 0.0 copy-start.6
  6.5 2.0 fusion.11
  8.6 0.0 copy-start.1
  8.6 0.0 all-reduce.5.cloned.1.call-update
  8.6 0.0 all-reduce.7.cloned.1.call-start
  8.6 260.4 %all-reduce.5.cloned.1.call-done = f32[128,256]{1,0:T(8,128)} async-done(((f32[128,256]{1,0:T(8,128)}), f32[128,256]{1,0:T(8,128)}) %all-reduce.5.cloned.1.call-update) | async-done | bytes 131088 | tf_op jit(solution)/shard_map/psum | solution.py:26
  269.0 0.0 copy-done.6
  269.0 2.0 convolution_bitcast_fusion
  271.0 0.0 copy-start.4
  271.0 0.0 all-reduce.7.cloned.1.call-update
  271.0 0.0 all-reduce.9.cloned.1.call-start
  271.1 432.0 %all-reduce.7.cloned.1.call-done = f32[256,256]{1,0:T(8,128)} async-done(((f32[256,256]{1,0:T(8,128)}), f32[256,256]{1,0:T(8,128)}) %all-reduce.7.cloned.1.call-update) | async-done | bytes 262160 | tf_op jit(solution)/shard_map/psum | solution.py:30
  703.1 0.0 copy-done.1
  703.1 0.0 copy-done.4
  703.1 0.0 copy-start.3
  703.1 2.0 convolution_bitcast_fusion.1
  705.1 0.0 all-reduce.9.cloned.1.call-update
  705.1 0.0 all-reduce.11.cloned.1.call-start
  705.2 0.0 copy-done
  705.2 0.0 copy-done.3
  705.2 0.0 copy-start.2
  705.2 0.6 fusion.1
  705.8 272.3 %all-reduce.9.cloned.1.call-done = f32[128,256]{1,0:T(8,128)} async-done(((f32[128,256]{1,0:T(8,128)}), f32[128,256]{1,0:T(8,128)}) %all-reduce.9.cloned.1.call-update) | async-done | bytes 131088 | tf_op jit(solution)/shard_map/psum | solution.py:34
  978.1 0.0 copy-done.2
  978.1 2.3 fusion.7
  980.4 0.0 copy-start.5
  980.4 0.0 all-reduce.11.cloned.1.call-update
  980.4 0.0 reduce-scatter.2.cloned.1.call-start
  980.4 432.3 %all-reduce.11.cloned.1.call-done = f32[512,256]{1,0:T(8,128)} async-done(((f32[512,256]{1,0:T(8,128)}), f32[512,256]{1,0:T(8,128)}) %all-reduce.11.cloned.1.call-update) | async-done | bytes 524304 | tf_op jit(solution)/shard_map/psum | solution.py:41
  1412.8 0.0 copy-done.5
  1412.8 2.0 fusion.2
  1414.8 0.8 copy.7
  1415.7 0.0 reduce-scatter.2.cloned.1.call-update
  1415.7 116.4 %reduce-scatter.2.cloned.1.call-done = f32[2,128,16]{1,2,0:T(8,128)} async-done(((f32[2,128,256]{1,2,0:T(8,128)}), f32[2,128,16]{1,2,0:T(8,128)}) %reduce-scatter.2.cloned.1.call-update) | async-done | bytes 16400 | tf_op jit(solution)/shard_map/reduce_scatter | solution.py:52
  1532.1 1.3 broadcast_multiply_fusion
Async XLA Ops:
  6.5 698.6 %copy-start = (f32[512,256]{1,0:T(8,128)S(1)}, f32[512,256]{1,0:T(8,128)}, u32[]{:S(2)}) copy-start(f32[512,256]{1,0:T(8,128)} %param.6) | copy-start | bytes 1572868
  6.5 262.5 %all-reduce.5.cloned.1.call-start = ((), (), s32[]{:S(2)}) async-start(), calls=%async_computation.1 | async-start | bytes 262144 | tf_op jit(solution)/shard_map/psum | solution.py:26
  6.5 262.5 %copy-start.6 = (f32[256,128]{1,0:T(8,128)S(1)}, f32[256,128]{1,0:T(8,128)}, u32[]{:S(2)}) copy-start(f32[256,128]{1,0:T(8,128)} %param.11) | copy-start | bytes 393220
  8.6 694.6 %copy-start.1 = (f32[2,256,256]{2,1,0:T(8,128)S(1)}, f32[2,256,256]{2,1,0:T(8,128)}, u32[]{:S(2)}) copy-start(f32[2,256,256]{2,1,0:T(8,128)} %param.9) | copy-start | bytes 1572868
  8.6 694.5 %all-reduce.7.cloned.1.call-start = ((), (), s32[]{:S(2)}) async-start(), calls=%async_computation.2 | async-start | bytes 524288 | tf_op jit(solution)/shard_map/psum | solution.py:30
  271.0 432.1 %copy-start.4 = (f32[2,128,256]{2,1,0:T(8,128)S(1)}, f32[2,128,256]{2,1,0:T(8,128)}, u32[]{:S(2)}) copy-start(f32[2,128,256]{2,1,0:T(8,128)} %param.10) | copy-start | bytes 786436
  271.0 707.1 %all-reduce.9.cloned.1.call-start = ((), (), s32[]{:S(2)}) async-start(), calls=%async_computation.3 | async-start | bytes 262144 | tf_op jit(solution)/shard_map/psum | solution.py:34
  703.1 2.0 copy-start.3
  705.1 707.7 %all-reduce.11.cloned.1.call-start = ((), (), s32[]{:S(2)}) async-start(), calls=%async_computation.4 | async-start | bytes 1048576 | tf_op jit(solution)/shard_map/psum | solution.py:41
  705.2 272.9 %copy-start.2 = (f32[128,256]{1,0:T(8,128)S(1)}, f32[128,256]{1,0:T(8,128)}, u32[]{:S(2)}) copy-start(f32[128,256]{1,0:T(8,128)} %all-reduce.5.cloned.1.call-done) | copy-start | bytes 393220
  980.4 432.4 %copy-start.5 = (bf16[512,256]{1,0:T(8,128)(2,1)S(1)}, bf16[512,256]{1,0:T(8,128)(2,1)}, u32[]{:S(2)}) copy-start(bf16[512,256]{1,0:T(8,128)(2,1)} %param.7) | copy-start | bytes 786436
  980.4 551.7 %reduce-scatter.2.cloned.1.call-start = ((), (), s32[]{:S(2)}) async-start(), calls=%async_computation.5 | async-start | bytes 278528 | tf_op jit(solution)/shard_map/reduce_scatter | solution.py:52
Sparse Core Ops, SparseCore 0:
  10.3 258.7 all-reduce.4
  272.2 430.8 all-reduce.6
  706.0 272.0 all-reduce.8
  981.1 431.6 all-reduce.10
  1417.2 114.7 reduce-scatter.1
where the time goes:
time: 1540 us
  waiting for transfers between devices  1510 us (98%)
    psum x1, waiting for transfers between devices, local(): pred = lax.psum(partial_pred, 'ctr')  432 us
    psum x1, waiting for transfers between devices, local(): lax.psum(jnp.dot(off_block, second, precision=high, preferred_element_typ...  432 us
    psum x1, waiting for transfers between devices, local(): lax.psum(jnp.dot(diag_inverse[0], rest, precision=high, preferred_element...  272 us
    psum x1, waiting for transfers between devices, local(): lax.psum(jnp.dot(diag_inverse[1], coeffs[1], precision=high, preferred_el...  260 us
    reduce_scatter x1, waiting for transfers between devices, local(): summed = lax.psum_scatter(term, 'pts', scatter_dimension=2, tiled=True)  116 us
  transfers between devices with their start and end apart: 5, of which 5 were waited for; matrix products, arithmetic and copies ran while one was open for 0% of the time, Pallas kernels for 0%

commit v1 on v0

v1 whole, which is shorter than its diff:
```python
import math

import jax
import jax.numpy as jnp
from jax import lax
from jax.sharding import Mesh
from jax.sharding import PartitionSpec as P

PTS = ("x", "h", "c")
CTR = ("w", "z", "y")
SIZES = {"x": 4, "h": 2, "c": 2, "w": 2, "z": 4, "y": 4}
HIGH = lax.Precision.HIGH


def dot(a, b, ca, cb):
    return lax.dot_general(
        a, b, ((ca, cb), ((), ())), precision=HIGH, preferred_element_type=jnp.float32
    )


def swap_sum(a, axis):
    return a + lax.ppermute(a, axis, [(0, 1), (1, 0)])


def shot(a, axes):
    return lax.all_to_all(a, axes, 0, 0, tiled=True)


def spread(a, axes, n):
    return shot(jnp.broadcast_to(a[None], (n, *a.shape)), axes)


def sum_ctr(a):
    a = jnp.sum(spread(a, "z", 4), 0)
    return swap_sum(a, "w")


def column_block(a, rows):
    a = a.reshape(4, 2, 2, 4, 4, rows)
    a = lax.dynamic_index_in_dim(a, lax.axis_index("y"), 3, keepdims=False)
    return a.transpose(0, 2, 1, 3, 4).reshape(64, rows)


def local(points, labels, centres, coeffs, diag_inverse, off_block):
    part = dot(coeffs[1], diag_inverse[1], (0,), (1,))
    part = part.reshape(4, 2, 2, 16, 128).transpose(0, 2, 1, 3, 4).reshape(8, 32, 128)
    part = jnp.sum(shot(part, ("x", "c")), 0)
    part = swap_sum(part, "h")
    part = part.reshape(2, 4, 4, 128).transpose(1, 0, 2, 3).reshape(1, 4, 8, 128)
    part = jnp.broadcast_to(part, (8, 4, 8, 128)).reshape(32, 8, 128)
    second = shot(part, ("x", "c", "y"))
    second = second.reshape(8, 4, 8, 128).transpose(0, 2, 1, 3).reshape(64, 512)

    off_y = lax.all_gather(off_block, "y", axis=1, tiled=True)
    diag_y = lax.all_gather(diag_inverse[0], "y", axis=0, tiled=True)
    centres_y = lax.all_gather(centres, "y", axis=0)

    carried = sum_ctr(dot(second, off_y, (1,), (1,)))
    rest = column_block(coeffs[0].T, 256) - carried
    first = dot(rest, diag_y, (1,), (1,))
    first = jnp.sum(shot(first.reshape(8, 8, 512), ("x", "c")), 0)
    first = swap_sum(first, "h")
    first = spread(first, ("x", "c"), 8).reshape(64, 512)

    def kernel_tile(panel):
        flat = centres_y[:, panel].reshape(512, 256)
        score = dot(points, flat, (1,), (1,)) / math.sqrt(points.shape[1])
        return score + score * score * score / 3.0

    kernel0, kernel1 = kernel_tile(0), kernel_tile(1)
    total_centres = 2 * 512 * 8
    pred_scale = 1.0 / (2.0 * math.sqrt(total_centres))
    pred = dot(first, kernel0, (1,), (1,)) + dot(second, kernel1, (1,), (1,))
    pred = sum_ctr(pred)
    target = column_block(labels.astype(jnp.float32).T, 512)
    weights = jnp.tanh(pred * pred_scale - target)

    total_points = points.shape[0] * 16
    scale = 1.0 / (2.0 * math.sqrt(total_points))
    term0 = dot(weights, kernel0, (1,), (0,)).reshape(8, 8, 4, 128)
    term1 = dot(weights, kernel1, (1,), (0,)).reshape(8, 8, 4, 128)
    term = jnp.stack([term0, term1], 3)
    term = term.transpose(0, 2, 1, 3, 4).reshape(32, 8, 256)
    term = jnp.sum(shot(term, ("x", "c", "y")).reshape(8, 4, 8, 256), 0)
    term = term.reshape(4, 2, 4, 256).transpose(1, 0, 2, 3).reshape(2, 16, 256)
    h = lax.axis_index("h")
    mine = lax.dynamic_index_in_dim(term, h, 0, keepdims=False)
    other = lax.dynamic_index_in_dim(term, 1 - h, 0, keepdims=False)
    mine = (mine + lax.ppermute(other, "h", [(0, 1), (1, 0)])) * scale
    return mine.reshape(16, 2, 128).transpose(1, 2, 0)


def solution(mesh):
    fine = Mesh(mesh.devices.reshape(tuple(SIZES.values())), tuple(SIZES))
    return jax.shard_map(
        local,
        mesh=fine,
        in_specs=(
            P(PTS, None),
            P(PTS, None),
            P(None, CTR, None),
            P(None, PTS, None),
            P(None, CTR, PTS),
            P(PTS, CTR),
        ),
        out_specs=P(None, CTR, PTS),
        check_vma=False,
    )
```

time: 1540 us -> 201 us (0.13)
  waiting for transfers between devices: 1510 us -> 24.7 us
  blocking collectives: 0 us -> 74.2 us
  starting transfers between devices: 0.17 us -> 69.5 us
    psum x4 -> x0, waiting for transfers between devices: 1400 us -> none  [the longest x1 432 us: local(): pred = lax.psum(partial_pred, 'ctr')]
    reduce_scatter x1 -> x0, waiting for transfers between devices: 116 us -> none  [local(): summed = lax.psum_scatter(term, 'pts', scatter_dimension=2, tiled=True)]
    ppermute x0 -> x5, starting transfers between devices: none -> 48.8 us  [the longest x4 38.7 us: swap_sum(): return a + lax.ppermute(a, axis, [(0, 1), (1, 0)])]
    all_to_all x0 -> x3, blocking collectives: none -> 47.8 us  [shot(): return lax.all_to_all(a, axes, 0, 0, tiled=True)]
    all_gather x0 -> x2, blocking collectives: none -> 26.4 us  [the longest x1 15.1 us: local(): off_y = lax.all_gather(off_block, 'y', axis=1, tiled=True)]
    all_to_all x0 -> x4, starting transfers between devices: none -> 20.7 us  [shot(): return lax.all_to_all(a, axes, 0, 0, tiled=True)]
  transfers between devices with their start and end apart: 5 -> 10, of which waited for: 5 -> 7; matrix products, arithmetic and copies ran while one was open for 0% -> 6% of each run, Pallas kernels for 0% -> 0%
where the time goes in v1:
time: 201 us; the launch traced here: 200 us
  blocking collectives  74.2 us (37%)
  starting transfers between devices  69.5 us (35%)
  waiting for transfers between devices  24.7 us (12%)
  between operations  13.7 us (7%)
  local copies, waits for them, and re-layouts  10.4 us (5%)
  matrix products  4.56 us (2%)
  other arithmetic  2.62 us (1%)
    all_to_all x3, blocking collectives, shot(): return lax.all_to_all(a, axes, 0, 0, tiled=True)  47.8 us
    ppermute x4, starting transfers between devices, swap_sum(): return a + lax.ppermute(a, axis, [(0, 1), (1, 0)])  38.7 us
    all_to_all x4, starting transfers between devices, shot(): return lax.all_to_all(a, axes, 0, 0, tiled=True)  20.7 us
    all_gather x1, blocking collectives, local(): off_y = lax.all_gather(off_block, 'y', axis=1, tiled=True)  15.1 us
    all_gather x1, blocking collectives, local(): diag_y = lax.all_gather(diag_inverse[0], 'y', axis=0, tiled=True)  11.3 us
    ppermute x4, waiting for transfers between devices, swap_sum(): return a + lax.ppermute(a, axis, [(0, 1), (1, 0)])  10.9 us
    all_to_all x4, waiting for transfers between devices, shot(): return lax.all_to_all(a, axes, 0, 0, tiled=True)  10.7 us
    ppermute x1, starting transfers between devices, local(): mine = (mine + lax.ppermute(other, 'h', [(0, 1), (1, 0)])) * scale  10.1 us
  transfers between devices with their start and end apart: 10, of which 7 were waited for; matrix products, arithmetic and copies ran while one was open for 6% of the time, Pallas kernels for 0%

profile of v1, /device:TPU:1, one launch (start us, length us, event | category | flops | bytes accessed | tf_op | source)
XLA Modules:
  0.0 199.7 jit_solution(14205393980233022840)
XLA Ops:
  6.5 1.1 slice_bitcast_fusion.1
  7.7 0.1 copy.40
  7.8 0.8 copy-done.1
  8.6 0.3 convolution_bitcast_fusion.1
  8.9 14.5 %all_to_all.35 = f32[8,32,128]{2,1,0:T(8,128)S(1)} all-to-all(f32[8,32,128]{2,1,0:T(8,128)S(1)} %bitcast.93), channel_id=1, replica_groups=mesh['x'=4,'h'=2,'c'=2,'w'=2,'z'=4,'y'=4] {'x','c'}, dimensions={0} | all-to-all | bytes 262144 | tf_op jit(solution)/shard_map/all_to_all | solution.py:26
  23.5 11.8 %collective-permute-start = (f32[32,128]{1,0:T(8,128)S(1)}, f32[32,128]{1,0:T(8,128)S(1)}, u32[]{:S(2)}, u32[]{:S(2)}) collective-permute-start(f32[32,128]{1,0:T(8,128)S(1)} %reduce_sum.45), channel_id=1, source_target_pairs={{0,64},{64,0},{1,65},{65,1},{2,66},{66,2},{3,67},{67,3},{4,68},{68... | collective-permute-start | bytes 49160 | tf_op jit(solution)/shard_map/ppermute | solution.py:22
  35.3 0.0 all-gather.4.cloned.1.call-update
  35.3 1.4 collective-permute-done
  36.7 0.7 broadcast_in_dim.11
  37.4 6.8 %all-to-all-start.1 = ((f32[32,8,128]{2,1,0:T(8,128)}), f32[32,8,128]{2,1,0:T(8,128)S(1)}, u32[]{:S(2)}, u32[]{:S(2)}) async-start(f32[32,8,128]{2,1,0:T(8,128)} %bitcast.15), calls=%async_computation.1 | async-start | bytes 262144 | tf_op jit(solution)/shard_map/all_to_all | solution.py:26
  44.2 15.1 %all_gather.12 = f32[256,512]{1,0:T(8,128)S(1)} all-gather(f32[256,128]{1,0:T(8,128)S(1)} %copy-done.2), channel_id=1, replica_groups=mesh['x'=4,'h'=2,'c'=2,'w'=2,'z'=4,'y'=4] {'y'}, dimensions={1}, use_global_device_ids=true | all-gather | bytes 655360 | tf_op jit(solution)/shard_map/all_gather | solution.py:54
  59.2 0.4 fusion.12
  59.6 0.7 broadcast_in_dim.12
  60.3 3.4 %all-to-all-start.2 = ((f32[4,64,256]{2,1,0:T(8,128)}), f32[4,64,256]{2,1,0:T(8,128)S(1)}, u32[]{:S(2)}, u32[]{:S(2)}) async-start(f32[4,64,256]{2,1,0:T(8,128)} %broadcast_in_dim.12), calls=%async_computation.2 | async-start | bytes 524288 | tf_op jit(solution)/shard_map/all_to_all | solution.py:26
  63.8 0.1 copy.38
  63.9 0.1 reshape.58
  64.0 0.8 slice-done
  64.8 11.3 %all-gather = f32[1,512,256]{2,1,0:T(8,128)S(1)} all-gather(f32[1,128,256]{2,1,0:T(8,128)S(1)} %slice-done), channel_id=2, replica_groups=mesh['x'=4,'h'=2,'c'=2,'w'=2,'z'=4,'y'=4] {'y'}, dimensions={1}, use_global_device_ids=true | all-gather | bytes 655360 | tf_op jit(solution)/shard_map/all_gather | solution.py:55
  76.2 7.2 %collective-permute-start.1 = (f32[64,256]{1,0:T(8,128)S(1)}, f32[64,256]{1,0:T(8,128)S(1)}, u32[]{:S(2)}, u32[]{:S(2)}) collective-permute-start(f32[64,256]{1,0:T(8,128)S(1)} %reduce_sum.46), channel_id=1, source_target_pairs={{0,16},{16,0},{1,17},{17,1},{2,18},{18,2},{3,19},{19,3},{4,20},{20... | collective-permute-start | bytes 196616 | tf_op jit(solution)/shard_map/ppermute | solution.py:22
  83.4 1.7 collective-permute-done.1
  85.1 0.4 convolution_bitcast_fusion
  85.5 14.0 %all_to_all.36 = f32[8,8,512]{2,1,0:T(8,128)S(1)} all-to-all(f32[8,8,512]{2,1,0:T(8,128)S(1)} %convolution_bitcast_fusion), channel_id=1, replica_groups=mesh['x'=4,'h'=2,'c'=2,'w'=2,'z'=4,'y'=4] {'x','c'}, dimensions={0} | all-to-all | bytes 262144 | tf_op jit(solution)/shard_map/all_to_all | solution.py:26
  99.5 11.7 %collective-permute-start.2 = (f32[8,512]{1,0:T(8,128)S(1)}, f32[8,512]{1,0:T(8,128)S(1)}, u32[]{:S(2)}, u32[]{:S(2)}) collective-permute-start(f32[8,512]{1,0:T(8,128)S(1)} %reduce_sum.47), channel_id=1, source_target_pairs={{0,64},{64,0},{1,65},{65,1},{2,66},{66,2},{3,67},{67,3},{4,68},{68... | collective-permute-start | bytes 49160 | tf_op jit(solution)/shard_map/ppermute | solution.py:22
  111.2 1.5 collective-permute-done.2
  112.7 0.7 broadcast_in_dim.13
  113.3 5.3 %all-to-all-start.4 = ((f32[8,8,512]{2,1,0:T(8,128)}), f32[8,8,512]{2,1,0:T(8,128)S(1)}, u32[]{:S(2)}, u32[]{:S(2)}) async-start(f32[8,8,512]{2,1,0:T(8,128)} %broadcast_in_dim.13), calls=%async_computation.4 | async-start | bytes 262144 | tf_op jit(solution)/shard_map/all_to_all | solution.py:26
  118.6 1.3 fusion.11
  119.9 0.7 fusion.3
  120.7 0.7 fusion.1
  121.4 0.6 fusion.13
  122.0 1.9 all-to-all-done.4
  123.9 0.6 convolution_add_fusion
  124.5 0.1 broadcast_in_dim.14
  124.6 19.3 %all_to_all.37 = f32[4,64,512]{2,1,0:T(8,128)S(1)} all-to-all(f32[4,64,512]{2,1,0:T(8,128)S(1)} %broadcast_in_dim.14), channel_id=1, replica_groups=mesh['x'=4,'h'=2,'c'=2,'w'=2,'z'=4,'y'=4] {'z'}, dimensions={0} | all-to-all | bytes 1048576 | tf_op jit(solution)/shard_map/all_to_all | solution.py:26
  143.9 8.0 %collective-permute-start.3 = (f32[64,512]{1,0:T(8,128)S(1)}, f32[64,512]{1,0:T(8,128)S(1)}, u32[]{:S(2)}, u32[]{:S(2)}) collective-permute-start(f32[64,512]{1,0:T(8,128)S(1)} %reduce_sum.48), channel_id=1, source_target_pairs={{0,16},{16,0},{1,17},{17,1},{2,18},{18,2},{3,19},{19,3},{4,20},{20... | collective-permute-start | bytes 393224 | tf_op jit(solution)/shard_map/ppermute | solution.py:22
  151.9 1.8 convert_bitcast_fusion
  153.7 1.2 copy.43
  154.9 0.9 reshape.76
  155.9 0.9 dynamic-slice_bitcast_fusion
  156.9 6.4 %collective-permute-done.3 = f32[64,512]{1,0:T(8,128)S(1)} collective-permute-done((f32[64,512]{1,0:T(8,128)S(1)}, f32[64,512]{1,0:T(8,128)S(1)}, u32[]{:S(2)}, u32[]{:S(2)}) %collective-permute-start.3) | collective-permute-done | bytes 131104 | tf_op jit(solution)/shard_map/ppermute | solution.py:22
  163.2 0.4 convolution_bitcast_fusion.3
  163.7 0.4 convolution_bitcast_fusion.2
  164.1 0.7 pad_maximum_fusion
  164.8 5.3 %all-to-all-start.6 = ((f32[32,8,256]{2,1,0:T(8,128)}), f32[32,8,256]{2,1,0:T(8,128)S(1)}, u32[]{:S(2)}, u32[]{:S(2)}) async-start(f32[32,8,256]{2,1,0:T(8,128)} %bitcast.35), calls=%async_computation.6 | async-start | bytes 524288 | tf_op jit(solution)/shard_map/all_to_all | solution.py:26
  170.1 8.8 %all-to-all-done.6 = f32[32,8,256]{2,1,0:T(8,128)S(1)} async-done(((f32[32,8,256]{2,1,0:T(8,128)}), f32[32,8,256]{2,1,0:T(8,128)S(1)}, u32[]{:S(2)}, u32[]{:S(2)}) %all-to-all-start.6) | async-done | bytes 262176 | tf_op jit(solution)/shard_map/all_to_all | solution.py:26
  179.0 10.1 %collective-permute-start.4 = (f32[16,256]{1,0:T(8,128)S(1)}, f32[16,256]{1,0:T(8,128)S(1)}, u32[]{:S(2)}, u32[]{:S(2)}) collective-permute-start(f32[16,256]{1,0:T(8,128)S(1)} %bitcast.99), channel_id=1, source_target_pairs={{0,64},{64,0},{1,65},{65,1},{2,66},{66,2},{3,67},{67,3},{4,68},{68... | collective-permute-start | bytes 49160 | tf_op jit(solution)/shard_map/ppermute | solution.py:89
  189.1 3.1 %collective-permute-done.4 = f32[16,256]{1,0:T(8,128)S(1)} collective-permute-done((f32[16,256]{1,0:T(8,128)S(1)}, f32[16,256]{1,0:T(8,128)S(1)}, u32[]{:S(2)}, u32[]{:S(2)}) %collective-permute-start.4) | collective-permute-done | bytes 16416 | tf_op jit(solution)/shard_map/ppermute | solution.py:89
  192.2 0.6 copy.49
  (30 shorter events, 0.4 us)
Async XLA Ops:
  6.5 113.4 %copy-start = (f32[512,256]{1,0:T(8,128)S(1)}, f32[512,256]{1,0:T(8,128)}, u32[]{:S(2)}) copy-start(f32[512,256]{1,0:T(8,128)} %param.6) | copy-start | bytes 1572868
  6.5 112.1 %all-gather.4.cloned.1.call-start = ((), (), s32[]{:S(2)}) async-start(), calls=%async_computation.7 | async-start | bytes 1310720 | tf_op jit(solution)/shard_map/all_gather | solution.py:56
  7.7 1.0 copy-start.1
  23.5 13.2 %collective-permute-start = (f32[32,128]{1,0:T(8,128)S(1)}, f32[32,128]{1,0:T(8,128)S(1)}, u32[]{:S(2)}, u32[]{:S(2)}) collective-permute-start(f32[32,128]{1,0:T(8,128)S(1)} %reduce_sum.45), channel_id=1, source_target_pairs={{0,64},{64,0},{1,65},{65,1},{2,66},{66,2},{3,67},{67,3},{4,68},{68... | collective-permute-start | bytes 49160 | tf_op jit(solution)/shard_map/ppermute | solution.py:22
  37.4 6.8 %copy-start.2 = (f32[256,128]{1,0:T(8,128)S(1)}, f32[256,128]{1,0:T(8,128)}, u32[]{:S(2)}) copy-start(f32[256,128]{1,0:T(8,128)} %param.11) | copy-start | bytes 393220
  37.4 21.8 %all-to-all-start.1 = ((f32[32,8,128]{2,1,0:T(8,128)}), f32[32,8,128]{2,1,0:T(8,128)S(1)}, u32[]{:S(2)}, u32[]{:S(2)}) async-start(f32[32,8,128]{2,1,0:T(8,128)} %bitcast.15), calls=%async_computation.1 | async-start | bytes 262144 | tf_op jit(solution)/shard_map/all_to_all | solution.py:26
  60.3 15.8 %all-to-all-start.2 = ((f32[4,64,256]{2,1,0:T(8,128)}), f32[4,64,256]{2,1,0:T(8,128)S(1)}, u32[]{:S(2)}, u32[]{:S(2)}) async-start(f32[4,64,256]{2,1,0:T(8,128)} %broadcast_in_dim.12), calls=%async_computation.2 | async-start | bytes 524288 | tf_op jit(solution)/shard_map/all_to_all | solution.py:26
  63.9 0.9 slice-start
  76.2 8.9 %collective-permute-start.1 = (f32[64,256]{1,0:T(8,128)S(1)}, f32[64,256]{1,0:T(8,128)S(1)}, u32[]{:S(2)}, u32[]{:S(2)}) collective-permute-start(f32[64,256]{1,0:T(8,128)S(1)} %reduce_sum.46), channel_id=1, source_target_pairs={{0,16},{16,0},{1,17},{17,1},{2,18},{18,2},{3,19},{19,3},{4,20},{20... | collective-permute-start | bytes 196616 | tf_op jit(solution)/shard_map/ppermute | solution.py:22
  99.5 13.2 %collective-permute-start.2 = (f32[8,512]{1,0:T(8,128)S(1)}, f32[8,512]{1,0:T(8,128)S(1)}, u32[]{:S(2)}, u32[]{:S(2)}) collective-permute-start(f32[8,512]{1,0:T(8,128)S(1)} %reduce_sum.47), channel_id=1, source_target_pairs={{0,64},{64,0},{1,65},{65,1},{2,66},{66,2},{3,67},{67,3},{4,68},{68... | collective-permute-start | bytes 49160 | tf_op jit(solution)/shard_map/ppermute | solution.py:22
  113.3 10.6 %all-to-all-start.4 = ((f32[8,8,512]{2,1,0:T(8,128)}), f32[8,8,512]{2,1,0:T(8,128)S(1)}, u32[]{:S(2)}, u32[]{:S(2)}) async-start(f32[8,8,512]{2,1,0:T(8,128)} %broadcast_in_dim.13), calls=%async_computation.4 | async-start | bytes 262144 | tf_op jit(solution)/shard_map/all_to_all | solution.py:26
  143.9 19.3 %collective-permute-start.3 = (f32[64,512]{1,0:T(8,128)S(1)}, f32[64,512]{1,0:T(8,128)S(1)}, u32[]{:S(2)}, u32[]{:S(2)}) collective-permute-start(f32[64,512]{1,0:T(8,128)S(1)} %reduce_sum.48), channel_id=1, source_target_pairs={{0,16},{16,0},{1,17},{17,1},{2,18},{18,2},{3,19},{19,3},{4,20},{20... | collective-permute-start | bytes 393224 | tf_op jit(solution)/shard_map/ppermute | solution.py:22
  164.8 14.1 %all-to-all-start.6 = ((f32[32,8,256]{2,1,0:T(8,128)}), f32[32,8,256]{2,1,0:T(8,128)S(1)}, u32[]{:S(2)}, u32[]{:S(2)}) async-start(f32[32,8,256]{2,1,0:T(8,128)} %bitcast.35), calls=%async_computation.6 | async-start | bytes 524288 | tf_op jit(solution)/shard_map/all_to_all | solution.py:26
  179.0 13.2 %collective-permute-start.4 = (f32[16,256]{1,0:T(8,128)S(1)}, f32[16,256]{1,0:T(8,128)S(1)}, u32[]{:S(2)}, u32[]{:S(2)}) collective-permute-start(f32[16,256]{1,0:T(8,128)S(1)} %bitcast.99), channel_id=1, source_target_pairs={{0,64},{64,0},{1,65},{65,1},{2,66},{66,2},{3,67},{67,3},{4,68},{68... | collective-permute-start | bytes 49160 | tf_op jit(solution)/shard_map/ppermute | solution.py:89
Sparse Core Ops, SparseCore 0:
  35.4 27.5 all-gather.3

commit v2 on v1

--- a/solution.py
+++ b/solution.py
@@ -30,40 +30,49 @@
     return shot(jnp.broadcast_to(a[None], (n, *a.shape)), axes)
 
 
-def sum_ctr(a):
-    a = jnp.sum(spread(a, "z", 4), 0)
-    return swap_sum(a, "w")
-
-
-def column_block(a, rows):
-    a = a.reshape(4, 2, 2, 4, 4, rows)
-    a = lax.dynamic_index_in_dim(a, lax.axis_index("y"), 3, keepdims=False)
-    return a.transpose(0, 2, 1, 3, 4).reshape(64, rows)
+def pick(first, count):
+    row = lax.broadcasted_iota(jnp.int32, (count, 256), 0) + first
+    column = lax.broadcasted_iota(jnp.int32, (count, 256), 1)
+    x, c, h, t = row // 16, row // 8 % 2, row // 4 % 2, row % 4
+    return column == ((x * 2 + h) * 2 + c) * 16 + lax.axis_index("y") * 4 + t
 
 
 def local(points, labels, centres, coeffs, diag_inverse, off_block):
     part = dot(coeffs[1], diag_inverse[1], (0,), (1,))
     part = part.reshape(4, 2, 2, 16, 128).transpose(0, 2, 1, 3, 4).reshape(8, 32, 128)
     part = jnp.sum(shot(part, ("x", "c")), 0)
+
+    off_wide = off_block.reshape(2, 128, 128).transpose(1, 0, 2).reshape(128, 256)
+    own = jnp.concatenate([off_wide, diag_inverse[0], centres.reshape(256, 256)], 0)
+    part, own = lax.optimization_barrier((part, own))
+    blocks = spread(own, "y", 4)
+    off_y = blocks[:, :128].reshape(4, 128, 2, 128).transpose(2, 1, 0, 3).reshape(256, 512)
+    diag_y = blocks[:, 128:256].reshape(512, 256)
+
     part = swap_sum(part, "h")
     part = part.reshape(2, 4, 4, 128).transpose(1, 0, 2, 3).reshape(1, 4, 8, 128)
     part = jnp.broadcast_to(part, (8, 4, 8, 128)).reshape(32, 8, 128)
     second = shot(part, ("x", "c", "y"))
     second = second.reshape(8, 4, 8, 128).transpose(0, 2, 1, 3).reshape(64, 512)
 
-    off_y = lax.all_gather(off_block, "y", axis=1, tiled=True)
-    diag_y = lax.all_gather(diag_inverse[0], "y", axis=0, tiled=True)
-    centres_y = lax.all_gather(centres, "y", axis=0)
-
-    carried = sum_ctr(dot(second, off_y, (1,), (1,)))
-    rest = column_block(coeffs[0].T, 256) - carried
-    first = dot(rest, diag_y, (1,), (1,))
-    first = jnp.sum(shot(first.reshape(8, 8, 512), ("x", "c")), 0)
+    carried = dot(second, off_y, (1,), (1,))
+    carried = jnp.sum(spread(carried, "z", 4), 0)
+    carried = swap_sum(carried, "w")
+    chosen = pick(0, 64).astype(jnp.float32)
+    rest = lax.dot_general(
+        chosen,
+        coeffs[0],
+        (((1,), (1,)), ((), ())),
+        precision=lax.Precision.HIGHEST,
+        preferred_element_type=jnp.float32,
+    )
+    first = dot(rest - carried, diag_y, (1,), (1,))
+    first = swap_sum(first, "c")
+    first = jnp.sum(spread(first, "x", 4), 0)
     first = swap_sum(first, "h")
-    first = spread(first, ("x", "c"), 8).reshape(64, 512)
 
     def kernel_tile(panel):
-        flat = centres_y[:, panel].reshape(512, 256)
+        flat = blocks[:, 256 + 128 * panel : 384 + 128 * panel].reshape(512, 256)
         score = dot(points, flat, (1,), (1,)) / math.sqrt(points.shape[1])
         return score + score * score * score / 3.0
 
@@ -71,9 +80,14 @@
     total_centres = 2 * 512 * 8
     pred_scale = 1.0 / (2.0 * math.sqrt(total_centres))
     pred = dot(first, kernel0, (1,), (1,)) + dot(second, kernel1, (1,), (1,))
-    pred = sum_ctr(pred)
-    target = column_block(labels.astype(jnp.float32).T, 512)
+    pred = jnp.sum(shot(pred.reshape(4, 16, 512), "z"), 0)
+    pred = swap_sum(pred, "w")
+    quarter = pick(lax.axis_index("z") * 16, 16).astype(labels.dtype)
+    target = lax.dot_general(
+        quarter, labels, (((1,), (1,)), ((), ())), preferred_element_type=jnp.float32
+    )
     weights = jnp.tanh(pred * pred_scale - target)
+    weights = spread(weights, "z", 4).reshape(64, 512)
 
     total_points = points.shape[0] * 16
     scale = 1.0 / (2.0 * math.sqrt(total_points))

time: 201 us -> 190 us (0.945)
  blocking collectives: 74.2 us -> 7.61 us
  starting transfers between devices: 69.5 us -> 101 us
  waiting for transfers between devices: 24.7 us -> 52.2 us
  between operations: 13.7 us -> 0.42 us
  matrix products: 4.56 us -> 12.5 us
  local copies, waits for them, and re-layouts: 10.4 us -> 14.8 us
  other arithmetic: 2.62 us -> 0.3 us
    all_to_all x3 -> x1, blocking collectives: 47.8 us -> 7.61 us  [shot(): return lax.all_to_all(a, axes, 0, 0, tiled=True)]
    all_to_all x4 -> x7, waiting for transfers between devices: 10.7 us -> 44.2 us  [shot(): return lax.all_to_all(a, axes, 0, 0, tiled=True)]
    all_gather x2 -> x0, blocking collectives: 26.4 us -> none  [the longest x1 15.1 us: local(): off_y = lax.all_gather(off_block, 'y', axis=1, tiled=True)]
    all_to_all x4 -> x7, starting transfers between devices: 20.7 us -> 39.8 us  [shot(): return lax.all_to_all(a, axes, 0, 0, tiled=True)]
    ppermute x4 -> x5, starting transfers between devices: 38.7 us -> 50.1 us  [swap_sum(): return a + lax.ppermute(a, axis, [(0, 1), (1, 0)])]
    dot_general x9, matrix products: 4.56 us -> 11.9 us  [dot(): lax.dot_general(a, b, ((ca, cb), ((), ())), precision=HIGH, preferred_ele...]
    ppermute x4 -> x5, waiting for transfers between devices: 10.9 us -> 6 us  [swap_sum(): return a + lax.ppermute(a, axis, [(0, 1), (1, 0)])]
    slice x3 -> x4, local copies, waits for them, and re-layouts: 2.09 us -> 4.52 us  [the longest x2 3.07 us: kernel_tile(): flat = blocks[:, 256 + 128 * panel:384 + 128 * panel].reshape(512, 256)]
  transfers between devices with their start and end apart: 10 -> 13, of which waited for: 7 -> 12; matrix products, arithmetic and copies ran while one was open for 6% -> 8% of each run, Pallas kernels for 0% -> 0%
where the time goes in v2:
time: 190 us; the launch traced here: 189 us
  starting transfers between devices  101 us (53%)
  waiting for transfers between devices  52.2 us (27%)
  local copies, waits for them, and re-layouts  14.8 us (8%)
  matrix products  12.5 us (7%)
  blocking collectives  7.61 us (4%)
    ppermute x5, starting transfers between devices, swap_sum(): return a + lax.ppermute(a, axis, [(0, 1), (1, 0)])  50.1 us
    all_to_all x7, waiting for transfers between devices, shot(): return lax.all_to_all(a, axes, 0, 0, tiled=True)  44.2 us
    all_to_all x7, starting transfers between devices, shot(): return lax.all_to_all(a, axes, 0, 0, tiled=True)  39.8 us
    dot_general x9, matrix products, dot(): lax.dot_general(a, b, ((ca, cb), ((), ())), precision=HIGH, preferred_ele...  11.9 us
    ppermute x1, starting transfers between devices, local(): mine = (mine + lax.ppermute(other, 'h', [(0, 1), (1, 0)])) * scale  11.2 us
    all_to_all x1, blocking collectives, shot(): return lax.all_to_all(a, axes, 0, 0, tiled=True)  7.61 us
    ppermute x5, waiting for transfers between devices, swap_sum(): return a + lax.ppermute(a, axis, [(0, 1), (1, 0)])  6 us
  transfers between devices with their start and end apart: 13, of which 12 were waited for; matrix products, arithmetic and copies ran while one was open for 8% of the time, Pallas kernels for 0%

profile of v2, /device:TPU:1, one launch (start us, length us, event | category | flops | bytes accessed | tf_op | source)
XLA Modules:
  0.0 188.9 jit_solution(12575220716369234416)
XLA Ops:
  0.0 1.1 slice_bitcast_fusion
  1.2 1.2 convolution_bitcast_fusion
  2.4 0.7 copy.61
  3.1 10.1 %all-to-all-start = ((f32[8,32,128]{2,1,0:T(8,128)}), f32[8,32,128]{2,1,0:T(8,128)S(1)}, u32[]{:S(2)}, u32[]{:S(2)}) async-start(f32[8,32,128]{2,1,0:T(8,128)} %bitcast.8), calls=%async_computation | async-start | bytes 262144 | tf_op jit(solution)/shard_map/all_to_all | solution.py:26
  13.7 4.9 %all-to-all-done = f32[8,32,128]{2,1,0:T(8,128)S(1)} async-done(((f32[8,32,128]{2,1,0:T(8,128)}), f32[8,32,128]{2,1,0:T(8,128)S(1)}, u32[]{:S(2)}, u32[]{:S(2)}) %all-to-all-start) | async-done | bytes 131104 | tf_op jit(solution)/shard_map/all_to_all | solution.py:26
  18.5 1.6 broadcast_in_dim.14
  20.2 3.6 %all-to-all-start.2 = ((f32[4,512,256]{1,2,0:T(8,128)}), f32[4,512,256]{1,2,0:T(8,128)S(1)}, u32[]{:S(2)}, u32[]{:S(2)}) async-start(f32[4,512,256]{1,2,0:T(8,128)} %broadcast_in_dim.14), calls=%async_computation.2 | async-start | bytes 4194304 | tf_op jit(solution)/shard_map/all_to_all | solution.py:26
  23.8 11.6 %collective-permute-start = (f32[32,128]{1,0:T(8,128)S(1)}, f32[32,128]{1,0:T(8,128)S(1)}, u32[]{:S(2)}, u32[]{:S(2)}) collective-permute-start(f32[32,128]{1,0:T(8,128)S(1)} %reduce_sum.45), channel_id=1, source_target_pairs={{0,64},{64,0},{1,65},{65,1},{2,66},{66,2},{3,67},{67,3},{4,68},{68... | collective-permute-start | bytes 49160 | tf_op jit(solution)/shard_map/ppermute | solution.py:22
  35.4 1.6 collective-permute-done
  37.1 12.2 %all-to-all-done.2 = f32[4,512,256]{1,2,0:T(8,128)S(1)} async-done(((f32[4,512,256]{1,2,0:T(8,128)}), f32[4,512,256]{1,2,0:T(8,128)S(1)}, u32[]{:S(2)}, u32[]{:S(2)}) %all-to-all-start.2) | async-done | bytes 2097184 | tf_op jit(solution)/shard_map/all_to_all | solution.py:26
  49.2 0.7 broadcast_in_dim.13
  49.9 5.3 %all-to-all-start.1 = ((f32[32,8,128]{2,1,0:T(8,128)}), f32[32,8,128]{2,1,0:T(8,128)S(1)}, u32[]{:S(2)}, u32[]{:S(2)}) async-start(f32[32,8,128]{2,1,0:T(8,128)} %bitcast.17), calls=%async_computation.1 | async-start | bytes 262144 | tf_op jit(solution)/shard_map/all_to_all | solution.py:26
  55.2 1.3 fusion.107
  56.5 1.4 copy.66
  57.8 5.0 %all-to-all-done.1 = f32[32,8,128]{2,1,0:T(8,128)S(1)} async-done(((f32[32,8,128]{2,1,0:T(8,128)}), f32[32,8,128]{2,1,0:T(8,128)S(1)}, u32[]{:S(2)}, u32[]{:S(2)}) %all-to-all-start.1) | async-done | bytes 131104 | tf_op jit(solution)/shard_map/all_to_all | solution.py:26
  62.9 0.4 fusion.13
  63.3 0.7 broadcast_in_dim.15
  64.0 3.4 %all-to-all-start.3 = ((f32[4,64,256]{2,1,0:T(8,128)}), f32[4,64,256]{2,1,0:T(8,128)S(1)}, u32[]{:S(2)}, u32[]{:S(2)}) async-start(f32[4,64,256]{2,1,0:T(8,128)} %broadcast_in_dim.15), calls=%async_computation.3 | async-start | bytes 524288 | tf_op jit(solution)/shard_map/all_to_all | solution.py:26
  67.5 7.2 %all-to-all-done.3 = f32[4,64,256]{2,1,0:T(8,128)S(1)} async-done(((f32[4,64,256]{2,1,0:T(8,128)}), f32[4,64,256]{2,1,0:T(8,128)S(1)}, u32[]{:S(2)}, u32[]{:S(2)}) %all-to-all-start.3) | async-done | bytes 262176 | tf_op jit(solution)/shard_map/all_to_all | solution.py:26
  74.7 7.5 %collective-permute-start.1 = (f32[64,256]{1,0:T(8,128)S(1)}, f32[64,256]{1,0:T(8,128)S(1)}, u32[]{:S(2)}, u32[]{:S(2)}) collective-permute-start(f32[64,256]{1,0:T(8,128)S(1)} %reduce_sum.46), channel_id=1, source_target_pairs={{0,16},{16,0},{1,17},{17,1},{2,18},{18,2},{3,19},{19,3},{4,20},{20... | collective-permute-start | bytes 196616 | tf_op jit(solution)/shard_map/ppermute | solution.py:22
  82.7 2.2 %collective-permute-done.1 = f32[64,256]{1,0:T(8,128)S(1)} collective-permute-done((f32[64,256]{1,0:T(8,128)S(1)}, f32[64,256]{1,0:T(8,128)S(1)}, u32[]{:S(2)}, u32[]{:S(2)}) %collective-permute-start.1) | collective-permute-done | bytes 65568 | tf_op jit(solution)/shard_map/ppermute | solution.py:22
  84.9 0.4 fusion.33
  85.3 6.2 %collective-permute-start.2 = (f32[64,512]{1,0:T(8,128)S(1)}, f32[64,512]{1,0:T(8,128)S(1)}, u32[]{:S(2)}, u32[]{:S(2)}) collective-permute-start(f32[64,512]{1,0:T(8,128)S(1)} %fusion.33), channel_id=1, source_target_pairs={{0,32},{32,0},{1,33},{33,1},{2,34},{34,2},{3,35},{35,3},{4,36},{36... | collective-permute-start | bytes 393224 | tf_op jit(solution)/shard_map/ppermute | solution.py:22
  91.5 1.0 copy.68
  92.5 0.9 broadcast_in_dim.16
  93.4 3.5 %all-to-all-start.4 = ((f32[4,64,512]{2,1,0:T(8,128)}), f32[4,64,512]{2,1,0:T(8,128)S(1)}, u32[]{:S(2)}, u32[]{:S(2)}) async-start(f32[4,64,512]{2,1,0:T(8,128)} %broadcast_in_dim.16), calls=%async_computation.4 | async-start | bytes 1048576 | tf_op jit(solution)/shard_map/all_to_all | solution.py:26
  96.9 1.8 fusion.8
  98.6 2.1 %copy.70 = f32[4,128,256]{2,1,0:T(8,128)} copy(f32[4,128,256]{1,2,0:T(8,128)} %get-tuple-element.10) | data formatting | bytes 1048576 | tf_op jit(solution)/shard_map/slice | solution.py:75
  100.7 1.3 copy.69
  102.0 2.7 %fusion.10 = (f32[512,512]{1,0:T(8,128)S(1)}, f32[512,512]{1,0:T(8,128)}) fusion(f32[512,256]{1,0:T(8,128)} %bitcast.106, f32[512,256]{1,0:T(8,128)S(1)} %copy-done), kind=kOutput, calls=%fused_computation.18 | convolution fusion | flops 403963904 | bytes 3145728 | tf_op jit(solution)/shard_map/dot_general | solution.py:16
  104.8 1.4 all-to-all-done.4
  106.2 11.8 %collective-permute-start.3 = (f32[64,512]{1,0:T(8,128)S(1)}, f32[64,512]{1,0:T(8,128)S(1)}, u32[]{:S(2)}, u32[]{:S(2)}) collective-permute-start(f32[64,512]{1,0:T(8,128)S(1)} %reduce_sum.47), channel_id=1, source_target_pairs={{0,64},{64,0},{1,65},{65,1},{2,66},{66,2},{3,67},{67,3},{4,68},{68... | collective-permute-start | bytes 393224 | tf_op jit(solution)/shard_map/ppermute | solution.py:22
  118.0 1.8 fusion.5
  119.8 1.1 collective-permute-done.3
  120.9 2.5 %convolution_add_fusion = f32[64,512]{1,0:T(8,128)} fusion(f32[64,512]{1,0:T(8,128)S(1)} %fusion.5, f32[512,512]{0,1:T(8,128)} %copy.69, f32[64,512]{1,0:T(8,128)S(1)} %reduce_sum.47, f32[64,512]{1,0:T(8,128)S(1)} %collective-permute-done.3), kind=kOutput, calls=%fused_computation.9 | convolution fusion | flops 101777408 | bytes 1572864 | tf_op jit(solution)/shard_map/dot_general | solution.py:16
  123.4 3.3 %all-to-all-start.5 = ((f32[4,16,512]{2,1,0:T(8,128)}), f32[4,16,512]{2,1,0:T(8,128)S(1)}, u32[]{:S(2)}, u32[]{:S(2)}) async-start(f32[4,16,512]{2,1,0:T(8,128)} %bitcast.30), calls=%async_computation.5 | async-start | bytes 262144 | tf_op jit(solution)/shard_map/all_to_all | solution.py:26
  126.8 4.7 %all-to-all-done.5 = f32[4,16,512]{2,1,0:T(8,128)S(1)} async-done(((f32[4,16,512]{2,1,0:T(8,128)}), f32[4,16,512]{2,1,0:T(8,128)S(1)}, u32[]{:S(2)}, u32[]{:S(2)}) %all-to-all-start.5) | async-done | bytes 131104 | tf_op jit(solution)/shard_map/all_to_all | solution.py:26
  131.5 13.0 %collective-permute-start.4 = (f32[16,512]{1,0:T(8,128)S(1)}, f32[16,512]{1,0:T(8,128)S(1)}, u32[]{:S(2)}, u32[]{:S(2)}) collective-permute-start(f32[16,512]{1,0:T(8,128)S(1)} %reduce_sum.48), channel_id=1, source_target_pairs={{0,16},{16,0},{1,17},{17,1},{2,18},{18,2},{3,19},{19,3},{4,20},{20... | collective-permute-start | bytes 98312 | tf_op jit(solution)/shard_map/ppermute | solution.py:22
  144.7 1.1 collective-permute-done.4
  145.8 7.6 %all_to_all.40 = f32[4,16,512]{2,1,0:T(8,128)S(1)} all-to-all(f32[4,16,512]{2,1,0:T(8,128)S(1)} %broadcast_in_dim.17), channel_id=1, replica_groups=mesh['x'=4,'h'=2,'c'=2,'w'=2,'z'=4,'y'=4] {'z'}, dimensions={0} | all-to-all | bytes 262144 | tf_op jit(solution)/shard_map/all_to_all | solution.py:26
  153.4 0.6 convolution_bitcast_fusion.2
  154.1 0.6 convolution_bitcast_fusion.1
  154.7 0.7 copy.72
  155.4 10.6 %all-to-all-start.7 = ((f32[32,8,256]{2,1,0:T(8,128)}), f32[32,8,256]{2,1,0:T(8,128)S(1)}, u32[]{:S(2)}, u32[]{:S(2)}) async-start(f32[32,8,256]{2,1,0:T(8,128)} %bitcast.43), calls=%async_computation.7 | async-start | bytes 524288 | tf_op jit(solution)/shard_map/all_to_all | solution.py:26
  166.0 8.9 %all-to-all-done.7 = f32[32,8,256]{2,1,0:T(8,128)S(1)} async-done(((f32[32,8,256]{2,1,0:T(8,128)}), f32[32,8,256]{2,1,0:T(8,128)S(1)}, u32[]{:S(2)}, u32[]{:S(2)}) %all-to-all-start.7) | async-done | bytes 262176 | tf_op jit(solution)/shard_map/all_to_all | solution.py:26
  175.1 11.2 %collective-permute-start.5 = (f32[16,256]{1,0:T(8,128)S(1)}, f32[16,256]{1,0:T(8,128)S(1)}, u32[]{:S(2)}, u32[]{:S(2)}) collective-permute-start(f32[16,256]{1,0:T(8,128)S(1)} %bitcast.122), channel_id=1, source_target_pairs={{0,64},{64,0},{1,65},{65,1},{2,66},{66,2},{3,67},{67,3},{4,68},{68... | collective-permute-start | bytes 49160 | tf_op jit(solution)/shard_map/ppermute | solution.py:103
  186.3 2.0 %collective-permute-done.5 = f32[16,256]{1,0:T(8,128)S(1)} collective-permute-done((f32[16,256]{1,0:T(8,128)S(1)}, f32[16,256]{1,0:T(8,128)S(1)}, u32[]{:S(2)}, u32[]{:S(2)}) %collective-permute-start.5) | collective-permute-done | bytes 16416 | tf_op jit(solution)/shard_map/ppermute | solution.py:103
  188.3 0.6 copy.75
  (53 shorter events, 1.6 us)
Async XLA Ops:
  0.0 96.8 %copy-start = (f32[512,256]{1,0:T(8,128)S(1)}, f32[512,256]{1,0:T(8,128)}, u32[]{:S(2)}) copy-start(f32[512,256]{1,0:T(8,128)} %param.6) | copy-start | bytes 1572868
  0.0 13.2 %copy-start.3 = (f32[2,128,256]{2,1,0:T(8,128)S(1)}, f32[2,128,256]{2,1,0:T(8,128)}, u32[]{:S(2)}) copy-start(f32[2,128,256]{2,1,0:T(8,128)} %param.10) | copy-start | bytes 786436
  0.0 13.3 %copy-start.2 = (f32[2,128,256]{2,1,0:T(8,128)S(1)}, f32[2,128,256]{2,1,0:T(8,128)}, u32[]{:S(2)}) copy-start(f32[2,128,256]{2,1,0:T(8,128)} %param.8) | copy-start | bytes 786436
  0.0 13.5 %copy-start.5 = (f32[256,128]{1,0:T(8,128)S(1)}, f32[256,128]{1,0:T(8,128)}, u32[]{:S(2)}) copy-start(f32[256,128]{1,0:T(8,128)} %param.11) | copy-start | bytes 393220
  3.1 15.4 %all-to-all-start = ((f32[8,32,128]{2,1,0:T(8,128)}), f32[8,32,128]{2,1,0:T(8,128)S(1)}, u32[]{:S(2)}, u32[]{:S(2)}) async-start(f32[8,32,128]{2,1,0:T(8,128)} %bitcast.8), calls=%async_computation | async-start | bytes 262144 | tf_op jit(solution)/shard_map/all_to_all | solution.py:26
  20.2 29.1 %all-to-all-start.2 = ((f32[4,512,256]{1,2,0:T(8,128)}), f32[4,512,256]{1,2,0:T(8,128)S(1)}, u32[]{:S(2)}, u32[]{:S(2)}) async-start(f32[4,512,256]{1,2,0:T(8,128)} %broadcast_in_dim.14), calls=%async_computation.2 | async-start | bytes 4194304 | tf_op jit(solution)/shard_map/all_to_all | solution.py:26
  23.8 13.3 %collective-permute-start = (f32[32,128]{1,0:T(8,128)S(1)}, f32[32,128]{1,0:T(8,128)S(1)}, u32[]{:S(2)}, u32[]{:S(2)}) collective-permute-start(f32[32,128]{1,0:T(8,128)S(1)} %reduce_sum.45), channel_id=1, source_target_pairs={{0,64},{64,0},{1,65},{65,1},{2,66},{66,2},{3,67},{67,3},{4,68},{68... | collective-permute-start | bytes 49160 | tf_op jit(solution)/shard_map/ppermute | solution.py:22
  49.9 13.0 %all-to-all-start.1 = ((f32[32,8,128]{2,1,0:T(8,128)}), f32[32,8,128]{2,1,0:T(8,128)S(1)}, u32[]{:S(2)}, u32[]{:S(2)}) async-start(f32[32,8,128]{2,1,0:T(8,128)} %bitcast.17), calls=%async_computation.1 | async-start | bytes 262144 | tf_op jit(solution)/shard_map/all_to_all | solution.py:26
  56.5 25.7 %copy-start.4 = (f32[2,256,256]{2,1,0:T(8,128)S(1)}, f32[2,256,256]{2,1,0:T(8,128)}, u32[]{:S(2)}) copy-start(f32[2,256,256]{2,1,0:T(8,128)} %param.9) | copy-start | bytes 1572868
  56.5 26.0 %copy-start.1 = (f32[4,128,256]{1,2,0:T(8,128)S(1)}, f32[4,128,256]{1,2,0:T(8,128)}, u32[]{:S(2)}) copy-start(f32[4,128,256]{1,2,0:T(8,128)} %get-tuple-element.12) | copy-start | bytes 1572868
  64.0 10.7 %all-to-all-start.3 = ((f32[4,64,256]{2,1,0:T(8,128)}), f32[4,64,256]{2,1,0:T(8,128)S(1)}, u32[]{:S(2)}, u32[]{:S(2)}) async-start(f32[4,64,256]{2,1,0:T(8,128)} %broadcast_in_dim.15), calls=%async_computation.3 | async-start | bytes 524288 | tf_op jit(solution)/shard_map/all_to_all | solution.py:26
  74.7 10.2 %collective-permute-start.1 = (f32[64,256]{1,0:T(8,128)S(1)}, f32[64,256]{1,0:T(8,128)S(1)}, u32[]{:S(2)}, u32[]{:S(2)}) collective-permute-start(f32[64,256]{1,0:T(8,128)S(1)} %reduce_sum.46), channel_id=1, source_target_pairs={{0,16},{16,0},{1,17},{17,1},{2,18},{18,2},{3,19},{19,3},{4,20},{20... | collective-permute-start | bytes 196616 | tf_op jit(solution)/shard_map/ppermute | solution.py:22
  85.3 7.2 %collective-permute-start.2 = (f32[64,512]{1,0:T(8,128)S(1)}, f32[64,512]{1,0:T(8,128)S(1)}, u32[]{:S(2)}, u32[]{:S(2)}) collective-permute-start(f32[64,512]{1,0:T(8,128)S(1)} %fusion.33), channel_id=1, source_target_pairs={{0,32},{32,0},{1,33},{33,1},{2,34},{34,2},{3,35},{35,3},{4,36},{36... | collective-permute-start | bytes 393224 | tf_op jit(solution)/shard_map/ppermute | solution.py:22
  93.4 12.8 %all-to-all-start.4 = ((f32[4,64,512]{2,1,0:T(8,128)}), f32[4,64,512]{2,1,0:T(8,128)S(1)}, u32[]{:S(2)}, u32[]{:S(2)}) async-start(f32[4,64,512]{2,1,0:T(8,128)} %broadcast_in_dim.16), calls=%async_computation.4 | async-start | bytes 1048576 | tf_op jit(solution)/shard_map/all_to_all | solution.py:26
  106.2 38.3 %copy-start.6 = (bf16[512,256]{1,0:T(8,128)(2,1)S(1)}, bf16[512,256]{1,0:T(8,128)(2,1)}, u32[]{:S(2)}) copy-start(bf16[512,256]{1,0:T(8,128)(2,1)} %param.7) | copy-start | bytes 786436
  106.2 14.7 %collective-permute-start.3 = (f32[64,512]{1,0:T(8,128)S(1)}, f32[64,512]{1,0:T(8,128)S(1)}, u32[]{:S(2)}, u32[]{:S(2)}) collective-permute-start(f32[64,512]{1,0:T(8,128)S(1)} %reduce_sum.47), channel_id=1, source_target_pairs={{0,64},{64,0},{1,65},{65,1},{2,66},{66,2},{3,67},{67,3},{4,68},{68... | collective-permute-start | bytes 393224 | tf_op jit(solution)/shard_map/ppermute | solution.py:22
  123.4 8.1 %all-to-all-start.5 = ((f32[4,16,512]{2,1,0:T(8,128)}), f32[4,16,512]{2,1,0:T(8,128)S(1)}, u32[]{:S(2)}, u32[]{:S(2)}) async-start(f32[4,16,512]{2,1,0:T(8,128)} %bitcast.30), calls=%async_computation.5 | async-start | bytes 262144 | tf_op jit(solution)/shard_map/all_to_all | solution.py:26
  131.5 14.3 %collective-permute-start.4 = (f32[16,512]{1,0:T(8,128)S(1)}, f32[16,512]{1,0:T(8,128)S(1)}, u32[]{:S(2)}, u32[]{:S(2)}) collective-permute-start(f32[16,512]{1,0:T(8,128)S(1)} %reduce_sum.48), channel_id=1, source_target_pairs={{0,16},{16,0},{1,17},{17,1},{2,18},{18,2},{3,19},{19,3},{4,20},{20... | collective-permute-start | bytes 98312 | tf_op jit(solution)/shard_map/ppermute | solution.py:22
  155.4 19.5 %all-to-all-start.7 = ((f32[32,8,256]{2,1,0:T(8,128)}), f32[32,8,256]{2,1,0:T(8,128)S(1)}, u32[]{:S(2)}, u32[]{:S(2)}) async-start(f32[32,8,256]{2,1,0:T(8,128)} %bitcast.43), calls=%async_computation.7 | async-start | bytes 524288 | tf_op jit(solution)/shard_map/all_to_all | solution.py:26
  175.1 13.2 %collective-permute-start.5 = (f32[16,256]{1,0:T(8,128)S(1)}, f32[16,256]{1,0:T(8,128)S(1)}, u32[]{:S(2)}, u32[]{:S(2)}) collective-permute-start(f32[16,256]{1,0:T(8,128)S(1)} %bitcast.122), channel_id=1, source_target_pairs={{0,64},{64,0},{1,65},{65,1},{2,66},{66,2},{3,67},{67,3},{4,68},{68... | collective-permute-start | bytes 49160 | tf_op jit(solution)/shard_map/ppermute | solution.py:103

commit v3 on v2

--- a/solution.py
+++ b/solution.py
@@ -42,14 +42,11 @@
     part = part.reshape(4, 2, 2, 16, 128).transpose(0, 2, 1, 3, 4).reshape(8, 32, 128)
     part = jnp.sum(shot(part, ("x", "c")), 0)
 
-    off_wide = off_block.reshape(2, 128, 128).transpose(1, 0, 2).reshape(128, 256)
-    own = jnp.concatenate([off_wide, diag_inverse[0], centres.reshape(256, 256)], 0)
-    part, own = lax.optimization_barrier((part, own))
-    blocks = spread(own, "y", 4)
-    off_y = blocks[:, :128].reshape(4, 128, 2, 128).transpose(2, 1, 0, 3).reshape(256, 512)
-    diag_y = blocks[:, 128:256].reshape(512, 256)
-
+    part, off_block = lax.optimization_barrier((part, off_block))
+    off_y = spread(off_block, "y", 4)
     part = swap_sum(part, "h")
+    part, off_y = lax.optimization_barrier((part, off_y))
+    off_y = off_y.transpose(1, 0, 2).reshape(256, 512)
     part = part.reshape(2, 4, 4, 128).transpose(1, 0, 2, 3).reshape(1, 4, 8, 128)
     part = jnp.broadcast_to(part, (8, 4, 8, 128)).reshape(32, 8, 128)
     second = shot(part, ("x", "c", "y"))
@@ -57,6 +54,8 @@
 
     carried = dot(second, off_y, (1,), (1,))
     carried = jnp.sum(spread(carried, "z", 4), 0)
+    carried, diag = lax.optimization_barrier((carried, diag_inverse[0]))
+    diag_y = spread(diag, "y", 4).reshape(512, 256)
     carried = swap_sum(carried, "w")
     chosen = pick(0, 64).astype(jnp.float32)
     rest = lax.dot_general(
@@ -67,12 +66,15 @@
         preferred_element_type=jnp.float32,
     )
     first = dot(rest - carried, diag_y, (1,), (1,))
-    first = swap_sum(first, "c")
-    first = jnp.sum(spread(first, "x", 4), 0)
+    first = jnp.sum(shot(first.reshape(8, 8, 512), ("x", "c")), 0)
+    first, centres = lax.optimization_barrier((first, centres))
+    centres_y = spread(centres.reshape(256, 256), "y", 4).reshape(4, 2, 128, 256)
     first = swap_sum(first, "h")
+    first, centres_y = lax.optimization_barrier((first, centres_y))
+    first = spread(first, ("x", "c"), 8).reshape(64, 512)
 
     def kernel_tile(panel):
-        flat = blocks[:, 256 + 128 * panel : 384 + 128 * panel].reshape(512, 256)
+        flat = centres_y[:, panel].reshape(512, 256)
         score = dot(points, flat, (1,), (1,)) / math.sqrt(points.shape[1])
         return score + score * score * score / 3.0
 

time: 190 us -> 187 us (0.984)
  blocking collectives: 7.61 us -> 50.1 us
  waiting for transfers between devices: 52.2 us -> 29.4 us
  starting transfers between devices: 101 us -> 85.2 us
  local copies, waits for them, and re-layouts: 14.8 us -> 11.2 us
  matrix products: 12.5 us -> 9.26 us
    all_to_all x1 -> x4, blocking collectives: 7.61 us -> 50.1 us  [shot(): return lax.all_to_all(a, axes, 0, 0, tiled=True)]
    all_to_all x7, waiting for transfers between devices: 44.2 us -> 21.6 us  [shot(): return lax.all_to_all(a, axes, 0, 0, tiled=True)]
    ppermute x5 -> x4, starting transfers between devices: 50.1 us -> 39.1 us  [swap_sum(): return a + lax.ppermute(a, axis, [(0, 1), (1, 0)])]
    all_to_all x7, starting transfers between devices: 39.8 us -> 34.4 us  [shot(): return lax.all_to_all(a, axes, 0, 0, tiled=True)]
    slice x4 -> x1, local copies, waits for them, and re-layouts: 4.52 us -> 0.07 us  [kernel_tile(): flat = centres_y[:, panel].reshape(512, 256)]
    dot_general x9, matrix products: 11.9 us -> 8.74 us  [dot(): lax.dot_general(a, b, ((ca, cb), ((), ())), precision=HIGH, preferred_ele...]
    broadcast_in_dim x4 -> x6, local copies, waits for them, and re-layouts: 3.22 us -> 4.19 us  [spread(): return shot(jnp.broadcast_to(a[None], (n, *a.shape)), axes)]
    ppermute x5 -> x4, waiting for transfers between devices: 6 us -> 6.31 us  [swap_sum(): return a + lax.ppermute(a, axis, [(0, 1), (1, 0)])]
  transfers between devices with their start and end apart: 13 -> 12, of which waited for: 12 -> 9; matrix products, arithmetic and copies ran while one was open for 8% -> 3% of each run, Pallas kernels for 0% -> 0%
where the time goes in v3:
time: 187 us; the launch traced here: 186 us
  starting transfers between devices  85.2 us (46%)
  blocking collectives  50.1 us (27%)
  waiting for transfers between devices  29.4 us (16%)
  local copies, waits for them, and re-layouts  11.2 us (6%)
  matrix products  9.26 us (5%)
    all_to_all x4, blocking collectives, shot(): return lax.all_to_all(a, axes, 0, 0, tiled=True)  50.1 us
    ppermute x4, starting transfers between devices, swap_sum(): return a + lax.ppermute(a, axis, [(0, 1), (1, 0)])  39.1 us
    all_to_all x7, starting transfers between devices, shot(): return lax.all_to_all(a, axes, 0, 0, tiled=True)  34.4 us
    all_to_all x7, waiting for transfers between devices, shot(): return lax.all_to_all(a, axes, 0, 0, tiled=True)  21.6 us
    ppermute x1, starting transfers between devices, local(): mine = (mine + lax.ppermute(other, 'h', [(0, 1), (1, 0)])) * scale  11.7 us
    dot_general x9, matrix products, dot(): lax.dot_general(a, b, ((ca, cb), ((), ())), precision=HIGH, preferred_ele...  8.74 us
    ppermute x4, waiting for transfers between devices, swap_sum(): return a + lax.ppermute(a, axis, [(0, 1), (1, 0)])  6.31 us
    broadcast_in_dim x6, local copies, waits for them, and re-layouts, spread(): return shot(jnp.broadcast_to(a[None], (n, *a.shape)), axes)  4.19 us
  transfers between devices with their start and end apart: 12, of which 9 were waited for; matrix products, arithmetic and copies ran while one was open for 3% of the time, Pallas kernels for 0%

profile of v3, /device:TPU:1, one launch (start us, length us, event | category | flops | bytes accessed | tf_op | source)
XLA Modules:
  0.0 185.7 jit_solution(713871255350238911)
XLA Ops:
  0.0 1.0 slice_bitcast_fusion
  1.0 0.1 copy.36
  1.2 0.8 copy-done.3
  2.0 0.3 convolution_bitcast_fusion
  2.3 14.5 %all_to_all.55 = f32[8,32,128]{2,1,0:T(8,128)S(1)} all-to-all(f32[8,32,128]{2,1,0:T(8,128)S(1)} %bitcast.113), channel_id=1, replica_groups=mesh['x'=4,'h'=2,'c'=2,'w'=2,'z'=4,'y'=4] {'x','c'}, dimensions={0} | all-to-all | bytes 262144 | tf_op jit(solution)/shard_map/all_to_all | solution.py:26
  16.8 0.9 copy-done.5
  17.8 0.9 broadcast_in_dim.18
  18.7 3.5 %all-to-all-start.1 = ((f32[4,256,128]{1,2,0:T(8,128)}), f32[4,256,128]{1,2,0:T(8,128)S(1)}, u32[]{:S(2)}, u32[]{:S(2)}) async-start(f32[4,256,128]{1,2,0:T(8,128)} %broadcast_in_dim.18), calls=%async_computation.1 | async-start | bytes 1048576 | tf_op jit(solution)/shard_map/all_to_all | solution.py:26
  22.2 12.5 %collective-permute-start = (f32[32,128]{1,0:T(8,128)S(1)}, f32[32,128]{1,0:T(8,128)S(1)}, u32[]{:S(2)}, u32[]{:S(2)}) collective-permute-start(f32[32,128]{1,0:T(8,128)S(1)} %reduce_sum.45), channel_id=1, source_target_pairs={{0,64},{64,0},{1,65},{65,1},{2,66},{66,2},{3,67},{67,3},{4,68},{68... | collective-permute-start | bytes 49160 | tf_op jit(solution)/shard_map/ppermute | solution.py:22
  34.6 1.1 collective-permute-done
  35.8 14.9 %all_to_all.56 = f32[32,8,128]{2,1,0:T(8,128)S(1)} all-to-all(f32[32,8,128]{2,1,0:T(8,128)S(1)} %bitcast.114), channel_id=1, replica_groups=mesh['x'=4,'h'=2,'c'=2,'w'=2,'z'=4,'y'=4] {'x','c','y'}, dimensions={0} | all-to-all | bytes 262144 | tf_op jit(solution)/shard_map/all_to_all | solution.py:26
  50.8 0.3 fusion.108
  51.0 0.7 broadcast_in_dim.21
  51.7 3.4 %all-to-all-start.3 = ((f32[4,64,256]{2,1,0:T(8,128)}), f32[4,64,256]{2,1,0:T(8,128)S(1)}, u32[]{:S(2)}, u32[]{:S(2)}) async-start(f32[4,64,256]{2,1,0:T(8,128)} %broadcast_in_dim.21), calls=%async_computation.3 | async-start | bytes 524288 | tf_op jit(solution)/shard_map/all_to_all | solution.py:26
  55.2 7.2 %all-to-all-done.3 = f32[4,64,256]{2,1,0:T(8,128)S(1)} async-done(((f32[4,64,256]{2,1,0:T(8,128)}), f32[4,64,256]{2,1,0:T(8,128)S(1)}, u32[]{:S(2)}, u32[]{:S(2)}) %all-to-all-start.3) | async-done | bytes 262176 | tf_op jit(solution)/shard_map/all_to_all | solution.py:26
  62.5 0.9 broadcast_in_dim.22
  63.3 3.6 %all-to-all-start.4 = ((f32[4,128,256]{2,1,0:T(8,128)}), f32[4,128,256]{2,1,0:T(8,128)S(1)}, u32[]{:S(2)}, u32[]{:S(2)}) async-start(f32[4,128,256]{2,1,0:T(8,128)} %broadcast_in_dim.22), calls=%async_computation.4 | async-start | bytes 1048576 | tf_op jit(solution)/shard_map/all_to_all | solution.py:26
  66.9 8.1 %collective-permute-start.1 = (f32[64,256]{1,0:T(8,128)S(1)}, f32[64,256]{1,0:T(8,128)S(1)}, u32[]{:S(2)}, u32[]{:S(2)}) collective-permute-start(f32[64,256]{1,0:T(8,128)S(1)} %reduce_sum.46), channel_id=1, source_target_pairs={{0,16},{16,0},{1,17},{17,1},{2,18},{18,2},{3,19},{19,3},{4,20},{20... | collective-permute-start | bytes 196616 | tf_op jit(solution)/shard_map/ppermute | solution.py:22
  75.1 0.3 fusion.15
  75.4 1.9 %collective-permute-done.1 = f32[64,256]{1,0:T(8,128)S(1)} collective-permute-done((f32[64,256]{1,0:T(8,128)S(1)}, f32[64,256]{1,0:T(8,128)S(1)}, u32[]{:S(2)}, u32[]{:S(2)}) %collective-permute-start.1) | collective-permute-done | bytes 65568 | tf_op jit(solution)/shard_map/ppermute | solution.py:22
  77.3 0.4 fusion.30
  77.7 12.5 %all_to_all.57 = f32[8,8,512]{2,1,0:T(8,128)S(1)} all-to-all(f32[8,8,512]{2,1,0:T(8,128)S(1)} %fusion.30), channel_id=1, replica_groups=mesh['x'=4,'h'=2,'c'=2,'w'=2,'z'=4,'y'=4] {'x','c'}, dimensions={0} | all-to-all | bytes 262144 | tf_op jit(solution)/shard_map/all_to_all | solution.py:26
  90.3 1.1 broadcast_in_dim.24
  91.3 4.2 %all-to-all-start.6 = ((f32[4,256,256]{2,1,0:T(8,128)}), f32[4,256,256]{2,1,0:T(8,128)S(1)}, u32[]{:S(2)}, u32[]{:S(2)}) async-start(f32[4,256,256]{2,1,0:T(8,128)} %broadcast_in_dim.24), calls=%async_computation.6 | async-start | bytes 2097152 | tf_op jit(solution)/shard_map/all_to_all | solution.py:26
  95.5 11.7 %collective-permute-start.2 = (f32[8,512]{1,0:T(8,128)S(1)}, f32[8,512]{1,0:T(8,128)S(1)}, u32[]{:S(2)}, u32[]{:S(2)}) collective-permute-start(f32[8,512]{1,0:T(8,128)S(1)} %reduce_sum.47), channel_id=1, source_target_pairs={{0,64},{64,0},{1,65},{65,1},{2,66},{66,2},{3,67},{67,3},{4,68},{68... | collective-permute-start | bytes 49160 | tf_op jit(solution)/shard_map/ppermute | solution.py:22
  107.2 1.5 collective-permute-done.2
  108.7 0.8 all-to-all-done.6
  109.6 0.7 broadcast_in_dim.25
  110.2 5.3 %all-to-all-start.7 = ((f32[8,8,512]{2,1,0:T(8,128)}), f32[8,8,512]{2,1,0:T(8,128)S(1)}, u32[]{:S(2)}, u32[]{:S(2)}) async-start(f32[8,8,512]{2,1,0:T(8,128)} %broadcast_in_dim.25), calls=%async_computation.7 | async-start | bytes 262144 | tf_op jit(solution)/shard_map/all_to_all | solution.py:26
  115.6 1.7 fusion.8
  117.3 1.7 fusion.10
  119.0 2.6 %copy.40 = f32[512,512]{0,1:T(8,128)} copy(f32[512,512]{1,0:T(8,128)} %get-tuple-element.32) | data formatting | bytes 2097152 | tf_op jit(solution)/shard_map/div | solution.py:78
  121.6 2.0 %fusion.2 = f32[64,512]{1,0:T(8,128)S(1)} fusion(f32[512,512]{0,1:T(8,128)} %copy.40, f32[8,8,512]{2,1,0:T(8,128)S(1)} %all-to-all-done.7), kind=kOutput, calls=%fused_computation.12 | convolution fusion | flops 101711872 | bytes 1310720 | tf_op jit(solution)/shard_map/dot_general | solution.py:16
  123.5 1.2 convolution_add_fusion
  124.7 3.5 %all-to-all-start.8 = ((f32[4,16,512]{2,1,0:T(8,128)}), f32[4,16,512]{2,1,0:T(8,128)S(1)}, u32[]{:S(2)}, u32[]{:S(2)}) async-start(f32[4,16,512]{2,1,0:T(8,128)} %bitcast.31), calls=%async_computation.8 | async-start | bytes 262144 | tf_op jit(solution)/shard_map/all_to_all | solution.py:26
  128.3 4.8 %all-to-all-done.8 = f32[4,16,512]{2,1,0:T(8,128)S(1)} async-done(((f32[4,16,512]{2,1,0:T(8,128)}), f32[4,16,512]{2,1,0:T(8,128)S(1)}, u32[]{:S(2)}, u32[]{:S(2)}) %all-to-all-start.8) | async-done | bytes 131104 | tf_op jit(solution)/shard_map/all_to_all | solution.py:26
  133.1 6.8 %collective-permute-start.3 = (f32[16,512]{1,0:T(8,128)S(1)}, f32[16,512]{1,0:T(8,128)S(1)}, u32[]{:S(2)}, u32[]{:S(2)}) collective-permute-start(f32[16,512]{1,0:T(8,128)S(1)} %reduce_sum.48), channel_id=1, source_target_pairs={{0,16},{16,0},{1,17},{17,1},{2,18},{18,2},{3,19},{19,3},{4,20},{20... | collective-permute-start | bytes 98312 | tf_op jit(solution)/shard_map/ppermute | solution.py:22
  139.9 1.8 collective-permute-done.3
  141.6 0.2 subtract_tanh_fusion
  141.9 8.1 %all_to_all.58 = f32[4,16,512]{2,1,0:T(8,128)S(1)} all-to-all(f32[4,16,512]{2,1,0:T(8,128)S(1)} %broadcast_in_dim.52), channel_id=1, replica_groups=mesh['x'=4,'h'=2,'c'=2,'w'=2,'z'=4,'y'=4] {'z'}, dimensions={0} | all-to-all | bytes 262144 | tf_op jit(solution)/shard_map/all_to_all | solution.py:26
  150.0 0.6 convolution_bitcast_fusion.2
  150.6 0.6 convolution_bitcast_fusion.1
  151.2 0.7 copy.42
  152.0 11.0 %all-to-all-start.10 = ((f32[32,8,256]{2,1,0:T(8,128)}), f32[32,8,256]{2,1,0:T(8,128)S(1)}, u32[]{:S(2)}, u32[]{:S(2)}) async-start(f32[32,8,256]{2,1,0:T(8,128)} %bitcast.44), calls=%async_computation.10 | async-start | bytes 524288 | tf_op jit(solution)/shard_map/all_to_all | solution.py:26
  162.9 8.8 %all-to-all-done.10 = f32[32,8,256]{2,1,0:T(8,128)S(1)} async-done(((f32[32,8,256]{2,1,0:T(8,128)}), f32[32,8,256]{2,1,0:T(8,128)S(1)}, u32[]{:S(2)}, u32[]{:S(2)}) %all-to-all-start.10) | async-done | bytes 262176 | tf_op jit(solution)/shard_map/all_to_all | solution.py:26
  171.9 11.7 %collective-permute-start.4 = (f32[16,256]{1,0:T(8,128)S(1)}, f32[16,256]{1,0:T(8,128)S(1)}, u32[]{:S(2)}, u32[]{:S(2)}) collective-permute-start(f32[16,256]{1,0:T(8,128)S(1)} %bitcast.123), channel_id=1, source_target_pairs={{0,64},{64,0},{1,65},{65,1},{2,66},{66,2},{3,67},{67,3},{4,68},{68... | collective-permute-start | bytes 49160 | tf_op jit(solution)/shard_map/ppermute | solution.py:105
  183.6 1.5 collective-permute-done.4
  185.1 0.6 copy.45
  (48 shorter events, 0.5 us)
Async XLA Ops:
  0.0 115.6 %copy-start = (f32[512,256]{1,0:T(8,128)S(1)}, f32[512,256]{1,0:T(8,128)}, u32[]{:S(2)}) copy-start(f32[512,256]{1,0:T(8,128)} %param.6) | copy-start | bytes 1572868
  1.0 1.0 copy-start.3
  16.8 0.9 copy-start.5
  18.7 17.1 %all-to-all-start.1 = ((f32[4,256,128]{1,2,0:T(8,128)}), f32[4,256,128]{1,2,0:T(8,128)S(1)}, u32[]{:S(2)}, u32[]{:S(2)}) async-start(f32[4,256,128]{1,2,0:T(8,128)} %broadcast_in_dim.18), calls=%async_computation.1 | async-start | bytes 1048576 | tf_op jit(solution)/shard_map/all_to_all | solution.py:26
  22.2 13.6 %collective-permute-start = (f32[32,128]{1,0:T(8,128)S(1)}, f32[32,128]{1,0:T(8,128)S(1)}, u32[]{:S(2)}, u32[]{:S(2)}) collective-permute-start(f32[32,128]{1,0:T(8,128)S(1)} %reduce_sum.45), channel_id=1, source_target_pairs={{0,64},{64,0},{1,65},{65,1},{2,66},{66,2},{3,67},{67,3},{4,68},{68... | collective-permute-start | bytes 49160 | tf_op jit(solution)/shard_map/ppermute | solution.py:22
  51.7 10.7 %all-to-all-start.3 = ((f32[4,64,256]{2,1,0:T(8,128)}), f32[4,64,256]{2,1,0:T(8,128)S(1)}, u32[]{:S(2)}, u32[]{:S(2)}) async-start(f32[4,64,256]{2,1,0:T(8,128)} %broadcast_in_dim.21), calls=%async_computation.3 | async-start | bytes 524288 | tf_op jit(solution)/shard_map/all_to_all | solution.py:26
  63.3 11.8 %copy-start.4 = (f32[2,256,256]{2,1,0:T(8,128)S(1)}, f32[2,256,256]{2,1,0:T(8,128)}, u32[]{:S(2)}) copy-start(f32[2,256,256]{2,1,0:T(8,128)} %param.9) | copy-start | bytes 1572868
  63.3 14.0 %all-to-all-start.4 = ((f32[4,128,256]{2,1,0:T(8,128)}), f32[4,128,256]{2,1,0:T(8,128)S(1)}, u32[]{:S(2)}, u32[]{:S(2)}) async-start(f32[4,128,256]{2,1,0:T(8,128)} %broadcast_in_dim.22), calls=%async_computation.4 | async-start | bytes 1048576 | tf_op jit(solution)/shard_map/all_to_all | solution.py:26
  66.9 10.4 %collective-permute-start.1 = (f32[64,256]{1,0:T(8,128)S(1)}, f32[64,256]{1,0:T(8,128)S(1)}, u32[]{:S(2)}, u32[]{:S(2)}) collective-permute-start(f32[64,256]{1,0:T(8,128)S(1)} %reduce_sum.46), channel_id=1, source_target_pairs={{0,16},{16,0},{1,17},{17,1},{2,18},{18,2},{3,19},{19,3},{4,20},{20... | collective-permute-start | bytes 196616 | tf_op jit(solution)/shard_map/ppermute | solution.py:22
  77.7 12.5 %copy-start.2 = (f32[2,128,256]{2,1,0:T(8,128)S(1)}, f32[2,128,256]{2,1,0:T(8,128)}, u32[]{:S(2)}) copy-start(f32[2,128,256]{2,1,0:T(8,128)} %param.8) | copy-start | bytes 786436
  91.3 18.2 %all-to-all-start.6 = ((f32[4,256,256]{2,1,0:T(8,128)}), f32[4,256,256]{2,1,0:T(8,128)S(1)}, u32[]{:S(2)}, u32[]{:S(2)}) async-start(f32[4,256,256]{2,1,0:T(8,128)} %broadcast_in_dim.24), calls=%async_computation.6 | async-start | bytes 2097152 | tf_op jit(solution)/shard_map/all_to_all | solution.py:26
  95.5 13.2 %collective-permute-start.2 = (f32[8,512]{1,0:T(8,128)S(1)}, f32[8,512]{1,0:T(8,128)S(1)}, u32[]{:S(2)}, u32[]{:S(2)}) collective-permute-start(f32[8,512]{1,0:T(8,128)S(1)} %reduce_sum.47), channel_id=1, source_target_pairs={{0,64},{64,0},{1,65},{65,1},{2,66},{66,2},{3,67},{67,3},{4,68},{68... | collective-permute-start | bytes 49160 | tf_op jit(solution)/shard_map/ppermute | solution.py:22
  110.2 11.3 %all-to-all-start.7 = ((f32[8,8,512]{2,1,0:T(8,128)}), f32[8,8,512]{2,1,0:T(8,128)S(1)}, u32[]{:S(2)}, u32[]{:S(2)}) async-start(f32[8,8,512]{2,1,0:T(8,128)} %broadcast_in_dim.25), calls=%async_computation.7 | async-start | bytes 262144 | tf_op jit(solution)/shard_map/all_to_all | solution.py:26
  121.6 2.0 %copy-start.1 = (f32[512,512]{1,0:T(8,128)S(1)}, f32[512,512]{1,0:T(8,128)}, u32[]{:S(2)}) copy-start(f32[512,512]{1,0:T(8,128)} %get-tuple-element.30) | copy-start | bytes 3145732
  124.7 16.9 %copy-start.6 = (bf16[512,256]{1,0:T(8,128)(2,1)S(1)}, bf16[512,256]{1,0:T(8,128)(2,1)}, u32[]{:S(2)}) copy-start(bf16[512,256]{1,0:T(8,128)(2,1)} %param.7) | copy-start | bytes 786436
  124.7 8.3 %all-to-all-start.8 = ((f32[4,16,512]{2,1,0:T(8,128)}), f32[4,16,512]{2,1,0:T(8,128)S(1)}, u32[]{:S(2)}, u32[]{:S(2)}) async-start(f32[4,16,512]{2,1,0:T(8,128)} %bitcast.31), calls=%async_computation.8 | async-start | bytes 262144 | tf_op jit(solution)/shard_map/all_to_all | solution.py:26
  133.1 8.6 %collective-permute-start.3 = (f32[16,512]{1,0:T(8,128)S(1)}, f32[16,512]{1,0:T(8,128)S(1)}, u32[]{:S(2)}, u32[]{:S(2)}) collective-permute-start(f32[16,512]{1,0:T(8,128)S(1)} %reduce_sum.48), channel_id=1, source_target_pairs={{0,16},{16,0},{1,17},{17,1},{2,18},{18,2},{3,19},{19,3},{4,20},{20... | collective-permute-start | bytes 98312 | tf_op jit(solution)/shard_map/ppermute | solution.py:22
  152.0 19.8 %all-to-all-start.10 = ((f32[32,8,256]{2,1,0:T(8,128)}), f32[32,8,256]{2,1,0:T(8,128)S(1)}, u32[]{:S(2)}, u32[]{:S(2)}) async-start(f32[32,8,256]{2,1,0:T(8,128)} %bitcast.44), calls=%async_computation.10 | async-start | bytes 524288 | tf_op jit(solution)/shard_map/all_to_all | solution.py:26
  171.9 13.2 %collective-permute-start.4 = (f32[16,256]{1,0:T(8,128)S(1)}, f32[16,256]{1,0:T(8,128)S(1)}, u32[]{:S(2)}, u32[]{:S(2)}) collective-permute-start(f32[16,256]{1,0:T(8,128)S(1)} %bitcast.123), channel_id=1, source_target_pairs={{0,64},{64,0},{1,65},{65,1},{2,66},{66,2},{3,67},{67,3},{4,68},{68... | collective-permute-start | bytes 49160 | tf_op jit(solution)/shard_map/ppermute | solution.py:105

commit v4 on v1

v4 whole, which is shorter than its diff:
```python
import math

import jax
import jax.numpy as jnp
from jax import lax
from jax.sharding import Mesh
from jax.sharding import PartitionSpec as P

PTS = ("x", "h", "c")
CTR = ("w", "z", "y")
SIZES = {"x": 4, "h": 2, "c": 2, "w": 2, "z": 4, "y": 4}
HIGH = lax.Precision.HIGH


def dot(a, b, ca, cb):
    return lax.dot_general(
        a, b, (((ca,), (cb,)), ((), ())), precision=HIGH, preferred_element_type=jnp.float32
    )


def swap(a, axis):
    return lax.ppermute(a, axis, [(0, 1), (1, 0)])


def scatter_sum(a, axes, n):
    a = a.reshape(n, a.shape[0] // n, a.shape[1])
    return jnp.sum(lax.all_to_all(a, axes, 0, 0, tiled=True), 0)


def gather(a, axes, n):
    a = jnp.broadcast_to(a[None], (n, *a.shape))
    return lax.all_to_all(a, axes, 0, 0, tiled=True).reshape(-1, a.shape[2])


def sum_pts(a):
    a = scatter_sum(a, ("x", "c"), 8)
    a = a + swap(a, "h")
    return gather(a, ("x", "c"), 8)


def columns(a):
    rows = a.shape[0]
    return a.reshape(rows, 4, 2, 2, 16).transpose(1, 3, 2, 4, 0).reshape(256, rows)


def local(points, labels, centres, coeffs, diag_inverse, off_block):
    second = sum_pts(dot(columns(coeffs[1]), diag_inverse[1], 1, 1))

    carried = dot(second, off_block, 1, 1)
    carried = scatter_sum(carried, ("z", "y"), 16)
    carried = carried + swap(carried, "w")
    carried = gather(carried, ("z", "y"), 16)

    first = sum_pts(dot(columns(coeffs[0]) - carried, diag_inverse[0], 1, 1))

    solved = jnp.concatenate([first, second], 1)
    score = dot(points, centres.reshape(256, 256), 1, 1) / math.sqrt(points.shape[1])
    kernel = score + score * score * score / 3.0
    pred_scale = 1.0 / (2.0 * math.sqrt(256 * 32))
    pred = scatter_sum(dot(solved, kernel, 1, 1), ("z", "y"), 16)
    pred = pred + swap(pred, "w")

    block = lax.axis_index("z") * 4 + lax.axis_index("y")
    x, c, h = block // 4, block // 2 % 2, block % 2
    start = ((x * 2 + h) * 2 + c) * 16
    row = lax.broadcasted_iota(jnp.int32, (16, 256), 0)
    chosen = lax.broadcasted_iota(jnp.int32, (16, 256), 1) == row + start
    target = lax.dot_general(
        chosen.astype(labels.dtype),
        labels,
        (((1,), (1,)), ((), ())),
        preferred_element_type=jnp.float32,
    )
    weights = gather(jnp.tanh(pred * pred_scale - target), ("z", "y"), 16)

    scale = 1.0 / (2.0 * math.sqrt(points.shape[0] * 16))
    term = scatter_sum(dot(weights, kernel, 1, 0), ("x", "c"), 8).reshape(2, 16, 256)
    h = lax.axis_index("h")
    mine = lax.dynamic_index_in_dim(term, h, 0, keepdims=False)
    other = lax.dynamic_index_in_dim(term, 1 - h, 0, keepdims=False)
    mine = (mine + swap(other, "h")) * scale
    return mine.reshape(16, 2, 128).transpose(1, 2, 0)


def solution(mesh):
    fine = Mesh(mesh.devices.reshape(tuple(SIZES.values())), tuple(SIZES))
    return jax.shard_map(
        local,
        mesh=fine,
        in_specs=(
            P(PTS, None),
            P(PTS, None),
            P(None, CTR, None),
            P(None, PTS, None),
            P(None, CTR, PTS),
            P(PTS, CTR),
        ),
        out_specs=P(None, CTR, PTS),
        check_vma=False,
    )
```

time: 201 us -> 190 us (0.945)
  waiting for transfers between devices: 24.7 us -> 41.5 us
  between operations: 13.7 us -> 0.26 us
  blocking collectives: 74.2 us -> 67.1 us
  local copies, waits for them, and re-layouts: 10.4 us -> 4.44 us
  other arithmetic: 2.62 us -> 0.16 us
    all_gather x2 -> x0, blocking collectives: 26.4 us -> none  [the longest x1 15.1 us: local(): off_y = lax.all_gather(off_block, 'y', axis=1, tiled=True)]
    all_to_all x4, waiting for transfers between devices: 10.7 us -> 33.9 us  [the longest x2 20.3 us: scatter_sum(): return jnp.sum(lax.all_to_all(a, axes, 0, 0, tiled=True), 0)]
    all_to_all x3 -> x5, blocking collectives: 47.8 us -> 67.1 us  [the longest x3 40.1 us: scatter_sum(): return jnp.sum(lax.all_to_all(a, axes, 0, 0, tiled=True), 0)]
    ppermute x5, waiting for transfers between devices: 14 us -> 7.66 us  [swap(): return lax.ppermute(a, axis, [(0, 1), (1, 0)])]
    reshape x5 -> x0, local copies, waits for them, and re-layouts: 2.33 us -> none  [the longest x3 2.26 us: column_block(): a = a.reshape(4, 2, 2, 4, 4, rows)]
    transpose x9 -> x1, local copies, waits for them, and re-layouts: 2.24 us -> 0.02 us  [columns(): a.reshape(rows, 4, 2, 2, 16).transpose(1, 3, 2, 4, 0).reshape(256, rows)]
    dot_general x9 -> x7, matrix products: 4.56 us -> 3.75 us  [the longest x6 3.56 us: dot(): lax.dot_general(a, b, (((ca,), (cb,)), ((), ())), precision=HIGH, preferr...]
  transfers between devices with their start and end apart: 10 -> 9, of which waited for: 7 -> 9; matrix products, arithmetic and copies ran while one was open for 6% -> 0% of each run, Pallas kernels for 0% -> 0%
where the time goes in v4:
time: 190 us; the launch traced here: 188 us
  starting transfers between devices  71.2 us (37%)
  blocking collectives  67.1 us (35%)
  waiting for transfers between devices  41.5 us (22%)
  local copies, waits for them, and re-layouts  4.44 us (2%)
  matrix products  3.75 us (2%)
    ppermute x5, starting transfers between devices, swap(): return lax.ppermute(a, axis, [(0, 1), (1, 0)])  50.5 us
    all_to_all x3, blocking collectives, scatter_sum(): return jnp.sum(lax.all_to_all(a, axes, 0, 0, tiled=True), 0)  40.1 us
    all_to_all x2, blocking collectives, gather(): return lax.all_to_all(a, axes, 0, 0, tiled=True).reshape(-1, a.shape[2])  27.1 us
    all_to_all x2, waiting for transfers between devices, scatter_sum(): return jnp.sum(lax.all_to_all(a, axes, 0, 0, tiled=True), 0)  20.3 us
    all_to_all x2, waiting for transfers between devices, gather(): return lax.all_to_all(a, axes, 0, 0, tiled=True).reshape(-1, a.shape[2])  13.6 us
    all_to_all x2, starting transfers between devices, scatter_sum(): return jnp.sum(lax.all_to_all(a, axes, 0, 0, tiled=True), 0)  11.1 us
    all_to_all x2, starting transfers between devices, gather(): return lax.all_to_all(a, axes, 0, 0, tiled=True).reshape(-1, a.shape[2])  9.67 us
    ppermute x5, waiting for transfers between devices, swap(): return lax.ppermute(a, axis, [(0, 1), (1, 0)])  7.66 us
  transfers between devices with their start and end apart: 9, of which 9 were waited for; matrix products, arithmetic and copies ran while one was open for 0% of the time, Pallas kernels for 0%

profile of v4, /device:TPU:1, one launch (start us, length us, event | category | flops | bytes accessed | tf_op | source)
XLA Modules:
  0.0 188.5 jit_solution(15812063192505864276)
XLA Ops:
  0.0 0.0 copy-start
  0.0 1.1 fusion.20
  1.1 0.1 copy.21
  1.3 0.0 copy-start.3
  1.3 0.9 copy-done.3
  2.2 0.3 fusion.12
  2.5 14.5 %all_to_all.45 = f32[8,32,128]{2,1,0:T(8,128)S(1)} all-to-all(f32[8,32,128]{2,1,0:T(8,128)S(1)} %fusion.12), channel_id=1, replica_groups=mesh['x'=4,'h'=2,'c'=2,'w'=2,'z'=4,'y'=4] {'x','c'}, dimensions={0} | all-to-all | bytes 262144 | tf_op jit(solution)/shard_map/all_to_all | solution.py:27
  17.0 11.8 %collective-permute-start = (f32[32,128]{1,0:T(8,128)S(1)}, f32[32,128]{1,0:T(8,128)S(1)}, u32[]{:S(2)}, u32[]{:S(2)}) collective-permute-start(f32[32,128]{1,0:T(8,128)S(1)} %reduce_sum.45), channel_id=1, source_target_pairs={{0,64},{64,0},{1,65},{65,1},{2,66},{66,2},{3,67},{67,3},{4,68},{68... | collective-permute-start | bytes 49160 | tf_op jit(solution)/shard_map/ppermute | solution.py:22
  28.8 1.4 collective-permute-done
  30.3 0.0 copy-start.4
  30.3 9.8 %all_to_all.46 = f32[8,32,128]{2,1,0:T(8,128)S(1)} all-to-all(f32[8,32,128]{2,1,0:T(8,128)S(1)} %broadcast_in_dim.8), channel_id=1, replica_groups=mesh['x'=4,'h'=2,'c'=2,'w'=2,'z'=4,'y'=4] {'x','c'}, dimensions={0} | all-to-all | bytes 262144 | tf_op jit(solution)/shard_map/all_to_all | solution.py:32
  40.1 0.0 copy-done.4
  40.1 0.3 fusion.10
  40.4 14.2 %all_to_all.47 = f32[16,16,256]{2,1,0:T(8,128)S(1)} all-to-all(f32[16,16,256]{2,1,0:T(8,128)S(1)} %fusion.10), channel_id=1, replica_groups=mesh['x'=4,'h'=2,'c'=2,'w'=2,'z'=4,'y'=4] {'z','y'}, dimensions={0} | all-to-all | bytes 524288 | tf_op jit(solution)/shard_map/all_to_all | solution.py:27
  54.5 8.4 %collective-permute-start.1 = (f32[16,256]{1,0:T(8,128)S(1)}, f32[16,256]{1,0:T(8,128)S(1)}, u32[]{:S(2)}, u32[]{:S(2)}) collective-permute-start(f32[16,256]{1,0:T(8,128)S(1)} %reduce_sum.46), channel_id=1, source_target_pairs={{0,16},{16,0},{1,17},{17,1},{2,18},{18,2},{3,19},{19,3},{4,20},{20... | collective-permute-start | bytes 49160 | tf_op jit(solution)/shard_map/ppermute | solution.py:22
  63.0 1.1 collective-permute-done.1
  64.1 0.7 broadcast_in_dim.9
  64.8 4.4 %all-to-all-start.3 = ((f32[16,16,256]{2,1,0:T(8,128)}), f32[16,16,256]{2,1,0:T(8,128)S(1)}, u32[]{:S(2)}, u32[]{:S(2)}) async-start(f32[16,16,256]{2,1,0:T(8,128)} %broadcast_in_dim.9), calls=%async_computation.3 | async-start | bytes 524288 | tf_op jit(solution)/shard_map/all_to_all | solution.py:32
  69.2 0.1 copy.20
  69.4 8.7 %all-to-all-done.3 = f32[16,16,256]{2,1,0:T(8,128)S(1)} async-done(((f32[16,16,256]{2,1,0:T(8,128)}), f32[16,16,256]{2,1,0:T(8,128)S(1)}, u32[]{:S(2)}, u32[]{:S(2)}) %all-to-all-start.3) | async-done | bytes 262176 | tf_op jit(solution)/shard_map/all_to_all | solution.py:32
  78.1 0.3 fusion.8
  78.4 11.4 %all_to_all.48 = f32[8,32,128]{2,1,0:T(8,128)S(1)} all-to-all(f32[8,32,128]{2,1,0:T(8,128)S(1)} %fusion.8), channel_id=1, replica_groups=mesh['x'=4,'h'=2,'c'=2,'w'=2,'z'=4,'y'=4] {'x','c'}, dimensions={0} | all-to-all | bytes 262144 | tf_op jit(solution)/shard_map/all_to_all | solution.py:27
  89.8 0.0 copy-start.1
  89.8 11.6 %collective-permute-start.2 = (f32[32,128]{1,0:T(8,128)S(1)}, f32[32,128]{1,0:T(8,128)S(1)}, u32[]{:S(2)}, u32[]{:S(2)}) collective-permute-start(f32[32,128]{1,0:T(8,128)S(1)} %reduce_sum.47), channel_id=1, source_target_pairs={{0,64},{64,0},{1,65},{65,1},{2,66},{66,2},{3,67},{67,3},{4,68},{68... | collective-permute-start | bytes 49160 | tf_op jit(solution)/shard_map/ppermute | solution.py:22
  101.5 1.7 collective-permute-done.2
  103.2 0.7 broadcast_in_dim.10
  103.8 5.3 %all-to-all-start.5 = ((f32[8,32,128]{2,1,0:T(8,128)}), f32[8,32,128]{2,1,0:T(8,128)S(1)}, u32[]{:S(2)}, u32[]{:S(2)}) async-start(f32[8,32,128]{2,1,0:T(8,128)} %broadcast_in_dim.10), calls=%async_computation.5 | async-start | bytes 262144 | tf_op jit(solution)/shard_map/all_to_all | solution.py:32
  109.1 0.0 copy-done
  109.1 0.0 copy-done.1
  109.1 0.4 fusion.1
  109.6 4.8 %all-to-all-done.5 = f32[8,32,128]{2,1,0:T(8,128)S(1)} async-done(((f32[8,32,128]{2,1,0:T(8,128)}), f32[8,32,128]{2,1,0:T(8,128)S(1)}, u32[]{:S(2)}, u32[]{:S(2)}) %all-to-all-start.5) | async-done | bytes 131104 | tf_op jit(solution)/shard_map/all_to_all | solution.py:32
  114.4 1.2 fusion.4
  115.6 3.6 %all-to-all-start.6 = ((f32[16,16,512]{2,1,0:T(8,128)}), f32[16,16,512]{2,1,0:T(8,128)S(1)}, u32[]{:S(2)}, u32[]{:S(2)}) async-start(f32[16,16,512]{2,1,0:T(8,128)} %bitcast.16), calls=%async_computation.6 | async-start | bytes 1048576 | tf_op jit(solution)/shard_map/all_to_all | solution.py:27
  119.3 0.0 copy-start.2
  119.3 13.8 %all-to-all-done.6 = f32[16,16,512]{2,1,0:T(8,128)S(1)} async-done(((f32[16,16,512]{2,1,0:T(8,128)}), f32[16,16,512]{2,1,0:T(8,128)S(1)}, u32[]{:S(2)}, u32[]{:S(2)}) %all-to-all-start.6) | async-done | bytes 524320 | tf_op jit(solution)/shard_map/all_to_all | solution.py:27
  133.1 7.6 %collective-permute-start.3 = (f32[16,512]{1,0:T(8,128)S(1)}, f32[16,512]{1,0:T(8,128)S(1)}, u32[]{:S(2)}, u32[]{:S(2)}) collective-permute-start(f32[16,512]{1,0:T(8,128)S(1)} %reduce_sum.48), channel_id=1, source_target_pairs={{0,16},{16,0},{1,17},{17,1},{2,18},{18,2},{3,19},{19,3},{4,20},{20... | collective-permute-start | bytes 98312 | tf_op jit(solution)/shard_map/ppermute | solution.py:22
  140.7 1.3 collective-permute-done.3
  141.9 0.0 copy-done.2
  141.9 0.2 subtract_tanh_fusion
  142.1 0.1 broadcast_in_dim.11
  142.2 17.3 %all_to_all.49 = f32[16,16,512]{2,1,0:T(8,128)S(1)} all-to-all(f32[16,16,512]{2,1,0:T(8,128)S(1)} %broadcast_in_dim.11), channel_id=1, replica_groups=mesh['x'=4,'h'=2,'c'=2,'w'=2,'z'=4,'y'=4] {'z','y'}, dimensions={0} | all-to-all | bytes 1048576 | tf_op jit(solution)/shard_map/all_to_all | solution.py:32
  159.5 1.1 fusion.2
  160.6 7.5 %all-to-all-start.8 = ((f32[8,32,256]{2,1,0:T(8,128)}), f32[8,32,256]{2,1,0:T(8,128)S(1)}, u32[]{:S(2)}, u32[]{:S(2)}) async-start(f32[8,32,256]{2,1,0:T(8,128)} %fusion.2), calls=%async_computation.8 | async-start | bytes 524288 | tf_op jit(solution)/shard_map/all_to_all | solution.py:27
  168.1 6.5 %all-to-all-done.8 = f32[8,32,256]{2,1,0:T(8,128)S(1)} async-done(((f32[8,32,256]{2,1,0:T(8,128)}), f32[8,32,256]{2,1,0:T(8,128)S(1)}, u32[]{:S(2)}, u32[]{:S(2)}) %all-to-all-start.8) | async-done | bytes 262176 | tf_op jit(solution)/shard_map/all_to_all | solution.py:27
  174.7 11.1 %collective-permute-start.4 = (f32[16,256]{1,0:T(8,128)S(1)}, f32[16,256]{1,0:T(8,128)S(1)}, u32[]{:S(2)}, u32[]{:S(2)}) collective-permute-start(f32[16,256]{1,0:T(8,128)S(1)} %dynamic-slice_bitcast_fusion), channel_id=1, source_target_pairs={{0,64},{64,0},{1,65},{65,1},{2,66},{66,2},{3,67},{67,3},{4,68},{68... | collective-permute-start | bytes 49160 | tf_op jit(solution)/shard_map/ppermute | solution.py:22
  185.7 2.1 %collective-permute-done.4 = f32[16,256]{1,0:T(8,128)S(1)} collective-permute-done((f32[16,256]{1,0:T(8,128)S(1)}, f32[16,256]{1,0:T(8,128)S(1)}, u32[]{:S(2)}, u32[]{:S(2)}) %collective-permute-start.4) | collective-permute-done | bytes 16416 | tf_op jit(solution)/shard_map/ppermute | solution.py:22
  187.9 0.6 copy.19
  (16 shorter events, 0.2 us)
Async XLA Ops:
  0.0 109.1 %copy-start = (f32[512,256]{1,0:T(8,128)S(1)}, f32[512,256]{1,0:T(8,128)}, u32[]{:S(2)}) copy-start(f32[512,256]{1,0:T(8,128)} %param.6) | copy-start | bytes 1572868
  1.3 1.0 copy-start.3
  17.0 13.2 %collective-permute-start = (f32[32,128]{1,0:T(8,128)S(1)}, f32[32,128]{1,0:T(8,128)S(1)}, u32[]{:S(2)}, u32[]{:S(2)}) collective-permute-start(f32[32,128]{1,0:T(8,128)S(1)} %reduce_sum.45), channel_id=1, source_target_pairs={{0,64},{64,0},{1,65},{65,1},{2,66},{66,2},{3,67},{67,3},{4,68},{68... | collective-permute-start | bytes 49160 | tf_op jit(solution)/shard_map/ppermute | solution.py:22
  30.3 9.8 %copy-start.4 = (f32[256,128]{1,0:T(8,128)S(1)}, f32[256,128]{1,0:T(8,128)}, u32[]{:S(2)}) copy-start(f32[256,128]{1,0:T(8,128)} %param.11) | copy-start | bytes 393220
  54.5 9.5 %collective-permute-start.1 = (f32[16,256]{1,0:T(8,128)S(1)}, f32[16,256]{1,0:T(8,128)S(1)}, u32[]{:S(2)}, u32[]{:S(2)}) collective-permute-start(f32[16,256]{1,0:T(8,128)S(1)} %reduce_sum.46), channel_id=1, source_target_pairs={{0,16},{16,0},{1,17},{17,1},{2,18},{18,2},{3,19},{19,3},{4,20},{20... | collective-permute-start | bytes 49160 | tf_op jit(solution)/shard_map/ppermute | solution.py:22
  64.8 13.3 %all-to-all-start.3 = ((f32[16,16,256]{2,1,0:T(8,128)}), f32[16,16,256]{2,1,0:T(8,128)S(1)}, u32[]{:S(2)}, u32[]{:S(2)}) async-start(f32[16,16,256]{2,1,0:T(8,128)} %broadcast_in_dim.9), calls=%async_computation.3 | async-start | bytes 524288 | tf_op jit(solution)/shard_map/all_to_all | solution.py:32
  89.8 19.3 %copy-start.1 = (f32[2,128,256]{2,1,0:T(8,128)S(1)}, f32[2,128,256]{2,1,0:T(8,128)}, u32[]{:S(2)}) copy-start(f32[2,128,256]{2,1,0:T(8,128)} %param.8) | copy-start | bytes 786436
  89.8 13.3 %collective-permute-start.2 = (f32[32,128]{1,0:T(8,128)S(1)}, f32[32,128]{1,0:T(8,128)S(1)}, u32[]{:S(2)}, u32[]{:S(2)}) collective-permute-start(f32[32,128]{1,0:T(8,128)S(1)} %reduce_sum.47), channel_id=1, source_target_pairs={{0,64},{64,0},{1,65},{65,1},{2,66},{66,2},{3,67},{67,3},{4,68},{68... | collective-permute-start | bytes 49160 | tf_op jit(solution)/shard_map/ppermute | solution.py:22
  103.8 10.6 %all-to-all-start.5 = ((f32[8,32,128]{2,1,0:T(8,128)}), f32[8,32,128]{2,1,0:T(8,128)S(1)}, u32[]{:S(2)}, u32[]{:S(2)}) async-start(f32[8,32,128]{2,1,0:T(8,128)} %broadcast_in_dim.10), calls=%async_computation.5 | async-start | bytes 262144 | tf_op jit(solution)/shard_map/all_to_all | solution.py:32
  115.6 17.4 %all-to-all-start.6 = ((f32[16,16,512]{2,1,0:T(8,128)}), f32[16,16,512]{2,1,0:T(8,128)S(1)}, u32[]{:S(2)}, u32[]{:S(2)}) async-start(f32[16,16,512]{2,1,0:T(8,128)} %bitcast.16), calls=%async_computation.6 | async-start | bytes 1048576 | tf_op jit(solution)/shard_map/all_to_all | solution.py:27
  119.3 22.7 %copy-start.2 = (bf16[512,256]{1,0:T(8,128)(2,1)S(1)}, bf16[512,256]{1,0:T(8,128)(2,1)}, u32[]{:S(2)}) copy-start(bf16[512,256]{1,0:T(8,128)(2,1)} %param.7) | copy-start | bytes 786436
  133.1 8.8 %collective-permute-start.3 = (f32[16,512]{1,0:T(8,128)S(1)}, f32[16,512]{1,0:T(8,128)S(1)}, u32[]{:S(2)}, u32[]{:S(2)}) collective-permute-start(f32[16,512]{1,0:T(8,128)S(1)} %reduce_sum.48), channel_id=1, source_target_pairs={{0,16},{16,0},{1,17},{17,1},{2,18},{18,2},{3,19},{19,3},{4,20},{20... | collective-permute-start | bytes 98312 | tf_op jit(solution)/shard_map/ppermute | solution.py:22
  160.6 14.0 %all-to-all-start.8 = ((f32[8,32,256]{2,1,0:T(8,128)}), f32[8,32,256]{2,1,0:T(8,128)S(1)}, u32[]{:S(2)}, u32[]{:S(2)}) async-start(f32[8,32,256]{2,1,0:T(8,128)} %fusion.2), calls=%async_computation.8 | async-start | bytes 524288 | tf_op jit(solution)/shard_map/all_to_all | solution.py:27
  174.7 13.2 %collective-permute-start.4 = (f32[16,256]{1,0:T(8,128)S(1)}, f32[16,256]{1,0:T(8,128)S(1)}, u32[]{:S(2)}, u32[]{:S(2)}) collective-permute-start(f32[16,256]{1,0:T(8,128)S(1)} %dynamic-slice_bitcast_fusion), channel_id=1, source_target_pairs={{0,64},{64,0},{1,65},{65,1},{2,66},{66,2},{3,67},{67,3},{4,68},{68... | collective-permute-start | bytes 49160 | tf_op jit(solution)/shard_map/ppermute | solution.py:22

commit v5 on v4

v5 whole, which is shorter than its diff:
```python
import math

import jax
import jax.numpy as jnp
from jax import lax
from jax.sharding import Mesh
from jax.sharding import PartitionSpec as P

PTS = ("x", "h", "c")
CTR = ("w", "z", "y")
SIZES = {"x": 4, "h": 2, "c": 2, "w": 2, "z": 4, "y": 4}
HIGH = lax.Precision.HIGH


def dot(a, b, ca, cb):
    return lax.dot_general(
        a, b, (((ca,), (cb,)), ((), ())), precision=HIGH, preferred_element_type=jnp.float32
    )


def swap(a, axis):
    return lax.ppermute(a, axis, [(0, 1), (1, 0)])


def scatter_sum(a, axes):
    return jnp.sum(lax.all_to_all(a, axes, 0, 0, tiled=True), 0)


def gather(a, axes, n):
    a = jnp.broadcast_to(a[None], (n, *a.shape))
    return lax.all_to_all(a, axes, 0, 0, tiled=True)


def columns(a):
    rows = a.shape[0]
    return a.reshape(rows, 4, 2, 2, 16).transpose(1, 3, 2, 4, 0).reshape(256, rows)


def local(points, labels, centres, coeffs, diag_inverse, off_block):
    xc, zy = ("x", "c"), ("z", "y")
    off_all = lax.all_gather(off_block, xc, axis=0, tiled=True)

    part = jnp.concatenate(
        [
            dot(columns(coeffs[1]), diag_inverse[1], 1, 1),
            dot(columns(coeffs[0]), diag_inverse[0], 1, 1),
        ],
        1,
    )
    part = scatter_sum(part.reshape(8, 32, 256), xc)

    block = lax.axis_index("z") * 4 + lax.axis_index("y")
    label_rows = lax.dynamic_slice_in_dim(labels, block * 32, 32, 0).astype(jnp.float32)
    own = jnp.concatenate([diag_inverse[0], label_rows], 0)
    part, own = lax.optimization_barrier((part, own))
    both = lax.all_gather(own, xc, axis=0)
    diag_all = both[:, :128].reshape(8, 128, 2, 128).transpose(0, 2, 1, 3).reshape(16, 128, 128)
    label_all = both[:, 128:].reshape(256, 256)

    part = part + swap(part, "h")
    part, points = lax.optimization_barrier((part, points))
    points_all = lax.all_gather(points, xc, axis=0)
    second, direct = part[:, :128], part[:, 128:]

    carried = dot(second, off_all.reshape(16, 128, 128), 1, 2).transpose(1, 0, 2)
    carried = scatter_sum(carried, zy)
    carried = carried + swap(carried, "w")
    carried = gather(carried, zy, 16)
    carried = lax.dot_general(
        carried,
        diag_all,
        (((0, 2), (0, 2)), ((), ())),
        precision=HIGH,
        preferred_element_type=jnp.float32,
    )
    first = direct - (carried + swap(carried, "h"))

    solved = jnp.concatenate([first, second], 1)
    points_all = points_all.reshape(8, 16, 32, 256).transpose(1, 0, 2, 3).reshape(4096, 256)
    score = dot(points_all, centres.reshape(256, 256), 1, 1) / math.sqrt(points.shape[1])
    kernel = (score + score * score * score / 3.0).reshape(16, 256, 256)
    pred_scale = 1.0 / (2.0 * math.sqrt(256 * 32))
    pred = dot(solved, kernel, 1, 2).transpose(1, 0, 2)
    pred = scatter_sum(pred, zy)
    pred = pred + swap(pred, "w")

    x, c, h = lax.axis_index("x"), lax.axis_index("c"), lax.axis_index("h")
    row = lax.broadcasted_iota(jnp.int32, (32, 256), 0)
    start = ((x * 2 + row // 16) * 2 + c) * 16 + row % 16
    chosen = lax.broadcasted_iota(jnp.int32, (32, 256), 1) == start
    target = lax.dot_general(
        chosen.astype(jnp.float32),
        label_all,
        (((1,), (1,)), ((), ())),
        precision=lax.Precision.HIGHEST,
        preferred_element_type=jnp.float32,
    )
    weights = gather(jnp.tanh(pred * pred_scale - target), zy, 16)

    scale = 1.0 / (2.0 * math.sqrt(points.shape[0] * 16))
    term = lax.dot_general(
        weights,
        kernel,
        (((0, 2), (0, 1)), ((), ())),
        precision=HIGH,
        preferred_element_type=jnp.float32,
    ).reshape(2, 16, 256)
    mine = lax.dynamic_index_in_dim(term, h, 0, keepdims=False)
    other = lax.dynamic_index_in_dim(term, 1 - h, 0, keepdims=False)
    mine = (mine + swap(other, "h")) * scale
    return mine.reshape(16, 2, 128).transpose(1, 2, 0)


def solution(mesh):
    fine = Mesh(mesh.devices.reshape(tuple(SIZES.values())), tuple(SIZES))
    return jax.shard_map(
        local,
        mesh=fine,
        in_specs=(
            P(PTS, None),
            P(PTS, None),
            P(None, CTR, None),
            P(None, PTS, None),
            P(None, CTR, PTS),
            P(PTS, CTR),
        ),
        out_specs=P(None, CTR, PTS),
        check_vma=False,
    )
```

time: 190 us -> 208 us (1.095)
  the two profiles are of different devices: /device:TPU:1 before, /device:TPU:32 now
where the time goes in v5:
time: 208 us; the launch traced here: 207 us
  waiting for transfers between devices  77.5 us (37%)
  starting transfers between devices  72.3 us (35%)
  blocking collectives  17.3 us (8%)
  matrix products  13.4 us (6%)
  between operations  13.4 us (6%)
  local copies, waits for them, and re-layouts  11.2 us (5%)
    ppermute x5, starting transfers between devices, swap(): return lax.ppermute(a, axis, [(0, 1), (1, 0)])  50.1 us
    all_to_all x2, waiting for transfers between devices, scatter_sum(): return jnp.sum(lax.all_to_all(a, axes, 0, 0, tiled=True), 0)  21.2 us
    all_to_all x2, waiting for transfers between devices, gather(): return lax.all_to_all(a, axes, 0, 0, tiled=True)  19.6 us
    all_gather x1, waiting for transfers between devices, local(): points_all = lax.all_gather(points, xc, axis=0)  18.2 us
    all_to_all x1, blocking collectives, scatter_sum(): return jnp.sum(lax.all_to_all(a, axes, 0, 0, tiled=True), 0)  17.3 us
    ppermute x5, waiting for transfers between devices, swap(): return lax.ppermute(a, axis, [(0, 1), (1, 0)])  13.8 us
    all_to_all x2, starting transfers between devices, scatter_sum(): return jnp.sum(lax.all_to_all(a, axes, 0, 0, tiled=True), 0)  12 us
    all_to_all x2, starting transfers between devices, gather(): return lax.all_to_all(a, axes, 0, 0, tiled=True)  10.1 us
  transfers between devices with their start and end apart: 12, of which 11 were waited for; matrix products, arithmetic and copies ran while one was open for 6% of the time, Pallas kernels for 0%

profile of v5, /device:TPU:32, one launch (start us, length us, event | category | flops | bytes accessed | tf_op | source)
XLA Modules:
  0.0 206.7 jit_solution(6187445052487252445)
XLA Ops:
  6.5 0.7 all-gather.6.cloned.1.call-update
  7.3 1.1 fusion.26
  8.3 0.1 copy.34
  8.5 0.1 copy.33
  8.7 1.2 fusion.24
  9.9 1.2 fusion.2
  11.1 0.8 copy.26
  11.9 4.3 %all-to-all-start = ((f32[8,32,256]{2,1,0:T(8,128)}), f32[8,32,256]{2,1,0:T(8,128)S(1)}, u32[]{:S(2)}, u32[]{:S(2)}) async-start(f32[8,32,256]{2,1,0:T(8,128)} %bitcast.8), calls=%async_computation | async-start | bytes 524288 | tf_op jit(solution)/shard_map/all_to_all | solution.py:26
  16.2 0.0 all-gather.8.cloned.1.call-start
  16.3 0.7 dynamic-slice_convert_fusion
  17.0 0.7 pad_maximum_fusion.2
  17.7 6.0 %all-to-all-done = f32[8,32,256]{2,1,0:T(8,128)S(1)} async-done(((f32[8,32,256]{2,1,0:T(8,128)}), f32[8,32,256]{2,1,0:T(8,128)S(1)}, u32[]{:S(2)}, u32[]{:S(2)}) %all-to-all-start) | async-done | bytes 262176 | tf_op jit(solution)/shard_map/all_to_all | solution.py:26
  23.8 0.0 all-gather.8.cloned.1.call-update
  23.8 0.0 all-gather.10.cloned.1.call-start
  23.9 14.8 %collective-permute-start = (f32[32,256]{1,0:T(8,128)S(1)}, f32[32,256]{1,0:T(8,128)S(1)}, u32[]{:S(2)}, u32[]{:S(2)}) collective-permute-start(f32[32,256]{1,0:T(8,128)S(1)} %reduce_sum.27), channel_id=1, source_target_pairs={{0,64},{64,0},{1,65},{65,1},{2,66},{66,2},{3,67},{67,3},{4,68},{68... | collective-permute-start | bytes 98312 | tf_op jit(solution)/shard_map/ppermute | solution.py:22
  38.7 2.0 collective-permute-done
  40.7 0.0 all-gather.10.cloned.1.call-update
  40.7 3.9 %all-gather.6.cloned.1.call-done = f32[2048,128]{1,0:T(8,128)} async-done(((f32[256,128]{1,0:T(8,128)}), f32[2048,128]{1,0:T(8,128)}) %all-gather.6.cloned.1.call-update) | async-done | bytes 1048592 | tf_op jit(solution)/shard_map/all_gather | solution.py:41
  44.7 1.8 convolution_bitcast_fusion.1
  46.5 17.3 %all_to_all.25 = f32[16,32,128]{2,1,0:T(8,128)S(1)} all-to-all(f32[16,32,128]{2,1,0:T(8,128)S(1)} %convolution_bitcast_fusion.1), channel_id=1, replica_groups=mesh['x'=4,'h'=2,'c'=2,'w'=2,'z'=4,'y'=4] {'z','y'}, dimensions={0} | all-to-all | bytes 524288 | tf_op jit(solution)/shard_map/all_to_all | solution.py:26
  63.9 7.6 %collective-permute-start.1 = (f32[32,128]{1,0:T(8,128)S(1)}, f32[32,128]{1,0:T(8,128)S(1)}, u32[]{:S(2)}, u32[]{:S(2)}) collective-permute-start(f32[32,128]{1,0:T(8,128)S(1)} %reduce_sum.28), channel_id=1, source_target_pairs={{0,16},{16,0},{1,17},{17,1},{2,18},{18,2},{3,19},{19,3},{4,20},{20... | collective-permute-start | bytes 49160 | tf_op jit(solution)/shard_map/ppermute | solution.py:22
  71.5 2.0 collective-permute-done.1
  73.5 0.7 broadcast_in_dim.4
  74.2 5.0 %all-to-all-start.2 = ((f32[16,32,128]{2,1,0:T(8,128)}), f32[16,32,128]{2,1,0:T(8,128)S(1)}, u32[]{:S(2)}, u32[]{:S(2)}) async-start(f32[16,32,128]{2,1,0:T(8,128)} %broadcast_in_dim.4), calls=%async_computation.2 | async-start | bytes 524288 | tf_op jit(solution)/shard_map/all_to_all | solution.py:31
  79.3 1.3 fusion.25
  80.6 0.1 pad_maximum_fusion
  80.6 6.6 %all-to-all-done.2 = f32[16,32,128]{2,1,0:T(8,128)S(1)} async-done(((f32[16,32,128]{2,1,0:T(8,128)}), f32[16,32,128]{2,1,0:T(8,128)S(1)}, u32[]{:S(2)}, u32[]{:S(2)}) %all-to-all-start.2) | async-done | bytes 262176 | tf_op jit(solution)/shard_map/all_to_all | solution.py:31
  87.2 0.6 convolution_bitcast_fusion.3
  87.8 10.1 %collective-permute-start.2 = (f32[32,128]{1,0:T(8,128)S(1)}, f32[32,128]{1,0:T(8,128)S(1)}, u32[]{:S(2)}, u32[]{:S(2)}) collective-permute-start(f32[32,128]{1,0:T(8,128)S(1)} %convolution_bitcast_fusion.3), channel_id=1, source_target_pairs={{0,64},{64,0},{1,65},{65,1},{2,66},{66,2},{3,67},{67,3},{4,68},{68... | collective-permute-start | bytes 49160 | tf_op jit(solution)/shard_map/ppermute | solution.py:22
  97.9 4.2 %collective-permute-done.2 = f32[32,128]{1,0:T(8,128)S(1)} collective-permute-done((f32[32,128]{1,0:T(8,128)S(1)}, f32[32,128]{1,0:T(8,128)S(1)}, u32[]{:S(2)}, u32[]{:S(2)}) %collective-permute-start.2) | collective-permute-done | bytes 16416 | tf_op jit(solution)/shard_map/ppermute | solution.py:22
  102.2 18.2 %all-gather.10.cloned.1.call-done = f32[4096,256]{1,0:T(8,128)} async-done(((f32[512,256]{1,0:T(8,128)}), f32[4096,256]{1,0:T(8,128)}) %all-gather.10.cloned.1.call-update) | async-done | bytes 4194320 | tf_op jit(solution)/shard_map/all_gather | solution.py:62
  120.4 2.5 %copy.27 = f32[16,8,32,256]{3,2,1,0:T(8,128)S(1)} copy(f32[16,8,32,256]{3,2,0,1:T(8,128)} %bitcast.71) | data formatting | bytes 8388608 | tf_op jit(solution)/shard_map/transpose | solution.py:79
  123.0 2.0 fusion.1
  125.0 1.9 copy-done.1
  127.0 2.8 %convolution_bitcast_fusion = f32[16,32,256]{2,1,0:T(8,128)} fusion(f32[16,256,256]{2,1,0:T(8,128)S(1)} %bitcast.68, f32[32,128]{1,0:T(8,128)S(1)} %get-tuple-element.18, f32[32,128]{1,0:T(8,128)S(1)} %get-tuple-element.17), kind=kOutput, calls=%fused_computation.4 | convolution fusion | flops 201334784 | bytes 4751360 | tf_op jit(solution)/shard_map/dot_general | solution.py:16
  129.7 7.7 %all-to-all-start.3 = ((f32[16,32,256]{2,1,0:T(8,128)}), f32[16,32,256]{2,1,0:T(8,128)S(1)}, u32[]{:S(2)}, u32[]{:S(2)}) async-start(f32[16,32,256]{2,1,0:T(8,128)} %convolution_bitcast_fusion), calls=%async_computation.3 | async-start | bytes 1048576 | tf_op jit(solution)/shard_map/all_to_all | solution.py:26
  137.5 15.2 %all-to-all-done.3 = f32[16,32,256]{2,1,0:T(8,128)S(1)} async-done(((f32[16,32,256]{2,1,0:T(8,128)}), f32[16,32,256]{2,1,0:T(8,128)S(1)}, u32[]{:S(2)}, u32[]{:S(2)}) %all-to-all-start.3) | async-done | bytes 524320 | tf_op jit(solution)/shard_map/all_to_all | solution.py:26
  152.7 7.6 %collective-permute-start.3 = (f32[32,256]{1,0:T(8,128)S(1)}, f32[32,256]{1,0:T(8,128)S(1)}, u32[]{:S(2)}, u32[]{:S(2)}) collective-permute-start(f32[32,256]{1,0:T(8,128)S(1)} %reduce_sum.29), channel_id=1, source_target_pairs={{0,16},{16,0},{1,17},{17,1},{2,18},{18,2},{3,19},{19,3},{4,20},{20... | collective-permute-start | bytes 98312 | tf_op jit(solution)/shard_map/ppermute | solution.py:22
  160.4 1.0 slice.42
  161.4 1.1 collective-permute-done.3
  162.4 0.3 subtract_tanh_fusion
  162.7 0.9 broadcast_in_dim.5
  163.6 5.1 %all-to-all-start.4 = ((f32[16,32,256]{2,1,0:T(8,128)}), f32[16,32,256]{2,1,0:T(8,128)S(1)}, u32[]{:S(2)}, u32[]{:S(2)}) async-start(f32[16,32,256]{2,1,0:T(8,128)} %broadcast_in_dim.5), calls=%async_computation.4 | async-start | bytes 1048576 | tf_op jit(solution)/shard_map/all_to_all | solution.py:31
  168.7 13.1 %all-to-all-done.4 = f32[16,32,256]{2,1,0:T(8,128)S(1)} async-done(((f32[16,32,256]{2,1,0:T(8,128)}), f32[16,32,256]{2,1,0:T(8,128)S(1)}, u32[]{:S(2)}, u32[]{:S(2)}) %all-to-all-start.4) | async-done | bytes 524320 | tf_op jit(solution)/shard_map/all_to_all | solution.py:31
  181.8 3.4 %convolution_bitcast_fusion.2 = f32[2,16,256]{2,1,0:T(8,128)S(1)} fusion(f32[2,16,16,256]{3,1,0,2:T(8,128)S(1)} %bitcast.73, f32[16,256,256,1]{2,1,3,0:T(8,128)} %bitcast.69), kind=kOutput, calls=%fused_computation.6 | convolution fusion | flops 201326592 | bytes 4751360 | tf_op jit(solution)/shard_map/dot_general | solution.py:101
  185.2 9.9 %collective-permute-start.4 = (f32[16,256]{1,0:T(8,128)S(1)}, f32[16,256]{1,0:T(8,128)S(1)}, u32[]{:S(2)}, u32[]{:S(2)}) collective-permute-start(f32[16,256]{1,0:T(8,128)S(1)} %dynamic-slice_bitcast_fusion), channel_id=1, source_target_pairs={{0,64},{64,0},{1,65},{65,1},{2,66},{66,2},{3,67},{67,3},{4,68},{68... | collective-permute-start | bytes 49160 | tf_op jit(solution)/shard_map/ppermute | solution.py:22
  195.1 4.4 %collective-permute-done.4 = f32[16,256]{1,0:T(8,128)S(1)} collective-permute-done((f32[16,256]{1,0:T(8,128)S(1)}, f32[16,256]{1,0:T(8,128)S(1)}, u32[]{:S(2)}, u32[]{:S(2)}) %collective-permute-start.4) | collective-permute-done | bytes 16416 | tf_op jit(solution)/shard_map/ppermute | solution.py:22
  199.6 0.6 copy.30
  (23 shorter events, 0.2 us)
Async XLA Ops:
  6.5 116.4 %copy-start = (f32[2,128,256]{2,1,0:T(8,128)S(1)}, f32[2,128,256]{2,1,0:T(8,128)}, u32[]{:S(2)}) copy-start(f32[2,128,256]{2,1,0:T(8,128)} %param.8) | copy-start | bytes 786436
  6.5 9.7 %copy-start.2 = (f32[2,128,256]{2,1,0:T(8,128)S(1)}, f32[2,128,256]{2,1,0:T(8,128)}, u32[]{:S(2)}) copy-start(f32[2,128,256]{2,1,0:T(8,128)} %param.10) | copy-start | bytes 786436
  6.5 38.1 %all-gather.6.cloned.1.call-start = ((), (), s32[]{:S(2)}) async-start(), calls=%async_computation.5 | async-start | bytes 1179648 | tf_op jit(solution)/shard_map/all_gather | solution.py:41
  11.9 11.8 %all-to-all-start = ((f32[8,32,256]{2,1,0:T(8,128)}), f32[8,32,256]{2,1,0:T(8,128)S(1)}, u32[]{:S(2)}, u32[]{:S(2)}) async-start(f32[8,32,256]{2,1,0:T(8,128)} %bitcast.8), calls=%async_computation | async-start | bytes 524288 | tf_op jit(solution)/shard_map/all_to_all | solution.py:26
  16.2 63.0 %all-gather.8.cloned.1.call-start = ((), (), s32[]{:S(2)}) async-start(), calls=%async_computation.6 | async-start | bytes 1474560 | tf_op jit(solution)/shard_map/all_gather | solution.py:56
  23.8 96.6 %all-gather.10.cloned.1.call-start = ((), (), s32[]{:S(2)}) async-start(), calls=%async_computation.7 | async-start | bytes 4718592 | tf_op jit(solution)/shard_map/all_gather | solution.py:62
  23.9 16.9 %collective-permute-start = (f32[32,256]{1,0:T(8,128)S(1)}, f32[32,256]{1,0:T(8,128)S(1)}, u32[]{:S(2)}, u32[]{:S(2)}) collective-permute-start(f32[32,256]{1,0:T(8,128)S(1)} %reduce_sum.27), channel_id=1, source_target_pairs={{0,64},{64,0},{1,65},{65,1},{2,66},{66,2},{3,67},{67,3},{4,68},{68... | collective-permute-start | bytes 98312 | tf_op jit(solution)/shard_map/ppermute | solution.py:22
  63.9 9.6 %collective-permute-start.1 = (f32[32,128]{1,0:T(8,128)S(1)}, f32[32,128]{1,0:T(8,128)S(1)}, u32[]{:S(2)}, u32[]{:S(2)}) collective-permute-start(f32[32,128]{1,0:T(8,128)S(1)} %reduce_sum.28), channel_id=1, source_target_pairs={{0,16},{16,0},{1,17},{17,1},{2,18},{18,2},{3,19},{19,3},{4,20},{20... | collective-permute-start | bytes 49160 | tf_op jit(solution)/shard_map/ppermute | solution.py:22
  74.2 13.0 %all-to-all-start.2 = ((f32[16,32,128]{2,1,0:T(8,128)}), f32[16,32,128]{2,1,0:T(8,128)S(1)}, u32[]{:S(2)}, u32[]{:S(2)}) async-start(f32[16,32,128]{2,1,0:T(8,128)} %broadcast_in_dim.4), calls=%async_computation.2 | async-start | bytes 524288 | tf_op jit(solution)/shard_map/all_to_all | solution.py:31
  87.8 14.3 %collective-permute-start.2 = (f32[32,128]{1,0:T(8,128)S(1)}, f32[32,128]{1,0:T(8,128)S(1)}, u32[]{:S(2)}, u32[]{:S(2)}) collective-permute-start(f32[32,128]{1,0:T(8,128)S(1)} %convolution_bitcast_fusion.3), channel_id=1, source_target_pairs={{0,64},{64,0},{1,65},{65,1},{2,66},{66,2},{3,67},{67,3},{4,68},{68... | collective-permute-start | bytes 49160 | tf_op jit(solution)/shard_map/ppermute | solution.py:22
  125.0 1.9 copy-start.1
  129.7 22.9 %all-to-all-start.3 = ((f32[16,32,256]{2,1,0:T(8,128)}), f32[16,32,256]{2,1,0:T(8,128)S(1)}, u32[]{:S(2)}, u32[]{:S(2)}) async-start(f32[16,32,256]{2,1,0:T(8,128)} %convolution_bitcast_fusion), calls=%async_computation.3 | async-start | bytes 1048576 | tf_op jit(solution)/shard_map/all_to_all | solution.py:26
  152.7 9.7 %collective-permute-start.3 = (f32[32,256]{1,0:T(8,128)S(1)}, f32[32,256]{1,0:T(8,128)S(1)}, u32[]{:S(2)}, u32[]{:S(2)}) collective-permute-start(f32[32,256]{1,0:T(8,128)S(1)} %reduce_sum.29), channel_id=1, source_target_pairs={{0,16},{16,0},{1,17},{17,1},{2,18},{18,2},{3,19},{19,3},{4,20},{20... | collective-permute-start | bytes 98312 | tf_op jit(solution)/shard_map/ppermute | solution.py:22
  163.6 18.2 %all-to-all-start.4 = ((f32[16,32,256]{2,1,0:T(8,128)}), f32[16,32,256]{2,1,0:T(8,128)S(1)}, u32[]{:S(2)}, u32[]{:S(2)}) async-start(f32[16,32,256]{2,1,0:T(8,128)} %broadcast_in_dim.5), calls=%async_computation.4 | async-start | bytes 1048576 | tf_op jit(solution)/shard_map/all_to_all | solution.py:31
  185.2 14.3 %collective-permute-start.4 = (f32[16,256]{1,0:T(8,128)S(1)}, f32[16,256]{1,0:T(8,128)S(1)}, u32[]{:S(2)}, u32[]{:S(2)}) collective-permute-start(f32[16,256]{1,0:T(8,128)S(1)} %dynamic-slice_bitcast_fusion), channel_id=1, source_target_pairs={{0,64},{64,0},{1,65},{65,1},{2,66},{66,2},{3,67},{67,3},{4,68},{68... | collective-permute-start | bytes 49160 | tf_op jit(solution)/shard_map/ppermute | solution.py:22
Sparse Core Ops, SparseCore 0:
  9.5 35.1 all-gather.5
  46.8 31.6 all-gather.7
  80.6 39.7 all-gather.9

commit v6 on v4

v6 whole, which is shorter than its diff:
```python
import math

import jax
import jax.numpy as jnp
from jax import lax
from jax.sharding import Mesh
from jax.sharding import PartitionSpec as P

PTS = ("u", "v", "h", "c")
CTR = ("w", "z", "y")
SIZES = {"u": 2, "v": 2, "h": 2, "c": 2, "w": 2, "z": 4, "y": 4}
HIGH = lax.Precision.HIGH


def dot(a, b, ca, cb):
    return lax.dot_general(
        a, b, (((ca,), (cb,)), ((), ())), precision=HIGH, preferred_element_type=jnp.float32
    )


def swap(a, axis):
    return lax.ppermute(a, axis, [(0, 1), (1, 0)])


def scatter_sum(a, axes):
    return jnp.sum(lax.all_to_all(a, axes, 0, 0, tiled=True), 0)


def gather(a, axes, n):
    a = jnp.broadcast_to(a[None], (n, *a.shape))
    return lax.all_to_all(a, axes, 0, 0, tiled=True)


def columns(a):
    rows = a.shape[0]
    return a.reshape(rows, 4, 2, 2, 16).transpose(1, 3, 2, 4, 0).reshape(256, rows)


def local(points, labels, centres, coeffs, diag_inverse, off_block):
    xc, zy = ("u", "v", "c"), ("z", "y")
    h = lax.axis_index("h")
    block = lax.axis_index("z") * 4 + lax.axis_index("y")

    row = lax.broadcasted_iota(jnp.int32, (16, 256), 0)
    side = jnp.where(row < 8, h, 1 - h)
    start = block // 4 * 64 + side * 32 + block // 2 % 2 * 16 + block % 2 * 8 + row % 8
    chosen = (lax.broadcasted_iota(jnp.int32, (16, 256), 1) == start).astype(jnp.float32)

    def pick(a):
        return lax.dot_general(
            chosen,
            a.astype(jnp.float32),
            (((1,), (1,)), ((), ())),
            precision=lax.Precision.HIGHEST,
            preferred_element_type=jnp.float32,
        )

    label_chunk = pick(labels)
    coeff_chunk = pick(coeffs[0])
    point_slice = lax.dynamic_slice_in_dim(points, block * 32, 32, 0)
    pack = jnp.concatenate(
        [
            diag_inverse[0],
            point_slice,
            label_chunk[8:, :256],
            label_chunk[8:, 256:],
            coeff_chunk[8:],
        ],
        0,
    )

    part = dot(columns(coeffs[1]), diag_inverse[1], 1, 1)
    part, off_block = lax.optimization_barrier((part, off_block))
    off_other = swap(off_block, "h")
    part = scatter_sum(part.reshape(8, 32, 128), xc).reshape(2, 16, 128)
    keep = lax.dynamic_index_in_dim(part, h, 0, keepdims=False)
    send = lax.dynamic_index_in_dim(part, 1 - h, 0, keepdims=False)
    send, pack = lax.optimization_barrier((send, pack))
    part = keep + swap(send, "h")
    pack = swap(pack, "h")
    second = gather(part, xc, 8).reshape(128, 128)

    carried = dot(second, jnp.concatenate([off_block, off_other], 0), 1, 1)
    carried = scatter_sum(carried.reshape(16, 8, 512), zy)
    carried = carried + swap(carried, "w")
    rest = jnp.concatenate([coeff_chunk[:8], pack[176:]], 1) - carried
    rest = gather(rest, zy, 16).reshape(128, 512)

    diag = jnp.concatenate([diag_inverse[0], pack[:128]], 1)
    first = dot(rest, diag, 1, 1)
    first, point_slice = lax.optimization_barrier((first, pack[128:160]))
    points_other = gather(point_slice, zy, 16).reshape(512, 256)
    first = first + swap(first, "c")
    first = first + swap(first, "v")
    first = first + swap(first, "u")
    first, points_other = lax.optimization_barrier((first, points_other))
    solved = jnp.concatenate([first, second], 1)

    flat = centres.reshape(256, 256)

    def kernel_tile(rows):
        score = dot(rows, flat, 1, 1) / math.sqrt(rows.shape[1])
        return score + score * score * score / 3.0

    kernel = jnp.concatenate([kernel_tile(points), kernel_tile(points_other)], 0)
    pred_scale = 1.0 / (2.0 * math.sqrt(256 * 32))
    pred = scatter_sum(dot(solved, kernel, 1, 1).reshape(16, 8, 1024), zy)
    pred = pred + swap(pred, "w")
    target = jnp.concatenate([label_chunk[:8], pack[160:168], pack[168:176]], 1)
    weights = gather(jnp.tanh(pred * pred_scale - target), zy, 16).reshape(128, 1024)

    scale = 1.0 / (2.0 * math.sqrt(points.shape[0] * 16))
    term = dot(weights, kernel, 1, 0)
    term = scatter_sum(term.reshape(8, 16, 256), xc) * scale
    return term.reshape(16, 2, 128).transpose(1, 2, 0)


def solution(mesh):
    fine = Mesh(mesh.devices.reshape(tuple(SIZES.values())), tuple(SIZES))
    return jax.shard_map(
        local,
        mesh=fine,
        in_specs=(
            P(PTS, None),
            P(PTS, None),
            P(None, CTR, None),
            P(None, PTS, None),
            P(None, CTR, PTS),
            P(PTS, CTR),
        ),
        out_specs=P(None, CTR, PTS),
        check_vma=False,
    )
```

time: 190 us -> 187 us (0.984)
  blocking collectives: 67.1 us -> 50.2 us
  waiting for transfers between devices: 41.5 us -> 51.2 us
  starting transfers between devices: 71.2 us -> 74.1 us
    ppermute x5 -> x8, waiting for transfers between devices: 7.66 us -> 31.7 us  [swap(): return lax.ppermute(a, axis, [(0, 1), (1, 0)])]
    ppermute x5 -> x8, starting transfers between devices: 50.5 us -> 34.4 us  [swap(): return lax.ppermute(a, axis, [(0, 1), (1, 0)])]
    all_to_all x2, starting transfers between devices: 11.1 us -> 21.9 us  [scatter_sum(): return jnp.sum(lax.all_to_all(a, axes, 0, 0, tiled=True), 0)]
    all_to_all x2, waiting for transfers between devices: 20.3 us -> 10.5 us  [scatter_sum(): return jnp.sum(lax.all_to_all(a, axes, 0, 0, tiled=True), 0)]
    all_to_all x2 -> x1, blocking collectives: 27.1 us -> 17.6 us  [gather(): return lax.all_to_all(a, axes, 0, 0, tiled=True)]
    all_to_all x2 -> x3, starting transfers between devices: 9.67 us -> 17.9 us  [gather(): return lax.all_to_all(a, axes, 0, 0, tiled=True)]
    all_to_all x3 -> x2, blocking collectives: 40.1 us -> 32.6 us  [scatter_sum(): return jnp.sum(lax.all_to_all(a, axes, 0, 0, tiled=True), 0)]
    all_to_all x2 -> x3, waiting for transfers between devices: 13.6 us -> 9.07 us  [gather(): return lax.all_to_all(a, axes, 0, 0, tiled=True)]
  transfers between devices with their start and end apart: 9 -> 13, of which waited for: 9 -> 10; matrix products, arithmetic and copies ran while one was open for 0% -> 1% of each run, Pallas kernels for 0% -> 0%
where the time goes in v6:
time: 187 us; the launch traced here: 186 us
  starting transfers between devices  74.1 us (40%)
  waiting for transfers between devices  51.2 us (27%)
  blocking collectives  50.2 us (27%)
  local copies, waits for them, and re-layouts  5.52 us (3%)
  matrix products  4.55 us (2%)
    ppermute x8, starting transfers between devices, swap(): return lax.ppermute(a, axis, [(0, 1), (1, 0)])  34.4 us
    all_to_all x2, blocking collectives, scatter_sum(): return jnp.sum(lax.all_to_all(a, axes, 0, 0, tiled=True), 0)  32.6 us
    ppermute x8, waiting for transfers between devices, swap(): return lax.ppermute(a, axis, [(0, 1), (1, 0)])  31.7 us
    all_to_all x2, starting transfers between devices, scatter_sum(): return jnp.sum(lax.all_to_all(a, axes, 0, 0, tiled=True), 0)  21.9 us
    all_to_all x3, starting transfers between devices, gather(): return lax.all_to_all(a, axes, 0, 0, tiled=True)  17.9 us
    all_to_all x1, blocking collectives, gather(): return lax.all_to_all(a, axes, 0, 0, tiled=True)  17.6 us
    all_to_all x2, waiting for transfers between devices, scatter_sum(): return jnp.sum(lax.all_to_all(a, axes, 0, 0, tiled=True), 0)  10.5 us
    all_to_all x3, waiting for transfers between devices, gather(): return lax.all_to_all(a, axes, 0, 0, tiled=True)  9.07 us
  transfers between devices with their start and end apart: 13, of which 10 were waited for; matrix products, arithmetic and copies ran while one was open for 1% of the time, Pallas kernels for 0%

profile of v6, /device:TPU:1, one launch (start us, length us, event | category | flops | bytes accessed | tf_op | source)
XLA Modules:
  0.0 186.1 jit_solution(3461779370416599929)
XLA Ops:
  0.0 1.0 slice-done
  1.0 0.1 copy.10
  1.2 0.0 copy-start.3
  1.2 0.9 copy-done.3
  2.1 0.9 fusion.20
  3.1 10.3 %all-to-all-start = ((f32[8,32,128]{2,1,0:T(8,128)}), f32[8,32,128]{2,1,0:T(8,128)S(1)}, u32[]{:S(2)}, u32[]{:S(2)}) async-start(f32[8,32,128]{2,1,0:T(8,128)} %bitcast.5), calls=%async_computation | async-start | bytes 262144 | tf_op jit(solution)/shard_map/all_to_all | solution.py:26
  13.4 0.2 fusion.14
  13.6 0.0 copy-done.6
  13.6 0.2 fusion.24
  13.9 0.5 copy-done.2
  14.4 4.2 %all-to-all-done = f32[8,32,128]{2,1,0:T(8,128)S(1)} async-done(((f32[8,32,128]{2,1,0:T(8,128)}), f32[8,32,128]{2,1,0:T(8,128)S(1)}, u32[]{:S(2)}, u32[]{:S(2)}) %all-to-all-start) | async-done | bytes 131104 | tf_op jit(solution)/shard_map/all_to_all | solution.py:26
  18.7 11.1 %collective-permute-start.1 = (f32[16,128]{1,0:T(8,128)S(1)}, f32[16,128]{1,0:T(8,128)S(1)}, u32[]{:S(2)}, u32[]{:S(2)}) collective-permute-start(f32[16,128]{1,0:T(8,128)S(1)} %dynamic-slice_bitcast_fusion), channel_id=1, source_target_pairs={{0,64},{64,0},{1,65},{65,1},{2,66},{66,2},{3,67},{67,3},{4,68},{68... | collective-permute-start | bytes 24584 | tf_op jit(solution)/shard_map/ppermute | solution.py:22
  29.8 2.9 %collective-permute-start.2 = (f32[256,128]{1,0:T(8,128)S(1)}, f32[256,128]{1,0:T(8,128)S(1)}, u32[]{:S(2)}, u32[]{:S(2)}) collective-permute-start(f32[256,128]{1,0:T(8,128)S(1)} %copy-done.5), channel_id=1, source_target_pairs={{0,64},{64,0},{1,65},{65,1},{2,66},{66,2},{3,67},{67,3},{4,68},{68... | collective-permute-start | bytes 393224 | tf_op jit(solution)/shard_map/ppermute | solution.py:22
  32.7 0.0 collective-permute-done.1
  32.7 0.6 broadcast_in_dim.18
  33.3 4.7 %all-to-all-start.1 = ((f32[8,16,128]{2,1,0:T(8,128)}), f32[8,16,128]{2,1,0:T(8,128)S(1)}, u32[]{:S(2)}, u32[]{:S(2)}) async-start(f32[8,16,128]{2,1,0:T(8,128)} %broadcast_in_dim.18), calls=%async_computation.1 | async-start | bytes 131072 | tf_op jit(solution)/shard_map/all_to_all | solution.py:31
  38.0 8.2 %collective-permute-done.2 = f32[256,128]{1,0:T(8,128)S(1)} collective-permute-done((f32[256,128]{1,0:T(8,128)S(1)}, f32[256,128]{1,0:T(8,128)S(1)}, u32[]{:S(2)}, u32[]{:S(2)}) %collective-permute-start.2) | collective-permute-done | bytes 131104 | tf_op jit(solution)/shard_map/ppermute | solution.py:22
  46.2 1.0 fusion.6
  47.2 11.6 %all-to-all-start.2 = ((f32[16,8,512]{2,1,0:T(8,128)}), f32[16,8,512]{2,1,0:T(8,128)S(1)}, u32[]{:S(2)}, u32[]{:S(2)}) async-start(f32[16,8,512]{2,1,0:T(8,128)} %fusion.6), calls=%async_computation.2 | async-start | bytes 524288 | tf_op jit(solution)/shard_map/all_to_all | solution.py:26
  58.8 2.7 %collective-permute-start = (f32[184,256]{1,0:T(8,128)S(1)}, f32[184,256]{1,0:T(8,128)S(1)}, u32[]{:S(2)}, u32[]{:S(2)}) collective-permute-start(f32[184,256]{1,0:T(8,128)S(1)} %get-tuple-element.14), channel_id=1, source_target_pairs={{0,64},{64,0},{1,65},{65,1},{2,66},{66,2},{3,67},{67,3},{4,68},{68... | collective-permute-start | bytes 565256 | tf_op jit(solution)/shard_map/ppermute | solution.py:22
  61.5 6.3 %all-to-all-done.2 = f32[16,8,512]{2,1,0:T(8,128)S(1)} async-done(((f32[16,8,512]{2,1,0:T(8,128)}), f32[16,8,512]{2,1,0:T(8,128)S(1)}, u32[]{:S(2)}, u32[]{:S(2)}) %all-to-all-start.2) | async-done | bytes 262176 | tf_op jit(solution)/shard_map/all_to_all | solution.py:26
  67.7 4.3 %collective-permute-start.3 = (f32[8,512]{1,0:T(8,128)S(1)}, f32[8,512]{1,0:T(8,128)S(1)}, u32[]{:S(2)}, u32[]{:S(2)}) collective-permute-start(f32[8,512]{1,0:T(8,128)S(1)} %reduce_sum.37), channel_id=1, source_target_pairs={{0,16},{16,0},{1,17},{17,1},{2,18},{18,2},{3,19},{19,3},{4,20},{20... | collective-permute-start | bytes 49160 | tf_op jit(solution)/shard_map/ppermute | solution.py:22
  72.0 3.9 %collective-permute-done = f32[184,256]{1,0:T(8,128)S(1)} collective-permute-done((f32[184,256]{1,0:T(8,128)S(1)}, f32[184,256]{1,0:T(8,128)S(1)}, u32[]{:S(2)}, u32[]{:S(2)}) %collective-permute-start) | collective-permute-done | bytes 188448 | tf_op jit(solution)/shard_map/ppermute | solution.py:22
  76.0 8.6 %collective-permute-done.3 = f32[8,512]{1,0:T(8,128)S(1)} collective-permute-done((f32[8,512]{1,0:T(8,128)S(1)}, f32[8,512]{1,0:T(8,128)S(1)}, u32[]{:S(2)}, u32[]{:S(2)}) %collective-permute-start.3) | collective-permute-done | bytes 16416 | tf_op jit(solution)/shard_map/ppermute | solution.py:22
  84.5 0.7 broadcast_in_dim.19
  85.3 8.7 %all-to-all-start.3 = ((f32[16,8,512]{2,1,0:T(8,128)}), f32[16,8,512]{2,1,0:T(8,128)S(1)}, u32[]{:S(2)}, u32[]{:S(2)}) async-start(f32[16,8,512]{2,1,0:T(8,128)} %broadcast_in_dim.19), calls=%async_computation.3 | async-start | bytes 524288 | tf_op jit(solution)/shard_map/all_to_all | solution.py:31
  94.0 0.0 slice-start.1
  94.0 9.1 %all-to-all-done.3 = f32[16,8,512]{2,1,0:T(8,128)S(1)} async-done(((f32[16,8,512]{2,1,0:T(8,128)}), f32[16,8,512]{2,1,0:T(8,128)S(1)}, u32[]{:S(2)}, u32[]{:S(2)}) %all-to-all-start.3) | async-done | bytes 262176 | tf_op jit(solution)/shard_map/all_to_all | solution.py:31
  103.1 0.3 fusion.9
  103.4 0.8 broadcast_in_dim.36
  104.2 4.5 %all-to-all-start.4 = ((f32[16,32,256]{2,1,0:T(8,128)}), f32[16,32,256]{2,1,0:T(8,128)S(1)}, u32[]{:S(2)}, u32[]{:S(2)}) async-start(f32[16,32,256]{2,1,0:T(8,128)} %broadcast_in_dim.36), calls=%async_computation.4 | async-start | bytes 1048576 | tf_op jit(solution)/shard_map/all_to_all | solution.py:31
  108.7 3.6 %collective-permute-start.4 = (f32[128,128]{1,0:T(8,128)S(1)}, f32[128,128]{1,0:T(8,128)S(1)}, u32[]{:S(2)}, u32[]{:S(2)}) collective-permute-start(f32[128,128]{1,0:T(8,128)S(1)} %fusion.9), channel_id=1, source_target_pairs={{0,32},{32,0},{1,33},{33,1},{2,34},{34,2},{3,35},{35,3},{4,36},{36... | collective-permute-start | bytes 196616 | tf_op jit(solution)/shard_map/ppermute | solution.py:22
  112.4 0.9 collective-permute-done.4
  113.3 2.2 %collective-permute-start.5 = (f32[128,128]{1,0:T(8,128)S(1)}, f32[128,128]{1,0:T(8,128)S(1)}, u32[]{:S(2)}, u32[]{:S(2)}) collective-permute-start(f32[128,128]{1,0:T(8,128)S(1)} %add.94), channel_id=1, source_target_pairs={{0,128},{128,0},{1,129},{129,1},{2,130},{130,2},{3,131},{131,3},{4... | collective-permute-start | bytes 196616 | tf_op jit(solution)/shard_map/ppermute | solution.py:22
  115.5 3.1 %collective-permute-done.5 = f32[128,128]{1,0:T(8,128)S(1)} collective-permute-done((f32[128,128]{1,0:T(8,128)S(1)}, f32[128,128]{1,0:T(8,128)S(1)}, u32[]{:S(2)}, u32[]{:S(2)}) %collective-permute-start.5) | collective-permute-done | bytes 65568 | tf_op jit(solution)/shard_map/ppermute | solution.py:22
  118.6 3.7 %collective-permute-start.6 = (f32[128,128]{1,0:T(8,128)S(1)}, f32[128,128]{1,0:T(8,128)S(1)}, u32[]{:S(2)}, u32[]{:S(2)}) collective-permute-start(f32[128,128]{1,0:T(8,128)S(1)} %add.95), channel_id=1, source_target_pairs={{0,256},{256,0},{1,257},{257,1},{2,258},{258,2},{3,259},{259,3},{4... | collective-permute-start | bytes 196616 | tf_op jit(solution)/shard_map/ppermute | solution.py:22
  122.3 0.4 fusion.3
  122.7 2.4 %collective-permute-done.6 = f32[128,128]{1,0:T(8,128)S(1)} collective-permute-done((f32[128,128]{1,0:T(8,128)S(1)}, f32[128,128]{1,0:T(8,128)S(1)}, u32[]{:S(2)}, u32[]{:S(2)}) %collective-permute-start.6) | collective-permute-done | bytes 65568 | tf_op jit(solution)/shard_map/ppermute | solution.py:22
  125.1 0.0 all-to-all-done.4
  125.1 0.4 fusion.5
  125.6 0.7 convolution_bitcast_fusion
  126.2 19.2 %all_to_all.40 = f32[16,8,1024]{2,1,0:T(8,128)S(1)} all-to-all(f32[16,8,1024]{2,1,0:T(8,128)S(1)} %convolution_bitcast_fusion), channel_id=1, replica_groups=mesh['u'=2,'v'=2,'h'=2,'c'=2,'w'=2,'z'=4,'y'=4] {'z','y'}, dimensions={0} | all-to-all | bytes 1048576 | tf_op jit(solution)/shard_map/all_to_all | solution.py:26
  145.5 3.9 %collective-permute-start.7 = (f32[8,1024]{1,0:T(8,128)S(1)}, f32[8,1024]{1,0:T(8,128)S(1)}, u32[]{:S(2)}, u32[]{:S(2)}) collective-permute-start(f32[8,1024]{1,0:T(8,128)S(1)} %reduce_sum.38), channel_id=1, source_target_pairs={{0,16},{16,0},{1,17},{17,1},{2,18},{18,2},{3,19},{19,3},{4,20},{20... | collective-permute-start | bytes 98312 | tf_op jit(solution)/shard_map/ppermute | solution.py:22
  149.4 4.7 %collective-permute-done.7 = f32[8,1024]{1,0:T(8,128)S(1)} collective-permute-done((f32[8,1024]{1,0:T(8,128)S(1)}, f32[8,1024]{1,0:T(8,128)S(1)}, u32[]{:S(2)}, u32[]{:S(2)}) %collective-permute-start.7) | collective-permute-done | bytes 32800 | tf_op jit(solution)/shard_map/ppermute | solution.py:22
  154.1 17.6 %all_to_all.41 = f32[16,8,1024]{2,1,0:T(8,128)S(1)} all-to-all(f32[16,8,1024]{2,1,0:T(8,128)S(1)} %broadcast_in_dim.37), channel_id=1, replica_groups=mesh['u'=2,'v'=2,'h'=2,'c'=2,'w'=2,'z'=4,'y'=4] {'z','y'}, dimensions={0} | all-to-all | bytes 1048576 | tf_op jit(solution)/shard_map/all_to_all | solution.py:31
  171.7 0.4 fusion
  172.1 13.4 %all_to_all.42 = f32[8,16,256]{2,1,0:T(8,128)S(1)} all-to-all(f32[8,16,256]{2,1,0:T(8,128)S(1)} %fusion), channel_id=1, replica_groups=mesh['u'=2,'v'=2,'h'=2,'c'=2,'w'=2,'z'=4,'y'=4] {'u','v','c'}, dimensions={0} | all-to-all | bytes 262144 | tf_op jit(solution)/shard_map/all_to_all | solution.py:26
  185.5 0.6 copy.9
  (40 shorter events, 0.3 us)
Async XLA Ops:
  0.0 122.3 %copy-start = (f32[2,128,256]{2,1,0:T(8,128)S(1)}, f32[2,128,256]{2,1,0:T(8,128)}, u32[]{:S(2)}) copy-start(f32[2,128,256]{2,1,0:T(8,128)} %param.8) | copy-start | bytes 786436
  0.0 1.0 slice-start
  1.2 1.0 copy-start.3
  2.1 11.3 %copy-start.1 = (f32[2,256,256]{2,1,0:T(8,128)S(1)}, f32[2,256,256]{2,1,0:T(8,128)}, u32[]{:S(2)}) copy-start(f32[2,256,256]{2,1,0:T(8,128)} %param.9) | copy-start | bytes 1572868
  3.0 10.6 %copy-start.6 = (bf16[512,256]{1,0:T(8,128)(2,1)S(1)}, bf16[512,256]{1,0:T(8,128)(2,1)}, u32[]{:S(2)}) copy-start(bf16[512,256]{1,0:T(8,128)(2,1)} %param.7) | copy-start | bytes 786436
  3.1 15.6 %all-to-all-start = ((f32[8,32,128]{2,1,0:T(8,128)}), f32[8,32,128]{2,1,0:T(8,128)S(1)}, u32[]{:S(2)}, u32[]{:S(2)}) async-start(f32[8,32,128]{2,1,0:T(8,128)} %bitcast.5), calls=%async_computation | async-start | bytes 262144 | tf_op jit(solution)/shard_map/all_to_all | solution.py:26
  13.3 1.0 copy-start.2
  14.4 15.4 %copy-start.5 = (f32[256,128]{1,0:T(8,128)S(1)}, f32[256,128]{1,0:T(8,128)}, u32[]{:S(2)}) copy-start(f32[256,128]{1,0:T(8,128)} %param.11) | copy-start | bytes 393220
  18.7 14.0 %collective-permute-start.1 = (f32[16,128]{1,0:T(8,128)S(1)}, f32[16,128]{1,0:T(8,128)S(1)}, u32[]{:S(2)}, u32[]{:S(2)}) collective-permute-start(f32[16,128]{1,0:T(8,128)S(1)} %dynamic-slice_bitcast_fusion), channel_id=1, source_target_pairs={{0,64},{64,0},{1,65},{65,1},{2,66},{66,2},{3,67},{67,3},{4,68},{68... | collective-permute-start | bytes 24584 | tf_op jit(solution)/shard_map/ppermute | solution.py:22
  29.8 16.4 %collective-permute-start.2 = (f32[256,128]{1,0:T(8,128)S(1)}, f32[256,128]{1,0:T(8,128)S(1)}, u32[]{:S(2)}, u32[]{:S(2)}) collective-permute-start(f32[256,128]{1,0:T(8,128)S(1)} %copy-done.5), channel_id=1, source_target_pairs={{0,64},{64,0},{1,65},{65,1},{2,66},{66,2},{3,67},{67,3},{4,68},{68... | collective-permute-start | bytes 393224 | tf_op jit(solution)/shard_map/ppermute | solution.py:22
  33.3 12.8 %all-to-all-start.1 = ((f32[8,16,128]{2,1,0:T(8,128)}), f32[8,16,128]{2,1,0:T(8,128)S(1)}, u32[]{:S(2)}, u32[]{:S(2)}) async-start(f32[8,16,128]{2,1,0:T(8,128)} %broadcast_in_dim.18), calls=%async_computation.1 | async-start | bytes 131072 | tf_op jit(solution)/shard_map/all_to_all | solution.py:31
  47.2 20.6 %all-to-all-start.2 = ((f32[16,8,512]{2,1,0:T(8,128)}), f32[16,8,512]{2,1,0:T(8,128)S(1)}, u32[]{:S(2)}, u32[]{:S(2)}) async-start(f32[16,8,512]{2,1,0:T(8,128)} %fusion.6), calls=%async_computation.2 | async-start | bytes 524288 | tf_op jit(solution)/shard_map/all_to_all | solution.py:26
  58.8 17.2 %collective-permute-start = (f32[184,256]{1,0:T(8,128)S(1)}, f32[184,256]{1,0:T(8,128)S(1)}, u32[]{:S(2)}, u32[]{:S(2)}) collective-permute-start(f32[184,256]{1,0:T(8,128)S(1)} %get-tuple-element.14), channel_id=1, source_target_pairs={{0,64},{64,0},{1,65},{65,1},{2,66},{66,2},{3,67},{67,3},{4,68},{68... | collective-permute-start | bytes 565256 | tf_op jit(solution)/shard_map/ppermute | solution.py:22
  67.7 16.8 %collective-permute-start.3 = (f32[8,512]{1,0:T(8,128)S(1)}, f32[8,512]{1,0:T(8,128)S(1)}, u32[]{:S(2)}, u32[]{:S(2)}) collective-permute-start(f32[8,512]{1,0:T(8,128)S(1)} %reduce_sum.37), channel_id=1, source_target_pairs={{0,16},{16,0},{1,17},{17,1},{2,18},{18,2},{3,19},{19,3},{4,20},{20... | collective-permute-start | bytes 49160 | tf_op jit(solution)/shard_map/ppermute | solution.py:22
  76.0 18.0 %copy-start.4 = (f32[184,256]{1,0:T(8,128)}, f32[184,256]{1,0:T(8,128)S(1)}, u32[]{:S(2)}) copy-start(f32[184,256]{1,0:T(8,128)S(1)} %collective-permute-done) | copy-start | bytes 565252
  85.3 17.8 %all-to-all-start.3 = ((f32[16,8,512]{2,1,0:T(8,128)}), f32[16,8,512]{2,1,0:T(8,128)S(1)}, u32[]{:S(2)}, u32[]{:S(2)}) async-start(f32[16,8,512]{2,1,0:T(8,128)} %broadcast_in_dim.19), calls=%async_computation.3 | async-start | bytes 524288 | tf_op jit(solution)/shard_map/all_to_all | solution.py:31
  94.0 9.4 %slice-start.1 = ((f32[184,256]{1,0:T(8,128)}), f32[32,256]{1,0:T(8,128)S(1)}, s32[]{:S(2)}) async-start(f32[184,256]{1,0:T(8,128)} %copy-done.4), calls=%async_computation.9 | async-start | bytes 65536 | tf_op jit(solution)/shard_map/slice | solution.py:91
  104.2 20.9 %all-to-all-start.4 = ((f32[16,32,256]{2,1,0:T(8,128)}), f32[16,32,256]{2,1,0:T(8,128)S(1)}, u32[]{:S(2)}, u32[]{:S(2)}) async-start(f32[16,32,256]{2,1,0:T(8,128)} %broadcast_in_dim.36), calls=%async_computation.4 | async-start | bytes 1048576 | tf_op jit(solution)/shard_map/all_to_all | solution.py:31
  108.7 4.5 %collective-permute-start.4 = (f32[128,128]{1,0:T(8,128)S(1)}, f32[128,128]{1,0:T(8,128)S(1)}, u32[]{:S(2)}, u32[]{:S(2)}) collective-permute-start(f32[128,128]{1,0:T(8,128)S(1)} %fusion.9), channel_id=1, source_target_pairs={{0,32},{32,0},{1,33},{33,1},{2,34},{34,2},{3,35},{35,3},{4,36},{36... | collective-permute-start | bytes 196616 | tf_op jit(solution)/shard_map/ppermute | solution.py:22
  113.3 5.3 %collective-permute-start.5 = (f32[128,128]{1,0:T(8,128)S(1)}, f32[128,128]{1,0:T(8,128)S(1)}, u32[]{:S(2)}, u32[]{:S(2)}) collective-permute-start(f32[128,128]{1,0:T(8,128)S(1)} %add.94), channel_id=1, source_target_pairs={{0,128},{128,0},{1,129},{129,1},{2,130},{130,2},{3,131},{131,3},{4... | collective-permute-start | bytes 196616 | tf_op jit(solution)/shard_map/ppermute | solution.py:22
  118.6 6.5 %collective-permute-start.6 = (f32[128,128]{1,0:T(8,128)S(1)}, f32[128,128]{1,0:T(8,128)S(1)}, u32[]{:S(2)}, u32[]{:S(2)}) collective-permute-start(f32[128,128]{1,0:T(8,128)S(1)} %add.95), channel_id=1, source_target_pairs={{0,256},{256,0},{1,257},{257,1},{2,258},{258,2},{3,259},{259,3},{4... | collective-permute-start | bytes 196616 | tf_op jit(solution)/shard_map/ppermute | solution.py:22
  145.5 8.6 %collective-permute-start.7 = (f32[8,1024]{1,0:T(8,128)S(1)}, f32[8,1024]{1,0:T(8,128)S(1)}, u32[]{:S(2)}, u32[]{:S(2)}) collective-permute-start(f32[8,1024]{1,0:T(8,128)S(1)} %reduce_sum.38), channel_id=1, source_target_pairs={{0,16},{16,0},{1,17},{17,1},{2,18},{18,2},{3,19},{19,3},{4,20},{20... | collective-permute-start | bytes 98312 | tf_op jit(solution)/shard_map/ppermute | solution.py:22

commit v7 on v4

v7 whole, which is shorter than its diff:
```python
import math

import jax
import jax.numpy as jnp
from jax import lax
from jax.sharding import Mesh
from jax.sharding import PartitionSpec as P

PTS = ("x", "h", "c")
CTR = ("w", "z", "y")
SIZES = {"x": 4, "h": 2, "c": 2, "w": 2, "z": 4, "y": 4}
HIGH = lax.Precision.HIGH


def dot(a, b, ca, cb):
    return lax.dot_general(
        a, b, (((ca,), (cb,)), ((), ())), precision=HIGH, preferred_element_type=jnp.float32
    )


def swap(a, axis):
    return lax.ppermute(a, axis, [(0, 1), (1, 0)])


def exchange(a, axes):
    return lax.all_to_all(a, axes, 0, 0, tiled=True)


def copies(a, n):
    return jnp.broadcast_to(a[None], (n, *a.shape))


def local(points, labels, centres, coeffs, diag_inverse, off_block):
    zy, xy = ("z", "y"), ("x", "y")
    y, z = lax.axis_index("y"), lax.axis_index("z")

    part = dot(coeffs[1], diag_inverse[1], 0, 1)
    part = jnp.sum(exchange(part.reshape(4, 64, 128), "x"), 0)

    diag = diag_inverse[0].reshape(128, 2, 128).transpose(1, 0, 2).reshape(256, 128)
    coeff = coeffs[0].T.reshape(4, 64, 2, 128).transpose(0, 2, 1, 3).reshape(4, 128, 128)
    own = jnp.concatenate([copies(off_block, 4), copies(diag, 4), coeff], 1)
    part, own = lax.optimization_barrier((part, own))
    blocks = exchange(own, "x")
    part = part + swap(part, "c")
    part = part + swap(part, "h")
    second, blocks = lax.optimization_barrier((part, blocks))

    carried = dot(second, blocks[:, :256], 1, 2)
    carried = carried.reshape(4, 16, 4, 256).transpose(0, 2, 1, 3).reshape(16, 16, 256)
    carried = jnp.sum(exchange(carried, zy), 0)
    coeff = blocks[:, 512:].reshape(4, 2, 64, 128)
    coeff = lax.dynamic_slice(coeff, (y, 0, z * 16, 0), (1, 2, 16, 128))
    coeff = coeff.reshape(2, 16, 128).transpose(1, 0, 2).reshape(16, 256)
    rest = (coeff - carried) - swap(carried, "w")
    rest, centres = lax.optimization_barrier((rest, centres))
    centre_copies = copies(centres.reshape(256, 256), 4)
    rest = exchange(copies(rest, 16), zy)
    rest = rest.reshape(4, 4, 16, 2, 128).transpose(0, 2, 1, 3, 4).reshape(64, 8, 128)

    diag = blocks[:, 256:512].reshape(8, 128, 128)
    first = lax.dot_general(
        rest,
        diag,
        (((1, 2), (0, 2)), ((), ())),
        precision=HIGH,
        preferred_element_type=jnp.float32,
    )
    first, centre_copies = lax.optimization_barrier((first, centre_copies))
    centres_y = exchange(centre_copies, "y").reshape(1024, 256)
    first = first + swap(first, "c")
    first = first + swap(first, "h")
    first, centres_y = lax.optimization_barrier((first, centres_y))

    solved = jnp.concatenate([first, second], 1).reshape(4, 16, 256)
    solved = exchange(copies(solved, 4).reshape(16, 16, 256), xy)
    solved = solved.reshape(4, 4, 16, 256).transpose(0, 2, 1, 3).reshape(64, 1024)

    score = dot(points, centres_y, 1, 1) / math.sqrt(points.shape[1])
    kernel = score + score * score * score / 3.0
    pred_scale = 1.0 / (2.0 * math.sqrt(256 * 32))
    pred = dot(solved, kernel, 1, 1).reshape(4, 16, 512)
    pred = jnp.sum(exchange(pred, "z"), 0)
    pred = pred + swap(pred, "w")

    row = lax.broadcasted_iota(jnp.int32, (16, 256), 0)
    chosen = lax.broadcasted_iota(jnp.int32, (16, 256), 1) == z * 64 + y * 16 + row
    target = lax.dot_general(
        chosen.astype(labels.dtype),
        labels,
        (((1,), (1,)), ((), ())),
        preferred_element_type=jnp.float32,
    )
    weights = jnp.tanh(pred * pred_scale - target)
    weights = exchange(copies(weights, 4), "z").reshape(64, 512)

    scale = 1.0 / (2.0 * math.sqrt(points.shape[0] * 16))
    term = dot(weights, kernel, 1, 0)
    term = term.reshape(4, 16, 4, 256).transpose(0, 2, 1, 3).reshape(16, 16, 256)
    term = jnp.sum(exchange(term, xy).reshape(4, 4, 16, 256), 0)
    term = jnp.sum(exchange(term, ("h", "c")), 0) * scale
    return term.reshape(16, 2, 128).transpose(1, 2, 0)


def solution(mesh):
    fine = Mesh(mesh.devices.reshape(tuple(SIZES.values())), tuple(SIZES))
    return jax.shard_map(
        local,
        mesh=fine,
        in_specs=(
            P(PTS, None),
            P(PTS, None),
            P(None, CTR, None),
            P(None, PTS, None),
            P(None, CTR, PTS),
            P(PTS, CTR),
        ),
        out_specs=P(None, CTR, PTS),
        check_vma=False,
    )
```

time: 190 us -> 192 us (1.011)
  blocking collectives: 67.1 us -> 48.8 us
  starting transfers between devices: 71.2 us -> 85.6 us
  matrix products: 3.75 us -> 11 us
  waiting for transfers between devices: 41.5 us -> 36.8 us
    all_to_all x5 -> x3, blocking collectives: 67.1 us -> 48.8 us  [exchange(): return lax.all_to_all(a, axes, 0, 0, tiled=True)]
    all_to_all x4 -> x7, starting transfers between devices: 20.7 us -> 31.7 us  [exchange(): return lax.all_to_all(a, axes, 0, 0, tiled=True)]
    dot_general x6 -> x5, matrix products: 3.56 us -> 10.4 us  [dot(): lax.dot_general(a, b, (((ca,), (cb,)), ((), ())), precision=HIGH, preferr...]
    all_to_all x4 -> x7, waiting for transfers between devices: 33.9 us -> 29.1 us  [exchange(): return lax.all_to_all(a, axes, 0, 0, tiled=True)]
    ppermute x5 -> x6, starting transfers between devices: 50.5 us -> 53.9 us  [swap(): return lax.ppermute(a, axis, [(0, 1), (1, 0)])]
    ppermute x5 -> x6, waiting for transfers between devices: 7.66 us -> 7.75 us  [swap(): return lax.ppermute(a, axis, [(0, 1), (1, 0)])]
  transfers between devices with their start and end apart: 9 -> 13, of which waited for: 9 -> 11; matrix products, arithmetic and copies ran while one was open for 0% -> 3% of each run, Pallas kernels for 0% -> 0%
where the time goes in v7:
time: 192 us; the launch traced here: 190 us
  starting transfers between devices  85.6 us (45%)
  blocking collectives  48.8 us (25%)
  waiting for transfers between devices  36.8 us (19%)
  matrix products  11 us (6%)
  local copies, waits for them, and re-layouts  6.19 us (3%)
    ppermute x6, starting transfers between devices, swap(): return lax.ppermute(a, axis, [(0, 1), (1, 0)])  53.9 us
    all_to_all x3, blocking collectives, exchange(): return lax.all_to_all(a, axes, 0, 0, tiled=True)  48.8 us
    all_to_all x7, starting transfers between devices, exchange(): return lax.all_to_all(a, axes, 0, 0, tiled=True)  31.7 us
    all_to_all x7, waiting for transfers between devices, exchange(): return lax.all_to_all(a, axes, 0, 0, tiled=True)  29.1 us
    dot_general x5, matrix products, dot(): lax.dot_general(a, b, (((ca,), (cb,)), ((), ())), precision=HIGH, preferr...  10.4 us
    ppermute x6, waiting for transfers between devices, swap(): return lax.ppermute(a, axis, [(0, 1), (1, 0)])  7.75 us
  transfers between devices with their start and end apart: 13, of which 11 were waited for; matrix products, arithmetic and copies ran while one was open for 3% of the time, Pallas kernels for 0%

profile of v7, /device:TPU:1, one launch (start us, length us, event | category | flops | bytes accessed | tf_op | source)
XLA Modules:
  0.0 190.0 jit_solution(7845643135101468918)
XLA Ops:
  0.0 1.1 slice_bitcast_fusion
  1.1 0.0 copy-start.4
  1.1 0.1 copy.21
  1.3 1.8 fusion.15
  3.1 4.8 %all-to-all-start = ((f32[4,64,128]{2,1,0:T(8,128)}), f32[4,64,128]{2,1,0:T(8,128)S(1)}, u32[]{:S(2)}, u32[]{:S(2)}) async-start(f32[4,64,128]{2,1,0:T(8,128)} %fusion.15), calls=%async_computation | async-start | bytes 262144 | tf_op jit(solution)/shard_map/all_to_all | solution.py:26
  8.0 0.1 copy.23
  8.1 0.1 reshape.66
  8.3 0.1 reshape_squeeze.3
  8.5 1.2 pad_maximum_fusion
  9.6 3.2 %all-to-all-done = f32[4,64,128]{2,1,0:T(8,128)S(1)} async-done(((f32[4,64,128]{2,1,0:T(8,128)}), f32[4,64,128]{2,1,0:T(8,128)S(1)}, u32[]{:S(2)}, u32[]{:S(2)}) %all-to-all-start) | async-done | bytes 131104 | tf_op jit(solution)/shard_map/all_to_all | solution.py:26
  12.8 3.6 %all-to-all-start.1 = ((f32[4,640,128]{2,1,0:T(8,128)}), f32[4,640,128]{2,1,0:T(8,128)S(1)}, u32[]{:S(2)}, u32[]{:S(2)}) async-start(f32[4,640,128]{2,1,0:T(8,128)} %pad_maximum_fusion), calls=%async_computation.1 | async-start | bytes 2621440 | tf_op jit(solution)/shard_map/all_to_all | solution.py:26
  16.4 8.4 %collective-permute-start = (f32[64,128]{1,0:T(8,128)S(1)}, f32[64,128]{1,0:T(8,128)S(1)}, u32[]{:S(2)}, u32[]{:S(2)}) collective-permute-start(f32[64,128]{1,0:T(8,128)S(1)} %reduce_sum.45), channel_id=1, source_target_pairs={{0,32},{32,0},{1,33},{33,1},{2,34},{34,2},{3,35},{35,3},{4,36},{36... | collective-permute-start | bytes 98312 | tf_op jit(solution)/shard_map/ppermute | solution.py:22
  24.8 0.8 collective-permute-done
  25.6 11.1 %collective-permute-start.1 = (f32[64,128]{1,0:T(8,128)S(1)}, f32[64,128]{1,0:T(8,128)S(1)}, u32[]{:S(2)}, u32[]{:S(2)}) collective-permute-start(f32[64,128]{1,0:T(8,128)S(1)} %add.37), channel_id=1, source_target_pairs={{0,64},{64,0},{1,65},{65,1},{2,66},{66,2},{3,67},{67,3},{4,68},{68... | collective-permute-start | bytes 98312 | tf_op jit(solution)/shard_map/ppermute | solution.py:22
  36.7 2.3 %collective-permute-done.1 = f32[64,128]{1,0:T(8,128)S(1)} collective-permute-done((f32[64,128]{1,0:T(8,128)S(1)}, f32[64,128]{1,0:T(8,128)S(1)}, u32[]{:S(2)}, u32[]{:S(2)}) %collective-permute-start.1) | collective-permute-done | bytes 32800 | tf_op jit(solution)/shard_map/ppermute | solution.py:22
  39.0 0.4 fusion.11
  39.4 0.7 copy.26
  40.1 4.6 %all-to-all-start.2 = ((f32[16,16,256]{2,1,0:T(8,128)}), f32[16,16,256]{2,1,0:T(8,128)S(1)}, u32[]{:S(2)}, u32[]{:S(2)}) async-start(f32[16,16,256]{2,1,0:T(8,128)} %bitcast.17), calls=%async_computation.2 | async-start | bytes 524288 | tf_op jit(solution)/shard_map/all_to_all | solution.py:26
  44.8 8.9 %all-to-all-done.2 = f32[16,16,256]{2,1,0:T(8,128)S(1)} async-done(((f32[16,16,256]{2,1,0:T(8,128)}), f32[16,16,256]{2,1,0:T(8,128)S(1)}, u32[]{:S(2)}, u32[]{:S(2)}) %all-to-all-start.2) | async-done | bytes 262176 | tf_op jit(solution)/shard_map/all_to_all | solution.py:26
  53.7 9.3 %collective-permute-start.2 = (f32[16,256]{1,0:T(8,128)S(1)}, f32[16,256]{1,0:T(8,128)S(1)}, u32[]{:S(2)}, u32[]{:S(2)}) collective-permute-start(f32[16,256]{1,0:T(8,128)S(1)} %reduce_sum.46), channel_id=1, source_target_pairs={{0,16},{16,0},{1,17},{17,1},{2,18},{18,2},{3,19},{19,3},{4,20},{20... | collective-permute-start | bytes 49160 | tf_op jit(solution)/shard_map/ppermute | solution.py:22
  63.1 1.1 collective-permute-done.2
  64.2 0.7 broadcast_in_dim.42
  64.9 4.3 %all-to-all-start.3 = ((f32[16,16,256]{2,1,0:T(8,128)}), f32[16,16,256]{2,1,0:T(8,128)S(1)}, u32[]{:S(2)}, u32[]{:S(2)}) async-start(f32[16,16,256]{2,1,0:T(8,128)} %broadcast_in_dim.42), calls=%async_computation.3 | async-start | bytes 524288 | tf_op jit(solution)/shard_map/all_to_all | solution.py:26
  69.2 8.8 %all-to-all-done.3 = f32[16,16,256]{2,1,0:T(8,128)S(1)} async-done(((f32[16,16,256]{2,1,0:T(8,128)}), f32[16,16,256]{2,1,0:T(8,128)S(1)}, u32[]{:S(2)}, u32[]{:S(2)}) %all-to-all-start.3) | async-done | bytes 262176 | tf_op jit(solution)/shard_map/all_to_all | solution.py:26
  78.1 0.1 reshape.73
  78.2 0.4 convolution_bitcast_fusion
  78.6 1.1 broadcast_in_dim.44
  79.7 3.5 %all-to-all-start.4 = ((f32[4,256,256]{2,1,0:T(8,128)}), f32[4,256,256]{2,1,0:T(8,128)S(1)}, u32[]{:S(2)}, u32[]{:S(2)}) async-start(f32[4,256,256]{2,1,0:T(8,128)} %broadcast_in_dim.44), calls=%async_computation.4 | async-start | bytes 2097152 | tf_op jit(solution)/shard_map/all_to_all | solution.py:26
  83.2 5.6 %collective-permute-start.3 = (f32[64,128]{1,0:T(8,128)S(1)}, f32[64,128]{1,0:T(8,128)S(1)}, u32[]{:S(2)}, u32[]{:S(2)}) collective-permute-start(f32[64,128]{1,0:T(8,128)S(1)} %convolution_bitcast_fusion), channel_id=1, source_target_pairs={{0,32},{32,0},{1,33},{33,1},{2,34},{34,2},{3,35},{35,3},{4,36},{36... | collective-permute-start | bytes 98312 | tf_op jit(solution)/shard_map/ppermute | solution.py:22
  88.9 0.8 collective-permute-done.3
  89.7 11.9 %collective-permute-start.4 = (f32[64,128]{1,0:T(8,128)S(1)}, f32[64,128]{1,0:T(8,128)S(1)}, u32[]{:S(2)}, u32[]{:S(2)}) collective-permute-start(f32[64,128]{1,0:T(8,128)S(1)} %add.41), channel_id=1, source_target_pairs={{0,64},{64,0},{1,65},{65,1},{2,66},{66,2},{3,67},{67,3},{4,68},{68... | collective-permute-start | bytes 98312 | tf_op jit(solution)/shard_map/ppermute | solution.py:22
  101.6 1.4 collective-permute-done.4
  103.1 0.8 broadcast_in_dim.46
  103.9 0.3 copy-done.1
  104.2 7.5 %all-to-all-start.5 = ((f32[16,16,256]{2,1,0:T(8,128)}), f32[16,16,256]{2,1,0:T(8,128)S(1)}, u32[]{:S(2)}, u32[]{:S(2)}) async-start(f32[16,16,256]{2,1,0:T(8,128)} %bitcast.25), calls=%async_computation.5 | async-start | bytes 524288 | tf_op jit(solution)/shard_map/all_to_all | solution.py:26
  111.7 3.8 %fusion.6 = (f32[1024,512]{1,0:T(8,128)S(1)}, f32[1024,512]{1,0:T(8,128)}) fusion(f32[1024,256]{1,0:T(8,128)} %bitcast.77, f32[512,256]{1,0:T(8,128)S(1)} %copy-done), kind=kOutput, calls=%fused_computation.7 | convolution fusion | flops 807927808 | bytes 5767168 | tf_op jit(solution)/shard_map/dot_general | solution.py:16
  115.5 3.5 %all-to-all-done.5 = f32[16,16,256]{2,1,0:T(8,128)S(1)} async-done(((f32[16,16,256]{2,1,0:T(8,128)}), f32[16,16,256]{2,1,0:T(8,128)S(1)}, u32[]{:S(2)}, u32[]{:S(2)}) %all-to-all-start.5) | async-done | bytes 262176 | tf_op jit(solution)/shard_map/all_to_all | solution.py:26
  119.0 3.2 %fusion.3 = f32[4,16,512]{2,1,0:T(8,128)} fusion(f32[4,16,1024]{2,1,0:T(8,128)S(1)} %bitcast.93, f32[1024,512]{1,0:T(8,128)} %get-tuple-element.28), kind=kOutput, calls=%fused_computation.5 | convolution fusion | flops 203948032 | bytes 2490368 | tf_op jit(solution)/shard_map/dot_general | solution.py:16
  122.3 3.3 %all-to-all-start.6 = ((f32[4,16,512]{2,1,0:T(8,128)}), f32[4,16,512]{2,1,0:T(8,128)S(1)}, u32[]{:S(2)}, u32[]{:S(2)}) async-start(f32[4,16,512]{2,1,0:T(8,128)} %fusion.3), calls=%async_computation.6 | async-start | bytes 262144 | tf_op jit(solution)/shard_map/all_to_all | solution.py:26
  125.6 4.7 %all-to-all-done.6 = f32[4,16,512]{2,1,0:T(8,128)S(1)} async-done(((f32[4,16,512]{2,1,0:T(8,128)}), f32[4,16,512]{2,1,0:T(8,128)S(1)}, u32[]{:S(2)}, u32[]{:S(2)}) %all-to-all-start.6) | async-done | bytes 131104 | tf_op jit(solution)/shard_map/all_to_all | solution.py:26
  130.4 7.6 %collective-permute-start.5 = (f32[16,512]{1,0:T(8,128)S(1)}, f32[16,512]{1,0:T(8,128)S(1)}, u32[]{:S(2)}, u32[]{:S(2)}) collective-permute-start(f32[16,512]{1,0:T(8,128)S(1)} %reduce_sum.47), channel_id=1, source_target_pairs={{0,16},{16,0},{1,17},{17,1},{2,18},{18,2},{3,19},{19,3},{4,20},{20... | collective-permute-start | bytes 98312 | tf_op jit(solution)/shard_map/ppermute | solution.py:22
  137.9 1.3 collective-permute-done.5
  139.2 0.2 subtract_tanh_fusion
  139.4 7.2 %all_to_all.50 = f32[4,16,512]{2,1,0:T(8,128)S(1)} all-to-all(f32[4,16,512]{2,1,0:T(8,128)S(1)} %broadcast_in_dim.47), channel_id=1, replica_groups=mesh['x'=4,'h'=2,'c'=2,'w'=2,'z'=4,'y'=4] {'z'}, dimensions={0} | all-to-all | bytes 262144 | tf_op jit(solution)/shard_map/all_to_all | solution.py:26
  146.6 1.1 fusion.13
  147.7 11.1 %all_to_all.51 = f32[16,16,256]{2,1,0:T(8,128)S(1)} all-to-all(f32[16,16,256]{2,1,0:T(8,128)S(1)} %bitcast.81), channel_id=1, replica_groups=mesh['x'=4,'h'=2,'c'=2,'w'=2,'z'=4,'y'=4] {'x','y'}, dimensions={0} | all-to-all | bytes 524288 | tf_op jit(solution)/shard_map/all_to_all | solution.py:26
  158.8 30.6 %all_to_all.52 = f32[4,16,256]{2,1,0:T(8,128)S(1)} all-to-all(f32[4,16,256]{2,1,0:T(8,128)S(1)} %reduce_sum.48), channel_id=1, replica_groups=mesh['x'=4,'h'=2,'c'=2,'w'=2,'z'=4,'y'=4] {'h','c'}, dimensions={0} | all-to-all | bytes 131072 | tf_op jit(solution)/shard_map/all_to_all | solution.py:26
  189.4 0.6 copy.30
  (37 shorter events, 0.4 us)
Async XLA Ops:
  0.0 111.7 %copy-start = (f32[512,256]{1,0:T(8,128)S(1)}, f32[512,256]{1,0:T(8,128)}, u32[]{:S(2)}) copy-start(f32[512,256]{1,0:T(8,128)} %param.6) | copy-start | bytes 1572868
  0.0 8.3 %slice-start = ((f32[2,128,256]{2,1,0:T(8,128)}), f32[1,128,256]{2,1,0:T(8,128)S(1)}, s32[]{:S(2)}) async-start(f32[2,128,256]{2,1,0:T(8,128)} %param.10), calls=%async_computation.10 | async-start | bytes 262144 | tf_op jit(solution)/shard_map/slice | solution.py:40
  1.1 7.3 %copy-start.4 = (f32[256,128]{1,0:T(8,128)S(1)}, f32[256,128]{1,0:T(8,128)}, u32[]{:S(2)}) copy-start(f32[256,128]{1,0:T(8,128)} %param.11) | copy-start | bytes 393220
  3.1 9.7 %all-to-all-start = ((f32[4,64,128]{2,1,0:T(8,128)}), f32[4,64,128]{2,1,0:T(8,128)S(1)}, u32[]{:S(2)}, u32[]{:S(2)}) async-start(f32[4,64,128]{2,1,0:T(8,128)} %fusion.15), calls=%async_computation | async-start | bytes 262144 | tf_op jit(solution)/shard_map/all_to_all | solution.py:26
  12.8 26.2 %all-to-all-start.1 = ((f32[4,640,128]{2,1,0:T(8,128)}), f32[4,640,128]{2,1,0:T(8,128)S(1)}, u32[]{:S(2)}, u32[]{:S(2)}) async-start(f32[4,640,128]{2,1,0:T(8,128)} %pad_maximum_fusion), calls=%async_computation.1 | async-start | bytes 2621440 | tf_op jit(solution)/shard_map/all_to_all | solution.py:26
  16.4 9.2 %collective-permute-start = (f32[64,128]{1,0:T(8,128)S(1)}, f32[64,128]{1,0:T(8,128)S(1)}, u32[]{:S(2)}, u32[]{:S(2)}) collective-permute-start(f32[64,128]{1,0:T(8,128)S(1)} %reduce_sum.45), channel_id=1, source_target_pairs={{0,32},{32,0},{1,33},{33,1},{2,34},{34,2},{3,35},{35,3},{4,36},{36... | collective-permute-start | bytes 98312 | tf_op jit(solution)/shard_map/ppermute | solution.py:22
  25.6 13.4 %collective-permute-start.1 = (f32[64,128]{1,0:T(8,128)S(1)}, f32[64,128]{1,0:T(8,128)S(1)}, u32[]{:S(2)}, u32[]{:S(2)}) collective-permute-start(f32[64,128]{1,0:T(8,128)S(1)} %add.37), channel_id=1, source_target_pairs={{0,64},{64,0},{1,65},{65,1},{2,66},{66,2},{3,67},{67,3},{4,68},{68... | collective-permute-start | bytes 98312 | tf_op jit(solution)/shard_map/ppermute | solution.py:22
  40.1 13.6 %all-to-all-start.2 = ((f32[16,16,256]{2,1,0:T(8,128)}), f32[16,16,256]{2,1,0:T(8,128)S(1)}, u32[]{:S(2)}, u32[]{:S(2)}) async-start(f32[16,16,256]{2,1,0:T(8,128)} %bitcast.17), calls=%async_computation.2 | async-start | bytes 524288 | tf_op jit(solution)/shard_map/all_to_all | solution.py:26
  44.8 33.8 %copy-start.2 = (f32[2,128,256]{2,1,0:T(8,128)S(1)}, f32[2,128,256]{2,1,0:T(8,128)}, u32[]{:S(2)}) copy-start(f32[2,128,256]{2,1,0:T(8,128)} %param.8) | copy-start | bytes 786436
  53.7 10.4 %collective-permute-start.2 = (f32[16,256]{1,0:T(8,128)S(1)}, f32[16,256]{1,0:T(8,128)S(1)}, u32[]{:S(2)}, u32[]{:S(2)}) collective-permute-start(f32[16,256]{1,0:T(8,128)S(1)} %reduce_sum.46), channel_id=1, source_target_pairs={{0,16},{16,0},{1,17},{17,1},{2,18},{18,2},{3,19},{19,3},{4,20},{20... | collective-permute-start | bytes 49160 | tf_op jit(solution)/shard_map/ppermute | solution.py:22
  64.9 13.2 %all-to-all-start.3 = ((f32[16,16,256]{2,1,0:T(8,128)}), f32[16,16,256]{2,1,0:T(8,128)S(1)}, u32[]{:S(2)}, u32[]{:S(2)}) async-start(f32[16,16,256]{2,1,0:T(8,128)} %broadcast_in_dim.42), calls=%async_computation.3 | async-start | bytes 524288 | tf_op jit(solution)/shard_map/all_to_all | solution.py:26
  79.7 23.4 %all-to-all-start.4 = ((f32[4,256,256]{2,1,0:T(8,128)}), f32[4,256,256]{2,1,0:T(8,128)S(1)}, u32[]{:S(2)}, u32[]{:S(2)}) async-start(f32[4,256,256]{2,1,0:T(8,128)} %broadcast_in_dim.44), calls=%async_computation.4 | async-start | bytes 2097152 | tf_op jit(solution)/shard_map/all_to_all | solution.py:26
  83.2 6.5 %collective-permute-start.3 = (f32[64,128]{1,0:T(8,128)S(1)}, f32[64,128]{1,0:T(8,128)S(1)}, u32[]{:S(2)}, u32[]{:S(2)}) collective-permute-start(f32[64,128]{1,0:T(8,128)S(1)} %convolution_bitcast_fusion), channel_id=1, source_target_pairs={{0,32},{32,0},{1,33},{33,1},{2,34},{34,2},{3,35},{35,3},{4,36},{36... | collective-permute-start | bytes 98312 | tf_op jit(solution)/shard_map/ppermute | solution.py:22
  89.7 13.4 %collective-permute-start.4 = (f32[64,128]{1,0:T(8,128)S(1)}, f32[64,128]{1,0:T(8,128)S(1)}, u32[]{:S(2)}, u32[]{:S(2)}) collective-permute-start(f32[64,128]{1,0:T(8,128)S(1)} %add.41), channel_id=1, source_target_pairs={{0,64},{64,0},{1,65},{65,1},{2,66},{66,2},{3,67},{67,3},{4,68},{68... | collective-permute-start | bytes 98312 | tf_op jit(solution)/shard_map/ppermute | solution.py:22
  103.1 1.1 copy-start.1
  104.2 14.8 %all-to-all-start.5 = ((f32[16,16,256]{2,1,0:T(8,128)}), f32[16,16,256]{2,1,0:T(8,128)S(1)}, u32[]{:S(2)}, u32[]{:S(2)}) async-start(f32[16,16,256]{2,1,0:T(8,128)} %bitcast.25), calls=%async_computation.5 | async-start | bytes 524288 | tf_op jit(solution)/shard_map/all_to_all | solution.py:26
  119.0 20.2 %copy-start.3 = (bf16[512,256]{1,0:T(8,128)(2,1)S(1)}, bf16[512,256]{1,0:T(8,128)(2,1)}, u32[]{:S(2)}) copy-start(bf16[512,256]{1,0:T(8,128)(2,1)} %param.7) | copy-start | bytes 786436
  122.3 8.1 %all-to-all-start.6 = ((f32[4,16,512]{2,1,0:T(8,128)}), f32[4,16,512]{2,1,0:T(8,128)S(1)}, u32[]{:S(2)}, u32[]{:S(2)}) async-start(f32[4,16,512]{2,1,0:T(8,128)} %fusion.3), calls=%async_computation.6 | async-start | bytes 262144 | tf_op jit(solution)/shard_map/all_to_all | solution.py:26
  130.4 8.9 %collective-permute-start.5 = (f32[16,512]{1,0:T(8,128)S(1)}, f32[16,512]{1,0:T(8,128)S(1)}, u32[]{:S(2)}, u32[]{:S(2)}) collective-permute-start(f32[16,512]{1,0:T(8,128)S(1)} %reduce_sum.47), channel_id=1, source_target_pairs={{0,16},{16,0},{1,17},{17,1},{2,18},{18,2},{3,19},{19,3},{4,20},{20... | collective-permute-start | bytes 98312 | tf_op jit(solution)/shard_map/ppermute | solution.py:22

commit v8 on v7

v8 whole, which is shorter than its diff:
```python
import math

import jax
import jax.numpy as jnp
from jax import lax
from jax.sharding import Mesh
from jax.sharding import PartitionSpec as P

PTS = ("x", "h", "c")
CTR = ("w", "z", "y")
SIZES = {"x": 4, "h": 2, "c": 2, "w": 2, "z": 4, "y": 4}
HIGH = lax.Precision.HIGH


def dot(a, b, ca, cb):
    return lax.dot_general(
        a, b, (((ca,), (cb,)), ((), ())), precision=HIGH, preferred_element_type=jnp.float32
    )


def halves(a):
    high = lax.reduce_precision(a, 8, 7)
    return high.astype(jnp.bfloat16), (a - high).astype(jnp.bfloat16)


def dot_halves(a, b, ca, cb, free):
    high, low = halves(a)

    def one(left, right):
        return lax.dot_general(
            left, right, ((ca, cb), ((), ())), preferred_element_type=jnp.float32
        )

    both = one(jnp.concatenate([high, low], free), b[0])
    rows = a.shape[free]
    return both[:rows] + (both[rows:] + one(high, b[1]))


def swap(a, axis):
    return lax.ppermute(a, axis, [(0, 1), (1, 0)])


def exchange(a, axes):
    return lax.all_to_all(a, axes, 0, 0, tiled=True)


def copies(a, n):
    return jnp.broadcast_to(a[None], (n, *a.shape))


def local(points, labels, centres, coeffs, diag_inverse, off_block):
    zy, yx = ("z", "y"), ("y", "x")
    y, z = lax.axis_index("y"), lax.axis_index("z")

    part = dot(coeffs[1], diag_inverse[1], 0, 1)
    part = jnp.sum(exchange(part.reshape(4, 64, 128), "x"), 0)

    diag = diag_inverse[0].reshape(128, 2, 128).transpose(1, 0, 2).reshape(256, 128)
    coeff = coeffs[0].T.reshape(4, 64, 2, 128).transpose(0, 2, 1, 3).reshape(4, 128, 128)
    own = jnp.concatenate([copies(off_block, 4), copies(diag, 4), coeff], 1)
    centre_copies = copies(centres.reshape(256, 256), 4)
    part, own, centre_copies = lax.optimization_barrier((part, own, centre_copies))
    blocks = exchange(own, "x")
    part = part + swap(part, "c")
    part = part + swap(part, "h")
    second, blocks = lax.optimization_barrier((part, blocks))

    carried = dot(second, blocks[:, :256], 1, 2).transpose(1, 0, 2)
    carried = jnp.sum(exchange(carried.reshape(16, 16, 256), zy), 0)
    coeff = blocks[:, 512:].reshape(4, 2, 64, 128)
    coeff = lax.dynamic_slice(coeff, (z, 0, y * 16, 0), (1, 2, 16, 128))
    coeff = coeff.reshape(2, 16, 128).transpose(1, 0, 2).reshape(16, 256)
    rest = (coeff - carried) - swap(carried, "w")
    rest = exchange(copies(rest, 16), zy).reshape(4, 64, 256)

    def solve(side):
        return lax.dot_general(
            rest[:, :, side * 128 : side * 128 + 128],
            blocks[:, 256 + side * 128 : 384 + side * 128],
            (((0, 2), (0, 2)), ((), ())),
            precision=HIGH,
            preferred_element_type=jnp.float32,
        )

    first = solve(0) + solve(1)
    first, centre_copies = lax.optimization_barrier((first, centre_copies))
    centres_y = exchange(centre_copies, "y").reshape(1024, 256)
    first = first + swap(first, "c")
    first = first + swap(first, "h")
    first, centres_y = lax.optimization_barrier((first, centres_y))

    solved = jnp.concatenate([first, second], 1).reshape(4, 1, 16, 256)
    solved = jnp.broadcast_to(solved, (4, 4, 16, 256)).reshape(16, 16, 256)
    solved = exchange(solved, yx).reshape(4, 64, 256)

    score = dot(points, centres_y, 1, 1) / math.sqrt(points.shape[1])
    kernel = lax.optimization_barrier(halves(score + score * score * score / 3.0))
    pred_scale = 1.0 / (2.0 * math.sqrt(256 * 32))
    by_y = [side.reshape(512, 4, 256) for side in kernel]
    pred = dot_halves(solved, by_y, (0, 2), (1, 2), 1).reshape(4, 16, 512)
    pred = jnp.sum(exchange(pred, "z"), 0)
    pred = pred + swap(pred, "w")

    row = lax.broadcasted_iota(jnp.int32, (16, 256), 0)
    chosen = lax.broadcasted_iota(jnp.int32, (16, 256), 1) == z * 64 + y * 16 + row
    target = lax.dot_general(
        chosen.astype(labels.dtype),
        labels,
        (((1,), (1,)), ((), ())),
        preferred_element_type=jnp.float32,
    )
    weights = jnp.tanh(pred * pred_scale - target)
    weights = exchange(copies(weights, 4), "z").reshape(64, 512)

    scale = 1.0 / (2.0 * math.sqrt(points.shape[0] * 16))
    term = dot_halves(weights, kernel, (1,), (0,), 0)
    term = term.reshape(64, 4, 256).transpose(1, 0, 2).reshape(16, 16, 256)
    term = jnp.sum(exchange(term, yx).reshape(4, 4, 16, 256), 1)
    c, h = lax.axis_index("c"), lax.axis_index("h")
    term = term.reshape(2, 2, 16, 256)
    keep = lax.dynamic_index_in_dim(term, c, 1, keepdims=False)
    send = lax.dynamic_index_in_dim(term, 1 - c, 1, keepdims=False)
    term = keep + swap(send, "c")
    keep = lax.dynamic_index_in_dim(term, h, 0, keepdims=False)
    send = lax.dynamic_index_in_dim(term, 1 - h, 0, keepdims=False)
    term = (keep + swap(send, "h")) * scale
    return term.reshape(16, 2, 128).transpose(1, 2, 0)


def solution(mesh):
    fine = Mesh(mesh.devices.reshape(tuple(SIZES.values())), tuple(SIZES))
    return jax.shard_map(
        local,
        mesh=fine,
        in_specs=(
            P(PTS, None),
            P(PTS, None),
            P(None, CTR, None),
            P(None, PTS, None),
            P(None, CTR, PTS),
            P(PTS, CTR),
        ),
        out_specs=P(None, CTR, PTS),
        check_vma=False,
    )
```

time: 192 us -> 181 us (0.943)
  blocking collectives: 48.8 us -> 20.4 us
  starting transfers between devices: 85.6 us -> 104 us
  matrix products: 11 us -> 7.6 us
  waiting for transfers between devices: 36.8 us -> 40.1 us
    all_to_all x3 -> x2, blocking collectives: 48.8 us -> 20.4 us  [exchange(): return lax.all_to_all(a, axes, 0, 0, tiled=True)]
    ppermute x6 -> x8, starting transfers between devices: 53.9 us -> 73.6 us  [swap(): return lax.ppermute(a, axis, [(0, 1), (1, 0)])]
    dot_general x5 -> x3, matrix products: 10.4 us -> 4.71 us  [dot(): lax.dot_general(a, b, (((ca,), (cb,)), ((), ())), precision=HIGH, preferr...]
    ppermute x6 -> x8, waiting for transfers between devices: 7.75 us -> 11.4 us  [swap(): return lax.ppermute(a, axis, [(0, 1), (1, 0)])]
    dot_general x1 -> x6, matrix products: 0.4 us -> 2.69 us  [the longest x4 2.17 us: one(): lax.dot_general(left, right, ((ca, cb), ((), ())), preferred_element_type...]
  transfers between devices with their start and end apart: 13 -> 15, of which waited for: 11 -> 13; matrix products, arithmetic and copies ran while one was open for 3% -> 2% of each run, Pallas kernels for 0% -> 0%
where the time goes in v8:
time: 181 us; the launch traced here: 180 us
  starting transfers between devices  104 us (57%)
  waiting for transfers between devices  40.1 us (22%)
  blocking collectives  20.4 us (11%)
  matrix products  7.6 us (4%)
  local copies, waits for them, and re-layouts  5.73 us (3%)
    ppermute x8, starting transfers between devices, swap(): return lax.ppermute(a, axis, [(0, 1), (1, 0)])  73.6 us
    all_to_all x7, starting transfers between devices, exchange(): return lax.all_to_all(a, axes, 0, 0, tiled=True)  30.9 us
    all_to_all x7, waiting for transfers between devices, exchange(): return lax.all_to_all(a, axes, 0, 0, tiled=True)  28.7 us
    all_to_all x2, blocking collectives, exchange(): return lax.all_to_all(a, axes, 0, 0, tiled=True)  20.4 us
    ppermute x8, waiting for transfers between devices, swap(): return lax.ppermute(a, axis, [(0, 1), (1, 0)])  11.4 us
    dot_general x3, matrix products, dot(): lax.dot_general(a, b, (((ca,), (cb,)), ((), ())), precision=HIGH, preferr...  4.71 us
  transfers between devices with their start and end apart: 15, of which 13 were waited for; matrix products, arithmetic and copies ran while one was open for 2% of the time, Pallas kernels for 0%

profile of v8, /device:TPU:1, one launch (start us, length us, event | category | flops | bytes accessed | tf_op | source)
XLA Modules:
  0.0 180.1 jit_solution(13235501991093638139)
XLA Ops:
  0.0 1.1 slice_bitcast_fusion
  1.3 0.9 fusion.22
  2.2 4.8 %all-to-all-start = ((f32[4,64,128]{2,1,0:T(8,128)}), f32[4,64,128]{2,1,0:T(8,128)S(1)}, u32[]{:S(2)}, u32[]{:S(2)}) async-start(f32[4,64,128]{2,1,0:T(8,128)} %fusion.22), calls=%async_computation | async-start | bytes 262144 | tf_op jit(solution)/shard_map/all_to_all | solution.py:44
  7.5 0.4 copy-done.5
  8.0 1.2 pad_maximum_fusion
  9.2 2.7 %all-to-all-done = f32[4,64,128]{2,1,0:T(8,128)S(1)} async-done(((f32[4,64,128]{2,1,0:T(8,128)}), f32[4,64,128]{2,1,0:T(8,128)S(1)}, u32[]{:S(2)}, u32[]{:S(2)}) %all-to-all-start) | async-done | bytes 131104 | tf_op jit(solution)/shard_map/all_to_all | solution.py:44
  11.9 1.1 broadcast_in_dim.43
  13.0 3.5 %all-to-all-start.1 = ((f32[4,640,128]{2,1,0:T(8,128)}), f32[4,640,128]{2,1,0:T(8,128)S(1)}, u32[]{:S(2)}, u32[]{:S(2)}) async-start(f32[4,640,128]{2,1,0:T(8,128)} %pad_maximum_fusion), calls=%async_computation.1 | async-start | bytes 2621440 | tf_op jit(solution)/shard_map/all_to_all | solution.py:44
  16.5 8.4 %collective-permute-start = (f32[64,128]{1,0:T(8,128)S(1)}, f32[64,128]{1,0:T(8,128)S(1)}, u32[]{:S(2)}, u32[]{:S(2)}) collective-permute-start(f32[64,128]{1,0:T(8,128)S(1)} %reduce_sum.36), channel_id=1, source_target_pairs={{0,32},{32,0},{1,33},{33,1},{2,34},{34,2},{3,35},{35,3},{4,36},{36... | collective-permute-start | bytes 98312 | tf_op jit(solution)/shard_map/ppermute | solution.py:40
  24.9 0.8 collective-permute-done
  25.8 11.1 %collective-permute-start.1 = (f32[64,128]{1,0:T(8,128)S(1)}, f32[64,128]{1,0:T(8,128)S(1)}, u32[]{:S(2)}, u32[]{:S(2)}) collective-permute-start(f32[64,128]{1,0:T(8,128)S(1)} %add.71), channel_id=1, source_target_pairs={{0,64},{64,0},{1,65},{65,1},{2,66},{66,2},{3,67},{67,3},{4,68},{68... | collective-permute-start | bytes 98312 | tf_op jit(solution)/shard_map/ppermute | solution.py:40
  36.8 2.3 %collective-permute-done.1 = f32[64,128]{1,0:T(8,128)S(1)} collective-permute-done((f32[64,128]{1,0:T(8,128)S(1)}, f32[64,128]{1,0:T(8,128)S(1)}, u32[]{:S(2)}, u32[]{:S(2)}) %collective-permute-start.1) | collective-permute-done | bytes 32800 | tf_op jit(solution)/shard_map/ppermute | solution.py:40
  39.2 1.1 fusion.7
  40.3 4.7 %all-to-all-start.2 = ((f32[16,16,256]{2,1,0:T(8,128)}), f32[16,16,256]{2,1,0:T(8,128)S(1)}, u32[]{:S(2)}, u32[]{:S(2)}) async-start(f32[16,16,256]{2,1,0:T(8,128)} %bitcast.17), calls=%async_computation.2 | async-start | bytes 524288 | tf_op jit(solution)/shard_map/all_to_all | solution.py:44
  45.0 8.9 %all-to-all-done.2 = f32[16,16,256]{2,1,0:T(8,128)S(1)} async-done(((f32[16,16,256]{2,1,0:T(8,128)}), f32[16,16,256]{2,1,0:T(8,128)S(1)}, u32[]{:S(2)}, u32[]{:S(2)}) %all-to-all-start.2) | async-done | bytes 262176 | tf_op jit(solution)/shard_map/all_to_all | solution.py:44
  53.9 9.3 %collective-permute-start.2 = (f32[16,256]{1,0:T(8,128)S(1)}, f32[16,256]{1,0:T(8,128)S(1)}, u32[]{:S(2)}, u32[]{:S(2)}) collective-permute-start(f32[16,256]{1,0:T(8,128)S(1)} %reduce_sum.37), channel_id=1, source_target_pairs={{0,16},{16,0},{1,17},{17,1},{2,18},{18,2},{3,19},{19,3},{4,20},{20... | collective-permute-start | bytes 49160 | tf_op jit(solution)/shard_map/ppermute | solution.py:40
  63.2 1.1 collective-permute-done.2
  64.3 13.0 %all_to_all.45 = f32[16,16,256]{2,1,0:T(8,128)S(1)} all-to-all(f32[16,16,256]{2,1,0:T(8,128)S(1)} %broadcast_in_dim.44), channel_id=1, replica_groups=mesh['x'=4,'h'=2,'c'=2,'w'=2,'z'=4,'y'=4] {'z','y'}, dimensions={0} | all-to-all | bytes 524288 | tf_op jit(solution)/shard_map/all_to_all | solution.py:44
  77.3 0.3 convolution_bitcast_fusion.3
  77.6 0.3 fusion.6
  77.8 3.5 %all-to-all-start.4 = ((f32[4,256,256]{2,1,0:T(8,128)}), f32[4,256,256]{2,1,0:T(8,128)S(1)}, u32[]{:S(2)}, u32[]{:S(2)}) async-start(f32[4,256,256]{2,1,0:T(8,128)} %broadcast_in_dim.43), calls=%async_computation.4 | async-start | bytes 2097152 | tf_op jit(solution)/shard_map/all_to_all | solution.py:44
  81.4 5.6 %collective-permute-start.3 = (f32[64,128]{1,0:T(8,128)S(1)}, f32[64,128]{1,0:T(8,128)S(1)}, u32[]{:S(2)}, u32[]{:S(2)}) collective-permute-start(f32[64,128]{1,0:T(8,128)S(1)} %fusion.6), channel_id=1, source_target_pairs={{0,32},{32,0},{1,33},{33,1},{2,34},{34,2},{3,35},{35,3},{4,36},{36... | collective-permute-start | bytes 98312 | tf_op jit(solution)/shard_map/ppermute | solution.py:40
  87.0 0.8 collective-permute-done.3
  87.8 11.2 %collective-permute-start.4 = (f32[64,128]{1,0:T(8,128)S(1)}, f32[64,128]{1,0:T(8,128)S(1)}, u32[]{:S(2)}, u32[]{:S(2)}) collective-permute-start(f32[64,128]{1,0:T(8,128)S(1)} %add.76), channel_id=1, source_target_pairs={{0,64},{64,0},{1,65},{65,1},{2,66},{66,2},{3,67},{67,3},{4,68},{68... | collective-permute-start | bytes 98312 | tf_op jit(solution)/shard_map/ppermute | solution.py:40
  99.1 2.1 %collective-permute-done.4 = f32[64,128]{1,0:T(8,128)S(1)} collective-permute-done((f32[64,128]{1,0:T(8,128)S(1)}, f32[64,128]{1,0:T(8,128)S(1)}, u32[]{:S(2)}, u32[]{:S(2)}) %collective-permute-start.4) | collective-permute-done | bytes 32800 | tf_op jit(solution)/shard_map/ppermute | solution.py:40
  101.2 0.8 broadcast_in_dim.46
  102.0 0.3 copy-done.1
  102.3 7.5 %all-to-all-start.5 = ((f32[16,16,256]{2,1,0:T(8,128)}), f32[16,16,256]{2,1,0:T(8,128)S(1)}, u32[]{:S(2)}, u32[]{:S(2)}) async-start(f32[16,16,256]{2,1,0:T(8,128)} %bitcast.23), calls=%async_computation.5 | async-start | bytes 524288 | tf_op jit(solution)/shard_map/all_to_all | solution.py:44
  109.8 2.7 %fusion = (bf16[512,1024]{0,1:T(8,128)(2,1)S(1)}, bf16[512,1024]{0,1:T(8,128)(2,1)S(1)}) fusion(f32[1024,256]{1,0:T(8,128)} %bitcast.102, f32[512,256]{1,0:T(8,128)S(1)} %copy-done), kind=kOutput, calls=%fused_computation.3 | convolution fusion | flops 810024960 | bytes 3670016 | tf_op jit(solution)/shard_map/dot_general | solution.py:16
  112.5 4.9 %all-to-all-done.5 = f32[16,16,256]{2,1,0:T(8,128)S(1)} async-done(((f32[16,16,256]{2,1,0:T(8,128)}), f32[16,16,256]{2,1,0:T(8,128)S(1)}, u32[]{:S(2)}, u32[]{:S(2)}) %all-to-all-start.5) | async-done | bytes 262176 | tf_op jit(solution)/shard_map/all_to_all | solution.py:44
  117.4 0.3 convolution_bitcast_fusion
  117.8 0.9 fusion.5
  118.7 3.3 %all-to-all-start.6 = ((f32[4,16,512]{2,1,0:T(8,128)}), f32[4,16,512]{2,1,0:T(8,128)S(1)}, u32[]{:S(2)}, u32[]{:S(2)}) async-start(f32[4,16,512]{2,1,0:T(8,128)} %bitcast.31), calls=%async_computation.6 | async-start | bytes 262144 | tf_op jit(solution)/shard_map/all_to_all | solution.py:44
  122.1 4.7 %all-to-all-done.6 = f32[4,16,512]{2,1,0:T(8,128)S(1)} async-done(((f32[4,16,512]{2,1,0:T(8,128)}), f32[4,16,512]{2,1,0:T(8,128)S(1)}, u32[]{:S(2)}, u32[]{:S(2)}) %all-to-all-start.6) | async-done | bytes 131104 | tf_op jit(solution)/shard_map/all_to_all | solution.py:44
  126.8 7.7 %collective-permute-start.5 = (f32[16,512]{1,0:T(8,128)S(1)}, f32[16,512]{1,0:T(8,128)S(1)}, u32[]{:S(2)}, u32[]{:S(2)}) collective-permute-start(f32[16,512]{1,0:T(8,128)S(1)} %reduce_sum.38), channel_id=1, source_target_pairs={{0,16},{16,0},{1,17},{17,1},{2,18},{18,2},{3,19},{19,3},{4,20},{20... | collective-permute-start | bytes 98312 | tf_op jit(solution)/shard_map/ppermute | solution.py:40
  134.5 1.3 collective-permute-done.5
  135.8 0.2 subtract_tanh_fusion
  136.0 7.4 %all_to_all.46 = f32[4,16,512]{2,1,0:T(8,128)S(1)} all-to-all(f32[4,16,512]{2,1,0:T(8,128)S(1)} %broadcast_in_dim.47), channel_id=1, replica_groups=mesh['x'=4,'h'=2,'c'=2,'w'=2,'z'=4,'y'=4] {'z'}, dimensions={0} | all-to-all | bytes 262144 | tf_op jit(solution)/shard_map/all_to_all | solution.py:44
  143.4 0.5 fusion.18
  143.9 0.4 fusion.3
  144.4 0.7 copy.36
  145.1 3.5 %all-to-all-start.8 = ((f32[16,16,256]{2,1,0:T(8,128)}), f32[16,16,256]{2,1,0:T(8,128)S(1)}, u32[]{:S(2)}, u32[]{:S(2)}) async-start(f32[16,16,256]{2,1,0:T(8,128)} %bitcast.34), calls=%async_computation.8 | async-start | bytes 524288 | tf_op jit(solution)/shard_map/all_to_all | solution.py:44
  148.6 7.5 %all-to-all-done.8 = f32[16,16,256]{2,1,0:T(8,128)S(1)} async-done(((f32[16,16,256]{2,1,0:T(8,128)}), f32[16,16,256]{2,1,0:T(8,128)S(1)}, u32[]{:S(2)}, u32[]{:S(2)}) %all-to-all-start.8) | async-done | bytes 262176 | tf_op jit(solution)/shard_map/all_to_all | solution.py:44
  156.2 9.1 %collective-permute-start.6 = (f32[2,16,256]{2,1,0:T(8,128)S(1)}, f32[2,16,256]{2,1,0:T(8,128)S(1)}, u32[]{:S(2)}, u32[]{:S(2)}) collective-permute-start(f32[2,16,256]{2,1,0:T(8,128)S(1)} %dynamic-slice_bitcast_fusion), channel_id=1, source_target_pairs={{0,32},{32,0},{1,33},{33,1},{2,34},{34,2},{3,35},{35,3},{4,36},{36... | collective-permute-start | bytes 98312 | tf_op jit(solution)/shard_map/ppermute | solution.py:40
  165.3 0.8 collective-permute-done.6
  166.1 11.2 %collective-permute-start.7 = (f32[16,256]{1,0:T(8,128)S(1)}, f32[16,256]{1,0:T(8,128)S(1)}, u32[]{:S(2)}, u32[]{:S(2)}) collective-permute-start(f32[16,256]{1,0:T(8,128)S(1)} %dynamic-slice_bitcast_fusion.1), channel_id=1, source_target_pairs={{0,64},{64,0},{1,65},{65,1},{2,66},{66,2},{3,67},{67,3},{4,68},{68... | collective-permute-start | bytes 49160 | tf_op jit(solution)/shard_map/ppermute | solution.py:40
  177.3 2.1 %collective-permute-done.7 = f32[16,256]{1,0:T(8,128)S(1)} collective-permute-done((f32[16,256]{1,0:T(8,128)S(1)}, f32[16,256]{1,0:T(8,128)S(1)}, u32[]{:S(2)}, u32[]{:S(2)}) %collective-permute-start.7) | collective-permute-done | bytes 16416 | tf_op jit(solution)/shard_map/ppermute | solution.py:40
  179.5 0.6 copy.29
  (46 shorter events, 0.9 us)
Async XLA Ops:
  0.0 109.8 %copy-start = (f32[512,256]{1,0:T(8,128)S(1)}, f32[512,256]{1,0:T(8,128)}, u32[]{:S(2)}) copy-start(f32[512,256]{1,0:T(8,128)} %param.6) | copy-start | bytes 1572868
  0.0 1.3 copy-start.2
  1.3 6.1 %slice-start = ((f32[2,128,256]{2,1,0:T(8,128)}), f32[1,128,256]{2,1,0:T(8,128)S(1)}, s32[]{:S(2)}) async-start(f32[2,128,256]{2,1,0:T(8,128)} %param.10), calls=%async_computation.9 | async-start | bytes 262144 | tf_op jit(solution)/shard_map/slice | solution.py:58
  2.2 9.7 %all-to-all-start = ((f32[4,64,128]{2,1,0:T(8,128)}), f32[4,64,128]{2,1,0:T(8,128)S(1)}, u32[]{:S(2)}, u32[]{:S(2)}) async-start(f32[4,64,128]{2,1,0:T(8,128)} %fusion.22), calls=%async_computation | async-start | bytes 262144 | tf_op jit(solution)/shard_map/all_to_all | solution.py:44
  7.1 0.9 copy-start.5
  8.0 3.9 %copy-start.3 = (f32[2,128,256]{2,1,0:T(8,128)S(1)}, f32[2,128,256]{2,1,0:T(8,128)}, u32[]{:S(2)}) copy-start(f32[2,128,256]{2,1,0:T(8,128)} %param.8) | copy-start | bytes 786436
  13.0 26.2 %all-to-all-start.1 = ((f32[4,640,128]{2,1,0:T(8,128)}), f32[4,640,128]{2,1,0:T(8,128)S(1)}, u32[]{:S(2)}, u32[]{:S(2)}) async-start(f32[4,640,128]{2,1,0:T(8,128)} %pad_maximum_fusion), calls=%async_computation.1 | async-start | bytes 2621440 | tf_op jit(solution)/shard_map/all_to_all | solution.py:44
  16.5 9.2 %collective-permute-start = (f32[64,128]{1,0:T(8,128)S(1)}, f32[64,128]{1,0:T(8,128)S(1)}, u32[]{:S(2)}, u32[]{:S(2)}) collective-permute-start(f32[64,128]{1,0:T(8,128)S(1)} %reduce_sum.36), channel_id=1, source_target_pairs={{0,32},{32,0},{1,33},{33,1},{2,34},{34,2},{3,35},{35,3},{4,36},{36... | collective-permute-start | bytes 98312 | tf_op jit(solution)/shard_map/ppermute | solution.py:40
  25.8 13.4 %collective-permute-start.1 = (f32[64,128]{1,0:T(8,128)S(1)}, f32[64,128]{1,0:T(8,128)S(1)}, u32[]{:S(2)}, u32[]{:S(2)}) collective-permute-start(f32[64,128]{1,0:T(8,128)S(1)} %add.71), channel_id=1, source_target_pairs={{0,64},{64,0},{1,65},{65,1},{2,66},{66,2},{3,67},{67,3},{4,68},{68... | collective-permute-start | bytes 98312 | tf_op jit(solution)/shard_map/ppermute | solution.py:40
  40.3 13.6 %all-to-all-start.2 = ((f32[16,16,256]{2,1,0:T(8,128)}), f32[16,16,256]{2,1,0:T(8,128)S(1)}, u32[]{:S(2)}, u32[]{:S(2)}) async-start(f32[16,16,256]{2,1,0:T(8,128)} %bitcast.17), calls=%async_computation.2 | async-start | bytes 524288 | tf_op jit(solution)/shard_map/all_to_all | solution.py:44
  53.9 10.4 %collective-permute-start.2 = (f32[16,256]{1,0:T(8,128)S(1)}, f32[16,256]{1,0:T(8,128)S(1)}, u32[]{:S(2)}, u32[]{:S(2)}) collective-permute-start(f32[16,256]{1,0:T(8,128)S(1)} %reduce_sum.37), channel_id=1, source_target_pairs={{0,16},{16,0},{1,17},{17,1},{2,18},{18,2},{3,19},{19,3},{4,20},{20... | collective-permute-start | bytes 49160 | tf_op jit(solution)/shard_map/ppermute | solution.py:40
  77.8 23.4 %all-to-all-start.4 = ((f32[4,256,256]{2,1,0:T(8,128)}), f32[4,256,256]{2,1,0:T(8,128)S(1)}, u32[]{:S(2)}, u32[]{:S(2)}) async-start(f32[4,256,256]{2,1,0:T(8,128)} %broadcast_in_dim.43), calls=%async_computation.4 | async-start | bytes 2097152 | tf_op jit(solution)/shard_map/all_to_all | solution.py:44
  81.4 6.5 %collective-permute-start.3 = (f32[64,128]{1,0:T(8,128)S(1)}, f32[64,128]{1,0:T(8,128)S(1)}, u32[]{:S(2)}, u32[]{:S(2)}) collective-permute-start(f32[64,128]{1,0:T(8,128)S(1)} %fusion.6), channel_id=1, source_target_pairs={{0,32},{32,0},{1,33},{33,1},{2,34},{34,2},{3,35},{35,3},{4,36},{36... | collective-permute-start | bytes 98312 | tf_op jit(solution)/shard_map/ppermute | solution.py:40
  87.8 13.4 %collective-permute-start.4 = (f32[64,128]{1,0:T(8,128)S(1)}, f32[64,128]{1,0:T(8,128)S(1)}, u32[]{:S(2)}, u32[]{:S(2)}) collective-permute-start(f32[64,128]{1,0:T(8,128)S(1)} %add.76), channel_id=1, source_target_pairs={{0,64},{64,0},{1,65},{65,1},{2,66},{66,2},{3,67},{67,3},{4,68},{68... | collective-permute-start | bytes 98312 | tf_op jit(solution)/shard_map/ppermute | solution.py:40
  101.2 1.1 copy-start.1
  102.3 15.1 %all-to-all-start.5 = ((f32[16,16,256]{2,1,0:T(8,128)}), f32[16,16,256]{2,1,0:T(8,128)S(1)}, u32[]{:S(2)}, u32[]{:S(2)}) async-start(f32[16,16,256]{2,1,0:T(8,128)} %bitcast.23), calls=%async_computation.5 | async-start | bytes 524288 | tf_op jit(solution)/shard_map/all_to_all | solution.py:44
  117.7 18.1 %copy-start.4 = (bf16[512,256]{1,0:T(8,128)(2,1)S(1)}, bf16[512,256]{1,0:T(8,128)(2,1)}, u32[]{:S(2)}) copy-start(bf16[512,256]{1,0:T(8,128)(2,1)} %param.7) | copy-start | bytes 786436
  118.7 8.1 %all-to-all-start.6 = ((f32[4,16,512]{2,1,0:T(8,128)}), f32[4,16,512]{2,1,0:T(8,128)S(1)}, u32[]{:S(2)}, u32[]{:S(2)}) async-start(f32[4,16,512]{2,1,0:T(8,128)} %bitcast.31), calls=%async_computation.6 | async-start | bytes 262144 | tf_op jit(solution)/shard_map/all_to_all | solution.py:44
  126.8 9.0 %collective-permute-start.5 = (f32[16,512]{1,0:T(8,128)S(1)}, f32[16,512]{1,0:T(8,128)S(1)}, u32[]{:S(2)}, u32[]{:S(2)}) collective-permute-start(f32[16,512]{1,0:T(8,128)S(1)} %reduce_sum.38), channel_id=1, source_target_pairs={{0,16},{16,0},{1,17},{17,1},{2,18},{18,2},{3,19},{19,3},{4,20},{20... | collective-permute-start | bytes 98312 | tf_op jit(solution)/shard_map/ppermute | solution.py:40
  145.1 11.0 %all-to-all-start.8 = ((f32[16,16,256]{2,1,0:T(8,128)}), f32[16,16,256]{2,1,0:T(8,128)S(1)}, u32[]{:S(2)}, u32[]{:S(2)}) async-start(f32[16,16,256]{2,1,0:T(8,128)} %bitcast.34), calls=%async_computation.8 | async-start | bytes 524288 | tf_op jit(solution)/shard_map/all_to_all | solution.py:44
  156.2 10.0 %collective-permute-start.6 = (f32[2,16,256]{2,1,0:T(8,128)S(1)}, f32[2,16,256]{2,1,0:T(8,128)S(1)}, u32[]{:S(2)}, u32[]{:S(2)}) collective-permute-start(f32[2,16,256]{2,1,0:T(8,128)S(1)} %dynamic-slice_bitcast_fusion), channel_id=1, source_target_pairs={{0,32},{32,0},{1,33},{33,1},{2,34},{34,2},{3,35},{35,3},{4,36},{36... | collective-permute-start | bytes 98312 | tf_op jit(solution)/shard_map/ppermute | solution.py:40
  166.1 13.3 %collective-permute-start.7 = (f32[16,256]{1,0:T(8,128)S(1)}, f32[16,256]{1,0:T(8,128)S(1)}, u32[]{:S(2)}, u32[]{:S(2)}) collective-permute-start(f32[16,256]{1,0:T(8,128)S(1)} %dynamic-slice_bitcast_fusion.1), channel_id=1, source_target_pairs={{0,64},{64,0},{1,65},{65,1},{2,66},{66,2},{3,67},{67,3},{4,68},{68... | collective-permute-start | bytes 49160 | tf_op jit(solution)/shard_map/ppermute | solution.py:40

commit v9 on v8

--- a/solution.py
+++ b/solution.py
@@ -58,14 +58,15 @@
     diag = diag_inverse[0].reshape(128, 2, 128).transpose(1, 0, 2).reshape(256, 128)
     coeff = coeffs[0].T.reshape(4, 64, 2, 128).transpose(0, 2, 1, 3).reshape(4, 128, 128)
     own = jnp.concatenate([copies(off_block, 4), copies(diag, 4), coeff], 1)
-    centre_copies = copies(centres.reshape(256, 256), 4)
-    part, own, centre_copies = lax.optimization_barrier((part, own, centre_copies))
+    part, own = lax.optimization_barrier((part, own))
     blocks = exchange(own, "x")
     part = part + swap(part, "c")
     part = part + swap(part, "h")
     second, blocks = lax.optimization_barrier((part, blocks))
 
     carried = dot(second, blocks[:, :256], 1, 2).transpose(1, 0, 2)
+    carried, flat = lax.optimization_barrier((carried, centres.reshape(256, 256)))
+    others = [flat] + [lax.ppermute(flat, "y", [(i, i ^ k) for i in range(4)]) for k in (1, 2, 3)]
     carried = jnp.sum(exchange(carried.reshape(16, 16, 256), zy), 0)
     coeff = blocks[:, 512:].reshape(4, 2, 64, 128)
     coeff = lax.dynamic_slice(coeff, (z, 0, y * 16, 0), (1, 2, 16, 128))
@@ -83,17 +84,17 @@
         )
 
     first = solve(0) + solve(1)
-    first, centre_copies = lax.optimization_barrier((first, centre_copies))
-    centres_y = exchange(centre_copies, "y").reshape(1024, 256)
     first = first + swap(first, "c")
+    first, others = lax.optimization_barrier((first, others))
     first = first + swap(first, "h")
-    first, centres_y = lax.optimization_barrier((first, centres_y))
 
     solved = jnp.concatenate([first, second], 1).reshape(4, 1, 16, 256)
     solved = jnp.broadcast_to(solved, (4, 4, 16, 256)).reshape(16, 16, 256)
     solved = exchange(solved, yx).reshape(4, 64, 256)
 
-    score = dot(points, centres_y, 1, 1) / math.sqrt(points.shape[1])
+    others = jnp.stack(others)
+    centres_y = [lax.dynamic_index_in_dim(others, y ^ k, 0, keepdims=False) for k in range(4)]
+    score = dot(points, jnp.concatenate(centres_y, 0), 1, 1) / math.sqrt(points.shape[1])
     kernel = lax.optimization_barrier(halves(score + score * score * score / 3.0))
     pred_scale = 1.0 / (2.0 * math.sqrt(256 * 32))
     by_y = [side.reshape(512, 4, 256) for side in kernel]

time: 181 us -> 184 us (1.017)
  blocking collectives: 20.4 us -> 7.43 us
  waiting for transfers between devices: 40.1 us -> 51.8 us
  starting transfers between devices: 104 us -> 108 us
    all_to_all x2 -> x1, blocking collectives: 20.4 us -> 7.43 us  [exchange(): return lax.all_to_all(a, axes, 0, 0, tiled=True)]
    ppermute x0 -> x3, starting transfers between devices: none -> 9.58 us  [local(): lax.ppermute(flat, 'y', [(i, i ^ k) for i in range(4)])]
    ppermute x0 -> x3, waiting for transfers between devices: none -> 6.19 us  [local(): lax.ppermute(flat, 'y', [(i, i ^ k) for i in range(4)])]
    ppermute x8, waiting for transfers between devices: 11.4 us -> 16.7 us  [swap(): return lax.ppermute(a, axis, [(0, 1), (1, 0)])]
    ppermute x8, starting transfers between devices: 73.6 us -> 68.8 us  [swap(): return lax.ppermute(a, axis, [(0, 1), (1, 0)])]
  transfers between devices with their start and end apart: 15 -> 18, of which waited for: 13 -> 15; matrix products, arithmetic and copies ran while one was open for 2% -> 3% of each run, Pallas kernels for 0% -> 0%
where the time goes in v9:
time: 184 us; the launch traced here: 182 us
  starting transfers between devices  108 us (59%)
  waiting for transfers between devices  51.8 us (28%)
  blocking collectives  7.43 us (4%)
  matrix products  7.4 us (4%)
  local copies, waits for them, and re-layouts  5.93 us (3%)
    ppermute x8, starting transfers between devices, swap(): return lax.ppermute(a, axis, [(0, 1), (1, 0)])  68.8 us
    all_to_all x7, starting transfers between devices, exchange(): return lax.all_to_all(a, axes, 0, 0, tiled=True)  29.7 us
    all_to_all x7, waiting for transfers between devices, exchange(): return lax.all_to_all(a, axes, 0, 0, tiled=True)  28.9 us
    ppermute x8, waiting for transfers between devices, swap(): return lax.ppermute(a, axis, [(0, 1), (1, 0)])  16.7 us
    ppermute x3, starting transfers between devices, local(): lax.ppermute(flat, 'y', [(i, i ^ k) for i in range(4)])  9.58 us
    all_to_all x1, blocking collectives, exchange(): return lax.all_to_all(a, axes, 0, 0, tiled=True)  7.43 us
    ppermute x3, waiting for transfers between devices, local(): lax.ppermute(flat, 'y', [(i, i ^ k) for i in range(4)])  6.19 us
    dot_general x3, matrix products, dot(): lax.dot_general(a, b, (((ca,), (cb,)), ((), ())), precision=HIGH, preferr...  4.53 us
  transfers between devices with their start and end apart: 18, of which 15 were waited for; matrix products, arithmetic and copies ran while one was open for 3% of the time, Pallas kernels for 0%

profile of v9, /device:TPU:1, one launch (start us, length us, event | category | flops | bytes accessed | tf_op | source)
XLA Modules:
  0.0 182.5 jit_solution(14988994665002554477)
XLA Ops:
  0.0 1.1 slice_bitcast_fusion
  1.3 0.9 fusion.28
  2.2 4.8 %all-to-all-start = ((f32[4,64,128]{2,1,0:T(8,128)}), f32[4,64,128]{2,1,0:T(8,128)S(1)}, u32[]{:S(2)}, u32[]{:S(2)}) async-start(f32[4,64,128]{2,1,0:T(8,128)} %fusion.28), calls=%async_computation | async-start | bytes 262144 | tf_op jit(solution)/shard_map/all_to_all | solution.py:44
  7.5 0.4 copy-done.4
  8.0 1.2 pad_maximum_fusion
  9.2 2.7 %all-to-all-done = f32[4,64,128]{2,1,0:T(8,128)S(1)} async-done(((f32[4,64,128]{2,1,0:T(8,128)}), f32[4,64,128]{2,1,0:T(8,128)S(1)}, u32[]{:S(2)}, u32[]{:S(2)}) %all-to-all-start) | async-done | bytes 131104 | tf_op jit(solution)/shard_map/all_to_all | solution.py:44
  11.9 3.6 %all-to-all-start.1 = ((f32[4,640,128]{2,1,0:T(8,128)}), f32[4,640,128]{2,1,0:T(8,128)S(1)}, u32[]{:S(2)}, u32[]{:S(2)}) async-start(f32[4,640,128]{2,1,0:T(8,128)} %pad_maximum_fusion), calls=%async_computation.1 | async-start | bytes 2621440 | tf_op jit(solution)/shard_map/all_to_all | solution.py:44
  15.5 8.4 %collective-permute-start = (f32[64,128]{1,0:T(8,128)S(1)}, f32[64,128]{1,0:T(8,128)S(1)}, u32[]{:S(2)}, u32[]{:S(2)}) collective-permute-start(f32[64,128]{1,0:T(8,128)S(1)} %reduce_sum.36), channel_id=1, source_target_pairs={{0,32},{32,0},{1,33},{33,1},{2,34},{34,2},{3,35},{35,3},{4,36},{36... | collective-permute-start | bytes 98312 | tf_op jit(solution)/shard_map/ppermute | solution.py:40
  23.9 0.8 collective-permute-done
  24.7 11.1 %collective-permute-start.1 = (f32[64,128]{1,0:T(8,128)S(1)}, f32[64,128]{1,0:T(8,128)S(1)}, u32[]{:S(2)}, u32[]{:S(2)}) collective-permute-start(f32[64,128]{1,0:T(8,128)S(1)} %add.84), channel_id=1, source_target_pairs={{0,64},{64,0},{1,65},{65,1},{2,66},{66,2},{3,67},{67,3},{4,68},{68... | collective-permute-start | bytes 98312 | tf_op jit(solution)/shard_map/ppermute | solution.py:40
  35.8 2.3 %collective-permute-done.1 = f32[64,128]{1,0:T(8,128)S(1)} collective-permute-done((f32[64,128]{1,0:T(8,128)S(1)}, f32[64,128]{1,0:T(8,128)S(1)}, u32[]{:S(2)}, u32[]{:S(2)}) %collective-permute-start.1) | collective-permute-done | bytes 32800 | tf_op jit(solution)/shard_map/ppermute | solution.py:40
  38.1 1.1 convolution_bitcast_fusion
  39.2 4.8 %all-to-all-start.2 = ((f32[16,16,256]{2,1,0:T(8,128)}), f32[16,16,256]{2,1,0:T(8,128)S(1)}, u32[]{:S(2)}, u32[]{:S(2)}) async-start(f32[16,16,256]{2,1,0:T(8,128)} %bitcast.17), calls=%async_computation.2 | async-start | bytes 524288 | tf_op jit(solution)/shard_map/all_to_all | solution.py:44
  44.0 8.9 %all-to-all-done.2 = f32[16,16,256]{2,1,0:T(8,128)S(1)} async-done(((f32[16,16,256]{2,1,0:T(8,128)}), f32[16,16,256]{2,1,0:T(8,128)S(1)}, u32[]{:S(2)}, u32[]{:S(2)}) %all-to-all-start.2) | async-done | bytes 262176 | tf_op jit(solution)/shard_map/all_to_all | solution.py:44
  52.9 9.3 %collective-permute-start.2 = (f32[16,256]{1,0:T(8,128)S(1)}, f32[16,256]{1,0:T(8,128)S(1)}, u32[]{:S(2)}, u32[]{:S(2)}) collective-permute-start(f32[16,256]{1,0:T(8,128)S(1)} %reduce_sum.37), channel_id=1, source_target_pairs={{0,16},{16,0},{1,17},{17,1},{2,18},{18,2},{3,19},{19,3},{4,20},{20... | collective-permute-start | bytes 49160 | tf_op jit(solution)/shard_map/ppermute | solution.py:40
  62.3 1.1 collective-permute-done.2
  63.4 0.7 broadcast_in_dim.17
  64.1 4.3 %all-to-all-start.3 = ((f32[16,16,256]{2,1,0:T(8,128)}), f32[16,16,256]{2,1,0:T(8,128)S(1)}, u32[]{:S(2)}, u32[]{:S(2)}) async-start(f32[16,16,256]{2,1,0:T(8,128)} %broadcast_in_dim.17), calls=%async_computation.3 | async-start | bytes 524288 | tf_op jit(solution)/shard_map/all_to_all | solution.py:44
  68.4 3.3 %collective-permute-start.4 = (f32[256,256]{1,0:T(8,128)S(1)}, f32[256,256]{1,0:T(8,128)S(1)}, u32[]{:S(2)}, u32[]{:S(2)}) collective-permute-start(f32[256,256]{1,0:T(8,128)S(1)} %bitcast.121), channel_id=1, source_target_pairs={{0,1},{1,0},{2,3},{3,2},{4,5},{5,4},{6,7},{7,6},{8,9},{9,8},{10,11... | collective-permute-start | bytes 786440 | tf_op jit(solution)/shard_map/ppermute | solution.py:69
  71.7 4.3 %collective-permute-start.5 = (f32[256,256]{1,0:T(8,128)S(1)}, f32[256,256]{1,0:T(8,128)S(1)}, u32[]{:S(2)}, u32[]{:S(2)}) collective-permute-start(f32[256,256]{1,0:T(8,128)S(1)} %bitcast.122), channel_id=1, source_target_pairs={{0,2},{1,3},{2,0},{3,1},{4,6},{5,7},{6,4},{7,5},{8,10},{9,11},{10,... | collective-permute-start | bytes 786440 | tf_op jit(solution)/shard_map/ppermute | solution.py:69
  76.0 2.0 %collective-permute-start.6 = (f32[256,256]{1,0:T(8,128)S(1)}, f32[256,256]{1,0:T(8,128)S(1)}, u32[]{:S(2)}, u32[]{:S(2)}) collective-permute-start(f32[256,256]{1,0:T(8,128)S(1)} %bitcast.123), channel_id=1, source_target_pairs={{0,3},{1,2},{2,1},{3,0},{4,7},{5,6},{6,5},{7,4},{8,11},{9,10},{10,... | collective-permute-start | bytes 786440 | tf_op jit(solution)/shard_map/ppermute | solution.py:69
  78.6 5.4 %collective-permute-start.3 = (f32[64,128]{1,0:T(8,128)S(1)}, f32[64,128]{1,0:T(8,128)S(1)}, u32[]{:S(2)}, u32[]{:S(2)}) collective-permute-start(f32[64,128]{1,0:T(8,128)S(1)} %fusion.6), channel_id=1, source_target_pairs={{0,32},{32,0},{1,33},{33,1},{2,34},{34,2},{3,35},{35,3},{4,36},{36... | collective-permute-start | bytes 98312 | tf_op jit(solution)/shard_map/ppermute | solution.py:40
  84.0 0.8 collective-permute-done.3
  84.8 1.8 collective-permute-done.5
  86.6 4.4 %collective-permute-done.6 = f32[256,256]{1,0:T(8,128)S(1)} collective-permute-done((f32[256,256]{1,0:T(8,128)S(1)}, f32[256,256]{1,0:T(8,128)S(1)}, u32[]{:S(2)}, u32[]{:S(2)}) %collective-permute-start.6) | collective-permute-done | bytes 262176 | tf_op jit(solution)/shard_map/ppermute | solution.py:69
  91.0 7.0 %collective-permute-start.7 = (f32[64,128]{1,0:T(8,128)S(1)}, f32[64,128]{1,0:T(8,128)S(1)}, u32[]{:S(2)}, u32[]{:S(2)}) collective-permute-start(f32[64,128]{1,0:T(8,128)S(1)} %add.89), channel_id=1, source_target_pairs={{0,64},{64,0},{1,65},{65,1},{2,66},{66,2},{3,67},{67,3},{4,68},{68... | collective-permute-start | bytes 98312 | tf_op jit(solution)/shard_map/ppermute | solution.py:40
  98.1 0.9 dynamic-slice_bitcast_fusion.3
  99.0 5.5 %collective-permute-done.7 = f32[64,128]{1,0:T(8,128)S(1)} collective-permute-done((f32[64,128]{1,0:T(8,128)S(1)}, f32[64,128]{1,0:T(8,128)S(1)}, u32[]{:S(2)}, u32[]{:S(2)}) %collective-permute-start.7) | collective-permute-done | bytes 32800 | tf_op jit(solution)/shard_map/ppermute | solution.py:40
  104.5 0.7 broadcast_in_dim.37
  105.2 4.6 %all-to-all-start.4 = ((f32[16,16,256]{2,1,0:T(8,128)}), f32[16,16,256]{2,1,0:T(8,128)S(1)}, u32[]{:S(2)}, u32[]{:S(2)}) async-start(f32[16,16,256]{2,1,0:T(8,128)} %bitcast.22), calls=%async_computation.4 | async-start | bytes 524288 | tf_op jit(solution)/shard_map/all_to_all | solution.py:44
  109.8 2.5 %fusion = (bf16[512,1024]{0,1:T(8,128)(2,1)S(1)}, bf16[512,1024]{0,1:T(8,128)(2,1)S(1)}) fusion(f32[512,256]{1,0:T(8,128)S(1)} %copy-done, f32[256,256]{1,0:T(8,128)S(1)} %get-tuple-element.34, f32[256,256]{1,0:T(8,128)} %get-tuple-element.35, f32[256,256]{1,0:T(8,128)} %get-tuple-element.36, f32[256,256]{1,0:T(8,128)S(1)} %get-tuple-element.33), kind=kOutput, calls=%fused_computation.3 | convolution fusion | flops 810811392 | bytes 3670016 | tf_op jit(solution)/shard_map/dot_general | solution.py:16
  112.3 5.0 %all-to-all-done.4 = f32[16,16,256]{2,1,0:T(8,128)S(1)} async-done(((f32[16,16,256]{2,1,0:T(8,128)}), f32[16,16,256]{2,1,0:T(8,128)S(1)}, u32[]{:S(2)}, u32[]{:S(2)}) %all-to-all-start.4) | async-done | bytes 262176 | tf_op jit(solution)/shard_map/all_to_all | solution.py:44
  117.7 0.9 fusion.5
  118.7 4.1 %all-to-all-start.5 = ((f32[4,16,512]{2,1,0:T(8,128)}), f32[4,16,512]{2,1,0:T(8,128)S(1)}, u32[]{:S(2)}, u32[]{:S(2)}) async-start(f32[4,16,512]{2,1,0:T(8,128)} %bitcast.38), calls=%async_computation.5 | async-start | bytes 262144 | tf_op jit(solution)/shard_map/all_to_all | solution.py:44
  122.8 4.8 %all-to-all-done.5 = f32[4,16,512]{2,1,0:T(8,128)S(1)} async-done(((f32[4,16,512]{2,1,0:T(8,128)}), f32[4,16,512]{2,1,0:T(8,128)S(1)}, u32[]{:S(2)}, u32[]{:S(2)}) %all-to-all-start.5) | async-done | bytes 131104 | tf_op jit(solution)/shard_map/all_to_all | solution.py:44
  127.6 7.4 %collective-permute-start.8 = (f32[16,512]{1,0:T(8,128)S(1)}, f32[16,512]{1,0:T(8,128)S(1)}, u32[]{:S(2)}, u32[]{:S(2)}) collective-permute-start(f32[16,512]{1,0:T(8,128)S(1)} %reduce_sum.38), channel_id=1, source_target_pairs={{0,16},{16,0},{1,17},{17,1},{2,18},{18,2},{3,19},{19,3},{4,20},{20... | collective-permute-start | bytes 98312 | tf_op jit(solution)/shard_map/ppermute | solution.py:40
  135.0 1.3 collective-permute-done.8
  136.5 7.4 %all_to_all.40 = f32[4,16,512]{2,1,0:T(8,128)S(1)} all-to-all(f32[4,16,512]{2,1,0:T(8,128)S(1)} %broadcast_in_dim.38), channel_id=1, replica_groups=mesh['x'=4,'h'=2,'c'=2,'w'=2,'z'=4,'y'=4] {'z'}, dimensions={0} | all-to-all | bytes 262144 | tf_op jit(solution)/shard_map/all_to_all | solution.py:44
  143.9 0.5 fusion.24
  144.4 0.4 fusion.3
  144.8 0.7 copy.36
  145.6 3.5 %all-to-all-start.7 = ((f32[16,16,256]{2,1,0:T(8,128)}), f32[16,16,256]{2,1,0:T(8,128)S(1)}, u32[]{:S(2)}, u32[]{:S(2)}) async-start(f32[16,16,256]{2,1,0:T(8,128)} %bitcast.41), calls=%async_computation.7 | async-start | bytes 524288 | tf_op jit(solution)/shard_map/all_to_all | solution.py:44
  149.1 7.5 %all-to-all-done.7 = f32[16,16,256]{2,1,0:T(8,128)S(1)} async-done(((f32[16,16,256]{2,1,0:T(8,128)}), f32[16,16,256]{2,1,0:T(8,128)S(1)}, u32[]{:S(2)}, u32[]{:S(2)}) %all-to-all-start.7) | async-done | bytes 262176 | tf_op jit(solution)/shard_map/all_to_all | solution.py:44
  156.7 11.1 %collective-permute-start.9 = (f32[2,16,256]{2,1,0:T(8,128)S(1)}, f32[2,16,256]{2,1,0:T(8,128)S(1)}, u32[]{:S(2)}, u32[]{:S(2)}) collective-permute-start(f32[2,16,256]{2,1,0:T(8,128)S(1)} %dynamic-slice_bitcast_fusion.4), channel_id=1, source_target_pairs={{0,32},{32,0},{1,33},{33,1},{2,34},{34,2},{3,35},{35,3},{4,36},{36... | collective-permute-start | bytes 98312 | tf_op jit(solution)/shard_map/ppermute | solution.py:40
  167.8 0.8 collective-permute-done.9
  168.6 9.2 %collective-permute-start.10 = (f32[16,256]{1,0:T(8,128)S(1)}, f32[16,256]{1,0:T(8,128)S(1)}, u32[]{:S(2)}, u32[]{:S(2)}) collective-permute-start(f32[16,256]{1,0:T(8,128)S(1)} %dynamic-slice_bitcast_fusion.5), channel_id=1, source_target_pairs={{0,64},{64,0},{1,65},{65,1},{2,66},{66,2},{3,67},{67,3},{4,68},{68... | collective-permute-start | bytes 49160 | tf_op jit(solution)/shard_map/ppermute | solution.py:40
  177.8 4.0 %collective-permute-done.10 = f32[16,256]{1,0:T(8,128)S(1)} collective-permute-done((f32[16,256]{1,0:T(8,128)S(1)}, f32[16,256]{1,0:T(8,128)S(1)}, u32[]{:S(2)}, u32[]{:S(2)}) %collective-permute-start.10) | collective-permute-done | bytes 16416 | tf_op jit(solution)/shard_map/ppermute | solution.py:40
  181.8 0.6 copy.29
  (50 shorter events, 2.0 us)
Async XLA Ops:
  0.0 109.8 %copy-start = (f32[512,256]{1,0:T(8,128)S(1)}, f32[512,256]{1,0:T(8,128)}, u32[]{:S(2)}) copy-start(f32[512,256]{1,0:T(8,128)} %param.6) | copy-start | bytes 1572868
  0.0 1.3 copy-start.1
  1.3 6.1 %slice-start = ((f32[2,128,256]{2,1,0:T(8,128)}), f32[1,128,256]{2,1,0:T(8,128)S(1)}, s32[]{:S(2)}) async-start(f32[2,128,256]{2,1,0:T(8,128)} %param.10), calls=%async_computation.8 | async-start | bytes 262144 | tf_op jit(solution)/shard_map/slice | solution.py:58
  2.2 9.7 %all-to-all-start = ((f32[4,64,128]{2,1,0:T(8,128)}), f32[4,64,128]{2,1,0:T(8,128)S(1)}, u32[]{:S(2)}, u32[]{:S(2)}) async-start(f32[4,64,128]{2,1,0:T(8,128)} %fusion.28), calls=%async_computation | async-start | bytes 262144 | tf_op jit(solution)/shard_map/all_to_all | solution.py:44
  7.1 0.9 copy-start.4
  11.9 26.2 %all-to-all-start.1 = ((f32[4,640,128]{2,1,0:T(8,128)}), f32[4,640,128]{2,1,0:T(8,128)S(1)}, u32[]{:S(2)}, u32[]{:S(2)}) async-start(f32[4,640,128]{2,1,0:T(8,128)} %pad_maximum_fusion), calls=%async_computation.1 | async-start | bytes 2621440 | tf_op jit(solution)/shard_map/all_to_all | solution.py:44
  15.5 9.2 %collective-permute-start = (f32[64,128]{1,0:T(8,128)S(1)}, f32[64,128]{1,0:T(8,128)S(1)}, u32[]{:S(2)}, u32[]{:S(2)}) collective-permute-start(f32[64,128]{1,0:T(8,128)S(1)} %reduce_sum.36), channel_id=1, source_target_pairs={{0,32},{32,0},{1,33},{33,1},{2,34},{34,2},{3,35},{35,3},{4,36},{36... | collective-permute-start | bytes 98312 | tf_op jit(solution)/shard_map/ppermute | solution.py:40
  24.7 13.4 %collective-permute-start.1 = (f32[64,128]{1,0:T(8,128)S(1)}, f32[64,128]{1,0:T(8,128)S(1)}, u32[]{:S(2)}, u32[]{:S(2)}) collective-permute-start(f32[64,128]{1,0:T(8,128)S(1)} %add.84), channel_id=1, source_target_pairs={{0,64},{64,0},{1,65},{65,1},{2,66},{66,2},{3,67},{67,3},{4,68},{68... | collective-permute-start | bytes 98312 | tf_op jit(solution)/shard_map/ppermute | solution.py:40
  39.2 29.2 %copy-start.3 = (f32[2,128,256]{2,1,0:T(8,128)S(1)}, f32[2,128,256]{2,1,0:T(8,128)}, u32[]{:S(2)}) copy-start(f32[2,128,256]{2,1,0:T(8,128)} %param.8) | copy-start | bytes 786436
  39.2 13.7 %all-to-all-start.2 = ((f32[16,16,256]{2,1,0:T(8,128)}), f32[16,16,256]{2,1,0:T(8,128)S(1)}, u32[]{:S(2)}, u32[]{:S(2)}) async-start(f32[16,16,256]{2,1,0:T(8,128)} %bitcast.17), calls=%async_computation.2 | async-start | bytes 524288 | tf_op jit(solution)/shard_map/all_to_all | solution.py:44
  52.9 10.4 %collective-permute-start.2 = (f32[16,256]{1,0:T(8,128)S(1)}, f32[16,256]{1,0:T(8,128)S(1)}, u32[]{:S(2)}, u32[]{:S(2)}) collective-permute-start(f32[16,256]{1,0:T(8,128)S(1)} %reduce_sum.37), channel_id=1, source_target_pairs={{0,16},{16,0},{1,17},{17,1},{2,18},{18,2},{3,19},{19,3},{4,20},{20... | collective-permute-start | bytes 49160 | tf_op jit(solution)/shard_map/ppermute | solution.py:40
  64.1 13.9 %all-to-all-start.3 = ((f32[16,16,256]{2,1,0:T(8,128)}), f32[16,16,256]{2,1,0:T(8,128)S(1)}, u32[]{:S(2)}, u32[]{:S(2)}) async-start(f32[16,16,256]{2,1,0:T(8,128)} %broadcast_in_dim.17), calls=%async_computation.3 | async-start | bytes 524288 | tf_op jit(solution)/shard_map/all_to_all | solution.py:44
  68.4 16.4 %collective-permute-start.4 = (f32[256,256]{1,0:T(8,128)S(1)}, f32[256,256]{1,0:T(8,128)S(1)}, u32[]{:S(2)}, u32[]{:S(2)}) collective-permute-start(f32[256,256]{1,0:T(8,128)S(1)} %bitcast.121), channel_id=1, source_target_pairs={{0,1},{1,0},{2,3},{3,2},{4,5},{5,4},{6,7},{7,6},{8,9},{9,8},{10,11... | collective-permute-start | bytes 786440 | tf_op jit(solution)/shard_map/ppermute | solution.py:69
  71.7 14.9 %collective-permute-start.5 = (f32[256,256]{1,0:T(8,128)S(1)}, f32[256,256]{1,0:T(8,128)S(1)}, u32[]{:S(2)}, u32[]{:S(2)}) collective-permute-start(f32[256,256]{1,0:T(8,128)S(1)} %bitcast.122), channel_id=1, source_target_pairs={{0,2},{1,3},{2,0},{3,1},{4,6},{5,7},{6,4},{7,5},{8,10},{9,11},{10,... | collective-permute-start | bytes 786440 | tf_op jit(solution)/shard_map/ppermute | solution.py:69
  76.0 15.0 %collective-permute-start.6 = (f32[256,256]{1,0:T(8,128)S(1)}, f32[256,256]{1,0:T(8,128)S(1)}, u32[]{:S(2)}, u32[]{:S(2)}) collective-permute-start(f32[256,256]{1,0:T(8,128)S(1)} %bitcast.123), channel_id=1, source_target_pairs={{0,3},{1,2},{2,1},{3,0},{4,7},{5,6},{6,5},{7,4},{8,11},{9,10},{10,... | collective-permute-start | bytes 786440 | tf_op jit(solution)/shard_map/ppermute | solution.py:69
  78.6 6.2 %collective-permute-start.3 = (f32[64,128]{1,0:T(8,128)S(1)}, f32[64,128]{1,0:T(8,128)S(1)}, u32[]{:S(2)}, u32[]{:S(2)}) collective-permute-start(f32[64,128]{1,0:T(8,128)S(1)} %fusion.6), channel_id=1, source_target_pairs={{0,32},{32,0},{1,33},{33,1},{2,34},{34,2},{3,35},{35,3},{4,36},{36... | collective-permute-start | bytes 98312 | tf_op jit(solution)/shard_map/ppermute | solution.py:40
  91.0 13.5 %collective-permute-start.7 = (f32[64,128]{1,0:T(8,128)S(1)}, f32[64,128]{1,0:T(8,128)S(1)}, u32[]{:S(2)}, u32[]{:S(2)}) collective-permute-start(f32[64,128]{1,0:T(8,128)S(1)} %add.89), channel_id=1, source_target_pairs={{0,64},{64,0},{1,65},{65,1},{2,66},{66,2},{3,67},{67,3},{4,68},{68... | collective-permute-start | bytes 98312 | tf_op jit(solution)/shard_map/ppermute | solution.py:40
  105.2 12.1 %all-to-all-start.4 = ((f32[16,16,256]{2,1,0:T(8,128)}), f32[16,16,256]{2,1,0:T(8,128)S(1)}, u32[]{:S(2)}, u32[]{:S(2)}) async-start(f32[16,16,256]{2,1,0:T(8,128)} %bitcast.22), calls=%async_computation.4 | async-start | bytes 524288 | tf_op jit(solution)/shard_map/all_to_all | solution.py:44
  117.7 18.6 %copy-start.2 = (bf16[512,256]{1,0:T(8,128)(2,1)S(1)}, bf16[512,256]{1,0:T(8,128)(2,1)}, u32[]{:S(2)}) copy-start(bf16[512,256]{1,0:T(8,128)(2,1)} %param.7) | copy-start | bytes 786436
  118.7 8.9 %all-to-all-start.5 = ((f32[4,16,512]{2,1,0:T(8,128)}), f32[4,16,512]{2,1,0:T(8,128)S(1)}, u32[]{:S(2)}, u32[]{:S(2)}) async-start(f32[4,16,512]{2,1,0:T(8,128)} %bitcast.38), calls=%async_computation.5 | async-start | bytes 262144 | tf_op jit(solution)/shard_map/all_to_all | solution.py:44
  127.6 8.7 %collective-permute-start.8 = (f32[16,512]{1,0:T(8,128)S(1)}, f32[16,512]{1,0:T(8,128)S(1)}, u32[]{:S(2)}, u32[]{:S(2)}) collective-permute-start(f32[16,512]{1,0:T(8,128)S(1)} %reduce_sum.38), channel_id=1, source_target_pairs={{0,16},{16,0},{1,17},{17,1},{2,18},{18,2},{3,19},{19,3},{4,20},{20... | collective-permute-start | bytes 98312 | tf_op jit(solution)/shard_map/ppermute | solution.py:40
  145.6 11.0 %all-to-all-start.7 = ((f32[16,16,256]{2,1,0:T(8,128)}), f32[16,16,256]{2,1,0:T(8,128)S(1)}, u32[]{:S(2)}, u32[]{:S(2)}) async-start(f32[16,16,256]{2,1,0:T(8,128)} %bitcast.41), calls=%async_computation.7 | async-start | bytes 524288 | tf_op jit(solution)/shard_map/all_to_all | solution.py:44
  156.7 12.0 %collective-permute-start.9 = (f32[2,16,256]{2,1,0:T(8,128)S(1)}, f32[2,16,256]{2,1,0:T(8,128)S(1)}, u32[]{:S(2)}, u32[]{:S(2)}) collective-permute-start(f32[2,16,256]{2,1,0:T(8,128)S(1)} %dynamic-slice_bitcast_fusion.4), channel_id=1, source_target_pairs={{0,32},{32,0},{1,33},{33,1},{2,34},{34,2},{3,35},{35,3},{4,36},{36... | collective-permute-start | bytes 98312 | tf_op jit(solution)/shard_map/ppermute | solution.py:40
  168.6 13.2 %collective-permute-start.10 = (f32[16,256]{1,0:T(8,128)S(1)}, f32[16,256]{1,0:T(8,128)S(1)}, u32[]{:S(2)}, u32[]{:S(2)}) collective-permute-start(f32[16,256]{1,0:T(8,128)S(1)} %dynamic-slice_bitcast_fusion.5), channel_id=1, source_target_pairs={{0,64},{64,0},{1,65},{65,1},{2,66},{66,2},{3,67},{67,3},{4,68},{68... | collective-permute-start | bytes 49160 | tf_op jit(solution)/shard_map/ppermute | solution.py:40

commit v10 on v9

--- a/solution.py
+++ b/solution.py
@@ -85,8 +85,8 @@
 
     first = solve(0) + solve(1)
     first = first + swap(first, "c")
+    first = first + swap(first, "h")
     first, others = lax.optimization_barrier((first, others))
-    first = first + swap(first, "h")
 
     solved = jnp.concatenate([first, second], 1).reshape(4, 1, 16, 256)
     solved = jnp.broadcast_to(solved, (4, 4, 16, 256)).reshape(16, 16, 256)

time: 184 us -> 179 us (0.973)
  waiting for transfers between devices: 51.8 us -> 38.6 us
  starting transfers between devices: 108 us -> 118 us
    ppermute x8, waiting for transfers between devices: 16.7 us -> 9.64 us  [swap(): return lax.ppermute(a, axis, [(0, 1), (1, 0)])]
    ppermute x8, starting transfers between devices: 68.8 us -> 75.8 us  [swap(): return lax.ppermute(a, axis, [(0, 1), (1, 0)])]
    ppermute x3, waiting for transfers between devices: 6.19 us -> 0.01 us  [local(): lax.ppermute(flat, 'y', [(i, i ^ k) for i in range(4)])]
    all_to_all x7, starting transfers between devices: 29.7 us -> 32.6 us  [exchange(): return lax.all_to_all(a, axes, 0, 0, tiled=True)]
  transfers between devices with their start and end apart: 18 -> 18, of which waited for: 15 -> 13; matrix products, arithmetic and copies ran while one was open for 3% -> 3% of each run, Pallas kernels for 0% -> 0%
where the time goes in v10:
time: 179 us; the launch traced here: 178 us
  starting transfers between devices  118 us (66%)
  waiting for transfers between devices  38.6 us (22%)
  blocking collectives  7.18 us (4%)
  matrix products  6.39 us (4%)
  local copies, waits for them, and re-layouts  5.2 us (3%)
  other arithmetic  2.39 us (1%)
    ppermute x8, starting transfers between devices, swap(): return lax.ppermute(a, axis, [(0, 1), (1, 0)])  75.8 us
    all_to_all x7, starting transfers between devices, exchange(): return lax.all_to_all(a, axes, 0, 0, tiled=True)  32.6 us
    all_to_all x7, waiting for transfers between devices, exchange(): return lax.all_to_all(a, axes, 0, 0, tiled=True)  28.9 us
    ppermute x8, waiting for transfers between devices, swap(): return lax.ppermute(a, axis, [(0, 1), (1, 0)])  9.64 us
    ppermute x3, starting transfers between devices, local(): lax.ppermute(flat, 'y', [(i, i ^ k) for i in range(4)])  9.58 us
    all_to_all x1, blocking collectives, exchange(): return lax.all_to_all(a, axes, 0, 0, tiled=True)  7.18 us
  transfers between devices with their start and end apart: 18, of which 13 were waited for; matrix products, arithmetic and copies ran while one was open for 3% of the time, Pallas kernels for 0%

profile of v10, /device:TPU:1, one launch (start us, length us, event | category | flops | bytes accessed | tf_op | source)
XLA Modules:
  0.0 178.1 jit_solution(8245023113414437775)
XLA Ops:
  0.0 1.1 slice_bitcast_fusion
  1.3 0.9 fusion.28
  2.2 4.8 %all-to-all-start = ((f32[4,64,128]{2,1,0:T(8,128)}), f32[4,64,128]{2,1,0:T(8,128)S(1)}, u32[]{:S(2)}, u32[]{:S(2)}) async-start(f32[4,64,128]{2,1,0:T(8,128)} %fusion.28), calls=%async_computation | async-start | bytes 262144 | tf_op jit(solution)/shard_map/all_to_all | solution.py:44
  7.5 0.4 copy-done.5
  8.0 1.2 pad_maximum_fusion
  9.2 2.7 %all-to-all-done = f32[4,64,128]{2,1,0:T(8,128)S(1)} async-done(((f32[4,64,128]{2,1,0:T(8,128)}), f32[4,64,128]{2,1,0:T(8,128)S(1)}, u32[]{:S(2)}, u32[]{:S(2)}) %all-to-all-start) | async-done | bytes 131104 | tf_op jit(solution)/shard_map/all_to_all | solution.py:44
  11.9 3.6 %all-to-all-start.1 = ((f32[4,640,128]{2,1,0:T(8,128)}), f32[4,640,128]{2,1,0:T(8,128)S(1)}, u32[]{:S(2)}, u32[]{:S(2)}) async-start(f32[4,640,128]{2,1,0:T(8,128)} %pad_maximum_fusion), calls=%async_computation.1 | async-start | bytes 2621440 | tf_op jit(solution)/shard_map/all_to_all | solution.py:44
  15.5 8.4 %collective-permute-start = (f32[64,128]{1,0:T(8,128)S(1)}, f32[64,128]{1,0:T(8,128)S(1)}, u32[]{:S(2)}, u32[]{:S(2)}) collective-permute-start(f32[64,128]{1,0:T(8,128)S(1)} %reduce_sum.36), channel_id=1, source_target_pairs={{0,32},{32,0},{1,33},{33,1},{2,34},{34,2},{3,35},{35,3},{4,36},{36... | collective-permute-start | bytes 98312 | tf_op jit(solution)/shard_map/ppermute | solution.py:40
  23.9 0.8 collective-permute-done
  24.7 11.1 %collective-permute-start.1 = (f32[64,128]{1,0:T(8,128)S(1)}, f32[64,128]{1,0:T(8,128)S(1)}, u32[]{:S(2)}, u32[]{:S(2)}) collective-permute-start(f32[64,128]{1,0:T(8,128)S(1)} %add.84), channel_id=1, source_target_pairs={{0,64},{64,0},{1,65},{65,1},{2,66},{66,2},{3,67},{67,3},{4,68},{68... | collective-permute-start | bytes 98312 | tf_op jit(solution)/shard_map/ppermute | solution.py:40
  35.8 2.3 %collective-permute-done.1 = f32[64,128]{1,0:T(8,128)S(1)} collective-permute-done((f32[64,128]{1,0:T(8,128)S(1)}, f32[64,128]{1,0:T(8,128)S(1)}, u32[]{:S(2)}, u32[]{:S(2)}) %collective-permute-start.1) | collective-permute-done | bytes 32800 | tf_op jit(solution)/shard_map/ppermute | solution.py:40
  38.1 1.1 convolution_bitcast_fusion
  39.2 4.8 %all-to-all-start.2 = ((f32[16,16,256]{2,1,0:T(8,128)}), f32[16,16,256]{2,1,0:T(8,128)S(1)}, u32[]{:S(2)}, u32[]{:S(2)}) async-start(f32[16,16,256]{2,1,0:T(8,128)} %bitcast.17), calls=%async_computation.2 | async-start | bytes 524288 | tf_op jit(solution)/shard_map/all_to_all | solution.py:44
  44.0 8.9 %all-to-all-done.2 = f32[16,16,256]{2,1,0:T(8,128)S(1)} async-done(((f32[16,16,256]{2,1,0:T(8,128)}), f32[16,16,256]{2,1,0:T(8,128)S(1)}, u32[]{:S(2)}, u32[]{:S(2)}) %all-to-all-start.2) | async-done | bytes 262176 | tf_op jit(solution)/shard_map/all_to_all | solution.py:44
  52.9 9.3 %collective-permute-start.2 = (f32[16,256]{1,0:T(8,128)S(1)}, f32[16,256]{1,0:T(8,128)S(1)}, u32[]{:S(2)}, u32[]{:S(2)}) collective-permute-start(f32[16,256]{1,0:T(8,128)S(1)} %reduce_sum.37), channel_id=1, source_target_pairs={{0,16},{16,0},{1,17},{17,1},{2,18},{18,2},{3,19},{19,3},{4,20},{20... | collective-permute-start | bytes 49160 | tf_op jit(solution)/shard_map/ppermute | solution.py:40
  62.3 1.1 collective-permute-done.2
  63.4 0.7 broadcast_in_dim.17
  64.1 4.3 %all-to-all-start.3 = ((f32[16,16,256]{2,1,0:T(8,128)}), f32[16,16,256]{2,1,0:T(8,128)S(1)}, u32[]{:S(2)}, u32[]{:S(2)}) async-start(f32[16,16,256]{2,1,0:T(8,128)} %broadcast_in_dim.17), calls=%async_computation.3 | async-start | bytes 524288 | tf_op jit(solution)/shard_map/all_to_all | solution.py:44
  68.4 3.3 %collective-permute-start.5 = (f32[256,256]{1,0:T(8,128)S(1)}, f32[256,256]{1,0:T(8,128)S(1)}, u32[]{:S(2)}, u32[]{:S(2)}) collective-permute-start(f32[256,256]{1,0:T(8,128)S(1)} %bitcast.121), channel_id=1, source_target_pairs={{0,1},{1,0},{2,3},{3,2},{4,5},{5,4},{6,7},{7,6},{8,9},{9,8},{10,11... | collective-permute-start | bytes 786440 | tf_op jit(solution)/shard_map/ppermute | solution.py:69
  71.7 4.3 %collective-permute-start.6 = (f32[256,256]{1,0:T(8,128)S(1)}, f32[256,256]{1,0:T(8,128)S(1)}, u32[]{:S(2)}, u32[]{:S(2)}) collective-permute-start(f32[256,256]{1,0:T(8,128)S(1)} %bitcast.122), channel_id=1, source_target_pairs={{0,2},{1,3},{2,0},{3,1},{4,6},{5,7},{6,4},{7,5},{8,10},{9,11},{10,... | collective-permute-start | bytes 786440 | tf_op jit(solution)/shard_map/ppermute | solution.py:69
  76.0 2.0 %collective-permute-start.7 = (f32[256,256]{1,0:T(8,128)S(1)}, f32[256,256]{1,0:T(8,128)S(1)}, u32[]{:S(2)}, u32[]{:S(2)}) collective-permute-start(f32[256,256]{1,0:T(8,128)S(1)} %bitcast.123), channel_id=1, source_target_pairs={{0,3},{1,2},{2,1},{3,0},{4,7},{5,6},{6,5},{7,4},{8,11},{9,10},{10,... | collective-permute-start | bytes 786440 | tf_op jit(solution)/shard_map/ppermute | solution.py:69
  78.0 0.3 convolution_bitcast_fusion.4
  78.6 5.4 %collective-permute-start.3 = (f32[64,128]{1,0:T(8,128)S(1)}, f32[64,128]{1,0:T(8,128)S(1)}, u32[]{:S(2)}, u32[]{:S(2)}) collective-permute-start(f32[64,128]{1,0:T(8,128)S(1)} %fusion.6), channel_id=1, source_target_pairs={{0,32},{32,0},{1,33},{33,1},{2,34},{34,2},{3,35},{35,3},{4,36},{36... | collective-permute-start | bytes 98312 | tf_op jit(solution)/shard_map/ppermute | solution.py:40
  83.9 0.8 collective-permute-done.3
  84.8 12.0 %collective-permute-start.4 = (f32[64,128]{1,0:T(8,128)S(1)}, f32[64,128]{1,0:T(8,128)S(1)}, u32[]{:S(2)}, u32[]{:S(2)}) collective-permute-start(f32[64,128]{1,0:T(8,128)S(1)} %add.89), channel_id=1, source_target_pairs={{0,64},{64,0},{1,65},{65,1},{2,66},{66,2},{3,67},{67,3},{4,68},{68... | collective-permute-start | bytes 98312 | tf_op jit(solution)/shard_map/ppermute | solution.py:40
  96.8 1.4 collective-permute-done.4
  98.2 0.8 broadcast_in_dim.37
  99.0 7.2 %all-to-all-start.4 = ((f32[16,16,256]{2,1,0:T(8,128)}), f32[16,16,256]{2,1,0:T(8,128)S(1)}, u32[]{:S(2)}, u32[]{:S(2)}) async-start(f32[16,16,256]{2,1,0:T(8,128)} %bitcast.22), calls=%async_computation.4 | async-start | bytes 524288 | tf_op jit(solution)/shard_map/all_to_all | solution.py:44
  106.2 1.0 pad_maximum_fusion.1
  107.3 1.5 fusion
  108.8 5.0 %all-to-all-done.4 = f32[16,16,256]{2,1,0:T(8,128)S(1)} async-done(((f32[16,16,256]{2,1,0:T(8,128)}), f32[16,16,256]{2,1,0:T(8,128)S(1)}, u32[]{:S(2)}, u32[]{:S(2)}) %all-to-all-start.4) | async-done | bytes 262176 | tf_op jit(solution)/shard_map/all_to_all | solution.py:44
  113.9 0.3 convolution_bitcast_fusion.1
  114.2 1.0 fusion.5
  115.2 4.4 %all-to-all-start.5 = ((f32[4,16,512]{2,1,0:T(8,128)}), f32[4,16,512]{2,1,0:T(8,128)S(1)}, u32[]{:S(2)}, u32[]{:S(2)}) async-start(f32[4,16,512]{2,1,0:T(8,128)} %bitcast.38), calls=%async_computation.5 | async-start | bytes 262144 | tf_op jit(solution)/shard_map/all_to_all | solution.py:44
  119.5 4.8 %all-to-all-done.5 = f32[4,16,512]{2,1,0:T(8,128)S(1)} async-done(((f32[4,16,512]{2,1,0:T(8,128)}), f32[4,16,512]{2,1,0:T(8,128)S(1)}, u32[]{:S(2)}, u32[]{:S(2)}) %all-to-all-start.5) | async-done | bytes 131104 | tf_op jit(solution)/shard_map/all_to_all | solution.py:44
  124.3 9.0 %collective-permute-start.8 = (f32[16,512]{1,0:T(8,128)S(1)}, f32[16,512]{1,0:T(8,128)S(1)}, u32[]{:S(2)}, u32[]{:S(2)}) collective-permute-start(f32[16,512]{1,0:T(8,128)S(1)} %reduce_sum.38), channel_id=1, source_target_pairs={{0,16},{16,0},{1,17},{17,1},{2,18},{18,2},{3,19},{19,3},{4,20},{20... | collective-permute-start | bytes 98312 | tf_op jit(solution)/shard_map/ppermute | solution.py:40
  133.3 1.3 collective-permute-done.8
  134.8 7.2 %all_to_all.40 = f32[4,16,512]{2,1,0:T(8,128)S(1)} all-to-all(f32[4,16,512]{2,1,0:T(8,128)S(1)} %broadcast_in_dim.38), channel_id=1, replica_groups=mesh['x'=4,'h'=2,'c'=2,'w'=2,'z'=4,'y'=4] {'z'}, dimensions={0} | all-to-all | bytes 262144 | tf_op jit(solution)/shard_map/all_to_all | solution.py:44
  142.0 0.5 fusion.24
  142.5 0.4 fusion.3
  142.9 0.7 copy.36
  143.7 3.5 %all-to-all-start.7 = ((f32[16,16,256]{2,1,0:T(8,128)}), f32[16,16,256]{2,1,0:T(8,128)S(1)}, u32[]{:S(2)}, u32[]{:S(2)}) async-start(f32[16,16,256]{2,1,0:T(8,128)} %bitcast.41), calls=%async_computation.7 | async-start | bytes 524288 | tf_op jit(solution)/shard_map/all_to_all | solution.py:44
  147.2 7.5 %all-to-all-done.7 = f32[16,16,256]{2,1,0:T(8,128)S(1)} async-done(((f32[16,16,256]{2,1,0:T(8,128)}), f32[16,16,256]{2,1,0:T(8,128)S(1)}, u32[]{:S(2)}, u32[]{:S(2)}) %all-to-all-start.7) | async-done | bytes 262176 | tf_op jit(solution)/shard_map/all_to_all | solution.py:44
  154.7 8.4 %collective-permute-start.9 = (f32[2,16,256]{2,1,0:T(8,128)S(1)}, f32[2,16,256]{2,1,0:T(8,128)S(1)}, u32[]{:S(2)}, u32[]{:S(2)}) collective-permute-start(f32[2,16,256]{2,1,0:T(8,128)S(1)} %dynamic-slice_bitcast_fusion.4), channel_id=1, source_target_pairs={{0,32},{32,0},{1,33},{33,1},{2,34},{34,2},{3,35},{35,3},{4,36},{36... | collective-permute-start | bytes 98312 | tf_op jit(solution)/shard_map/ppermute | solution.py:40
  163.2 0.8 collective-permute-done.9
  164.0 12.4 %collective-permute-start.10 = (f32[16,256]{1,0:T(8,128)S(1)}, f32[16,256]{1,0:T(8,128)S(1)}, u32[]{:S(2)}, u32[]{:S(2)}) collective-permute-start(f32[16,256]{1,0:T(8,128)S(1)} %dynamic-slice_bitcast_fusion.5), channel_id=1, source_target_pairs={{0,64},{64,0},{1,65},{65,1},{2,66},{66,2},{3,67},{67,3},{4,68},{68... | collective-permute-start | bytes 49160 | tf_op jit(solution)/shard_map/ppermute | solution.py:40
  176.4 1.1 collective-permute-done.10
  177.5 0.6 copy.29
  (52 shorter events, 1.4 us)
Async XLA Ops:
  0.0 107.3 %copy-start = (f32[512,256]{1,0:T(8,128)S(1)}, f32[512,256]{1,0:T(8,128)}, u32[]{:S(2)}) copy-start(f32[512,256]{1,0:T(8,128)} %param.6) | copy-start | bytes 1572868
  0.0 1.3 copy-start.1
  1.3 6.1 %slice-start = ((f32[2,128,256]{2,1,0:T(8,128)}), f32[1,128,256]{2,1,0:T(8,128)S(1)}, s32[]{:S(2)}) async-start(f32[2,128,256]{2,1,0:T(8,128)} %param.10), calls=%async_computation.8 | async-start | bytes 262144 | tf_op jit(solution)/shard_map/slice | solution.py:58
  2.2 9.7 %all-to-all-start = ((f32[4,64,128]{2,1,0:T(8,128)}), f32[4,64,128]{2,1,0:T(8,128)S(1)}, u32[]{:S(2)}, u32[]{:S(2)}) async-start(f32[4,64,128]{2,1,0:T(8,128)} %fusion.28), calls=%async_computation | async-start | bytes 262144 | tf_op jit(solution)/shard_map/all_to_all | solution.py:44
  7.1 0.9 copy-start.5
  11.9 26.2 %all-to-all-start.1 = ((f32[4,640,128]{2,1,0:T(8,128)}), f32[4,640,128]{2,1,0:T(8,128)S(1)}, u32[]{:S(2)}, u32[]{:S(2)}) async-start(f32[4,640,128]{2,1,0:T(8,128)} %pad_maximum_fusion), calls=%async_computation.1 | async-start | bytes 2621440 | tf_op jit(solution)/shard_map/all_to_all | solution.py:44
  15.5 9.2 %collective-permute-start = (f32[64,128]{1,0:T(8,128)S(1)}, f32[64,128]{1,0:T(8,128)S(1)}, u32[]{:S(2)}, u32[]{:S(2)}) collective-permute-start(f32[64,128]{1,0:T(8,128)S(1)} %reduce_sum.36), channel_id=1, source_target_pairs={{0,32},{32,0},{1,33},{33,1},{2,34},{34,2},{3,35},{35,3},{4,36},{36... | collective-permute-start | bytes 98312 | tf_op jit(solution)/shard_map/ppermute | solution.py:40
  24.7 13.4 %collective-permute-start.1 = (f32[64,128]{1,0:T(8,128)S(1)}, f32[64,128]{1,0:T(8,128)S(1)}, u32[]{:S(2)}, u32[]{:S(2)}) collective-permute-start(f32[64,128]{1,0:T(8,128)S(1)} %add.84), channel_id=1, source_target_pairs={{0,64},{64,0},{1,65},{65,1},{2,66},{66,2},{3,67},{67,3},{4,68},{68... | collective-permute-start | bytes 98312 | tf_op jit(solution)/shard_map/ppermute | solution.py:40
  39.2 29.2 %copy-start.3 = (f32[2,128,256]{2,1,0:T(8,128)S(1)}, f32[2,128,256]{2,1,0:T(8,128)}, u32[]{:S(2)}) copy-start(f32[2,128,256]{2,1,0:T(8,128)} %param.8) | copy-start | bytes 786436
  39.2 13.7 %all-to-all-start.2 = ((f32[16,16,256]{2,1,0:T(8,128)}), f32[16,16,256]{2,1,0:T(8,128)S(1)}, u32[]{:S(2)}, u32[]{:S(2)}) async-start(f32[16,16,256]{2,1,0:T(8,128)} %bitcast.17), calls=%async_computation.2 | async-start | bytes 524288 | tf_op jit(solution)/shard_map/all_to_all | solution.py:44
  52.9 10.4 %collective-permute-start.2 = (f32[16,256]{1,0:T(8,128)S(1)}, f32[16,256]{1,0:T(8,128)S(1)}, u32[]{:S(2)}, u32[]{:S(2)}) collective-permute-start(f32[16,256]{1,0:T(8,128)S(1)} %reduce_sum.37), channel_id=1, source_target_pairs={{0,16},{16,0},{1,17},{17,1},{2,18},{18,2},{3,19},{19,3},{4,20},{20... | collective-permute-start | bytes 49160 | tf_op jit(solution)/shard_map/ppermute | solution.py:40
  64.1 13.9 %all-to-all-start.3 = ((f32[16,16,256]{2,1,0:T(8,128)}), f32[16,16,256]{2,1,0:T(8,128)S(1)}, u32[]{:S(2)}, u32[]{:S(2)}) async-start(f32[16,16,256]{2,1,0:T(8,128)} %broadcast_in_dim.17), calls=%async_computation.3 | async-start | bytes 524288 | tf_op jit(solution)/shard_map/all_to_all | solution.py:44
  68.4 29.7 %collective-permute-start.5 = (f32[256,256]{1,0:T(8,128)S(1)}, f32[256,256]{1,0:T(8,128)S(1)}, u32[]{:S(2)}, u32[]{:S(2)}) collective-permute-start(f32[256,256]{1,0:T(8,128)S(1)} %bitcast.121), channel_id=1, source_target_pairs={{0,1},{1,0},{2,3},{3,2},{4,5},{5,4},{6,7},{7,6},{8,9},{9,8},{10,11... | collective-permute-start | bytes 786440 | tf_op jit(solution)/shard_map/ppermute | solution.py:69
  71.7 26.5 %collective-permute-start.6 = (f32[256,256]{1,0:T(8,128)S(1)}, f32[256,256]{1,0:T(8,128)S(1)}, u32[]{:S(2)}, u32[]{:S(2)}) collective-permute-start(f32[256,256]{1,0:T(8,128)S(1)} %bitcast.122), channel_id=1, source_target_pairs={{0,2},{1,3},{2,0},{3,1},{4,6},{5,7},{6,4},{7,5},{8,10},{9,11},{10,... | collective-permute-start | bytes 786440 | tf_op jit(solution)/shard_map/ppermute | solution.py:69
  76.0 22.2 %collective-permute-start.7 = (f32[256,256]{1,0:T(8,128)S(1)}, f32[256,256]{1,0:T(8,128)S(1)}, u32[]{:S(2)}, u32[]{:S(2)}) collective-permute-start(f32[256,256]{1,0:T(8,128)S(1)} %bitcast.123), channel_id=1, source_target_pairs={{0,3},{1,2},{2,1},{3,0},{4,7},{5,6},{6,5},{7,4},{8,11},{9,10},{10,... | collective-permute-start | bytes 786440 | tf_op jit(solution)/shard_map/ppermute | solution.py:69
  78.6 6.2 %collective-permute-start.3 = (f32[64,128]{1,0:T(8,128)S(1)}, f32[64,128]{1,0:T(8,128)S(1)}, u32[]{:S(2)}, u32[]{:S(2)}) collective-permute-start(f32[64,128]{1,0:T(8,128)S(1)} %fusion.6), channel_id=1, source_target_pairs={{0,32},{32,0},{1,33},{33,1},{2,34},{34,2},{3,35},{35,3},{4,36},{36... | collective-permute-start | bytes 98312 | tf_op jit(solution)/shard_map/ppermute | solution.py:40
  84.8 13.4 %collective-permute-start.4 = (f32[64,128]{1,0:T(8,128)S(1)}, f32[64,128]{1,0:T(8,128)S(1)}, u32[]{:S(2)}, u32[]{:S(2)}) collective-permute-start(f32[64,128]{1,0:T(8,128)S(1)} %add.89), channel_id=1, source_target_pairs={{0,64},{64,0},{1,65},{65,1},{2,66},{66,2},{3,67},{67,3},{4,68},{68... | collective-permute-start | bytes 98312 | tf_op jit(solution)/shard_map/ppermute | solution.py:40
  98.2 0.8 copy-start.4
  99.0 14.8 %all-to-all-start.4 = ((f32[16,16,256]{2,1,0:T(8,128)}), f32[16,16,256]{2,1,0:T(8,128)S(1)}, u32[]{:S(2)}, u32[]{:S(2)}) async-start(f32[16,16,256]{2,1,0:T(8,128)} %bitcast.22), calls=%async_computation.4 | async-start | bytes 524288 | tf_op jit(solution)/shard_map/all_to_all | solution.py:44
  114.2 20.4 %copy-start.2 = (bf16[512,256]{1,0:T(8,128)(2,1)S(1)}, bf16[512,256]{1,0:T(8,128)(2,1)}, u32[]{:S(2)}) copy-start(bf16[512,256]{1,0:T(8,128)(2,1)} %param.7) | copy-start | bytes 786436
  115.2 9.1 %all-to-all-start.5 = ((f32[4,16,512]{2,1,0:T(8,128)}), f32[4,16,512]{2,1,0:T(8,128)S(1)}, u32[]{:S(2)}, u32[]{:S(2)}) async-start(f32[4,16,512]{2,1,0:T(8,128)} %bitcast.38), calls=%async_computation.5 | async-start | bytes 262144 | tf_op jit(solution)/shard_map/all_to_all | solution.py:44
  124.3 10.3 %collective-permute-start.8 = (f32[16,512]{1,0:T(8,128)S(1)}, f32[16,512]{1,0:T(8,128)S(1)}, u32[]{:S(2)}, u32[]{:S(2)}) collective-permute-start(f32[16,512]{1,0:T(8,128)S(1)} %reduce_sum.38), channel_id=1, source_target_pairs={{0,16},{16,0},{1,17},{17,1},{2,18},{18,2},{3,19},{19,3},{4,20},{20... | collective-permute-start | bytes 98312 | tf_op jit(solution)/shard_map/ppermute | solution.py:40
  143.7 11.0 %all-to-all-start.7 = ((f32[16,16,256]{2,1,0:T(8,128)}), f32[16,16,256]{2,1,0:T(8,128)S(1)}, u32[]{:S(2)}, u32[]{:S(2)}) async-start(f32[16,16,256]{2,1,0:T(8,128)} %bitcast.41), calls=%async_computation.7 | async-start | bytes 524288 | tf_op jit(solution)/shard_map/all_to_all | solution.py:44
  154.7 9.3 %collective-permute-start.9 = (f32[2,16,256]{2,1,0:T(8,128)S(1)}, f32[2,16,256]{2,1,0:T(8,128)S(1)}, u32[]{:S(2)}, u32[]{:S(2)}) collective-permute-start(f32[2,16,256]{2,1,0:T(8,128)S(1)} %dynamic-slice_bitcast_fusion.4), channel_id=1, source_target_pairs={{0,32},{32,0},{1,33},{33,1},{2,34},{34,2},{3,35},{35,3},{4,36},{36... | collective-permute-start | bytes 98312 | tf_op jit(solution)/shard_map/ppermute | solution.py:40
  164.0 13.5 %collective-permute-start.10 = (f32[16,256]{1,0:T(8,128)S(1)}, f32[16,256]{1,0:T(8,128)S(1)}, u32[]{:S(2)}, u32[]{:S(2)}) collective-permute-start(f32[16,256]{1,0:T(8,128)S(1)} %dynamic-slice_bitcast_fusion.5), channel_id=1, source_target_pairs={{0,64},{64,0},{1,65},{65,1},{2,66},{66,2},{3,67},{67,3},{4,68},{68... | collective-permute-start | bytes 49160 | tf_op jit(solution)/shard_map/ppermute | solution.py:40

commit v11 on v10

--- a/solution.py
+++ b/solution.py
@@ -66,12 +66,13 @@
 
     carried = dot(second, blocks[:, :256], 1, 2).transpose(1, 0, 2)
     carried, flat = lax.optimization_barrier((carried, centres.reshape(256, 256)))
-    others = [flat] + [lax.ppermute(flat, "y", [(i, i ^ k) for i in range(4)]) for k in (1, 2, 3)]
+    near, far, wrap = (lax.ppermute(flat, "y", [(i, i ^ k) for i in range(4)]) for k in (1, 2, 3))
     carried = jnp.sum(exchange(carried.reshape(16, 16, 256), zy), 0)
     coeff = blocks[:, 512:].reshape(4, 2, 64, 128)
     coeff = lax.dynamic_slice(coeff, (z, 0, y * 16, 0), (1, 2, 16, 128))
     coeff = coeff.reshape(2, 16, 128).transpose(1, 0, 2).reshape(16, 256)
     rest = (coeff - carried) - swap(carried, "w")
+    rest, near, wrap = lax.optimization_barrier((rest, near, wrap))
     rest = exchange(copies(rest, 16), zy).reshape(4, 64, 256)
 
     def solve(side):
@@ -84,15 +85,14 @@
         )
 
     first = solve(0) + solve(1)
-    first = first + swap(first, "c")
-    first = first + swap(first, "h")
-    first, others = lax.optimization_barrier((first, others))
+    first = jnp.sum(exchange(copies(first, 4), ("h", "c")), 0)
+    first, far = lax.optimization_barrier((first, far))
 
     solved = jnp.concatenate([first, second], 1).reshape(4, 1, 16, 256)
     solved = jnp.broadcast_to(solved, (4, 4, 16, 256)).reshape(16, 16, 256)
     solved = exchange(solved, yx).reshape(4, 64, 256)
 
-    others = jnp.stack(others)
+    others = jnp.stack([flat, near, far, wrap])
     centres_y = [lax.dynamic_index_in_dim(others, y ^ k, 0, keepdims=False) for k in range(4)]
     score = dot(points, jnp.concatenate(centres_y, 0), 1, 1) / math.sqrt(points.shape[1])
     kernel = lax.optimization_barrier(halves(score + score * score * score / 3.0))

time: 179 us -> 184 us (1.028)
  starting transfers between devices: 118 us -> 98.5 us
  blocking collectives: 7.18 us -> 20.3 us
  waiting for transfers between devices: 38.6 us -> 49.4 us
    ppermute x8 -> x6, starting transfers between devices: 75.8 us -> 47.9 us  [swap(): return lax.ppermute(a, axis, [(0, 1), (1, 0)])]
    all_to_all x1 -> x2, blocking collectives: 7.18 us -> 20.3 us  [exchange(): return lax.all_to_all(a, axes, 0, 0, tiled=True)]
    all_to_all x7, starting transfers between devices: 32.6 us -> 41.7 us  [exchange(): return lax.all_to_all(a, axes, 0, 0, tiled=True)]
    ppermute x8 -> x6, waiting for transfers between devices: 9.64 us -> 17.1 us  [swap(): return lax.ppermute(a, axis, [(0, 1), (1, 0)])]
    all_to_all x7, waiting for transfers between devices: 28.9 us -> 32.3 us  [exchange(): return lax.all_to_all(a, axes, 0, 0, tiled=True)]
  transfers between devices with their start and end apart: 18 -> 16, of which waited for: 13 -> 12; matrix products, arithmetic and copies ran while one was open for 3% -> 2% of each run, Pallas kernels for 0% -> 0%
where the time goes in v11:
time: 184 us; the launch traced here: 183 us
  starting transfers between devices  98.5 us (54%)
  waiting for transfers between devices  49.4 us (27%)
  blocking collectives  20.3 us (11%)
  matrix products  6.36 us (3%)
  local copies, waits for them, and re-layouts  5.07 us (3%)
  other arithmetic  2.39 us (1%)
    ppermute x6, starting transfers between devices, swap(): return lax.ppermute(a, axis, [(0, 1), (1, 0)])  47.9 us
    all_to_all x7, starting transfers between devices, exchange(): return lax.all_to_all(a, axes, 0, 0, tiled=True)  41.7 us
    all_to_all x7, waiting for transfers between devices, exchange(): return lax.all_to_all(a, axes, 0, 0, tiled=True)  32.3 us
    all_to_all x2, blocking collectives, exchange(): return lax.all_to_all(a, axes, 0, 0, tiled=True)  20.3 us
    ppermute x6, waiting for transfers between devices, swap(): return lax.ppermute(a, axis, [(0, 1), (1, 0)])  17.1 us
    ppermute x3, starting transfers between devices, local(): lax.ppermute(flat, 'y', [(i, i ^ k) for i in range(4)])  8.87 us
  transfers between devices with their start and end apart: 16, of which 12 were waited for; matrix products, arithmetic and copies ran while one was open for 2% of the time, Pallas kernels for 0%

profile of v11, /device:TPU:1, one launch (start us, length us, event | category | flops | bytes accessed | tf_op | source)
XLA Modules:
  0.0 182.5 jit_solution(1627591401271135388)
XLA Ops:
  0.0 1.1 slice_bitcast_fusion
  1.3 0.9 fusion.28
  2.2 4.8 %all-to-all-start = ((f32[4,64,128]{2,1,0:T(8,128)}), f32[4,64,128]{2,1,0:T(8,128)S(1)}, u32[]{:S(2)}, u32[]{:S(2)}) async-start(f32[4,64,128]{2,1,0:T(8,128)} %fusion.28), calls=%async_computation | async-start | bytes 262144 | tf_op jit(solution)/shard_map/all_to_all | solution.py:44
  7.5 0.4 copy-done.5
  8.0 1.2 pad_maximum_fusion
  9.2 2.7 %all-to-all-done = f32[4,64,128]{2,1,0:T(8,128)S(1)} async-done(((f32[4,64,128]{2,1,0:T(8,128)}), f32[4,64,128]{2,1,0:T(8,128)S(1)}, u32[]{:S(2)}, u32[]{:S(2)}) %all-to-all-start) | async-done | bytes 131104 | tf_op jit(solution)/shard_map/all_to_all | solution.py:44
  11.9 3.6 %all-to-all-start.1 = ((f32[4,640,128]{2,1,0:T(8,128)}), f32[4,640,128]{2,1,0:T(8,128)S(1)}, u32[]{:S(2)}, u32[]{:S(2)}) async-start(f32[4,640,128]{2,1,0:T(8,128)} %pad_maximum_fusion), calls=%async_computation.1 | async-start | bytes 2621440 | tf_op jit(solution)/shard_map/all_to_all | solution.py:44
  15.5 8.5 %collective-permute-start = (f32[64,128]{1,0:T(8,128)S(1)}, f32[64,128]{1,0:T(8,128)S(1)}, u32[]{:S(2)}, u32[]{:S(2)}) collective-permute-start(f32[64,128]{1,0:T(8,128)S(1)} %reduce_sum.45), channel_id=1, source_target_pairs={{0,32},{32,0},{1,33},{33,1},{2,34},{34,2},{3,35},{35,3},{4,36},{36... | collective-permute-start | bytes 98312 | tf_op jit(solution)/shard_map/ppermute | solution.py:40
  24.0 0.8 collective-permute-done
  24.9 11.1 %collective-permute-start.1 = (f32[64,128]{1,0:T(8,128)S(1)}, f32[64,128]{1,0:T(8,128)S(1)}, u32[]{:S(2)}, u32[]{:S(2)}) collective-permute-start(f32[64,128]{1,0:T(8,128)S(1)} %add.78), channel_id=1, source_target_pairs={{0,64},{64,0},{1,65},{65,1},{2,66},{66,2},{3,67},{67,3},{4,68},{68... | collective-permute-start | bytes 98312 | tf_op jit(solution)/shard_map/ppermute | solution.py:40
  35.9 2.3 %collective-permute-done.1 = f32[64,128]{1,0:T(8,128)S(1)} collective-permute-done((f32[64,128]{1,0:T(8,128)S(1)}, f32[64,128]{1,0:T(8,128)S(1)}, u32[]{:S(2)}, u32[]{:S(2)}) %collective-permute-start.1) | collective-permute-done | bytes 32800 | tf_op jit(solution)/shard_map/ppermute | solution.py:40
  38.2 1.1 convolution_bitcast_fusion
  39.3 4.7 %all-to-all-start.2 = ((f32[16,16,256]{2,1,0:T(8,128)}), f32[16,16,256]{2,1,0:T(8,128)S(1)}, u32[]{:S(2)}, u32[]{:S(2)}) async-start(f32[16,16,256]{2,1,0:T(8,128)} %bitcast.17), calls=%async_computation.2 | async-start | bytes 524288 | tf_op jit(solution)/shard_map/all_to_all | solution.py:44
  44.0 3.3 %collective-permute-start.3 = (f32[256,256]{1,0:T(8,128)S(1)}, f32[256,256]{1,0:T(8,128)S(1)}, u32[]{:S(2)}, u32[]{:S(2)}) collective-permute-start(f32[256,256]{1,0:T(8,128)S(1)} %bitcast.121), channel_id=1, source_target_pairs={{0,1},{1,0},{2,3},{3,2},{4,5},{5,4},{6,7},{7,6},{8,9},{9,8},{10,11... | collective-permute-start | bytes 786440 | tf_op jit(solution)/shard_map/ppermute | solution.py:69
  47.3 3.7 %collective-permute-start.4 = (f32[256,256]{1,0:T(8,128)S(1)}, f32[256,256]{1,0:T(8,128)S(1)}, u32[]{:S(2)}, u32[]{:S(2)}) collective-permute-start(f32[256,256]{1,0:T(8,128)S(1)} %bitcast.122), channel_id=1, source_target_pairs={{0,3},{1,2},{2,1},{3,0},{4,7},{5,6},{6,5},{7,4},{8,11},{9,10},{10,... | collective-permute-start | bytes 786440 | tf_op jit(solution)/shard_map/ppermute | solution.py:69
  51.0 1.9 %all-to-all-done.2 = f32[16,16,256]{2,1,0:T(8,128)S(1)} async-done(((f32[16,16,256]{2,1,0:T(8,128)}), f32[16,16,256]{2,1,0:T(8,128)S(1)}, u32[]{:S(2)}, u32[]{:S(2)}) %all-to-all-start.2) | async-done | bytes 262176 | tf_op jit(solution)/shard_map/all_to_all | solution.py:44
  52.9 9.3 %collective-permute-start.2 = (f32[16,256]{1,0:T(8,128)S(1)}, f32[16,256]{1,0:T(8,128)S(1)}, u32[]{:S(2)}, u32[]{:S(2)}) collective-permute-start(f32[16,256]{1,0:T(8,128)S(1)} %reduce_sum.46), channel_id=1, source_target_pairs={{0,16},{16,0},{1,17},{17,1},{2,18},{18,2},{3,19},{19,3},{4,20},{20... | collective-permute-start | bytes 49160 | tf_op jit(solution)/shard_map/ppermute | solution.py:40
  62.3 1.1 collective-permute-done.2
  63.4 13.0 %all_to_all.45 = f32[16,16,256]{2,1,0:T(8,128)S(1)} all-to-all(f32[16,16,256]{2,1,0:T(8,128)S(1)} %broadcast_in_dim.19), channel_id=1, replica_groups=mesh['x'=4,'h'=2,'c'=2,'w'=2,'z'=4,'y'=4] {'z','y'}, dimensions={0} | all-to-all | bytes 524288 | tf_op jit(solution)/shard_map/all_to_all | solution.py:44
  76.5 0.3 convolution_bitcast_fusion.4
  76.7 0.3 fusion.6
  77.0 0.7 broadcast_in_dim.20
  77.6 14.6 %all-to-all-start.4 = ((f32[4,64,128]{2,1,0:T(8,128)}), f32[4,64,128]{2,1,0:T(8,128)S(1)}, u32[]{:S(2)}, u32[]{:S(2)}) async-start(f32[4,64,128]{2,1,0:T(8,128)} %broadcast_in_dim.20), calls=%async_computation.4 | async-start | bytes 262144 | tf_op jit(solution)/shard_map/all_to_all | solution.py:44
  92.3 1.9 %collective-permute-start.5 = (f32[256,256]{1,0:T(8,128)S(1)}, f32[256,256]{1,0:T(8,128)S(1)}, u32[]{:S(2)}, u32[]{:S(2)}) collective-permute-start(f32[256,256]{1,0:T(8,128)S(1)} %bitcast.123), channel_id=1, source_target_pairs={{0,2},{1,3},{2,0},{3,1},{4,6},{5,7},{6,4},{7,5},{8,10},{9,11},{10,... | collective-permute-start | bytes 786440 | tf_op jit(solution)/shard_map/ppermute | solution.py:69
  94.2 10.4 %all-to-all-done.4 = f32[4,64,128]{2,1,0:T(8,128)S(1)} async-done(((f32[4,64,128]{2,1,0:T(8,128)}), f32[4,64,128]{2,1,0:T(8,128)S(1)}, u32[]{:S(2)}, u32[]{:S(2)}) %all-to-all-start.4) | async-done | bytes 131104 | tf_op jit(solution)/shard_map/all_to_all | solution.py:44
  104.6 0.7 broadcast_in_dim.44
  105.3 4.6 %all-to-all-start.5 = ((f32[16,16,256]{2,1,0:T(8,128)}), f32[16,16,256]{2,1,0:T(8,128)S(1)}, u32[]{:S(2)}, u32[]{:S(2)}) async-start(f32[16,16,256]{2,1,0:T(8,128)} %bitcast.22), calls=%async_computation.5 | async-start | bytes 524288 | tf_op jit(solution)/shard_map/all_to_all | solution.py:44
  109.9 1.0 pad_maximum_fusion.1
  111.1 1.5 fusion
  112.5 5.1 %all-to-all-done.5 = f32[16,16,256]{2,1,0:T(8,128)S(1)} async-done(((f32[16,16,256]{2,1,0:T(8,128)}), f32[16,16,256]{2,1,0:T(8,128)S(1)}, u32[]{:S(2)}, u32[]{:S(2)}) %all-to-all-start.5) | async-done | bytes 262176 | tf_op jit(solution)/shard_map/all_to_all | solution.py:44
  117.6 0.3 convolution_bitcast_fusion.1
  118.0 0.9 fusion.5
  118.9 6.0 %all-to-all-start.6 = ((f32[4,16,512]{2,1,0:T(8,128)}), f32[4,16,512]{2,1,0:T(8,128)S(1)}, u32[]{:S(2)}, u32[]{:S(2)}) async-start(f32[4,16,512]{2,1,0:T(8,128)} %bitcast.38), calls=%async_computation.6 | async-start | bytes 262144 | tf_op jit(solution)/shard_map/all_to_all | solution.py:44
  124.9 4.8 %all-to-all-done.6 = f32[4,16,512]{2,1,0:T(8,128)S(1)} async-done(((f32[4,16,512]{2,1,0:T(8,128)}), f32[4,16,512]{2,1,0:T(8,128)S(1)}, u32[]{:S(2)}, u32[]{:S(2)}) %all-to-all-start.6) | async-done | bytes 131104 | tf_op jit(solution)/shard_map/all_to_all | solution.py:44
  129.7 1.9 %collective-permute-start.6 = (f32[16,512]{1,0:T(8,128)S(1)}, f32[16,512]{1,0:T(8,128)S(1)}, u32[]{:S(2)}, u32[]{:S(2)}) collective-permute-start(f32[16,512]{1,0:T(8,128)S(1)} %reduce_sum.48), channel_id=1, source_target_pairs={{0,16},{16,0},{1,17},{17,1},{2,18},{18,2},{3,19},{19,3},{4,20},{20... | collective-permute-start | bytes 98312 | tf_op jit(solution)/shard_map/ppermute | solution.py:40
  131.6 6.6 %collective-permute-done.6 = f32[16,512]{1,0:T(8,128)S(1)} collective-permute-done((f32[16,512]{1,0:T(8,128)S(1)}, f32[16,512]{1,0:T(8,128)S(1)}, u32[]{:S(2)}, u32[]{:S(2)}) %collective-permute-start.6) | collective-permute-done | bytes 32800 | tf_op jit(solution)/shard_map/ppermute | solution.py:40
  138.3 0.2 subtract_tanh_fusion
  138.5 7.2 %all_to_all.46 = f32[4,16,512]{2,1,0:T(8,128)S(1)} all-to-all(f32[4,16,512]{2,1,0:T(8,128)S(1)} %broadcast_in_dim.45), channel_id=1, replica_groups=mesh['x'=4,'h'=2,'c'=2,'w'=2,'z'=4,'y'=4] {'z'}, dimensions={0} | all-to-all | bytes 262144 | tf_op jit(solution)/shard_map/all_to_all | solution.py:44
  145.7 0.5 fusion.24
  146.2 0.4 fusion.3
  146.7 0.7 copy.45
  147.4 3.5 %all-to-all-start.8 = ((f32[16,16,256]{2,1,0:T(8,128)}), f32[16,16,256]{2,1,0:T(8,128)S(1)}, u32[]{:S(2)}, u32[]{:S(2)}) async-start(f32[16,16,256]{2,1,0:T(8,128)} %bitcast.41), calls=%async_computation.8 | async-start | bytes 524288 | tf_op jit(solution)/shard_map/all_to_all | solution.py:44
  150.9 7.5 %all-to-all-done.8 = f32[16,16,256]{2,1,0:T(8,128)S(1)} async-done(((f32[16,16,256]{2,1,0:T(8,128)}), f32[16,16,256]{2,1,0:T(8,128)S(1)}, u32[]{:S(2)}, u32[]{:S(2)}) %all-to-all-start.8) | async-done | bytes 262176 | tf_op jit(solution)/shard_map/all_to_all | solution.py:44
  158.5 9.3 %collective-permute-start.7 = (f32[2,16,256]{2,1,0:T(8,128)S(1)}, f32[2,16,256]{2,1,0:T(8,128)S(1)}, u32[]{:S(2)}, u32[]{:S(2)}) collective-permute-start(f32[2,16,256]{2,1,0:T(8,128)S(1)} %dynamic-slice_bitcast_fusion.4), channel_id=1, source_target_pairs={{0,32},{32,0},{1,33},{33,1},{2,34},{34,2},{3,35},{35,3},{4,36},{36... | collective-permute-start | bytes 98312 | tf_op jit(solution)/shard_map/ppermute | solution.py:40
  167.8 0.8 collective-permute-done.7
  168.7 7.8 %collective-permute-start.8 = (f32[16,256]{1,0:T(8,128)S(1)}, f32[16,256]{1,0:T(8,128)S(1)}, u32[]{:S(2)}, u32[]{:S(2)}) collective-permute-start(f32[16,256]{1,0:T(8,128)S(1)} %dynamic-slice_bitcast_fusion.5), channel_id=1, source_target_pairs={{0,64},{64,0},{1,65},{65,1},{2,66},{66,2},{3,67},{67,3},{4,68},{68... | collective-permute-start | bytes 49160 | tf_op jit(solution)/shard_map/ppermute | solution.py:40
  176.4 5.4 %collective-permute-done.8 = f32[16,256]{1,0:T(8,128)S(1)} collective-permute-done((f32[16,256]{1,0:T(8,128)S(1)}, f32[16,256]{1,0:T(8,128)S(1)}, u32[]{:S(2)}, u32[]{:S(2)}) %collective-permute-start.8) | collective-permute-done | bytes 16416 | tf_op jit(solution)/shard_map/ppermute | solution.py:40
  181.9 0.6 copy.38
  (49 shorter events, 1.0 us)
Async XLA Ops:
  0.0 111.1 %copy-start = (f32[512,256]{1,0:T(8,128)S(1)}, f32[512,256]{1,0:T(8,128)}, u32[]{:S(2)}) copy-start(f32[512,256]{1,0:T(8,128)} %param.6) | copy-start | bytes 1572868
  0.0 1.3 copy-start.1
  1.3 6.1 %slice-start = ((f32[2,128,256]{2,1,0:T(8,128)}), f32[1,128,256]{2,1,0:T(8,128)S(1)}, s32[]{:S(2)}) async-start(f32[2,128,256]{2,1,0:T(8,128)} %param.10), calls=%async_computation.9 | async-start | bytes 262144 | tf_op jit(solution)/shard_map/slice | solution.py:58
  2.2 9.7 %all-to-all-start = ((f32[4,64,128]{2,1,0:T(8,128)}), f32[4,64,128]{2,1,0:T(8,128)S(1)}, u32[]{:S(2)}, u32[]{:S(2)}) async-start(f32[4,64,128]{2,1,0:T(8,128)} %fusion.28), calls=%async_computation | async-start | bytes 262144 | tf_op jit(solution)/shard_map/all_to_all | solution.py:44
  7.1 0.9 copy-start.5
  11.9 26.3 %all-to-all-start.1 = ((f32[4,640,128]{2,1,0:T(8,128)}), f32[4,640,128]{2,1,0:T(8,128)S(1)}, u32[]{:S(2)}, u32[]{:S(2)}) async-start(f32[4,640,128]{2,1,0:T(8,128)} %pad_maximum_fusion), calls=%async_computation.1 | async-start | bytes 2621440 | tf_op jit(solution)/shard_map/all_to_all | solution.py:44
  15.5 28.6 %copy-start.3 = (f32[2,128,256]{2,1,0:T(8,128)S(1)}, f32[2,128,256]{2,1,0:T(8,128)}, u32[]{:S(2)}) copy-start(f32[2,128,256]{2,1,0:T(8,128)} %param.8) | copy-start | bytes 786436
  15.5 9.4 %collective-permute-start = (f32[64,128]{1,0:T(8,128)S(1)}, f32[64,128]{1,0:T(8,128)S(1)}, u32[]{:S(2)}, u32[]{:S(2)}) collective-permute-start(f32[64,128]{1,0:T(8,128)S(1)} %reduce_sum.45), channel_id=1, source_target_pairs={{0,32},{32,0},{1,33},{33,1},{2,34},{34,2},{3,35},{35,3},{4,36},{36... | collective-permute-start | bytes 98312 | tf_op jit(solution)/shard_map/ppermute | solution.py:40
  24.9 13.4 %collective-permute-start.1 = (f32[64,128]{1,0:T(8,128)S(1)}, f32[64,128]{1,0:T(8,128)S(1)}, u32[]{:S(2)}, u32[]{:S(2)}) collective-permute-start(f32[64,128]{1,0:T(8,128)S(1)} %add.78), channel_id=1, source_target_pairs={{0,64},{64,0},{1,65},{65,1},{2,66},{66,2},{3,67},{67,3},{4,68},{68... | collective-permute-start | bytes 98312 | tf_op jit(solution)/shard_map/ppermute | solution.py:40
  39.3 13.6 %all-to-all-start.2 = ((f32[16,16,256]{2,1,0:T(8,128)}), f32[16,16,256]{2,1,0:T(8,128)S(1)}, u32[]{:S(2)}, u32[]{:S(2)}) async-start(f32[16,16,256]{2,1,0:T(8,128)} %bitcast.17), calls=%async_computation.2 | async-start | bytes 524288 | tf_op jit(solution)/shard_map/all_to_all | solution.py:44
  44.0 19.3 %collective-permute-start.3 = (f32[256,256]{1,0:T(8,128)S(1)}, f32[256,256]{1,0:T(8,128)S(1)}, u32[]{:S(2)}, u32[]{:S(2)}) collective-permute-start(f32[256,256]{1,0:T(8,128)S(1)} %bitcast.121), channel_id=1, source_target_pairs={{0,1},{1,0},{2,3},{3,2},{4,5},{5,4},{6,7},{7,6},{8,9},{9,8},{10,11... | collective-permute-start | bytes 786440 | tf_op jit(solution)/shard_map/ppermute | solution.py:69
  47.3 16.1 %collective-permute-start.4 = (f32[256,256]{1,0:T(8,128)S(1)}, f32[256,256]{1,0:T(8,128)S(1)}, u32[]{:S(2)}, u32[]{:S(2)}) collective-permute-start(f32[256,256]{1,0:T(8,128)S(1)} %bitcast.122), channel_id=1, source_target_pairs={{0,3},{1,2},{2,1},{3,0},{4,7},{5,6},{6,5},{7,4},{8,11},{9,10},{10,... | collective-permute-start | bytes 786440 | tf_op jit(solution)/shard_map/ppermute | solution.py:69
  52.9 10.4 %collective-permute-start.2 = (f32[16,256]{1,0:T(8,128)S(1)}, f32[16,256]{1,0:T(8,128)S(1)}, u32[]{:S(2)}, u32[]{:S(2)}) collective-permute-start(f32[16,256]{1,0:T(8,128)S(1)} %reduce_sum.46), channel_id=1, source_target_pairs={{0,16},{16,0},{1,17},{17,1},{2,18},{18,2},{3,19},{19,3},{4,20},{20... | collective-permute-start | bytes 49160 | tf_op jit(solution)/shard_map/ppermute | solution.py:40
  63.4 42.0 %copy-start.4 = (f32[256,256]{1,0:T(8,128)}, f32[256,256]{1,0:T(8,128)S(1)}, u32[]{:S(2)}) copy-start(f32[256,256]{1,0:T(8,128)S(1)} %collective-permute-done.4) | copy-start | bytes 786436
  77.6 26.9 %all-to-all-start.4 = ((f32[4,64,128]{2,1,0:T(8,128)}), f32[4,64,128]{2,1,0:T(8,128)S(1)}, u32[]{:S(2)}, u32[]{:S(2)}) async-start(f32[4,64,128]{2,1,0:T(8,128)} %broadcast_in_dim.20), calls=%async_computation.4 | async-start | bytes 262144 | tf_op jit(solution)/shard_map/all_to_all | solution.py:44
  92.3 12.3 %collective-permute-start.5 = (f32[256,256]{1,0:T(8,128)S(1)}, f32[256,256]{1,0:T(8,128)S(1)}, u32[]{:S(2)}, u32[]{:S(2)}) collective-permute-start(f32[256,256]{1,0:T(8,128)S(1)} %bitcast.123), channel_id=1, source_target_pairs={{0,2},{1,3},{2,0},{3,1},{4,6},{5,7},{6,4},{7,5},{8,10},{9,11},{10,... | collective-permute-start | bytes 786440 | tf_op jit(solution)/shard_map/ppermute | solution.py:69
  105.3 12.3 %all-to-all-start.5 = ((f32[16,16,256]{2,1,0:T(8,128)}), f32[16,16,256]{2,1,0:T(8,128)S(1)}, u32[]{:S(2)}, u32[]{:S(2)}) async-start(f32[16,16,256]{2,1,0:T(8,128)} %bitcast.22), calls=%async_computation.5 | async-start | bytes 524288 | tf_op jit(solution)/shard_map/all_to_all | solution.py:44
  117.9 20.3 %copy-start.2 = (bf16[512,256]{1,0:T(8,128)(2,1)S(1)}, bf16[512,256]{1,0:T(8,128)(2,1)}, u32[]{:S(2)}) copy-start(bf16[512,256]{1,0:T(8,128)(2,1)} %param.7) | copy-start | bytes 786436
  118.9 10.8 %all-to-all-start.6 = ((f32[4,16,512]{2,1,0:T(8,128)}), f32[4,16,512]{2,1,0:T(8,128)S(1)}, u32[]{:S(2)}, u32[]{:S(2)}) async-start(f32[4,16,512]{2,1,0:T(8,128)} %bitcast.38), calls=%async_computation.6 | async-start | bytes 262144 | tf_op jit(solution)/shard_map/all_to_all | solution.py:44
  129.7 8.6 %collective-permute-start.6 = (f32[16,512]{1,0:T(8,128)S(1)}, f32[16,512]{1,0:T(8,128)S(1)}, u32[]{:S(2)}, u32[]{:S(2)}) collective-permute-start(f32[16,512]{1,0:T(8,128)S(1)} %reduce_sum.48), channel_id=1, source_target_pairs={{0,16},{16,0},{1,17},{17,1},{2,18},{18,2},{3,19},{19,3},{4,20},{20... | collective-permute-start | bytes 98312 | tf_op jit(solution)/shard_map/ppermute | solution.py:40
  147.4 11.0 %all-to-all-start.8 = ((f32[16,16,256]{2,1,0:T(8,128)}), f32[16,16,256]{2,1,0:T(8,128)S(1)}, u32[]{:S(2)}, u32[]{:S(2)}) async-start(f32[16,16,256]{2,1,0:T(8,128)} %bitcast.41), calls=%async_computation.8 | async-start | bytes 524288 | tf_op jit(solution)/shard_map/all_to_all | solution.py:44
  158.5 10.2 %collective-permute-start.7 = (f32[2,16,256]{2,1,0:T(8,128)S(1)}, f32[2,16,256]{2,1,0:T(8,128)S(1)}, u32[]{:S(2)}, u32[]{:S(2)}) collective-permute-start(f32[2,16,256]{2,1,0:T(8,128)S(1)} %dynamic-slice_bitcast_fusion.4), channel_id=1, source_target_pairs={{0,32},{32,0},{1,33},{33,1},{2,34},{34,2},{3,35},{35,3},{4,36},{36... | collective-permute-start | bytes 98312 | tf_op jit(solution)/shard_map/ppermute | solution.py:40
  168.7 13.2 %collective-permute-start.8 = (f32[16,256]{1,0:T(8,128)S(1)}, f32[16,256]{1,0:T(8,128)S(1)}, u32[]{:S(2)}, u32[]{:S(2)}) collective-permute-start(f32[16,256]{1,0:T(8,128)S(1)} %dynamic-slice_bitcast_fusion.5), channel_id=1, source_target_pairs={{0,64},{64,0},{1,65},{65,1},{2,66},{66,2},{3,67},{67,3},{4,68},{68... | collective-permute-start | bytes 49160 | tf_op jit(solution)/shard_map/ppermute | solution.py:40

commit v12 on v11

--- a/solution.py
+++ b/solution.py
@@ -85,7 +85,8 @@
         )
 
     first = solve(0) + solve(1)
-    first = jnp.sum(exchange(copies(first, 4), ("h", "c")), 0)
+    first = first + swap(first, "c")
+    first = first + swap(first, "h")
     first, far = lax.optimization_barrier((first, far))
 
     solved = jnp.concatenate([first, second], 1).reshape(4, 1, 16, 256)

time: 184 us -> 175 us (0.951)
  starting transfers between devices: 98.5 us -> 116 us
  blocking collectives: 20.3 us -> 7.19 us
  waiting for transfers between devices: 49.4 us -> 36.8 us
    ppermute x6 -> x8, starting transfers between devices: 47.9 us -> 75.3 us  [swap(): return lax.ppermute(a, axis, [(0, 1), (1, 0)])]
    all_to_all x2 -> x1, blocking collectives: 20.3 us -> 7.19 us  [exchange(): return lax.all_to_all(a, axes, 0, 0, tiled=True)]
    all_to_all x7, starting transfers between devices: 41.7 us -> 28.8 us  [exchange(): return lax.all_to_all(a, axes, 0, 0, tiled=True)]
    ppermute x6 -> x8, waiting for transfers between devices: 17.1 us -> 10.8 us  [swap(): return lax.ppermute(a, axis, [(0, 1), (1, 0)])]
    all_to_all x7, waiting for transfers between devices: 32.3 us -> 26 us  [exchange(): return lax.all_to_all(a, axes, 0, 0, tiled=True)]
    ppermute x3, starting transfers between devices: 8.87 us -> 11.7 us  [local(): lax.ppermute(flat, 'y', [(i, i ^ k) for i in range(4)])]
  transfers between devices with their start and end apart: 16 -> 18, of which waited for: 12 -> 14; matrix products, arithmetic and copies ran while one was open for 2% -> 3% of each run, Pallas kernels for 0% -> 0%
where the time goes in v12:
time: 175 us; the launch traced here: 174 us
  starting transfers between devices  116 us (66%)
  waiting for transfers between devices  36.8 us (21%)
  blocking collectives  7.19 us (4%)
  matrix products  6.37 us (4%)
  local copies, waits for them, and re-layouts  5.2 us (3%)
  other arithmetic  2.39 us (1%)
    ppermute x8, starting transfers between devices, swap(): return lax.ppermute(a, axis, [(0, 1), (1, 0)])  75.3 us
    all_to_all x7, starting transfers between devices, exchange(): return lax.all_to_all(a, axes, 0, 0, tiled=True)  28.8 us
    all_to_all x7, waiting for transfers between devices, exchange(): return lax.all_to_all(a, axes, 0, 0, tiled=True)  26 us
    ppermute x3, starting transfers between devices, local(): lax.ppermute(flat, 'y', [(i, i ^ k) for i in range(4)])  11.7 us
    ppermute x8, waiting for transfers between devices, swap(): return lax.ppermute(a, axis, [(0, 1), (1, 0)])  10.8 us
    all_to_all x1, blocking collectives, exchange(): return lax.all_to_all(a, axes, 0, 0, tiled=True)  7.19 us
  transfers between devices with their start and end apart: 18, of which 14 were waited for; matrix products, arithmetic and copies ran while one was open for 3% of the time, Pallas kernels for 0%

profile of v12, /device:TPU:1, one launch (start us, length us, event | category | flops | bytes accessed | tf_op | source)
XLA Modules:
  0.0 174.3 jit_solution(12946633859805425677)
XLA Ops:
  0.0 1.1 slice_bitcast_fusion
  1.3 0.9 fusion.28
  2.2 4.8 %all-to-all-start = ((f32[4,64,128]{2,1,0:T(8,128)}), f32[4,64,128]{2,1,0:T(8,128)S(1)}, u32[]{:S(2)}, u32[]{:S(2)}) async-start(f32[4,64,128]{2,1,0:T(8,128)} %fusion.28), calls=%async_computation | async-start | bytes 262144 | tf_op jit(solution)/shard_map/all_to_all | solution.py:44
  7.5 0.4 copy-done.5
  8.0 1.2 pad_maximum_fusion
  9.2 2.7 %all-to-all-done = f32[4,64,128]{2,1,0:T(8,128)S(1)} async-done(((f32[4,64,128]{2,1,0:T(8,128)}), f32[4,64,128]{2,1,0:T(8,128)S(1)}, u32[]{:S(2)}, u32[]{:S(2)}) %all-to-all-start) | async-done | bytes 131104 | tf_op jit(solution)/shard_map/all_to_all | solution.py:44
  11.9 3.6 %all-to-all-start.1 = ((f32[4,640,128]{2,1,0:T(8,128)}), f32[4,640,128]{2,1,0:T(8,128)S(1)}, u32[]{:S(2)}, u32[]{:S(2)}) async-start(f32[4,640,128]{2,1,0:T(8,128)} %pad_maximum_fusion), calls=%async_computation.1 | async-start | bytes 2621440 | tf_op jit(solution)/shard_map/all_to_all | solution.py:44
  15.5 8.5 %collective-permute-start = (f32[64,128]{1,0:T(8,128)S(1)}, f32[64,128]{1,0:T(8,128)S(1)}, u32[]{:S(2)}, u32[]{:S(2)}) collective-permute-start(f32[64,128]{1,0:T(8,128)S(1)} %reduce_sum.36), channel_id=1, source_target_pairs={{0,32},{32,0},{1,33},{33,1},{2,34},{34,2},{3,35},{35,3},{4,36},{36... | collective-permute-start | bytes 98312 | tf_op jit(solution)/shard_map/ppermute | solution.py:40
  24.0 0.8 collective-permute-done
  24.9 11.1 %collective-permute-start.1 = (f32[64,128]{1,0:T(8,128)S(1)}, f32[64,128]{1,0:T(8,128)S(1)}, u32[]{:S(2)}, u32[]{:S(2)}) collective-permute-start(f32[64,128]{1,0:T(8,128)S(1)} %add.84), channel_id=1, source_target_pairs={{0,64},{64,0},{1,65},{65,1},{2,66},{66,2},{3,67},{67,3},{4,68},{68... | collective-permute-start | bytes 98312 | tf_op jit(solution)/shard_map/ppermute | solution.py:40
  35.9 2.3 %collective-permute-done.1 = f32[64,128]{1,0:T(8,128)S(1)} collective-permute-done((f32[64,128]{1,0:T(8,128)S(1)}, f32[64,128]{1,0:T(8,128)S(1)}, u32[]{:S(2)}, u32[]{:S(2)}) %collective-permute-start.1) | collective-permute-done | bytes 32800 | tf_op jit(solution)/shard_map/ppermute | solution.py:40
  38.2 1.1 convolution_bitcast_fusion
  39.3 4.7 %all-to-all-start.2 = ((f32[16,16,256]{2,1,0:T(8,128)}), f32[16,16,256]{2,1,0:T(8,128)S(1)}, u32[]{:S(2)}, u32[]{:S(2)}) async-start(f32[16,16,256]{2,1,0:T(8,128)} %bitcast.17), calls=%async_computation.2 | async-start | bytes 524288 | tf_op jit(solution)/shard_map/all_to_all | solution.py:44
  44.0 3.3 %collective-permute-start.3 = (f32[256,256]{1,0:T(8,128)S(1)}, f32[256,256]{1,0:T(8,128)S(1)}, u32[]{:S(2)}, u32[]{:S(2)}) collective-permute-start(f32[256,256]{1,0:T(8,128)S(1)} %bitcast.121), channel_id=1, source_target_pairs={{0,1},{1,0},{2,3},{3,2},{4,5},{5,4},{6,7},{7,6},{8,9},{9,8},{10,11... | collective-permute-start | bytes 786440 | tf_op jit(solution)/shard_map/ppermute | solution.py:69
  47.3 3.7 %collective-permute-start.4 = (f32[256,256]{1,0:T(8,128)S(1)}, f32[256,256]{1,0:T(8,128)S(1)}, u32[]{:S(2)}, u32[]{:S(2)}) collective-permute-start(f32[256,256]{1,0:T(8,128)S(1)} %bitcast.122), channel_id=1, source_target_pairs={{0,3},{1,2},{2,1},{3,0},{4,7},{5,6},{6,5},{7,4},{8,11},{9,10},{10,... | collective-permute-start | bytes 786440 | tf_op jit(solution)/shard_map/ppermute | solution.py:69
  51.0 1.9 %all-to-all-done.2 = f32[16,16,256]{2,1,0:T(8,128)S(1)} async-done(((f32[16,16,256]{2,1,0:T(8,128)}), f32[16,16,256]{2,1,0:T(8,128)S(1)}, u32[]{:S(2)}, u32[]{:S(2)}) %all-to-all-start.2) | async-done | bytes 262176 | tf_op jit(solution)/shard_map/all_to_all | solution.py:44
  52.9 9.3 %collective-permute-start.2 = (f32[16,256]{1,0:T(8,128)S(1)}, f32[16,256]{1,0:T(8,128)S(1)}, u32[]{:S(2)}, u32[]{:S(2)}) collective-permute-start(f32[16,256]{1,0:T(8,128)S(1)} %reduce_sum.37), channel_id=1, source_target_pairs={{0,16},{16,0},{1,17},{17,1},{2,18},{18,2},{3,19},{19,3},{4,20},{20... | collective-permute-start | bytes 49160 | tf_op jit(solution)/shard_map/ppermute | solution.py:40
  62.3 1.1 collective-permute-done.2
  63.4 0.8 broadcast_in_dim.17
  64.2 4.3 %all-to-all-start.3 = ((f32[16,16,256]{2,1,0:T(8,128)}), f32[16,16,256]{2,1,0:T(8,128)S(1)}, u32[]{:S(2)}, u32[]{:S(2)}) async-start(f32[16,16,256]{2,1,0:T(8,128)} %broadcast_in_dim.17), calls=%async_computation.3 | async-start | bytes 524288 | tf_op jit(solution)/shard_map/all_to_all | solution.py:44
  68.5 4.8 %collective-permute-start.7 = (f32[256,256]{1,0:T(8,128)S(1)}, f32[256,256]{1,0:T(8,128)S(1)}, u32[]{:S(2)}, u32[]{:S(2)}) collective-permute-start(f32[256,256]{1,0:T(8,128)S(1)} %bitcast.123), channel_id=1, source_target_pairs={{0,2},{1,3},{2,0},{3,1},{4,6},{5,7},{6,4},{7,5},{8,10},{9,11},{10,... | collective-permute-start | bytes 786440 | tf_op jit(solution)/shard_map/ppermute | solution.py:69
  73.3 4.2 %all-to-all-done.3 = f32[16,16,256]{2,1,0:T(8,128)S(1)} async-done(((f32[16,16,256]{2,1,0:T(8,128)}), f32[16,16,256]{2,1,0:T(8,128)S(1)}, u32[]{:S(2)}, u32[]{:S(2)}) %all-to-all-start.3) | async-done | bytes 262176 | tf_op jit(solution)/shard_map/all_to_all | solution.py:44
  78.0 5.7 %collective-permute-start.5 = (f32[64,128]{1,0:T(8,128)S(1)}, f32[64,128]{1,0:T(8,128)S(1)}, u32[]{:S(2)}, u32[]{:S(2)}) collective-permute-start(f32[64,128]{1,0:T(8,128)S(1)} %fusion.6), channel_id=1, source_target_pairs={{0,32},{32,0},{1,33},{33,1},{2,34},{34,2},{3,35},{35,3},{4,36},{36... | collective-permute-start | bytes 98312 | tf_op jit(solution)/shard_map/ppermute | solution.py:40
  83.7 0.8 collective-permute-done.5
  84.6 11.6 %collective-permute-start.6 = (f32[64,128]{1,0:T(8,128)S(1)}, f32[64,128]{1,0:T(8,128)S(1)}, u32[]{:S(2)}, u32[]{:S(2)}) collective-permute-start(f32[64,128]{1,0:T(8,128)S(1)} %add.89), channel_id=1, source_target_pairs={{0,64},{64,0},{1,65},{65,1},{2,66},{66,2},{3,67},{67,3},{4,68},{68... | collective-permute-start | bytes 98312 | tf_op jit(solution)/shard_map/ppermute | solution.py:40
  96.3 1.7 collective-permute-done.6
  98.0 0.7 broadcast_in_dim.37
  98.7 4.6 %all-to-all-start.4 = ((f32[16,16,256]{2,1,0:T(8,128)}), f32[16,16,256]{2,1,0:T(8,128)S(1)}, u32[]{:S(2)}, u32[]{:S(2)}) async-start(f32[16,16,256]{2,1,0:T(8,128)} %bitcast.22), calls=%async_computation.4 | async-start | bytes 524288 | tf_op jit(solution)/shard_map/all_to_all | solution.py:44
  103.3 1.0 pad_maximum_fusion.1
  104.4 1.5 fusion
  105.9 5.0 %all-to-all-done.4 = f32[16,16,256]{2,1,0:T(8,128)S(1)} async-done(((f32[16,16,256]{2,1,0:T(8,128)}), f32[16,16,256]{2,1,0:T(8,128)S(1)}, u32[]{:S(2)}, u32[]{:S(2)}) %all-to-all-start.4) | async-done | bytes 262176 | tf_op jit(solution)/shard_map/all_to_all | solution.py:44
  110.9 0.3 convolution_bitcast_fusion.1
  111.3 1.0 fusion.5
  112.2 3.3 %all-to-all-start.5 = ((f32[4,16,512]{2,1,0:T(8,128)}), f32[4,16,512]{2,1,0:T(8,128)S(1)}, u32[]{:S(2)}, u32[]{:S(2)}) async-start(f32[4,16,512]{2,1,0:T(8,128)} %bitcast.38), calls=%async_computation.5 | async-start | bytes 262144 | tf_op jit(solution)/shard_map/all_to_all | solution.py:44
  115.5 4.7 %all-to-all-done.5 = f32[4,16,512]{2,1,0:T(8,128)S(1)} async-done(((f32[4,16,512]{2,1,0:T(8,128)}), f32[4,16,512]{2,1,0:T(8,128)S(1)}, u32[]{:S(2)}, u32[]{:S(2)}) %all-to-all-start.5) | async-done | bytes 131104 | tf_op jit(solution)/shard_map/all_to_all | solution.py:44
  120.3 7.7 %collective-permute-start.8 = (f32[16,512]{1,0:T(8,128)S(1)}, f32[16,512]{1,0:T(8,128)S(1)}, u32[]{:S(2)}, u32[]{:S(2)}) collective-permute-start(f32[16,512]{1,0:T(8,128)S(1)} %reduce_sum.38), channel_id=1, source_target_pairs={{0,16},{16,0},{1,17},{17,1},{2,18},{18,2},{3,19},{19,3},{4,20},{20... | collective-permute-start | bytes 98312 | tf_op jit(solution)/shard_map/ppermute | solution.py:40
  128.0 1.3 collective-permute-done.8
  129.5 7.2 %all_to_all.40 = f32[4,16,512]{2,1,0:T(8,128)S(1)} all-to-all(f32[4,16,512]{2,1,0:T(8,128)S(1)} %broadcast_in_dim.38), channel_id=1, replica_groups=mesh['x'=4,'h'=2,'c'=2,'w'=2,'z'=4,'y'=4] {'z'}, dimensions={0} | all-to-all | bytes 262144 | tf_op jit(solution)/shard_map/all_to_all | solution.py:44
  136.7 0.5 fusion.24
  137.2 0.4 fusion.3
  137.6 0.7 copy.36
  138.4 3.5 %all-to-all-start.7 = ((f32[16,16,256]{2,1,0:T(8,128)}), f32[16,16,256]{2,1,0:T(8,128)S(1)}, u32[]{:S(2)}, u32[]{:S(2)}) async-start(f32[16,16,256]{2,1,0:T(8,128)} %bitcast.41), calls=%async_computation.7 | async-start | bytes 524288 | tf_op jit(solution)/shard_map/all_to_all | solution.py:44
  141.9 7.5 %all-to-all-done.7 = f32[16,16,256]{2,1,0:T(8,128)S(1)} async-done(((f32[16,16,256]{2,1,0:T(8,128)}), f32[16,16,256]{2,1,0:T(8,128)S(1)}, u32[]{:S(2)}, u32[]{:S(2)}) %all-to-all-start.7) | async-done | bytes 262176 | tf_op jit(solution)/shard_map/all_to_all | solution.py:44
  149.4 10.1 %collective-permute-start.9 = (f32[2,16,256]{2,1,0:T(8,128)S(1)}, f32[2,16,256]{2,1,0:T(8,128)S(1)}, u32[]{:S(2)}, u32[]{:S(2)}) collective-permute-start(f32[2,16,256]{2,1,0:T(8,128)S(1)} %dynamic-slice_bitcast_fusion.4), channel_id=1, source_target_pairs={{0,32},{32,0},{1,33},{33,1},{2,34},{34,2},{3,35},{35,3},{4,36},{36... | collective-permute-start | bytes 98312 | tf_op jit(solution)/shard_map/ppermute | solution.py:40
  159.6 0.8 collective-permute-done.9
  160.4 11.3 %collective-permute-start.10 = (f32[16,256]{1,0:T(8,128)S(1)}, f32[16,256]{1,0:T(8,128)S(1)}, u32[]{:S(2)}, u32[]{:S(2)}) collective-permute-start(f32[16,256]{1,0:T(8,128)S(1)} %dynamic-slice_bitcast_fusion.5), channel_id=1, source_target_pairs={{0,64},{64,0},{1,65},{65,1},{2,66},{66,2},{3,67},{67,3},{4,68},{68... | collective-permute-start | bytes 49160 | tf_op jit(solution)/shard_map/ppermute | solution.py:40
  171.7 1.9 %collective-permute-done.10 = f32[16,256]{1,0:T(8,128)S(1)} collective-permute-done((f32[16,256]{1,0:T(8,128)S(1)}, f32[16,256]{1,0:T(8,128)S(1)}, u32[]{:S(2)}, u32[]{:S(2)}) %collective-permute-start.10) | collective-permute-done | bytes 16416 | tf_op jit(solution)/shard_map/ppermute | solution.py:40
  173.7 0.6 copy.29
  (52 shorter events, 1.7 us)
Async XLA Ops:
  0.0 104.4 %copy-start = (f32[512,256]{1,0:T(8,128)S(1)}, f32[512,256]{1,0:T(8,128)}, u32[]{:S(2)}) copy-start(f32[512,256]{1,0:T(8,128)} %param.6) | copy-start | bytes 1572868
  0.0 1.3 copy-start.1
  1.3 6.1 %slice-start = ((f32[2,128,256]{2,1,0:T(8,128)}), f32[1,128,256]{2,1,0:T(8,128)S(1)}, s32[]{:S(2)}) async-start(f32[2,128,256]{2,1,0:T(8,128)} %param.10), calls=%async_computation.8 | async-start | bytes 262144 | tf_op jit(solution)/shard_map/slice | solution.py:58
  2.2 9.7 %all-to-all-start = ((f32[4,64,128]{2,1,0:T(8,128)}), f32[4,64,128]{2,1,0:T(8,128)S(1)}, u32[]{:S(2)}, u32[]{:S(2)}) async-start(f32[4,64,128]{2,1,0:T(8,128)} %fusion.28), calls=%async_computation | async-start | bytes 262144 | tf_op jit(solution)/shard_map/all_to_all | solution.py:44
  7.1 0.9 copy-start.5
  11.9 26.3 %all-to-all-start.1 = ((f32[4,640,128]{2,1,0:T(8,128)}), f32[4,640,128]{2,1,0:T(8,128)S(1)}, u32[]{:S(2)}, u32[]{:S(2)}) async-start(f32[4,640,128]{2,1,0:T(8,128)} %pad_maximum_fusion), calls=%async_computation.1 | async-start | bytes 2621440 | tf_op jit(solution)/shard_map/all_to_all | solution.py:44
  15.5 28.6 %copy-start.3 = (f32[2,128,256]{2,1,0:T(8,128)S(1)}, f32[2,128,256]{2,1,0:T(8,128)}, u32[]{:S(2)}) copy-start(f32[2,128,256]{2,1,0:T(8,128)} %param.8) | copy-start | bytes 786436
  15.5 9.4 %collective-permute-start = (f32[64,128]{1,0:T(8,128)S(1)}, f32[64,128]{1,0:T(8,128)S(1)}, u32[]{:S(2)}, u32[]{:S(2)}) collective-permute-start(f32[64,128]{1,0:T(8,128)S(1)} %reduce_sum.36), channel_id=1, source_target_pairs={{0,32},{32,0},{1,33},{33,1},{2,34},{34,2},{3,35},{35,3},{4,36},{36... | collective-permute-start | bytes 98312 | tf_op jit(solution)/shard_map/ppermute | solution.py:40
  24.9 13.4 %collective-permute-start.1 = (f32[64,128]{1,0:T(8,128)S(1)}, f32[64,128]{1,0:T(8,128)S(1)}, u32[]{:S(2)}, u32[]{:S(2)}) collective-permute-start(f32[64,128]{1,0:T(8,128)S(1)} %add.84), channel_id=1, source_target_pairs={{0,64},{64,0},{1,65},{65,1},{2,66},{66,2},{3,67},{67,3},{4,68},{68... | collective-permute-start | bytes 98312 | tf_op jit(solution)/shard_map/ppermute | solution.py:40
  39.3 13.6 %all-to-all-start.2 = ((f32[16,16,256]{2,1,0:T(8,128)}), f32[16,16,256]{2,1,0:T(8,128)S(1)}, u32[]{:S(2)}, u32[]{:S(2)}) async-start(f32[16,16,256]{2,1,0:T(8,128)} %bitcast.17), calls=%async_computation.2 | async-start | bytes 524288 | tf_op jit(solution)/shard_map/all_to_all | solution.py:44
  44.0 19.3 %collective-permute-start.3 = (f32[256,256]{1,0:T(8,128)S(1)}, f32[256,256]{1,0:T(8,128)S(1)}, u32[]{:S(2)}, u32[]{:S(2)}) collective-permute-start(f32[256,256]{1,0:T(8,128)S(1)} %bitcast.121), channel_id=1, source_target_pairs={{0,1},{1,0},{2,3},{3,2},{4,5},{5,4},{6,7},{7,6},{8,9},{9,8},{10,11... | collective-permute-start | bytes 786440 | tf_op jit(solution)/shard_map/ppermute | solution.py:69
  47.3 16.1 %collective-permute-start.4 = (f32[256,256]{1,0:T(8,128)S(1)}, f32[256,256]{1,0:T(8,128)S(1)}, u32[]{:S(2)}, u32[]{:S(2)}) collective-permute-start(f32[256,256]{1,0:T(8,128)S(1)} %bitcast.122), channel_id=1, source_target_pairs={{0,3},{1,2},{2,1},{3,0},{4,7},{5,6},{6,5},{7,4},{8,11},{9,10},{10,... | collective-permute-start | bytes 786440 | tf_op jit(solution)/shard_map/ppermute | solution.py:69
  52.9 10.4 %collective-permute-start.2 = (f32[16,256]{1,0:T(8,128)S(1)}, f32[16,256]{1,0:T(8,128)S(1)}, u32[]{:S(2)}, u32[]{:S(2)}) collective-permute-start(f32[16,256]{1,0:T(8,128)S(1)} %reduce_sum.37), channel_id=1, source_target_pairs={{0,16},{16,0},{1,17},{17,1},{2,18},{18,2},{3,19},{19,3},{4,20},{20... | collective-permute-start | bytes 49160 | tf_op jit(solution)/shard_map/ppermute | solution.py:40
  63.4 35.3 %copy-start.4 = (f32[256,256]{1,0:T(8,128)}, f32[256,256]{1,0:T(8,128)S(1)}, u32[]{:S(2)}) copy-start(f32[256,256]{1,0:T(8,128)S(1)} %collective-permute-done.4) | copy-start | bytes 786436
  64.2 13.3 %all-to-all-start.3 = ((f32[16,16,256]{2,1,0:T(8,128)}), f32[16,16,256]{2,1,0:T(8,128)S(1)}, u32[]{:S(2)}, u32[]{:S(2)}) async-start(f32[16,16,256]{2,1,0:T(8,128)} %broadcast_in_dim.17), calls=%async_computation.3 | async-start | bytes 524288 | tf_op jit(solution)/shard_map/all_to_all | solution.py:44
  68.5 29.5 %collective-permute-start.7 = (f32[256,256]{1,0:T(8,128)S(1)}, f32[256,256]{1,0:T(8,128)S(1)}, u32[]{:S(2)}, u32[]{:S(2)}) collective-permute-start(f32[256,256]{1,0:T(8,128)S(1)} %bitcast.123), channel_id=1, source_target_pairs={{0,2},{1,3},{2,0},{3,1},{4,6},{5,7},{6,4},{7,5},{8,10},{9,11},{10,... | collective-permute-start | bytes 786440 | tf_op jit(solution)/shard_map/ppermute | solution.py:69
  78.0 6.6 %collective-permute-start.5 = (f32[64,128]{1,0:T(8,128)S(1)}, f32[64,128]{1,0:T(8,128)S(1)}, u32[]{:S(2)}, u32[]{:S(2)}) collective-permute-start(f32[64,128]{1,0:T(8,128)S(1)} %fusion.6), channel_id=1, source_target_pairs={{0,32},{32,0},{1,33},{33,1},{2,34},{34,2},{3,35},{35,3},{4,36},{36... | collective-permute-start | bytes 98312 | tf_op jit(solution)/shard_map/ppermute | solution.py:40
  84.6 13.4 %collective-permute-start.6 = (f32[64,128]{1,0:T(8,128)S(1)}, f32[64,128]{1,0:T(8,128)S(1)}, u32[]{:S(2)}, u32[]{:S(2)}) collective-permute-start(f32[64,128]{1,0:T(8,128)S(1)} %add.89), channel_id=1, source_target_pairs={{0,64},{64,0},{1,65},{65,1},{2,66},{66,2},{3,67},{67,3},{4,68},{68... | collective-permute-start | bytes 98312 | tf_op jit(solution)/shard_map/ppermute | solution.py:40
  98.7 12.2 %all-to-all-start.4 = ((f32[16,16,256]{2,1,0:T(8,128)}), f32[16,16,256]{2,1,0:T(8,128)S(1)}, u32[]{:S(2)}, u32[]{:S(2)}) async-start(f32[16,16,256]{2,1,0:T(8,128)} %bitcast.22), calls=%async_computation.4 | async-start | bytes 524288 | tf_op jit(solution)/shard_map/all_to_all | solution.py:44
  111.2 18.1 %copy-start.2 = (bf16[512,256]{1,0:T(8,128)(2,1)S(1)}, bf16[512,256]{1,0:T(8,128)(2,1)}, u32[]{:S(2)}) copy-start(bf16[512,256]{1,0:T(8,128)(2,1)} %param.7) | copy-start | bytes 786436
  112.2 8.1 %all-to-all-start.5 = ((f32[4,16,512]{2,1,0:T(8,128)}), f32[4,16,512]{2,1,0:T(8,128)S(1)}, u32[]{:S(2)}, u32[]{:S(2)}) async-start(f32[4,16,512]{2,1,0:T(8,128)} %bitcast.38), calls=%async_computation.5 | async-start | bytes 262144 | tf_op jit(solution)/shard_map/all_to_all | solution.py:44
  120.3 9.0 %collective-permute-start.8 = (f32[16,512]{1,0:T(8,128)S(1)}, f32[16,512]{1,0:T(8,128)S(1)}, u32[]{:S(2)}, u32[]{:S(2)}) collective-permute-start(f32[16,512]{1,0:T(8,128)S(1)} %reduce_sum.38), channel_id=1, source_target_pairs={{0,16},{16,0},{1,17},{17,1},{2,18},{18,2},{3,19},{19,3},{4,20},{20... | collective-permute-start | bytes 98312 | tf_op jit(solution)/shard_map/ppermute | solution.py:40
  138.4 11.0 %all-to-all-start.7 = ((f32[16,16,256]{2,1,0:T(8,128)}), f32[16,16,256]{2,1,0:T(8,128)S(1)}, u32[]{:S(2)}, u32[]{:S(2)}) async-start(f32[16,16,256]{2,1,0:T(8,128)} %bitcast.41), calls=%async_computation.7 | async-start | bytes 524288 | tf_op jit(solution)/shard_map/all_to_all | solution.py:44
  149.4 11.0 %collective-permute-start.9 = (f32[2,16,256]{2,1,0:T(8,128)S(1)}, f32[2,16,256]{2,1,0:T(8,128)S(1)}, u32[]{:S(2)}, u32[]{:S(2)}) collective-permute-start(f32[2,16,256]{2,1,0:T(8,128)S(1)} %dynamic-slice_bitcast_fusion.4), channel_id=1, source_target_pairs={{0,32},{32,0},{1,33},{33,1},{2,34},{34,2},{3,35},{35,3},{4,36},{36... | collective-permute-start | bytes 98312 | tf_op jit(solution)/shard_map/ppermute | solution.py:40
  160.4 13.2 %collective-permute-start.10 = (f32[16,256]{1,0:T(8,128)S(1)}, f32[16,256]{1,0:T(8,128)S(1)}, u32[]{:S(2)}, u32[]{:S(2)}) collective-permute-start(f32[16,256]{1,0:T(8,128)S(1)} %dynamic-slice_bitcast_fusion.5), channel_id=1, source_target_pairs={{0,64},{64,0},{1,65},{65,1},{2,66},{66,2},{3,67},{67,3},{4,68},{68... | collective-permute-start | bytes 49160 | tf_op jit(solution)/shard_map/ppermute | solution.py:40

commit v13 on v12

--- a/solution.py
+++ b/solution.py
@@ -52,6 +52,16 @@
     zy, yx = ("z", "y"), ("y", "x")
     y, z = lax.axis_index("y"), lax.axis_index("z")
 
+    row = lax.broadcasted_iota(jnp.int32, (16, 256), 0)
+    chosen = lax.broadcasted_iota(jnp.int32, (16, 256), 1) == z * 64 + y * 16 + row
+    target = lax.dot_general(
+        chosen.astype(labels.dtype),
+        labels,
+        (((1,), (1,)), ((), ())),
+        preferred_element_type=jnp.float32,
+    )
+    c0, h0 = lax.axis_index("c") == 0, lax.axis_index("h") == 0
+
     part = dot(coeffs[1], diag_inverse[1], 0, 1)
     part = jnp.sum(exchange(part.reshape(4, 64, 128), "x"), 0)
 
@@ -87,7 +97,7 @@
     first = solve(0) + solve(1)
     first = first + swap(first, "c")
     first = first + swap(first, "h")
-    first, far = lax.optimization_barrier((first, far))
+    first, far, target, c0, h0 = lax.optimization_barrier((first, far, target, c0, h0))
 
     solved = jnp.concatenate([first, second], 1).reshape(4, 1, 16, 256)
     solved = jnp.broadcast_to(solved, (4, 4, 16, 256)).reshape(16, 16, 256)
@@ -103,14 +113,6 @@
     pred = jnp.sum(exchange(pred, "z"), 0)
     pred = pred + swap(pred, "w")
 
-    row = lax.broadcasted_iota(jnp.int32, (16, 256), 0)
-    chosen = lax.broadcasted_iota(jnp.int32, (16, 256), 1) == z * 64 + y * 16 + row
-    target = lax.dot_general(
-        chosen.astype(labels.dtype),
-        labels,
-        (((1,), (1,)), ((), ())),
-        preferred_element_type=jnp.float32,
-    )
     weights = jnp.tanh(pred * pred_scale - target)
     weights = exchange(copies(weights, 4), "z").reshape(64, 512)
 
@@ -118,15 +120,10 @@
     term = dot_halves(weights, kernel, (1,), (0,), 0)
     term = term.reshape(64, 4, 256).transpose(1, 0, 2).reshape(16, 16, 256)
     term = jnp.sum(exchange(term, yx).reshape(4, 4, 16, 256), 1)
-    c, h = lax.axis_index("c"), lax.axis_index("h")
-    term = term.reshape(2, 2, 16, 256)
-    keep = lax.dynamic_index_in_dim(term, c, 1, keepdims=False)
-    send = lax.dynamic_index_in_dim(term, 1 - c, 1, keepdims=False)
-    term = keep + swap(send, "c")
-    keep = lax.dynamic_index_in_dim(term, h, 0, keepdims=False)
-    send = lax.dynamic_index_in_dim(term, 1 - h, 0, keepdims=False)
-    term = (keep + swap(send, "h")) * scale
-    return term.reshape(16, 2, 128).transpose(1, 2, 0)
+    term = term.reshape(2, 2, 16, 2, 128).transpose(0, 1, 3, 2, 4)
+    term = jnp.where(c0, term[:, 0], term[:, 1]) + swap(jnp.where(c0, term[:, 1], term[:, 0]), "c")
+    term = jnp.where(h0, term[0], term[1]) + swap(jnp.where(h0, term[1], term[0]), "h")
+    return (term * scale).transpose(0, 2, 1)
 
 
 def solution(mesh):

time: 175 us -> 173 us (0.989)
  blocking collectives: 7.19 us -> 25.3 us
  waiting for transfers between devices: 36.8 us -> 23.8 us
  starting transfers between devices: 116 us -> 109 us
    all_to_all x1 -> x3, blocking collectives: 7.19 us -> 25.3 us  [exchange(): return lax.all_to_all(a, axes, 0, 0, tiled=True)]
    all_to_all x7 -> x5, waiting for transfers between devices: 26 us -> 13.6 us  [exchange(): return lax.all_to_all(a, axes, 0, 0, tiled=True)]
    all_to_all x7 -> x5, starting transfers between devices: 28.8 us -> 21.9 us  [exchange(): return lax.all_to_all(a, axes, 0, 0, tiled=True)]
  transfers between devices with their start and end apart: 18 -> 16, of which waited for: 14 -> 12; matrix products, arithmetic and copies ran while one was open for 3% -> 3% of each run, Pallas kernels for 0% -> 0%
where the time goes in v13:
time: 173 us; the launch traced here: 172 us
  starting transfers between devices  109 us (63%)
  blocking collectives  25.3 us (15%)
  waiting for transfers between devices  23.8 us (14%)
  matrix products  5.7 us (3%)
  local copies, waits for them, and re-layouts  4.4 us (3%)
  other arithmetic  2.47 us (1%)
    ppermute x8, starting transfers between devices, swap(): return lax.ppermute(a, axis, [(0, 1), (1, 0)])  75.7 us
    all_to_all x3, blocking collectives, exchange(): return lax.all_to_all(a, axes, 0, 0, tiled=True)  25.3 us
    all_to_all x5, starting transfers between devices, exchange(): return lax.all_to_all(a, axes, 0, 0, tiled=True)  21.9 us
    all_to_all x5, waiting for transfers between devices, exchange(): return lax.all_to_all(a, axes, 0, 0, tiled=True)  13.6 us
    ppermute x3, starting transfers between devices, local(): lax.ppermute(flat, 'y', [(i, i ^ k) for i in range(4)])  11.9 us
    ppermute x8, waiting for transfers between devices, swap(): return lax.ppermute(a, axis, [(0, 1), (1, 0)])  10.2 us
    dot_general x3, matrix products, dot(): lax.dot_general(a, b, (((ca,), (cb,)), ((), ())), precision=HIGH, preferr...  3.48 us
  transfers between devices with their start and end apart: 16, of which 12 were waited for; matrix products, arithmetic and copies ran while one was open for 3% of the time, Pallas kernels for 0%

profile of v13, /device:TPU:1, one launch (start us, length us, event | category | flops | bytes accessed | tf_op | source)
XLA Modules:
  0.0 171.6 jit_solution(10188169746509327768)
XLA Ops:
  0.0 1.1 slice_bitcast_fusion
  1.3 0.9 fusion.28
  2.2 4.8 %all-to-all-start = ((f32[4,64,128]{2,1,0:T(8,128)}), f32[4,64,128]{2,1,0:T(8,128)S(1)}, u32[]{:S(2)}, u32[]{:S(2)}) async-start(f32[4,64,128]{2,1,0:T(8,128)} %fusion.28), calls=%async_computation | async-start | bytes 262144 | tf_op jit(solution)/shard_map/all_to_all | solution.py:44
  7.5 0.4 copy-done.4
  8.0 1.2 pad_maximum_fusion
  9.2 2.7 %all-to-all-done = f32[4,64,128]{2,1,0:T(8,128)S(1)} async-done(((f32[4,64,128]{2,1,0:T(8,128)}), f32[4,64,128]{2,1,0:T(8,128)S(1)}, u32[]{:S(2)}, u32[]{:S(2)}) %all-to-all-start) | async-done | bytes 131104 | tf_op jit(solution)/shard_map/all_to_all | solution.py:44
  11.9 3.6 %all-to-all-start.1 = ((f32[4,640,128]{2,1,0:T(8,128)}), f32[4,640,128]{2,1,0:T(8,128)S(1)}, u32[]{:S(2)}, u32[]{:S(2)}) async-start(f32[4,640,128]{2,1,0:T(8,128)} %pad_maximum_fusion), calls=%async_computation.1 | async-start | bytes 2621440 | tf_op jit(solution)/shard_map/all_to_all | solution.py:44
  15.5 8.5 %collective-permute-start = (f32[64,128]{1,0:T(8,128)S(1)}, f32[64,128]{1,0:T(8,128)S(1)}, u32[]{:S(2)}, u32[]{:S(2)}) collective-permute-start(f32[64,128]{1,0:T(8,128)S(1)} %reduce_sum.36), channel_id=1, source_target_pairs={{0,32},{32,0},{1,33},{33,1},{2,34},{34,2},{3,35},{35,3},{4,36},{36... | collective-permute-start | bytes 98312 | tf_op jit(solution)/shard_map/ppermute | solution.py:40
  24.0 0.8 collective-permute-done
  24.9 11.1 %collective-permute-start.1 = (f32[64,128]{1,0:T(8,128)S(1)}, f32[64,128]{1,0:T(8,128)S(1)}, u32[]{:S(2)}, u32[]{:S(2)}) collective-permute-start(f32[64,128]{1,0:T(8,128)S(1)} %add.68), channel_id=1, source_target_pairs={{0,64},{64,0},{1,65},{65,1},{2,66},{66,2},{3,67},{67,3},{4,68},{68... | collective-permute-start | bytes 98312 | tf_op jit(solution)/shard_map/ppermute | solution.py:40
  35.9 2.3 %collective-permute-done.1 = f32[64,128]{1,0:T(8,128)S(1)} collective-permute-done((f32[64,128]{1,0:T(8,128)S(1)}, f32[64,128]{1,0:T(8,128)S(1)}, u32[]{:S(2)}, u32[]{:S(2)}) %collective-permute-start.1) | collective-permute-done | bytes 32800 | tf_op jit(solution)/shard_map/ppermute | solution.py:40
  38.2 1.1 convolution_bitcast_fusion
  39.3 4.7 %all-to-all-start.2 = ((f32[16,16,256]{2,1,0:T(8,128)}), f32[16,16,256]{2,1,0:T(8,128)S(1)}, u32[]{:S(2)}, u32[]{:S(2)}) async-start(f32[16,16,256]{2,1,0:T(8,128)} %bitcast.17), calls=%async_computation.2 | async-start | bytes 524288 | tf_op jit(solution)/shard_map/all_to_all | solution.py:44
  44.0 3.4 %collective-permute-start.3 = (f32[256,256]{1,0:T(8,128)S(1)}, f32[256,256]{1,0:T(8,128)S(1)}, u32[]{:S(2)}, u32[]{:S(2)}) collective-permute-start(f32[256,256]{1,0:T(8,128)S(1)} %bitcast.142), channel_id=1, source_target_pairs={{0,1},{1,0},{2,3},{3,2},{4,5},{5,4},{6,7},{7,6},{8,9},{9,8},{10,11... | collective-permute-start | bytes 786440 | tf_op jit(solution)/shard_map/ppermute | solution.py:79
  47.4 3.7 %collective-permute-start.4 = (f32[256,256]{1,0:T(8,128)S(1)}, f32[256,256]{1,0:T(8,128)}, u32[]{:S(2)}, u32[]{:S(2)}) collective-permute-start(f32[256,256]{1,0:T(8,128)S(1)} %bitcast.143), channel_id=1, source_target_pairs={{0,3},{1,2},{2,1},{3,0},{4,7},{5,6},{6,5},{7,4},{8,11},{9,10},{10,... | collective-permute-start | bytes 786440 | tf_op jit(solution)/shard_map/ppermute | solution.py:79
  51.1 1.8 %all-to-all-done.2 = f32[16,16,256]{2,1,0:T(8,128)S(1)} async-done(((f32[16,16,256]{2,1,0:T(8,128)}), f32[16,16,256]{2,1,0:T(8,128)S(1)}, u32[]{:S(2)}, u32[]{:S(2)}) %all-to-all-start.2) | async-done | bytes 262176 | tf_op jit(solution)/shard_map/all_to_all | solution.py:44
  52.9 9.3 %collective-permute-start.2 = (f32[16,256]{1,0:T(8,128)S(1)}, f32[16,256]{1,0:T(8,128)S(1)}, u32[]{:S(2)}, u32[]{:S(2)}) collective-permute-start(f32[16,256]{1,0:T(8,128)S(1)} %reduce_sum.37), channel_id=1, source_target_pairs={{0,16},{16,0},{1,17},{17,1},{2,18},{18,2},{3,19},{19,3},{4,20},{20... | collective-permute-start | bytes 49160 | tf_op jit(solution)/shard_map/ppermute | solution.py:40
  62.3 1.1 collective-permute-done.2
  63.4 0.7 broadcast_in_dim.17
  64.1 4.3 %all-to-all-start.3 = ((f32[16,16,256]{2,1,0:T(8,128)}), f32[16,16,256]{2,1,0:T(8,128)S(1)}, u32[]{:S(2)}, u32[]{:S(2)}) async-start(f32[16,16,256]{2,1,0:T(8,128)} %broadcast_in_dim.17), calls=%async_computation.3 | async-start | bytes 524288 | tf_op jit(solution)/shard_map/all_to_all | solution.py:44
  68.4 4.8 %collective-permute-start.7 = (f32[256,256]{1,0:T(8,128)S(1)}, f32[256,256]{1,0:T(8,128)S(1)}, u32[]{:S(2)}, u32[]{:S(2)}) collective-permute-start(f32[256,256]{1,0:T(8,128)S(1)} %bitcast.144), channel_id=1, source_target_pairs={{0,2},{1,3},{2,0},{3,1},{4,6},{5,7},{6,4},{7,5},{8,10},{9,11},{10,... | collective-permute-start | bytes 786440 | tf_op jit(solution)/shard_map/ppermute | solution.py:79
  73.2 4.2 %all-to-all-done.3 = f32[16,16,256]{2,1,0:T(8,128)S(1)} async-done(((f32[16,16,256]{2,1,0:T(8,128)}), f32[16,16,256]{2,1,0:T(8,128)S(1)}, u32[]{:S(2)}, u32[]{:S(2)}) %all-to-all-start.3) | async-done | bytes 262176 | tf_op jit(solution)/shard_map/all_to_all | solution.py:44
  77.4 0.3 convolution_bitcast_fusion.4
  77.6 0.3 fusion.6
  77.9 5.7 %collective-permute-start.5 = (f32[64,128]{1,0:T(8,128)S(1)}, f32[64,128]{1,0:T(8,128)S(1)}, u32[]{:S(2)}, u32[]{:S(2)}) collective-permute-start(f32[64,128]{1,0:T(8,128)S(1)} %fusion.6), channel_id=1, source_target_pairs={{0,32},{32,0},{1,33},{33,1},{2,34},{34,2},{3,35},{35,3},{4,36},{36... | collective-permute-start | bytes 98312 | tf_op jit(solution)/shard_map/ppermute | solution.py:40
  83.7 0.8 collective-permute-done.5
  84.5 11.7 %collective-permute-start.6 = (f32[64,128]{1,0:T(8,128)S(1)}, f32[64,128]{1,0:T(8,128)S(1)}, u32[]{:S(2)}, u32[]{:S(2)}) collective-permute-start(f32[64,128]{1,0:T(8,128)S(1)} %add.73), channel_id=1, source_target_pairs={{0,64},{64,0},{1,65},{65,1},{2,66},{66,2},{3,67},{67,3},{4,68},{68... | collective-permute-start | bytes 98312 | tf_op jit(solution)/shard_map/ppermute | solution.py:40
  96.2 0.2 fusion.38
  96.3 1.5 collective-permute-done.6
  97.9 0.7 broadcast_in_dim.37
  98.6 4.6 %all-to-all-start.4 = ((f32[16,16,256]{2,1,0:T(8,128)}), f32[16,16,256]{2,1,0:T(8,128)S(1)}, u32[]{:S(2)}, u32[]{:S(2)}) async-start(f32[16,16,256]{2,1,0:T(8,128)} %bitcast.22), calls=%async_computation.4 | async-start | bytes 524288 | tf_op jit(solution)/shard_map/all_to_all | solution.py:44
  103.2 1.0 pad_maximum_fusion.1
  104.3 1.5 fusion
  105.8 5.0 %all-to-all-done.4 = f32[16,16,256]{2,1,0:T(8,128)S(1)} async-done(((f32[16,16,256]{2,1,0:T(8,128)}), f32[16,16,256]{2,1,0:T(8,128)S(1)}, u32[]{:S(2)}, u32[]{:S(2)}) %all-to-all-start.4) | async-done | bytes 262176 | tf_op jit(solution)/shard_map/all_to_all | solution.py:44
  110.8 0.3 convolution_bitcast_fusion.1
  111.1 0.3 fusion.5
  111.4 7.4 %all_to_all.40 = f32[4,16,512]{2,1,0:T(8,128)S(1)} all-to-all(f32[4,16,512]{2,1,0:T(8,128)S(1)} %bitcast.139), channel_id=1, replica_groups=mesh['x'=4,'h'=2,'c'=2,'w'=2,'z'=4,'y'=4] {'z'}, dimensions={0} | all-to-all | bytes 262144 | tf_op jit(solution)/shard_map/all_to_all | solution.py:44
  118.9 7.5 %collective-permute-start.8 = (f32[16,512]{1,0:T(8,128)S(1)}, f32[16,512]{1,0:T(8,128)S(1)}, u32[]{:S(2)}, u32[]{:S(2)}) collective-permute-start(f32[16,512]{1,0:T(8,128)S(1)} %reduce_sum.38), channel_id=1, source_target_pairs={{0,16},{16,0},{1,17},{17,1},{2,18},{18,2},{3,19},{19,3},{4,20},{20... | collective-permute-start | bytes 98312 | tf_op jit(solution)/shard_map/ppermute | solution.py:40
  126.4 1.3 collective-permute-done.8
  127.8 7.6 %all_to_all.41 = f32[4,16,512]{2,1,0:T(8,128)S(1)} all-to-all(f32[4,16,512]{2,1,0:T(8,128)S(1)} %broadcast_in_dim.38), channel_id=1, replica_groups=mesh['x'=4,'h'=2,'c'=2,'w'=2,'z'=4,'y'=4] {'z'}, dimensions={0} | all-to-all | bytes 262144 | tf_op jit(solution)/shard_map/all_to_all | solution.py:44
  135.4 0.5 fusion.24
  135.8 0.4 fusion.3
  136.3 10.3 %all_to_all.42 = f32[16,16,256]{2,1,0:T(8,128)S(1)} all-to-all(f32[16,16,256]{2,1,0:T(8,128)S(1)} %bitcast.133), channel_id=1, replica_groups=mesh['x'=4,'h'=2,'c'=2,'w'=2,'z'=4,'y'=4] {'y','x'}, dimensions={0} | all-to-all | bytes 524288 | tf_op jit(solution)/shard_map/all_to_all | solution.py:44
  146.7 10.2 %collective-permute-start.9 = (f32[2,2,16,128]{3,1,2,0:T(2,128)S(1)}, f32[2,2,16,128]{3,1,2,0:T(2,128)S(1)}, u32[]{:S(2)}, u32[]{:S(2)}) collective-permute-start(f32[2,2,16,128]{3,1,2,0:T(2,128)S(1)} %fusion.31), channel_id=1, source_target_pairs={{0,32},{32,0},{1,33},{33,1},{2,34},{34,2},{3,35},{35,3},{4,36},{36... | collective-permute-start | bytes 98312 | tf_op jit(solution)/shard_map/ppermute | solution.py:40
  156.9 0.8 collective-permute-done.9
  157.8 11.7 %collective-permute-start.10 = (f32[2,16,128]{2,0,1:T(2,128)S(1)}, f32[2,16,128]{2,0,1:T(2,128)S(1)}, u32[]{:S(2)}, u32[]{:S(2)}) collective-permute-start(f32[2,16,128]{2,0,1:T(2,128)S(1)} %select_bitcast_fusion), channel_id=1, source_target_pairs={{0,64},{64,0},{1,65},{65,1},{2,66},{66,2},{3,67},{67,3},{4,68},{68... | collective-permute-start | bytes 49160 | tf_op jit(solution)/shard_map/ppermute | solution.py:40
  169.5 1.5 collective-permute-done.10
  171.0 0.6 copy.24
  (49 shorter events, 1.1 us)
Async XLA Ops:
  0.0 104.3 %copy-start = (f32[512,256]{1,0:T(8,128)S(1)}, f32[512,256]{1,0:T(8,128)}, u32[]{:S(2)}) copy-start(f32[512,256]{1,0:T(8,128)} %param.6) | copy-start | bytes 1572868
  0.0 1.3 copy-start.1
  1.3 6.1 %slice-start = ((f32[2,128,256]{2,1,0:T(8,128)}), f32[1,128,256]{2,1,0:T(8,128)S(1)}, s32[]{:S(2)}) async-start(f32[2,128,256]{2,1,0:T(8,128)} %param.10), calls=%async_computation.8 | async-start | bytes 262144 | tf_op jit(solution)/shard_map/slice | solution.py:68
  2.2 9.7 %all-to-all-start = ((f32[4,64,128]{2,1,0:T(8,128)}), f32[4,64,128]{2,1,0:T(8,128)S(1)}, u32[]{:S(2)}, u32[]{:S(2)}) async-start(f32[4,64,128]{2,1,0:T(8,128)} %fusion.28), calls=%async_computation | async-start | bytes 262144 | tf_op jit(solution)/shard_map/all_to_all | solution.py:44
  7.1 0.9 copy-start.4
  11.9 26.3 %all-to-all-start.1 = ((f32[4,640,128]{2,1,0:T(8,128)}), f32[4,640,128]{2,1,0:T(8,128)S(1)}, u32[]{:S(2)}, u32[]{:S(2)}) async-start(f32[4,640,128]{2,1,0:T(8,128)} %pad_maximum_fusion), calls=%async_computation.1 | async-start | bytes 2621440 | tf_op jit(solution)/shard_map/all_to_all | solution.py:44
  15.5 28.6 %copy-start.3 = (f32[2,128,256]{2,1,0:T(8,128)S(1)}, f32[2,128,256]{2,1,0:T(8,128)}, u32[]{:S(2)}) copy-start(f32[2,128,256]{2,1,0:T(8,128)} %param.8) | copy-start | bytes 786436
  15.5 9.4 %collective-permute-start = (f32[64,128]{1,0:T(8,128)S(1)}, f32[64,128]{1,0:T(8,128)S(1)}, u32[]{:S(2)}, u32[]{:S(2)}) collective-permute-start(f32[64,128]{1,0:T(8,128)S(1)} %reduce_sum.36), channel_id=1, source_target_pairs={{0,32},{32,0},{1,33},{33,1},{2,34},{34,2},{3,35},{35,3},{4,36},{36... | collective-permute-start | bytes 98312 | tf_op jit(solution)/shard_map/ppermute | solution.py:40
  24.9 13.4 %collective-permute-start.1 = (f32[64,128]{1,0:T(8,128)S(1)}, f32[64,128]{1,0:T(8,128)S(1)}, u32[]{:S(2)}, u32[]{:S(2)}) collective-permute-start(f32[64,128]{1,0:T(8,128)S(1)} %add.68), channel_id=1, source_target_pairs={{0,64},{64,0},{1,65},{65,1},{2,66},{66,2},{3,67},{67,3},{4,68},{68... | collective-permute-start | bytes 98312 | tf_op jit(solution)/shard_map/ppermute | solution.py:40
  39.3 13.6 %all-to-all-start.2 = ((f32[16,16,256]{2,1,0:T(8,128)}), f32[16,16,256]{2,1,0:T(8,128)S(1)}, u32[]{:S(2)}, u32[]{:S(2)}) async-start(f32[16,16,256]{2,1,0:T(8,128)} %bitcast.17), calls=%async_computation.2 | async-start | bytes 524288 | tf_op jit(solution)/shard_map/all_to_all | solution.py:44
  44.0 52.2 %copy-start.2 = (bf16[512,256]{1,0:T(8,128)(2,1)S(1)}, bf16[512,256]{1,0:T(8,128)(2,1)}, u32[]{:S(2)}) copy-start(bf16[512,256]{1,0:T(8,128)(2,1)} %param.7) | copy-start | bytes 786436
  44.0 19.3 %collective-permute-start.3 = (f32[256,256]{1,0:T(8,128)S(1)}, f32[256,256]{1,0:T(8,128)S(1)}, u32[]{:S(2)}, u32[]{:S(2)}) collective-permute-start(f32[256,256]{1,0:T(8,128)S(1)} %bitcast.142), channel_id=1, source_target_pairs={{0,1},{1,0},{2,3},{3,2},{4,5},{5,4},{6,7},{7,6},{8,9},{9,8},{10,11... | collective-permute-start | bytes 786440 | tf_op jit(solution)/shard_map/ppermute | solution.py:79
  47.4 15.9 %collective-permute-start.4 = (f32[256,256]{1,0:T(8,128)S(1)}, f32[256,256]{1,0:T(8,128)}, u32[]{:S(2)}, u32[]{:S(2)}) collective-permute-start(f32[256,256]{1,0:T(8,128)S(1)} %bitcast.143), channel_id=1, source_target_pairs={{0,3},{1,2},{2,1},{3,0},{4,7},{5,6},{6,5},{7,4},{8,11},{9,10},{10,... | collective-permute-start | bytes 786440 | tf_op jit(solution)/shard_map/ppermute | solution.py:79
  52.9 10.4 %collective-permute-start.2 = (f32[16,256]{1,0:T(8,128)S(1)}, f32[16,256]{1,0:T(8,128)S(1)}, u32[]{:S(2)}, u32[]{:S(2)}) collective-permute-start(f32[16,256]{1,0:T(8,128)S(1)} %reduce_sum.37), channel_id=1, source_target_pairs={{0,16},{16,0},{1,17},{17,1},{2,18},{18,2},{3,19},{19,3},{4,20},{20... | collective-permute-start | bytes 49160 | tf_op jit(solution)/shard_map/ppermute | solution.py:40
  64.1 13.3 %all-to-all-start.3 = ((f32[16,16,256]{2,1,0:T(8,128)}), f32[16,16,256]{2,1,0:T(8,128)S(1)}, u32[]{:S(2)}, u32[]{:S(2)}) async-start(f32[16,16,256]{2,1,0:T(8,128)} %broadcast_in_dim.17), calls=%async_computation.3 | async-start | bytes 524288 | tf_op jit(solution)/shard_map/all_to_all | solution.py:44
  68.4 29.4 %collective-permute-start.7 = (f32[256,256]{1,0:T(8,128)S(1)}, f32[256,256]{1,0:T(8,128)S(1)}, u32[]{:S(2)}, u32[]{:S(2)}) collective-permute-start(f32[256,256]{1,0:T(8,128)S(1)} %bitcast.144), channel_id=1, source_target_pairs={{0,2},{1,3},{2,0},{3,1},{4,6},{5,7},{6,4},{7,5},{8,10},{9,11},{10,... | collective-permute-start | bytes 786440 | tf_op jit(solution)/shard_map/ppermute | solution.py:79
  77.9 6.6 %collective-permute-start.5 = (f32[64,128]{1,0:T(8,128)S(1)}, f32[64,128]{1,0:T(8,128)S(1)}, u32[]{:S(2)}, u32[]{:S(2)}) collective-permute-start(f32[64,128]{1,0:T(8,128)S(1)} %fusion.6), channel_id=1, source_target_pairs={{0,32},{32,0},{1,33},{33,1},{2,34},{34,2},{3,35},{35,3},{4,36},{36... | collective-permute-start | bytes 98312 | tf_op jit(solution)/shard_map/ppermute | solution.py:40
  84.5 13.4 %collective-permute-start.6 = (f32[64,128]{1,0:T(8,128)S(1)}, f32[64,128]{1,0:T(8,128)S(1)}, u32[]{:S(2)}, u32[]{:S(2)}) collective-permute-start(f32[64,128]{1,0:T(8,128)S(1)} %add.73), channel_id=1, source_target_pairs={{0,64},{64,0},{1,65},{65,1},{2,66},{66,2},{3,67},{67,3},{4,68},{68... | collective-permute-start | bytes 98312 | tf_op jit(solution)/shard_map/ppermute | solution.py:40
  98.6 12.2 %all-to-all-start.4 = ((f32[16,16,256]{2,1,0:T(8,128)}), f32[16,16,256]{2,1,0:T(8,128)S(1)}, u32[]{:S(2)}, u32[]{:S(2)}) async-start(f32[16,16,256]{2,1,0:T(8,128)} %bitcast.22), calls=%async_computation.4 | async-start | bytes 524288 | tf_op jit(solution)/shard_map/all_to_all | solution.py:44
  118.9 8.8 %collective-permute-start.8 = (f32[16,512]{1,0:T(8,128)S(1)}, f32[16,512]{1,0:T(8,128)S(1)}, u32[]{:S(2)}, u32[]{:S(2)}) collective-permute-start(f32[16,512]{1,0:T(8,128)S(1)} %reduce_sum.38), channel_id=1, source_target_pairs={{0,16},{16,0},{1,17},{17,1},{2,18},{18,2},{3,19},{19,3},{4,20},{20... | collective-permute-start | bytes 98312 | tf_op jit(solution)/shard_map/ppermute | solution.py:40
  146.7 11.1 %collective-permute-start.9 = (f32[2,2,16,128]{3,1,2,0:T(2,128)S(1)}, f32[2,2,16,128]{3,1,2,0:T(2,128)S(1)}, u32[]{:S(2)}, u32[]{:S(2)}) collective-permute-start(f32[2,2,16,128]{3,1,2,0:T(2,128)S(1)} %fusion.31), channel_id=1, source_target_pairs={{0,32},{32,0},{1,33},{33,1},{2,34},{34,2},{3,35},{35,3},{4,36},{36... | collective-permute-start | bytes 98312 | tf_op jit(solution)/shard_map/ppermute | solution.py:40
  157.8 13.2 %collective-permute-start.10 = (f32[2,16,128]{2,0,1:T(2,128)S(1)}, f32[2,16,128]{2,0,1:T(2,128)S(1)}, u32[]{:S(2)}, u32[]{:S(2)}) collective-permute-start(f32[2,16,128]{2,0,1:T(2,128)S(1)} %select_bitcast_fusion), channel_id=1, source_target_pairs={{0,64},{64,0},{1,65},{65,1},{2,66},{66,2},{3,67},{67,3},{4,68},{68... | collective-permute-start | bytes 49160 | tf_op jit(solution)/shard_map/ppermute | solution.py:40

commit v14 on v13

--- a/solution.py
+++ b/solution.py
@@ -63,6 +63,7 @@
     c0, h0 = lax.axis_index("c") == 0, lax.axis_index("h") == 0
 
     part = dot(coeffs[1], diag_inverse[1], 0, 1)
+    part, coeffs = lax.optimization_barrier((part, coeffs))
     part = jnp.sum(exchange(part.reshape(4, 64, 128), "x"), 0)
 
     diag = diag_inverse[0].reshape(128, 2, 128).transpose(1, 0, 2).reshape(256, 128)
@@ -96,17 +97,18 @@
 
     first = solve(0) + solve(1)
     first = first + swap(first, "c")
+    first, far = lax.optimization_barrier((first, far))
+    others = jnp.stack([flat, near, far, wrap])
+    centres_y = [lax.dynamic_index_in_dim(others, y ^ k, 0, keepdims=False) for k in range(4)]
+    score = dot(points, jnp.concatenate(centres_y, 0), 1, 1) / math.sqrt(points.shape[1])
+    kernel = halves(score + score * score * score / 3.0)
     first = first + swap(first, "h")
-    first, far, target, c0, h0 = lax.optimization_barrier((first, far, target, c0, h0))
+    first, kernel, target, c0, h0 = lax.optimization_barrier((first, kernel, target, c0, h0))
 
     solved = jnp.concatenate([first, second], 1).reshape(4, 1, 16, 256)
     solved = jnp.broadcast_to(solved, (4, 4, 16, 256)).reshape(16, 16, 256)
     solved = exchange(solved, yx).reshape(4, 64, 256)
 
-    others = jnp.stack([flat, near, far, wrap])
-    centres_y = [lax.dynamic_index_in_dim(others, y ^ k, 0, keepdims=False) for k in range(4)]
-    score = dot(points, jnp.concatenate(centres_y, 0), 1, 1) / math.sqrt(points.shape[1])
-    kernel = lax.optimization_barrier(halves(score + score * score * score / 3.0))
     pred_scale = 1.0 / (2.0 * math.sqrt(256 * 32))
     by_y = [side.reshape(512, 4, 256) for side in kernel]
     pred = dot_halves(solved, by_y, (0, 2), (1, 2), 1).reshape(4, 16, 512)
@@ -118,9 +120,9 @@
 
     scale = 1.0 / (2.0 * math.sqrt(points.shape[0] * 16))
     term = dot_halves(weights, kernel, (1,), (0,), 0)
-    term = term.reshape(64, 4, 256).transpose(1, 0, 2).reshape(16, 16, 256)
-    term = jnp.sum(exchange(term, yx).reshape(4, 4, 16, 256), 1)
-    term = term.reshape(2, 2, 16, 2, 128).transpose(0, 1, 3, 2, 4)
+    term = term.reshape(4, 16, 4, 2, 128).transpose(2, 0, 3, 1, 4).reshape(16, 2, 16, 128)
+    term = jnp.sum(exchange(term, yx).reshape(4, 4, 2, 16, 128), 1)
+    term = term.reshape(2, 2, 2, 16, 128)
     term = jnp.where(c0, term[:, 0], term[:, 1]) + swap(jnp.where(c0, term[:, 1], term[:, 0]), "c")
     term = jnp.where(h0, term[0], term[1]) + swap(jnp.where(h0, term[1], term[0]), "h")
     return (term * scale).transpose(0, 2, 1)

time: 173 us -> 172 us (level)
  blocking collectives: 25.3 us -> 37 us
  waiting for transfers between devices: 23.8 us -> 16.7 us
  starting transfers between devices: 109 us -> 105 us
    all_to_all x3 -> x4, blocking collectives: 25.3 us -> 37 us  [exchange(): return lax.all_to_all(a, axes, 0, 0, tiled=True)]
    all_to_all x5 -> x4, waiting for transfers between devices: 13.6 us -> 7.68 us  [exchange(): return lax.all_to_all(a, axes, 0, 0, tiled=True)]
    all_to_all x5 -> x4, starting transfers between devices: 21.9 us -> 17.5 us  [exchange(): return lax.all_to_all(a, axes, 0, 0, tiled=True)]
  transfers between devices with their start and end apart: 16 -> 15, of which waited for: 12 -> 11; matrix products, arithmetic and copies ran while one was open for 3% -> 3% of each run, Pallas kernels for 0% -> 0%
where the time goes in v14:
time: 172 us; the launch traced here: 171 us
  starting transfers between devices  105 us (61%)
  blocking collectives  37 us (22%)
  waiting for transfers between devices  16.7 us (10%)
  matrix products  6.84 us (4%)
  local copies, waits for them, and re-layouts  3 us (2%)
  other arithmetic  2.06 us (1%)
    ppermute x8, starting transfers between devices, swap(): return lax.ppermute(a, axis, [(0, 1), (1, 0)])  75.6 us
    all_to_all x4, blocking collectives, exchange(): return lax.all_to_all(a, axes, 0, 0, tiled=True)  37 us
    all_to_all x4, starting transfers between devices, exchange(): return lax.all_to_all(a, axes, 0, 0, tiled=True)  17.5 us
    ppermute x3, starting transfers between devices, local(): lax.ppermute(flat, 'y', [(i, i ^ k) for i in range(4)])  11.9 us
    ppermute x8, waiting for transfers between devices, swap(): return lax.ppermute(a, axis, [(0, 1), (1, 0)])  9.01 us
    all_to_all x4, waiting for transfers between devices, exchange(): return lax.all_to_all(a, axes, 0, 0, tiled=True)  7.68 us
    dot_general x3, matrix products, dot(): lax.dot_general(a, b, (((ca,), (cb,)), ((), ())), precision=HIGH, preferr...  4.63 us
  transfers between devices with their start and end apart: 15, of which 11 were waited for; matrix products, arithmetic and copies ran while one was open for 3% of the time, Pallas kernels for 0%

profile of v14, /device:TPU:1, one launch (start us, length us, event | category | flops | bytes accessed | tf_op | source)
XLA Modules:
  0.0 171.0 jit_solution(6691811706939051098)
XLA Ops:
  0.0 2.1 %fusion.19 = f32[256,128]{1,0:T(8,128)} fusion(f32[2,256,256]{2,1,0:T(8,128)} %param.9, f32[2,128,256]{2,1,0:T(8,128)} %param.10), kind=kOutput, calls=%fused_computation.33 | convolution fusion | flops 50331648 | bytes 524288 | tf_op jit(solution)/shard_map/dot_general | solution.py:16
  2.1 5.0 %all-to-all-start = ((f32[4,64,128]{2,1,0:T(8,128)}), f32[4,64,128]{2,1,0:T(8,128)S(1)}, u32[]{:S(2)}, u32[]{:S(2)}) async-start(f32[4,64,128]{2,1,0:T(8,128)} %bitcast.2), calls=%async_computation | async-start | bytes 262144 | tf_op jit(solution)/shard_map/all_to_all | solution.py:44
  7.1 1.0 slice_bitcast_fusion
  8.0 0.1 copy.12
  8.2 0.1 reshape.73
  8.5 0.4 copy-done.3
  9.0 1.2 pad_maximum_fusion
  10.1 1.7 %all-to-all-done = f32[4,64,128]{2,1,0:T(8,128)S(1)} async-done(((f32[4,64,128]{2,1,0:T(8,128)}), f32[4,64,128]{2,1,0:T(8,128)S(1)}, u32[]{:S(2)}, u32[]{:S(2)}) %all-to-all-start) | async-done | bytes 131104 | tf_op jit(solution)/shard_map/all_to_all | solution.py:44
  11.9 3.6 %all-to-all-start.1 = ((f32[4,640,128]{2,1,0:T(8,128)}), f32[4,640,128]{2,1,0:T(8,128)S(1)}, u32[]{:S(2)}, u32[]{:S(2)}) async-start(f32[4,640,128]{2,1,0:T(8,128)} %pad_maximum_fusion), calls=%async_computation.1 | async-start | bytes 2621440 | tf_op jit(solution)/shard_map/all_to_all | solution.py:44
  15.5 8.5 %collective-permute-start = (f32[64,128]{1,0:T(8,128)S(1)}, f32[64,128]{1,0:T(8,128)S(1)}, u32[]{:S(2)}, u32[]{:S(2)}) collective-permute-start(f32[64,128]{1,0:T(8,128)S(1)} %reduce_sum.36), channel_id=1, source_target_pairs={{0,32},{32,0},{1,33},{33,1},{2,34},{34,2},{3,35},{35,3},{4,36},{36... | collective-permute-start | bytes 98312 | tf_op jit(solution)/shard_map/ppermute | solution.py:40
  24.0 0.8 collective-permute-done
  24.8 11.1 %collective-permute-start.1 = (f32[64,128]{1,0:T(8,128)S(1)}, f32[64,128]{1,0:T(8,128)S(1)}, u32[]{:S(2)}, u32[]{:S(2)}) collective-permute-start(f32[64,128]{1,0:T(8,128)S(1)} %add.68), channel_id=1, source_target_pairs={{0,64},{64,0},{1,65},{65,1},{2,66},{66,2},{3,67},{67,3},{4,68},{68... | collective-permute-start | bytes 98312 | tf_op jit(solution)/shard_map/ppermute | solution.py:40
  35.9 2.3 %collective-permute-done.1 = f32[64,128]{1,0:T(8,128)S(1)} collective-permute-done((f32[64,128]{1,0:T(8,128)S(1)}, f32[64,128]{1,0:T(8,128)S(1)}, u32[]{:S(2)}, u32[]{:S(2)}) %collective-permute-start.1) | collective-permute-done | bytes 32800 | tf_op jit(solution)/shard_map/ppermute | solution.py:40
  38.2 1.1 convolution_bitcast_fusion
  39.3 4.7 %all-to-all-start.2 = ((f32[16,16,256]{2,1,0:T(8,128)}), f32[16,16,256]{2,1,0:T(8,128)S(1)}, u32[]{:S(2)}, u32[]{:S(2)}) async-start(f32[16,16,256]{2,1,0:T(8,128)} %bitcast.15), calls=%async_computation.2 | async-start | bytes 524288 | tf_op jit(solution)/shard_map/all_to_all | solution.py:44
  44.0 3.4 %collective-permute-start.3 = (f32[256,256]{1,0:T(8,128)S(1)}, f32[256,256]{1,0:T(8,128)S(1)}, u32[]{:S(2)}, u32[]{:S(2)}) collective-permute-start(f32[256,256]{1,0:T(8,128)S(1)} %bitcast.132), channel_id=1, source_target_pairs={{0,1},{1,0},{2,3},{3,2},{4,5},{5,4},{6,7},{7,6},{8,9},{9,8},{10,11... | collective-permute-start | bytes 786440 | tf_op jit(solution)/shard_map/ppermute | solution.py:80
  47.4 3.7 %collective-permute-start.4 = (f32[256,256]{1,0:T(8,128)S(1)}, f32[256,256]{1,0:T(8,128)S(1)}, u32[]{:S(2)}, u32[]{:S(2)}) collective-permute-start(f32[256,256]{1,0:T(8,128)S(1)} %bitcast.133), channel_id=1, source_target_pairs={{0,3},{1,2},{2,1},{3,0},{4,7},{5,6},{6,5},{7,4},{8,11},{9,10},{10,... | collective-permute-start | bytes 786440 | tf_op jit(solution)/shard_map/ppermute | solution.py:80
  51.1 1.8 %all-to-all-done.2 = f32[16,16,256]{2,1,0:T(8,128)S(1)} async-done(((f32[16,16,256]{2,1,0:T(8,128)}), f32[16,16,256]{2,1,0:T(8,128)S(1)}, u32[]{:S(2)}, u32[]{:S(2)}) %all-to-all-start.2) | async-done | bytes 262176 | tf_op jit(solution)/shard_map/all_to_all | solution.py:44
  52.9 9.3 %collective-permute-start.2 = (f32[16,256]{1,0:T(8,128)S(1)}, f32[16,256]{1,0:T(8,128)S(1)}, u32[]{:S(2)}, u32[]{:S(2)}) collective-permute-start(f32[16,256]{1,0:T(8,128)S(1)} %reduce_sum.37), channel_id=1, source_target_pairs={{0,16},{16,0},{1,17},{17,1},{2,18},{18,2},{3,19},{19,3},{4,20},{20... | collective-permute-start | bytes 49160 | tf_op jit(solution)/shard_map/ppermute | solution.py:40
  62.3 1.1 collective-permute-done.2
  63.4 0.7 broadcast_in_dim.17
  64.1 4.3 %all-to-all-start.3 = ((f32[16,16,256]{2,1,0:T(8,128)}), f32[16,16,256]{2,1,0:T(8,128)S(1)}, u32[]{:S(2)}, u32[]{:S(2)}) async-start(f32[16,16,256]{2,1,0:T(8,128)} %broadcast_in_dim.17), calls=%async_computation.3 | async-start | bytes 524288 | tf_op jit(solution)/shard_map/all_to_all | solution.py:44
  68.4 4.8 %collective-permute-start.6 = (f32[256,256]{1,0:T(8,128)S(1)}, f32[256,256]{1,0:T(8,128)S(1)}, u32[]{:S(2)}, u32[]{:S(2)}) collective-permute-start(f32[256,256]{1,0:T(8,128)S(1)} %bitcast.134), channel_id=1, source_target_pairs={{0,2},{1,3},{2,0},{3,1},{4,6},{5,7},{6,4},{7,5},{8,10},{9,11},{10,... | collective-permute-start | bytes 786440 | tf_op jit(solution)/shard_map/ppermute | solution.py:80
  73.2 4.2 %all-to-all-done.3 = f32[16,16,256]{2,1,0:T(8,128)S(1)} async-done(((f32[16,16,256]{2,1,0:T(8,128)}), f32[16,16,256]{2,1,0:T(8,128)S(1)}, u32[]{:S(2)}, u32[]{:S(2)}) %all-to-all-start.3) | async-done | bytes 262176 | tf_op jit(solution)/shard_map/all_to_all | solution.py:44
  77.4 0.3 convolution_bitcast_fusion.4
  77.6 0.3 fusion.6
  77.9 5.7 %collective-permute-start.5 = (f32[64,128]{1,0:T(8,128)S(1)}, f32[64,128]{1,0:T(8,128)S(1)}, u32[]{:S(2)}, u32[]{:S(2)}) collective-permute-start(f32[64,128]{1,0:T(8,128)S(1)} %fusion.6), channel_id=1, source_target_pairs={{0,32},{32,0},{1,33},{33,1},{2,34},{34,2},{3,35},{35,3},{4,36},{36... | collective-permute-start | bytes 98312 | tf_op jit(solution)/shard_map/ppermute | solution.py:40
  83.6 0.2 fusion.39
  83.8 0.7 collective-permute-done.5
  84.5 11.6 %collective-permute-start.7 = (f32[64,128]{1,0:T(8,128)S(1)}, f32[64,128]{1,0:T(8,128)S(1)}, u32[]{:S(2)}, u32[]{:S(2)}) collective-permute-start(f32[64,128]{1,0:T(8,128)S(1)} %add.73), channel_id=1, source_target_pairs={{0,64},{64,0},{1,65},{65,1},{2,66},{66,2},{3,67},{67,3},{4,68},{68... | collective-permute-start | bytes 98312 | tf_op jit(solution)/shard_map/ppermute | solution.py:40
  96.2 0.1 dynamic-slice_bitcast_fusion.3
  96.3 1.5 fusion
  97.9 12.0 %all_to_all.40 = f32[16,16,256]{2,1,0:T(8,128)S(1)} all-to-all(f32[16,16,256]{2,1,0:T(8,128)S(1)} %bitcast.121), channel_id=1, replica_groups=mesh['x'=4,'h'=2,'c'=2,'w'=2,'z'=4,'y'=4] {'y','x'}, dimensions={0} | all-to-all | bytes 524288 | tf_op jit(solution)/shard_map/all_to_all | solution.py:44
  109.9 0.3 convolution_bitcast_fusion.1
  110.2 0.3 fusion.5
  110.5 7.4 %all_to_all.41 = f32[4,16,512]{2,1,0:T(8,128)S(1)} all-to-all(f32[4,16,512]{2,1,0:T(8,128)S(1)} %bitcast.129), channel_id=1, replica_groups=mesh['x'=4,'h'=2,'c'=2,'w'=2,'z'=4,'y'=4] {'z'}, dimensions={0} | all-to-all | bytes 262144 | tf_op jit(solution)/shard_map/all_to_all | solution.py:44
  118.0 7.9 %collective-permute-start.8 = (f32[16,512]{1,0:T(8,128)S(1)}, f32[16,512]{1,0:T(8,128)S(1)}, u32[]{:S(2)}, u32[]{:S(2)}) collective-permute-start(f32[16,512]{1,0:T(8,128)S(1)} %reduce_sum.38), channel_id=1, source_target_pairs={{0,16},{16,0},{1,17},{17,1},{2,18},{18,2},{3,19},{19,3},{4,20},{20... | collective-permute-start | bytes 98312 | tf_op jit(solution)/shard_map/ppermute | solution.py:40
  125.8 1.3 collective-permute-done.8
  127.2 7.5 %all_to_all.42 = f32[4,16,512]{2,1,0:T(8,128)S(1)} all-to-all(f32[4,16,512]{2,1,0:T(8,128)S(1)} %broadcast_in_dim.38), channel_id=1, replica_groups=mesh['x'=4,'h'=2,'c'=2,'w'=2,'z'=4,'y'=4] {'z'}, dimensions={0} | all-to-all | bytes 262144 | tf_op jit(solution)/shard_map/all_to_all | solution.py:44
  134.7 0.5 fusion.27
  135.2 0.4 fusion.3
  135.6 0.2 reshape.87
  135.9 10.2 %all_to_all.43 = f32[16,2,16,128]{3,2,1,0:T(8,128)S(1)} all-to-all(f32[16,2,16,128]{3,2,1,0:T(8,128)S(1)} %bitcast.123), channel_id=1, replica_groups=mesh['x'=4,'h'=2,'c'=2,'w'=2,'z'=4,'y'=4] {'y','x'}, dimensions={0} | all-to-all | bytes 524288 | tf_op jit(solution)/shard_map/all_to_all | solution.py:44
  146.1 10.2 %collective-permute-start.9 = (f32[2,2,16,128]{3,2,1,0:T(8,128)S(1)}, f32[2,2,16,128]{3,2,1,0:T(8,128)S(1)}, u32[]{:S(2)}, u32[]{:S(2)}) collective-permute-start(f32[2,2,16,128]{3,2,1,0:T(8,128)S(1)} %select_bitcast_fusion), channel_id=1, source_target_pairs={{0,32},{32,0},{1,33},{33,1},{2,34},{34,2},{3,35},{35,3},{4,36},{36... | collective-permute-start | bytes 98312 | tf_op jit(solution)/shard_map/ppermute | solution.py:40
  156.4 0.8 collective-permute-done.9
  157.2 11.2 %collective-permute-start.10 = (f32[2,16,128]{2,1,0:T(8,128)S(1)}, f32[2,16,128]{2,1,0:T(8,128)S(1)}, u32[]{:S(2)}, u32[]{:S(2)}) collective-permute-start(f32[2,16,128]{2,1,0:T(8,128)S(1)} %select_bitcast_fusion.1), channel_id=1, source_target_pairs={{0,64},{64,0},{1,65},{65,1},{2,66},{66,2},{3,67},{67,3},{4,68},{68... | collective-permute-start | bytes 49160 | tf_op jit(solution)/shard_map/ppermute | solution.py:40
  168.4 2.0 %collective-permute-done.10 = f32[2,16,128]{2,1,0:T(8,128)S(1)} collective-permute-done((f32[2,16,128]{2,1,0:T(8,128)S(1)}, f32[2,16,128]{2,1,0:T(8,128)S(1)}, u32[]{:S(2)}, u32[]{:S(2)}) %collective-permute-start.10) | collective-permute-done | bytes 16416 | tf_op jit(solution)/shard_map/ppermute | solution.py:40
  170.4 0.6 fusion.38
  (44 shorter events, 0.7 us)
Async XLA Ops:
  0.0 96.3 %copy-start = (f32[512,256]{1,0:T(8,128)S(1)}, f32[512,256]{1,0:T(8,128)}, u32[]{:S(2)}) copy-start(f32[512,256]{1,0:T(8,128)} %param.6) | copy-start | bytes 1572868
  2.1 6.3 %slice-start = ((f32[2,128,256]{2,1,0:T(8,128)}), f32[1,128,256]{2,1,0:T(8,128)S(1)}, s32[]{:S(2)}) async-start(f32[2,128,256]{2,1,0:T(8,128)} %param.10), calls=%async_computation.8 | async-start | bytes 262144 | tf_op jit(solution)/shard_map/slice | solution.py:69
  2.1 9.8 %all-to-all-start = ((f32[4,64,128]{2,1,0:T(8,128)}), f32[4,64,128]{2,1,0:T(8,128)S(1)}, u32[]{:S(2)}, u32[]{:S(2)}) async-start(f32[4,64,128]{2,1,0:T(8,128)} %bitcast.2), calls=%async_computation | async-start | bytes 262144 | tf_op jit(solution)/shard_map/all_to_all | solution.py:44
  8.0 0.9 copy-start.3
  11.9 26.3 %all-to-all-start.1 = ((f32[4,640,128]{2,1,0:T(8,128)}), f32[4,640,128]{2,1,0:T(8,128)S(1)}, u32[]{:S(2)}, u32[]{:S(2)}) async-start(f32[4,640,128]{2,1,0:T(8,128)} %pad_maximum_fusion), calls=%async_computation.1 | async-start | bytes 2621440 | tf_op jit(solution)/shard_map/all_to_all | solution.py:44
  15.5 28.6 %copy-start.2 = (f32[2,128,256]{2,1,0:T(8,128)S(1)}, f32[2,128,256]{2,1,0:T(8,128)}, u32[]{:S(2)}) copy-start(f32[2,128,256]{2,1,0:T(8,128)} %param.8) | copy-start | bytes 786436
  15.5 9.4 %collective-permute-start = (f32[64,128]{1,0:T(8,128)S(1)}, f32[64,128]{1,0:T(8,128)S(1)}, u32[]{:S(2)}, u32[]{:S(2)}) collective-permute-start(f32[64,128]{1,0:T(8,128)S(1)} %reduce_sum.36), channel_id=1, source_target_pairs={{0,32},{32,0},{1,33},{33,1},{2,34},{34,2},{3,35},{35,3},{4,36},{36... | collective-permute-start | bytes 98312 | tf_op jit(solution)/shard_map/ppermute | solution.py:40
  24.8 13.4 %collective-permute-start.1 = (f32[64,128]{1,0:T(8,128)S(1)}, f32[64,128]{1,0:T(8,128)S(1)}, u32[]{:S(2)}, u32[]{:S(2)}) collective-permute-start(f32[64,128]{1,0:T(8,128)S(1)} %add.68), channel_id=1, source_target_pairs={{0,64},{64,0},{1,65},{65,1},{2,66},{66,2},{3,67},{67,3},{4,68},{68... | collective-permute-start | bytes 98312 | tf_op jit(solution)/shard_map/ppermute | solution.py:40
  39.3 13.6 %all-to-all-start.2 = ((f32[16,16,256]{2,1,0:T(8,128)}), f32[16,16,256]{2,1,0:T(8,128)S(1)}, u32[]{:S(2)}, u32[]{:S(2)}) async-start(f32[16,16,256]{2,1,0:T(8,128)} %bitcast.15), calls=%async_computation.2 | async-start | bytes 524288 | tf_op jit(solution)/shard_map/all_to_all | solution.py:44
  44.0 39.7 %copy-start.1 = (bf16[512,256]{1,0:T(8,128)(2,1)S(1)}, bf16[512,256]{1,0:T(8,128)(2,1)}, u32[]{:S(2)}) copy-start(bf16[512,256]{1,0:T(8,128)(2,1)} %param.7) | copy-start | bytes 786436
  44.0 19.3 %collective-permute-start.3 = (f32[256,256]{1,0:T(8,128)S(1)}, f32[256,256]{1,0:T(8,128)S(1)}, u32[]{:S(2)}, u32[]{:S(2)}) collective-permute-start(f32[256,256]{1,0:T(8,128)S(1)} %bitcast.132), channel_id=1, source_target_pairs={{0,1},{1,0},{2,3},{3,2},{4,5},{5,4},{6,7},{7,6},{8,9},{9,8},{10,11... | collective-permute-start | bytes 786440 | tf_op jit(solution)/shard_map/ppermute | solution.py:80
  47.4 15.9 %collective-permute-start.4 = (f32[256,256]{1,0:T(8,128)S(1)}, f32[256,256]{1,0:T(8,128)S(1)}, u32[]{:S(2)}, u32[]{:S(2)}) collective-permute-start(f32[256,256]{1,0:T(8,128)S(1)} %bitcast.133), channel_id=1, source_target_pairs={{0,3},{1,2},{2,1},{3,0},{4,7},{5,6},{6,5},{7,4},{8,11},{9,10},{10,... | collective-permute-start | bytes 786440 | tf_op jit(solution)/shard_map/ppermute | solution.py:80
  52.9 10.4 %collective-permute-start.2 = (f32[16,256]{1,0:T(8,128)S(1)}, f32[16,256]{1,0:T(8,128)S(1)}, u32[]{:S(2)}, u32[]{:S(2)}) collective-permute-start(f32[16,256]{1,0:T(8,128)S(1)} %reduce_sum.37), channel_id=1, source_target_pairs={{0,16},{16,0},{1,17},{17,1},{2,18},{18,2},{3,19},{19,3},{4,20},{20... | collective-permute-start | bytes 49160 | tf_op jit(solution)/shard_map/ppermute | solution.py:40
  64.1 13.3 %all-to-all-start.3 = ((f32[16,16,256]{2,1,0:T(8,128)}), f32[16,16,256]{2,1,0:T(8,128)S(1)}, u32[]{:S(2)}, u32[]{:S(2)}) async-start(f32[16,16,256]{2,1,0:T(8,128)} %broadcast_in_dim.17), calls=%async_computation.3 | async-start | bytes 524288 | tf_op jit(solution)/shard_map/all_to_all | solution.py:44
  68.4 16.1 %collective-permute-start.6 = (f32[256,256]{1,0:T(8,128)S(1)}, f32[256,256]{1,0:T(8,128)S(1)}, u32[]{:S(2)}, u32[]{:S(2)}) collective-permute-start(f32[256,256]{1,0:T(8,128)S(1)} %bitcast.134), channel_id=1, source_target_pairs={{0,2},{1,3},{2,0},{3,1},{4,6},{5,7},{6,4},{7,5},{8,10},{9,11},{10,... | collective-permute-start | bytes 786440 | tf_op jit(solution)/shard_map/ppermute | solution.py:80
  77.9 6.6 %collective-permute-start.5 = (f32[64,128]{1,0:T(8,128)S(1)}, f32[64,128]{1,0:T(8,128)S(1)}, u32[]{:S(2)}, u32[]{:S(2)}) collective-permute-start(f32[64,128]{1,0:T(8,128)S(1)} %fusion.6), channel_id=1, source_target_pairs={{0,32},{32,0},{1,33},{33,1},{2,34},{34,2},{3,35},{35,3},{4,36},{36... | collective-permute-start | bytes 98312 | tf_op jit(solution)/shard_map/ppermute | solution.py:40
  84.5 13.4 %collective-permute-start.7 = (f32[64,128]{1,0:T(8,128)S(1)}, f32[64,128]{1,0:T(8,128)S(1)}, u32[]{:S(2)}, u32[]{:S(2)}) collective-permute-start(f32[64,128]{1,0:T(8,128)S(1)} %add.73), channel_id=1, source_target_pairs={{0,64},{64,0},{1,65},{65,1},{2,66},{66,2},{3,67},{67,3},{4,68},{68... | collective-permute-start | bytes 98312 | tf_op jit(solution)/shard_map/ppermute | solution.py:40
  118.0 9.2 %collective-permute-start.8 = (f32[16,512]{1,0:T(8,128)S(1)}, f32[16,512]{1,0:T(8,128)S(1)}, u32[]{:S(2)}, u32[]{:S(2)}) collective-permute-start(f32[16,512]{1,0:T(8,128)S(1)} %reduce_sum.38), channel_id=1, source_target_pairs={{0,16},{16,0},{1,17},{17,1},{2,18},{18,2},{3,19},{19,3},{4,20},{20... | collective-permute-start | bytes 98312 | tf_op jit(solution)/shard_map/ppermute | solution.py:40
  146.1 11.1 %collective-permute-start.9 = (f32[2,2,16,128]{3,2,1,0:T(8,128)S(1)}, f32[2,2,16,128]{3,2,1,0:T(8,128)S(1)}, u32[]{:S(2)}, u32[]{:S(2)}) collective-permute-start(f32[2,2,16,128]{3,2,1,0:T(8,128)S(1)} %select_bitcast_fusion), channel_id=1, source_target_pairs={{0,32},{32,0},{1,33},{33,1},{2,34},{34,2},{3,35},{35,3},{4,36},{36... | collective-permute-start | bytes 98312 | tf_op jit(solution)/shard_map/ppermute | solution.py:40
  157.2 13.2 %collective-permute-start.10 = (f32[2,16,128]{2,1,0:T(8,128)S(1)}, f32[2,16,128]{2,1,0:T(8,128)S(1)}, u32[]{:S(2)}, u32[]{:S(2)}) collective-permute-start(f32[2,16,128]{2,1,0:T(8,128)S(1)} %select_bitcast_fusion.1), channel_id=1, source_target_pairs={{0,64},{64,0},{1,65},{65,1},{2,66},{66,2},{3,67},{67,3},{4,68},{68... | collective-permute-start | bytes 49160 | tf_op jit(solution)/shard_map/ppermute | solution.py:40

commit v15 on v14

--- a/solution.py
+++ b/solution.py
@@ -62,8 +62,9 @@
     )
     c0, h0 = lax.axis_index("c") == 0, lax.axis_index("h") == 0
 
-    part = dot(coeffs[1], diag_inverse[1], 0, 1)
+    part = dot(diag_inverse[1], coeffs[1], 1, 0)
     part, coeffs = lax.optimization_barrier((part, coeffs))
+    part = part.T
     part = jnp.sum(exchange(part.reshape(4, 64, 128), "x"), 0)
 
     diag = diag_inverse[0].reshape(128, 2, 128).transpose(1, 0, 2).reshape(256, 128)

time: 172 us -> 172 us (level)
  transfers between devices with their start and end apart: 15 -> 15, of which waited for: 11 -> 11; matrix products, arithmetic and copies ran while one was open for 3% -> 2% of each run, Pallas kernels for 0% -> 0%
where the time goes in v15:
time: 172 us; the launch traced here: 171 us
  starting transfers between devices  105 us (61%)
  blocking collectives  37 us (22%)
  waiting for transfers between devices  17.6 us (10%)
  matrix products  6.12 us (4%)
  local copies, waits for them, and re-layouts  2.83 us (2%)
  other arithmetic  2.07 us (1%)
    ppermute x8, starting transfers between devices, swap(): return lax.ppermute(a, axis, [(0, 1), (1, 0)])  75.6 us
    all_to_all x4, blocking collectives, exchange(): return lax.all_to_all(a, axes, 0, 0, tiled=True)  37 us
    all_to_all x4, starting transfers between devices, exchange(): return lax.all_to_all(a, axes, 0, 0, tiled=True)  17.5 us
    ppermute x3, starting transfers between devices, local(): lax.ppermute(flat, 'y', [(i, i ^ k) for i in range(4)])  11.9 us
    ppermute x8, waiting for transfers between devices, swap(): return lax.ppermute(a, axis, [(0, 1), (1, 0)])  9 us
    all_to_all x4, waiting for transfers between devices, exchange(): return lax.all_to_all(a, axes, 0, 0, tiled=True)  8.61 us
    dot_general x3, matrix products, dot(): lax.dot_general(a, b, (((ca,), (cb,)), ((), ())), precision=HIGH, preferr...  3.91 us
  transfers between devices with their start and end apart: 15, of which 11 were waited for; matrix products, arithmetic and copies ran while one was open for 2% of the time, Pallas kernels for 0%

profile of v15, /device:TPU:1, one launch (start us, length us, event | category | flops | bytes accessed | tf_op | source)
XLA Modules:
  0.0 171.1 jit_solution(6947018209575948034)
XLA Ops:
  0.0 1.3 fusion.19
  1.3 0.8 copy.11
  2.1 5.0 %all-to-all-start = ((f32[4,64,128]{2,1,0:T(8,128)}), f32[4,64,128]{2,1,0:T(8,128)S(1)}, u32[]{:S(2)}, u32[]{:S(2)}) async-start(f32[4,64,128]{2,1,0:T(8,128)} %bitcast.3), calls=%async_computation | async-start | bytes 262144 | tf_op jit(solution)/shard_map/all_to_all | solution.py:44
  7.1 0.1 copy.13
  7.2 0.1 reshape.73
  7.6 0.4 copy-done.4
  8.0 1.2 pad_maximum_fusion
  9.2 2.7 %all-to-all-done = f32[4,64,128]{2,1,0:T(8,128)S(1)} async-done(((f32[4,64,128]{2,1,0:T(8,128)}), f32[4,64,128]{2,1,0:T(8,128)S(1)}, u32[]{:S(2)}, u32[]{:S(2)}) %all-to-all-start) | async-done | bytes 131104 | tf_op jit(solution)/shard_map/all_to_all | solution.py:44
  11.9 3.6 %all-to-all-start.1 = ((f32[4,640,128]{2,1,0:T(8,128)}), f32[4,640,128]{2,1,0:T(8,128)S(1)}, u32[]{:S(2)}, u32[]{:S(2)}) async-start(f32[4,640,128]{2,1,0:T(8,128)} %pad_maximum_fusion), calls=%async_computation.1 | async-start | bytes 2621440 | tf_op jit(solution)/shard_map/all_to_all | solution.py:44
  15.5 8.5 %collective-permute-start = (f32[64,128]{1,0:T(8,128)S(1)}, f32[64,128]{1,0:T(8,128)S(1)}, u32[]{:S(2)}, u32[]{:S(2)}) collective-permute-start(f32[64,128]{1,0:T(8,128)S(1)} %reduce_sum.36), channel_id=1, source_target_pairs={{0,32},{32,0},{1,33},{33,1},{2,34},{34,2},{3,35},{35,3},{4,36},{36... | collective-permute-start | bytes 98312 | tf_op jit(solution)/shard_map/ppermute | solution.py:40
  24.0 0.8 collective-permute-done
  24.9 11.1 %collective-permute-start.1 = (f32[64,128]{1,0:T(8,128)S(1)}, f32[64,128]{1,0:T(8,128)S(1)}, u32[]{:S(2)}, u32[]{:S(2)}) collective-permute-start(f32[64,128]{1,0:T(8,128)S(1)} %add.68), channel_id=1, source_target_pairs={{0,64},{64,0},{1,65},{65,1},{2,66},{66,2},{3,67},{67,3},{4,68},{68... | collective-permute-start | bytes 98312 | tf_op jit(solution)/shard_map/ppermute | solution.py:40
  35.9 2.3 %collective-permute-done.1 = f32[64,128]{1,0:T(8,128)S(1)} collective-permute-done((f32[64,128]{1,0:T(8,128)S(1)}, f32[64,128]{1,0:T(8,128)S(1)}, u32[]{:S(2)}, u32[]{:S(2)}) %collective-permute-start.1) | collective-permute-done | bytes 32800 | tf_op jit(solution)/shard_map/ppermute | solution.py:40
  38.2 1.1 convolution_bitcast_fusion
  39.3 4.6 %all-to-all-start.2 = ((f32[16,16,256]{2,1,0:T(8,128)}), f32[16,16,256]{2,1,0:T(8,128)S(1)}, u32[]{:S(2)}, u32[]{:S(2)}) async-start(f32[16,16,256]{2,1,0:T(8,128)} %bitcast.16), calls=%async_computation.2 | async-start | bytes 524288 | tf_op jit(solution)/shard_map/all_to_all | solution.py:44
  44.1 3.4 %collective-permute-start.3 = (f32[256,256]{1,0:T(8,128)S(1)}, f32[256,256]{1,0:T(8,128)S(1)}, u32[]{:S(2)}, u32[]{:S(2)}) collective-permute-start(f32[256,256]{1,0:T(8,128)S(1)} %bitcast.134), channel_id=1, source_target_pairs={{0,1},{1,0},{2,3},{3,2},{4,5},{5,4},{6,7},{7,6},{8,9},{9,8},{10,11... | collective-permute-start | bytes 786440 | tf_op jit(solution)/shard_map/ppermute | solution.py:81
  47.5 3.7 %collective-permute-start.4 = (f32[256,256]{1,0:T(8,128)S(1)}, f32[256,256]{1,0:T(8,128)S(1)}, u32[]{:S(2)}, u32[]{:S(2)}) collective-permute-start(f32[256,256]{1,0:T(8,128)S(1)} %bitcast.135), channel_id=1, source_target_pairs={{0,3},{1,2},{2,1},{3,0},{4,7},{5,6},{6,5},{7,4},{8,11},{9,10},{10,... | collective-permute-start | bytes 786440 | tf_op jit(solution)/shard_map/ppermute | solution.py:81
  51.2 1.8 %all-to-all-done.2 = f32[16,16,256]{2,1,0:T(8,128)S(1)} async-done(((f32[16,16,256]{2,1,0:T(8,128)}), f32[16,16,256]{2,1,0:T(8,128)S(1)}, u32[]{:S(2)}, u32[]{:S(2)}) %all-to-all-start.2) | async-done | bytes 262176 | tf_op jit(solution)/shard_map/all_to_all | solution.py:44
  52.9 9.3 %collective-permute-start.2 = (f32[16,256]{1,0:T(8,128)S(1)}, f32[16,256]{1,0:T(8,128)S(1)}, u32[]{:S(2)}, u32[]{:S(2)}) collective-permute-start(f32[16,256]{1,0:T(8,128)S(1)} %reduce_sum.37), channel_id=1, source_target_pairs={{0,16},{16,0},{1,17},{17,1},{2,18},{18,2},{3,19},{19,3},{4,20},{20... | collective-permute-start | bytes 49160 | tf_op jit(solution)/shard_map/ppermute | solution.py:40
  62.3 1.1 collective-permute-done.2
  63.4 0.7 broadcast_in_dim.17
  64.1 4.3 %all-to-all-start.3 = ((f32[16,16,256]{2,1,0:T(8,128)}), f32[16,16,256]{2,1,0:T(8,128)S(1)}, u32[]{:S(2)}, u32[]{:S(2)}) async-start(f32[16,16,256]{2,1,0:T(8,128)} %broadcast_in_dim.17), calls=%async_computation.3 | async-start | bytes 524288 | tf_op jit(solution)/shard_map/all_to_all | solution.py:44
  68.5 4.8 %collective-permute-start.6 = (f32[256,256]{1,0:T(8,128)S(1)}, f32[256,256]{1,0:T(8,128)S(1)}, u32[]{:S(2)}, u32[]{:S(2)}) collective-permute-start(f32[256,256]{1,0:T(8,128)S(1)} %bitcast.136), channel_id=1, source_target_pairs={{0,2},{1,3},{2,0},{3,1},{4,6},{5,7},{6,4},{7,5},{8,10},{9,11},{10,... | collective-permute-start | bytes 786440 | tf_op jit(solution)/shard_map/ppermute | solution.py:81
  73.2 4.2 %all-to-all-done.3 = f32[16,16,256]{2,1,0:T(8,128)S(1)} async-done(((f32[16,16,256]{2,1,0:T(8,128)}), f32[16,16,256]{2,1,0:T(8,128)S(1)}, u32[]{:S(2)}, u32[]{:S(2)}) %all-to-all-start.3) | async-done | bytes 262176 | tf_op jit(solution)/shard_map/all_to_all | solution.py:44
  77.4 0.3 convolution_bitcast_fusion.4
  77.7 0.3 fusion.6
  77.9 5.7 %collective-permute-start.5 = (f32[64,128]{1,0:T(8,128)S(1)}, f32[64,128]{1,0:T(8,128)S(1)}, u32[]{:S(2)}, u32[]{:S(2)}) collective-permute-start(f32[64,128]{1,0:T(8,128)S(1)} %fusion.6), channel_id=1, source_target_pairs={{0,32},{32,0},{1,33},{33,1},{2,34},{34,2},{3,35},{35,3},{4,36},{36... | collective-permute-start | bytes 98312 | tf_op jit(solution)/shard_map/ppermute | solution.py:40
  83.7 0.2 fusion.39
  83.9 0.7 collective-permute-done.5
  84.5 11.7 %collective-permute-start.7 = (f32[64,128]{1,0:T(8,128)S(1)}, f32[64,128]{1,0:T(8,128)S(1)}, u32[]{:S(2)}, u32[]{:S(2)}) collective-permute-start(f32[64,128]{1,0:T(8,128)S(1)} %add.73), channel_id=1, source_target_pairs={{0,64},{64,0},{1,65},{65,1},{2,66},{66,2},{3,67},{67,3},{4,68},{68... | collective-permute-start | bytes 98312 | tf_op jit(solution)/shard_map/ppermute | solution.py:40
  96.3 0.1 dynamic-slice_bitcast_fusion.3
  96.4 1.5 fusion
  98.0 12.0 %all_to_all.40 = f32[16,16,256]{2,1,0:T(8,128)S(1)} all-to-all(f32[16,16,256]{2,1,0:T(8,128)S(1)} %bitcast.122), channel_id=1, replica_groups=mesh['x'=4,'h'=2,'c'=2,'w'=2,'z'=4,'y'=4] {'y','x'}, dimensions={0} | all-to-all | bytes 524288 | tf_op jit(solution)/shard_map/all_to_all | solution.py:44
  110.0 0.3 convolution_bitcast_fusion.1
  110.3 0.3 fusion.5
  110.6 7.4 %all_to_all.41 = f32[4,16,512]{2,1,0:T(8,128)S(1)} all-to-all(f32[4,16,512]{2,1,0:T(8,128)S(1)} %bitcast.131), channel_id=1, replica_groups=mesh['x'=4,'h'=2,'c'=2,'w'=2,'z'=4,'y'=4] {'z'}, dimensions={0} | all-to-all | bytes 262144 | tf_op jit(solution)/shard_map/all_to_all | solution.py:44
  118.0 7.9 %collective-permute-start.8 = (f32[16,512]{1,0:T(8,128)S(1)}, f32[16,512]{1,0:T(8,128)S(1)}, u32[]{:S(2)}, u32[]{:S(2)}) collective-permute-start(f32[16,512]{1,0:T(8,128)S(1)} %reduce_sum.38), channel_id=1, source_target_pairs={{0,16},{16,0},{1,17},{17,1},{2,18},{18,2},{3,19},{19,3},{4,20},{20... | collective-permute-start | bytes 98312 | tf_op jit(solution)/shard_map/ppermute | solution.py:40
  125.9 1.3 collective-permute-done.8
  127.2 7.5 %all_to_all.42 = f32[4,16,512]{2,1,0:T(8,128)S(1)} all-to-all(f32[4,16,512]{2,1,0:T(8,128)S(1)} %broadcast_in_dim.38), channel_id=1, replica_groups=mesh['x'=4,'h'=2,'c'=2,'w'=2,'z'=4,'y'=4] {'z'}, dimensions={0} | all-to-all | bytes 262144 | tf_op jit(solution)/shard_map/all_to_all | solution.py:44
  134.8 0.5 fusion.27
  135.2 0.4 fusion.3
  135.7 0.2 reshape.87
  136.0 10.2 %all_to_all.43 = f32[16,2,16,128]{3,2,1,0:T(8,128)S(1)} all-to-all(f32[16,2,16,128]{3,2,1,0:T(8,128)S(1)} %bitcast.124), channel_id=1, replica_groups=mesh['x'=4,'h'=2,'c'=2,'w'=2,'z'=4,'y'=4] {'y','x'}, dimensions={0} | all-to-all | bytes 524288 | tf_op jit(solution)/shard_map/all_to_all | solution.py:44
  146.2 10.2 %collective-permute-start.9 = (f32[2,2,16,128]{3,2,1,0:T(8,128)S(1)}, f32[2,2,16,128]{3,2,1,0:T(8,128)S(1)}, u32[]{:S(2)}, u32[]{:S(2)}) collective-permute-start(f32[2,2,16,128]{3,2,1,0:T(8,128)S(1)} %select_bitcast_fusion), channel_id=1, source_target_pairs={{0,32},{32,0},{1,33},{33,1},{2,34},{34,2},{3,35},{35,3},{4,36},{36... | collective-permute-start | bytes 98312 | tf_op jit(solution)/shard_map/ppermute | solution.py:40
  156.4 0.8 collective-permute-done.9
  157.3 11.2 %collective-permute-start.10 = (f32[2,16,128]{2,1,0:T(8,128)S(1)}, f32[2,16,128]{2,1,0:T(8,128)S(1)}, u32[]{:S(2)}, u32[]{:S(2)}) collective-permute-start(f32[2,16,128]{2,1,0:T(8,128)S(1)} %select_bitcast_fusion.1), channel_id=1, source_target_pairs={{0,64},{64,0},{1,65},{65,1},{2,66},{66,2},{3,67},{67,3},{4,68},{68... | collective-permute-start | bytes 49160 | tf_op jit(solution)/shard_map/ppermute | solution.py:40
  168.5 2.0 %collective-permute-done.10 = f32[2,16,128]{2,1,0:T(8,128)S(1)} collective-permute-done((f32[2,16,128]{2,1,0:T(8,128)S(1)}, f32[2,16,128]{2,1,0:T(8,128)S(1)}, u32[]{:S(2)}, u32[]{:S(2)}) %collective-permute-start.10) | collective-permute-done | bytes 16416 | tf_op jit(solution)/shard_map/ppermute | solution.py:40
  170.5 0.6 fusion.38
  (47 shorter events, 0.7 us)
Async XLA Ops:
  0.0 96.4 %copy-start = (f32[512,256]{1,0:T(8,128)S(1)}, f32[512,256]{1,0:T(8,128)}, u32[]{:S(2)}) copy-start(f32[512,256]{1,0:T(8,128)} %param.6) | copy-start | bytes 1572868
  0.0 7.1 %copy-start.1 = (f32[2,256,256]{2,1,0:T(8,128)S(1)}, f32[2,256,256]{2,1,0:T(8,128)}, u32[]{:S(2)}) copy-start(f32[2,256,256]{2,1,0:T(8,128)} %param.9) | copy-start | bytes 1572868
  2.1 5.3 %slice-start = ((f32[2,128,256]{2,1,0:T(8,128)}), f32[1,128,256]{2,1,0:T(8,128)S(1)}, s32[]{:S(2)}) async-start(f32[2,128,256]{2,1,0:T(8,128)} %param.10), calls=%async_computation.8 | async-start | bytes 262144 | tf_op jit(solution)/shard_map/slice | solution.py:70
  2.1 9.8 %all-to-all-start = ((f32[4,64,128]{2,1,0:T(8,128)}), f32[4,64,128]{2,1,0:T(8,128)S(1)}, u32[]{:S(2)}, u32[]{:S(2)}) async-start(f32[4,64,128]{2,1,0:T(8,128)} %bitcast.3), calls=%async_computation | async-start | bytes 262144 | tf_op jit(solution)/shard_map/all_to_all | solution.py:44
  7.1 0.9 copy-start.4
  11.9 26.3 %all-to-all-start.1 = ((f32[4,640,128]{2,1,0:T(8,128)}), f32[4,640,128]{2,1,0:T(8,128)S(1)}, u32[]{:S(2)}, u32[]{:S(2)}) async-start(f32[4,640,128]{2,1,0:T(8,128)} %pad_maximum_fusion), calls=%async_computation.1 | async-start | bytes 2621440 | tf_op jit(solution)/shard_map/all_to_all | solution.py:44
  15.5 28.6 %copy-start.3 = (f32[2,128,256]{2,1,0:T(8,128)S(1)}, f32[2,128,256]{2,1,0:T(8,128)}, u32[]{:S(2)}) copy-start(f32[2,128,256]{2,1,0:T(8,128)} %param.8) | copy-start | bytes 786436
  15.5 9.4 %collective-permute-start = (f32[64,128]{1,0:T(8,128)S(1)}, f32[64,128]{1,0:T(8,128)S(1)}, u32[]{:S(2)}, u32[]{:S(2)}) collective-permute-start(f32[64,128]{1,0:T(8,128)S(1)} %reduce_sum.36), channel_id=1, source_target_pairs={{0,32},{32,0},{1,33},{33,1},{2,34},{34,2},{3,35},{35,3},{4,36},{36... | collective-permute-start | bytes 98312 | tf_op jit(solution)/shard_map/ppermute | solution.py:40
  24.9 13.4 %collective-permute-start.1 = (f32[64,128]{1,0:T(8,128)S(1)}, f32[64,128]{1,0:T(8,128)S(1)}, u32[]{:S(2)}, u32[]{:S(2)}) collective-permute-start(f32[64,128]{1,0:T(8,128)S(1)} %add.68), channel_id=1, source_target_pairs={{0,64},{64,0},{1,65},{65,1},{2,66},{66,2},{3,67},{67,3},{4,68},{68... | collective-permute-start | bytes 98312 | tf_op jit(solution)/shard_map/ppermute | solution.py:40
  39.3 13.6 %all-to-all-start.2 = ((f32[16,16,256]{2,1,0:T(8,128)}), f32[16,16,256]{2,1,0:T(8,128)S(1)}, u32[]{:S(2)}, u32[]{:S(2)}) async-start(f32[16,16,256]{2,1,0:T(8,128)} %bitcast.16), calls=%async_computation.2 | async-start | bytes 524288 | tf_op jit(solution)/shard_map/all_to_all | solution.py:44
  44.0 39.7 %copy-start.2 = (bf16[512,256]{1,0:T(8,128)(2,1)S(1)}, bf16[512,256]{1,0:T(8,128)(2,1)}, u32[]{:S(2)}) copy-start(bf16[512,256]{1,0:T(8,128)(2,1)} %param.7) | copy-start | bytes 786436
  44.1 19.3 %collective-permute-start.3 = (f32[256,256]{1,0:T(8,128)S(1)}, f32[256,256]{1,0:T(8,128)S(1)}, u32[]{:S(2)}, u32[]{:S(2)}) collective-permute-start(f32[256,256]{1,0:T(8,128)S(1)} %bitcast.134), channel_id=1, source_target_pairs={{0,1},{1,0},{2,3},{3,2},{4,5},{5,4},{6,7},{7,6},{8,9},{9,8},{10,11... | collective-permute-start | bytes 786440 | tf_op jit(solution)/shard_map/ppermute | solution.py:81
  47.5 15.9 %collective-permute-start.4 = (f32[256,256]{1,0:T(8,128)S(1)}, f32[256,256]{1,0:T(8,128)S(1)}, u32[]{:S(2)}, u32[]{:S(2)}) collective-permute-start(f32[256,256]{1,0:T(8,128)S(1)} %bitcast.135), channel_id=1, source_target_pairs={{0,3},{1,2},{2,1},{3,0},{4,7},{5,6},{6,5},{7,4},{8,11},{9,10},{10,... | collective-permute-start | bytes 786440 | tf_op jit(solution)/shard_map/ppermute | solution.py:81
  52.9 10.4 %collective-permute-start.2 = (f32[16,256]{1,0:T(8,128)S(1)}, f32[16,256]{1,0:T(8,128)S(1)}, u32[]{:S(2)}, u32[]{:S(2)}) collective-permute-start(f32[16,256]{1,0:T(8,128)S(1)} %reduce_sum.37), channel_id=1, source_target_pairs={{0,16},{16,0},{1,17},{17,1},{2,18},{18,2},{3,19},{19,3},{4,20},{20... | collective-permute-start | bytes 49160 | tf_op jit(solution)/shard_map/ppermute | solution.py:40
  64.1 13.3 %all-to-all-start.3 = ((f32[16,16,256]{2,1,0:T(8,128)}), f32[16,16,256]{2,1,0:T(8,128)S(1)}, u32[]{:S(2)}, u32[]{:S(2)}) async-start(f32[16,16,256]{2,1,0:T(8,128)} %broadcast_in_dim.17), calls=%async_computation.3 | async-start | bytes 524288 | tf_op jit(solution)/shard_map/all_to_all | solution.py:44
  68.5 16.1 %collective-permute-start.6 = (f32[256,256]{1,0:T(8,128)S(1)}, f32[256,256]{1,0:T(8,128)S(1)}, u32[]{:S(2)}, u32[]{:S(2)}) collective-permute-start(f32[256,256]{1,0:T(8,128)S(1)} %bitcast.136), channel_id=1, source_target_pairs={{0,2},{1,3},{2,0},{3,1},{4,6},{5,7},{6,4},{7,5},{8,10},{9,11},{10,... | collective-permute-start | bytes 786440 | tf_op jit(solution)/shard_map/ppermute | solution.py:81
  77.9 6.6 %collective-permute-start.5 = (f32[64,128]{1,0:T(8,128)S(1)}, f32[64,128]{1,0:T(8,128)S(1)}, u32[]{:S(2)}, u32[]{:S(2)}) collective-permute-start(f32[64,128]{1,0:T(8,128)S(1)} %fusion.6), channel_id=1, source_target_pairs={{0,32},{32,0},{1,33},{33,1},{2,34},{34,2},{3,35},{35,3},{4,36},{36... | collective-permute-start | bytes 98312 | tf_op jit(solution)/shard_map/ppermute | solution.py:40
  84.5 13.4 %collective-permute-start.7 = (f32[64,128]{1,0:T(8,128)S(1)}, f32[64,128]{1,0:T(8,128)S(1)}, u32[]{:S(2)}, u32[]{:S(2)}) collective-permute-start(f32[64,128]{1,0:T(8,128)S(1)} %add.73), channel_id=1, source_target_pairs={{0,64},{64,0},{1,65},{65,1},{2,66},{66,2},{3,67},{67,3},{4,68},{68... | collective-permute-start | bytes 98312 | tf_op jit(solution)/shard_map/ppermute | solution.py:40
  118.0 9.2 %collective-permute-start.8 = (f32[16,512]{1,0:T(8,128)S(1)}, f32[16,512]{1,0:T(8,128)S(1)}, u32[]{:S(2)}, u32[]{:S(2)}) collective-permute-start(f32[16,512]{1,0:T(8,128)S(1)} %reduce_sum.38), channel_id=1, source_target_pairs={{0,16},{16,0},{1,17},{17,1},{2,18},{18,2},{3,19},{19,3},{4,20},{20... | collective-permute-start | bytes 98312 | tf_op jit(solution)/shard_map/ppermute | solution.py:40
  146.2 11.1 %collective-permute-start.9 = (f32[2,2,16,128]{3,2,1,0:T(8,128)S(1)}, f32[2,2,16,128]{3,2,1,0:T(8,128)S(1)}, u32[]{:S(2)}, u32[]{:S(2)}) collective-permute-start(f32[2,2,16,128]{3,2,1,0:T(8,128)S(1)} %select_bitcast_fusion), channel_id=1, source_target_pairs={{0,32},{32,0},{1,33},{33,1},{2,34},{34,2},{3,35},{35,3},{4,36},{36... | collective-permute-start | bytes 98312 | tf_op jit(solution)/shard_map/ppermute | solution.py:40
  157.3 13.2 %collective-permute-start.10 = (f32[2,16,128]{2,1,0:T(8,128)S(1)}, f32[2,16,128]{2,1,0:T(8,128)S(1)}, u32[]{:S(2)}, u32[]{:S(2)}) collective-permute-start(f32[2,16,128]{2,1,0:T(8,128)S(1)} %select_bitcast_fusion.1), channel_id=1, source_target_pairs={{0,64},{64,0},{1,65},{65,1},{2,66},{66,2},{3,67},{67,3},{4,68},{68... | collective-permute-start | bytes 49160 | tf_op jit(solution)/shard_map/ppermute | solution.py:40

commit v16 on v15

--- a/solution.py
+++ b/solution.py
@@ -49,17 +49,19 @@
 
 
 def local(points, labels, centres, coeffs, diag_inverse, off_block):
-    zy, yx = ("z", "y"), ("y", "x")
-    y, z = lax.axis_index("y"), lax.axis_index("z")
+    zy = ("z", "y")
+    x, y, z = lax.axis_index("x"), lax.axis_index("y"), lax.axis_index("z")
 
-    row = lax.broadcasted_iota(jnp.int32, (16, 256), 0)
-    chosen = lax.broadcasted_iota(jnp.int32, (16, 256), 1) == z * 64 + y * 16 + row
-    target = lax.dot_general(
+    row = lax.broadcasted_iota(jnp.int32, (64, 256), 0)
+    start = row // 16 * 64 + y * 16 + row % 16
+    chosen = lax.broadcasted_iota(jnp.int32, (64, 256), 1) == start
+    label = lax.dot_general(
         chosen.astype(labels.dtype),
         labels,
         (((1,), (1,)), ((), ())),
         preferred_element_type=jnp.float32,
     )
+    label = label.reshape(4, 16, 4, 128).transpose(0, 2, 1, 3).reshape(4, 64, 128)
     c0, h0 = lax.axis_index("c") == 0, lax.axis_index("h") == 0
 
     part = dot(diag_inverse[1], coeffs[1], 1, 0)
@@ -69,7 +71,7 @@
 
     diag = diag_inverse[0].reshape(128, 2, 128).transpose(1, 0, 2).reshape(256, 128)
     coeff = coeffs[0].T.reshape(4, 64, 2, 128).transpose(0, 2, 1, 3).reshape(4, 128, 128)
-    own = jnp.concatenate([copies(off_block, 4), copies(diag, 4), coeff], 1)
+    own = jnp.concatenate([copies(off_block, 4), copies(diag, 4), coeff, label], 1)
     part, own = lax.optimization_barrier((part, own))
     blocks = exchange(own, "x")
     part = part + swap(part, "c")
@@ -77,10 +79,12 @@
     second, blocks = lax.optimization_barrier((part, blocks))
 
     carried = dot(second, blocks[:, :256], 1, 2).transpose(1, 0, 2)
-    carried, flat = lax.optimization_barrier((carried, centres.reshape(256, 256)))
-    near, far, wrap = (lax.ppermute(flat, "y", [(i, i ^ k) for i in range(4)]) for k in (1, 2, 3))
+    carried, flat = lax.optimization_barrier((carried, points))
+    near, far, wrap = (lax.ppermute(flat, "x", [(i, i ^ k) for i in range(4)]) for k in (1, 2, 3))
+    target = lax.dynamic_index_in_dim(blocks[:, 640:], z, 0, keepdims=False)
+    target = target.reshape(4, 16, 128).transpose(1, 0, 2).reshape(16, 512)
     carried = jnp.sum(exchange(carried.reshape(16, 16, 256), zy), 0)
-    coeff = blocks[:, 512:].reshape(4, 2, 64, 128)
+    coeff = blocks[:, 512:640].reshape(4, 2, 64, 128)
     coeff = lax.dynamic_slice(coeff, (z, 0, y * 16, 0), (1, 2, 16, 128))
     coeff = coeff.reshape(2, 16, 128).transpose(1, 0, 2).reshape(16, 256)
     rest = (coeff - carried) - swap(carried, "w")
@@ -100,30 +104,27 @@
     first = first + swap(first, "c")
     first, far = lax.optimization_barrier((first, far))
     others = jnp.stack([flat, near, far, wrap])
-    centres_y = [lax.dynamic_index_in_dim(others, y ^ k, 0, keepdims=False) for k in range(4)]
-    score = dot(points, jnp.concatenate(centres_y, 0), 1, 1) / math.sqrt(points.shape[1])
+    points_x = [lax.dynamic_index_in_dim(others, x ^ k, 0, keepdims=False) for k in range(4)]
+    score = dot(jnp.concatenate(points_x, 0), centres.reshape(256, 256), 1, 1)
+    score = score / math.sqrt(points.shape[1])
     kernel = halves(score + score * score * score / 3.0)
     first = first + swap(first, "h")
     first, kernel, target, c0, h0 = lax.optimization_barrier((first, kernel, target, c0, h0))
 
-    solved = jnp.concatenate([first, second], 1).reshape(4, 1, 16, 256)
-    solved = jnp.broadcast_to(solved, (4, 4, 16, 256)).reshape(16, 16, 256)
-    solved = exchange(solved, yx).reshape(4, 64, 256)
-
+    solved = jnp.concatenate([first, second], 1)
     pred_scale = 1.0 / (2.0 * math.sqrt(256 * 32))
-    by_y = [side.reshape(512, 4, 256) for side in kernel]
-    pred = dot_halves(solved, by_y, (0, 2), (1, 2), 1).reshape(4, 16, 512)
-    pred = jnp.sum(exchange(pred, "z"), 0)
+    pred = dot_halves(solved, kernel, (1,), (1,), 0)
+    pred = pred.reshape(64, 4, 512).transpose(1, 0, 2).reshape(16, 16, 512)
+    pred = jnp.sum(exchange(pred, zy), 0)
     pred = pred + swap(pred, "w")
 
     weights = jnp.tanh(pred * pred_scale - target)
-    weights = exchange(copies(weights, 4), "z").reshape(64, 512)
+    weights = exchange(copies(weights, 16), zy).reshape(4, 64, 512)
 
     scale = 1.0 / (2.0 * math.sqrt(points.shape[0] * 16))
-    term = dot_halves(weights, kernel, (1,), (0,), 0)
-    term = term.reshape(4, 16, 4, 2, 128).transpose(2, 0, 3, 1, 4).reshape(16, 2, 16, 128)
-    term = jnp.sum(exchange(term, yx).reshape(4, 4, 2, 16, 128), 1)
-    term = term.reshape(2, 2, 2, 16, 128)
+    by_x = [side.reshape(4, 512, 256) for side in kernel]
+    term = dot_halves(weights, by_x, (0, 2), (0, 1), 1)
+    term = term.reshape(2, 2, 16, 2, 128).transpose(0, 1, 3, 2, 4)
     term = jnp.where(c0, term[:, 0], term[:, 1]) + swap(jnp.where(c0, term[:, 1], term[:, 0]), "c")
     term = jnp.where(h0, term[0], term[1]) + swap(jnp.where(h0, term[1], term[0]), "h")
     return (term * scale).transpose(0, 2, 1)

time: 172 us -> 169 us (0.983)
  blocking collectives: 37 us -> 28.7 us
  local copies, waits for them, and re-layouts: 2.83 us -> 5.81 us
    all_to_all x4 -> x2, blocking collectives: 37 us -> 28.7 us  [exchange(): return lax.all_to_all(a, axes, 0, 0, tiled=True)]
    all_to_all x4, starting transfers between devices: 17.5 us -> 19.3 us  [exchange(): return lax.all_to_all(a, axes, 0, 0, tiled=True)]
  transfers between devices with their start and end apart: 15 -> 15, of which waited for: 11 -> 9; matrix products, arithmetic and copies ran while one was open for 2% -> 6% of each run, Pallas kernels for 0% -> 0%
where the time goes in v16:
time: 169 us; the launch traced here: 168 us
  starting transfers between devices  105 us (62%)
  blocking collectives  28.7 us (17%)
  waiting for transfers between devices  17.6 us (10%)
  matrix products  6.98 us (4%)
  local copies, waits for them, and re-layouts  5.81 us (3%)
  other arithmetic  3.28 us (2%)
    ppermute x8, starting transfers between devices, swap(): return lax.ppermute(a, axis, [(0, 1), (1, 0)])  75.1 us
    all_to_all x2, blocking collectives, exchange(): return lax.all_to_all(a, axes, 0, 0, tiled=True)  28.7 us
    all_to_all x4, starting transfers between devices, exchange(): return lax.all_to_all(a, axes, 0, 0, tiled=True)  19.3 us
    ppermute x3, starting transfers between devices, local(): lax.ppermute(flat, 'x', [(i, i ^ k) for i in range(4)])  10.5 us
    ppermute x8, waiting for transfers between devices, swap(): return lax.ppermute(a, axis, [(0, 1), (1, 0)])  10 us
    all_to_all x4, waiting for transfers between devices, exchange(): return lax.all_to_all(a, axes, 0, 0, tiled=True)  7.54 us
    dot_general x3, matrix products, dot(): lax.dot_general(a, b, (((ca,), (cb,)), ((), ())), precision=HIGH, preferr...  3.7 us
  transfers between devices with their start and end apart: 15, of which 9 were waited for; matrix products, arithmetic and copies ran while one was open for 6% of the time, Pallas kernels for 0%

profile of v16, /device:TPU:1, one launch (start us, length us, event | category | flops | bytes accessed | tf_op | source)
XLA Modules:
  0.0 167.9 jit_solution(4534737489980475873)
XLA Ops:
  0.0 1.3 fusion.19
  1.3 0.8 copy.19
  2.1 4.8 %all-to-all-start = ((f32[4,64,128]{2,1,0:T(8,128)}), f32[4,64,128]{2,1,0:T(8,128)S(1)}, u32[]{:S(2)}, u32[]{:S(2)}) async-start(f32[4,64,128]{2,1,0:T(8,128)} %bitcast.3), calls=%async_computation | async-start | bytes 262144 | tf_op jit(solution)/shard_map/all_to_all | solution.py:44
  7.0 1.2 fusion.33
  8.6 0.1 reshape.72
  8.8 1.2 pad_maximum_fusion.1
  10.0 1.7 %all-to-all-done = f32[4,64,128]{2,1,0:T(8,128)S(1)} async-done(((f32[4,64,128]{2,1,0:T(8,128)}), f32[4,64,128]{2,1,0:T(8,128)S(1)}, u32[]{:S(2)}, u32[]{:S(2)}) %all-to-all-start) | async-done | bytes 131104 | tf_op jit(solution)/shard_map/all_to_all | solution.py:44
  11.8 3.7 %all-to-all-start.1 = ((f32[4,704,128]{2,1,0:T(8,128)}), f32[4,704,128]{2,1,0:T(8,128)S(1)}, u32[]{:S(2)}, u32[]{:S(2)}) async-start(f32[4,704,128]{2,1,0:T(8,128)} %pad_maximum_fusion.1), calls=%async_computation.1 | async-start | bytes 2883584 | tf_op jit(solution)/shard_map/all_to_all | solution.py:44
  15.5 8.4 %collective-permute-start = (f32[64,128]{1,0:T(8,128)S(1)}, f32[64,128]{1,0:T(8,128)S(1)}, u32[]{:S(2)}, u32[]{:S(2)}) collective-permute-start(f32[64,128]{1,0:T(8,128)S(1)} %reduce_sum.27), channel_id=1, source_target_pairs={{0,32},{32,0},{1,33},{33,1},{2,34},{34,2},{3,35},{35,3},{4,36},{36... | collective-permute-start | bytes 98312 | tf_op jit(solution)/shard_map/ppermute | solution.py:40
  23.9 0.8 collective-permute-done
  24.7 11.1 %collective-permute-start.1 = (f32[64,128]{1,0:T(8,128)S(1)}, f32[64,128]{1,0:T(8,128)S(1)}, u32[]{:S(2)}, u32[]{:S(2)}) collective-permute-start(f32[64,128]{1,0:T(8,128)S(1)} %add.82), channel_id=1, source_target_pairs={{0,64},{64,0},{1,65},{65,1},{2,66},{66,2},{3,67},{67,3},{4,68},{68... | collective-permute-start | bytes 98312 | tf_op jit(solution)/shard_map/ppermute | solution.py:40
  35.8 2.3 %collective-permute-done.1 = f32[64,128]{1,0:T(8,128)S(1)} collective-permute-done((f32[64,128]{1,0:T(8,128)S(1)}, f32[64,128]{1,0:T(8,128)S(1)}, u32[]{:S(2)}, u32[]{:S(2)}) %collective-permute-start.1) | collective-permute-done | bytes 32800 | tf_op jit(solution)/shard_map/ppermute | solution.py:40
  38.1 1.1 convolution_bitcast_fusion
  39.2 4.7 %all-to-all-start.2 = ((f32[16,16,256]{2,1,0:T(8,128)}), f32[16,16,256]{2,1,0:T(8,128)S(1)}, u32[]{:S(2)}, u32[]{:S(2)}) async-start(f32[16,16,256]{2,1,0:T(8,128)} %bitcast.17), calls=%async_computation.2 | async-start | bytes 524288 | tf_op jit(solution)/shard_map/all_to_all | solution.py:44
  43.9 4.8 %collective-permute-start.4 = (f32[512,256]{1,0:T(8,128)S(1)}, f32[512,256]{1,0:T(8,128)S(1)}, u32[]{:S(2)}, u32[]{:S(2)}) collective-permute-start(f32[512,256]{1,0:T(8,128)S(1)} %copy-done.2), channel_id=1, source_target_pairs={{0,384},{128,256},{256,128},{384,0},{1,385},{129,257},{257,129},{3... | collective-permute-start | bytes 1572872 | tf_op jit(solution)/shard_map/ppermute | solution.py:83
  48.7 1.9 %collective-permute-start.3 = (f32[512,256]{1,0:T(8,128)S(1)}, f32[512,256]{1,0:T(8,128)S(1)}, u32[]{:S(2)}, u32[]{:S(2)}) collective-permute-start(f32[512,256]{1,0:T(8,128)S(1)} %copy-done.2), channel_id=1, source_target_pairs={{0,128},{128,0},{256,384},{384,256},{1,129},{129,1},{257,385},{385... | collective-permute-start | bytes 1572872 | tf_op jit(solution)/shard_map/ppermute | solution.py:83
  50.7 0.7 slice.65
  51.4 1.4 all-to-all-done.2
  52.7 8.9 %collective-permute-start.2 = (f32[16,256]{1,0:T(8,128)S(1)}, f32[16,256]{1,0:T(8,128)S(1)}, u32[]{:S(2)}, u32[]{:S(2)}) collective-permute-start(f32[16,256]{1,0:T(8,128)S(1)} %reduce_sum.28), channel_id=1, source_target_pairs={{0,16},{16,0},{1,17},{17,1},{2,18},{18,2},{3,19},{19,3},{4,20},{20... | collective-permute-start | bytes 49160 | tf_op jit(solution)/shard_map/ppermute | solution.py:40
  61.7 0.7 constant_dynamic-slice_fusion.1
  62.4 0.4 collective-permute-done.2
  62.8 0.7 broadcast_in_dim.13
  63.5 6.1 %all-to-all-start.3 = ((f32[16,16,256]{2,1,0:T(8,128)}), f32[16,16,256]{2,1,0:T(8,128)S(1)}, u32[]{:S(2)}, u32[]{:S(2)}) async-start(f32[16,16,256]{2,1,0:T(8,128)} %broadcast_in_dim.13), calls=%async_computation.3 | async-start | bytes 524288 | tf_op jit(solution)/shard_map/all_to_all | solution.py:44
  69.6 3.8 %collective-permute-start.6 = (f32[512,256]{1,0:T(8,128)S(1)}, f32[512,256]{1,0:T(8,128)}, u32[]{:S(2)}, u32[]{:S(2)}) collective-permute-start(f32[512,256]{1,0:T(8,128)S(1)} %copy-done.2), channel_id=1, source_target_pairs={{0,256},{128,384},{256,0},{384,128},{1,257},{129,385},{257,1},{385... | collective-permute-start | bytes 1572872 | tf_op jit(solution)/shard_map/ppermute | solution.py:83
  73.5 0.7 slice.71
  74.1 4.5 %all-to-all-done.3 = f32[16,16,256]{2,1,0:T(8,128)S(1)} async-done(((f32[16,16,256]{2,1,0:T(8,128)}), f32[16,16,256]{2,1,0:T(8,128)S(1)}, u32[]{:S(2)}, u32[]{:S(2)}) %all-to-all-start.3) | async-done | bytes 262176 | tf_op jit(solution)/shard_map/all_to_all | solution.py:44
  78.6 0.3 convolution_bitcast_fusion.4
  78.8 0.3 fusion.13
  79.1 6.2 %collective-permute-start.5 = (f32[64,128]{1,0:T(8,128)S(1)}, f32[64,128]{1,0:T(8,128)S(1)}, u32[]{:S(2)}, u32[]{:S(2)}) collective-permute-start(f32[64,128]{1,0:T(8,128)S(1)} %fusion.13), channel_id=1, source_target_pairs={{0,32},{32,0},{1,33},{33,1},{2,34},{34,2},{3,35},{35,3},{4,36},{36... | collective-permute-start | bytes 98312 | tf_op jit(solution)/shard_map/ppermute | solution.py:40
  85.3 0.8 constant_dynamic-slice_fusion
  86.1 0.6 copy.37
  86.7 12.2 %collective-permute-start.7 = (f32[64,128]{1,0:T(8,128)S(1)}, f32[64,128]{1,0:T(8,128)S(1)}, u32[]{:S(2)}, u32[]{:S(2)}) collective-permute-start(f32[64,128]{1,0:T(8,128)S(1)} %add.87), channel_id=1, source_target_pairs={{0,64},{64,0},{1,65},{65,1},{2,66},{66,2},{3,67},{67,3},{4,68},{68... | collective-permute-start | bytes 98312 | tf_op jit(solution)/shard_map/ppermute | solution.py:40
  98.9 1.2 pad_maximum_fusion
  100.1 0.1 dynamic-slice_bitcast_fusion.3
  100.3 1.3 fusion.1
  101.6 0.5 fusion.29
  102.1 0.4 fusion
  102.6 13.8 %all_to_all.30 = f32[16,16,512]{2,1,0:T(8,128)S(1)} all-to-all(f32[16,16,512]{2,1,0:T(8,128)S(1)} %bitcast.110), channel_id=1, replica_groups=mesh['x'=4,'h'=2,'c'=2,'w'=2,'z'=4,'y'=4] {'z','y'}, dimensions={0} | all-to-all | bytes 1048576 | tf_op jit(solution)/shard_map/all_to_all | solution.py:44
  116.4 8.7 %collective-permute-start.8 = (f32[16,512]{1,0:T(8,128)S(1)}, f32[16,512]{1,0:T(8,128)S(1)}, u32[]{:S(2)}, u32[]{:S(2)}) collective-permute-start(f32[16,512]{1,0:T(8,128)S(1)} %reduce_sum.29), channel_id=1, source_target_pairs={{0,16},{16,0},{1,17},{17,1},{2,18},{18,2},{3,19},{19,3},{4,20},{20... | collective-permute-start | bytes 98312 | tf_op jit(solution)/shard_map/ppermute | solution.py:40
  125.1 1.3 collective-permute-done.8
  126.6 14.9 %all_to_all.31 = f32[16,16,512]{2,1,0:T(8,128)S(1)} all-to-all(f32[16,16,512]{2,1,0:T(8,128)S(1)} %broadcast_in_dim.14), channel_id=1, replica_groups=mesh['x'=4,'h'=2,'c'=2,'w'=2,'z'=4,'y'=4] {'z','y'}, dimensions={0} | all-to-all | bytes 1048576 | tf_op jit(solution)/shard_map/all_to_all | solution.py:44
  141.6 0.3 convolution_bitcast_fusion.1
  141.9 0.3 fusion.12
  142.3 10.9 %collective-permute-start.9 = (f32[2,2,16,128]{3,2,1,0:T(8,128)S(1)}, f32[2,2,16,128]{3,2,1,0:T(8,128)S(1)}, u32[]{:S(2)}, u32[]{:S(2)}) collective-permute-start(f32[2,2,16,128]{3,2,1,0:T(8,128)S(1)} %select_bitcast_fusion), channel_id=1, source_target_pairs={{0,32},{32,0},{1,33},{33,1},{2,34},{34,2},{3,35},{35,3},{4,36},{36... | collective-permute-start | bytes 98312 | tf_op jit(solution)/shard_map/ppermute | solution.py:40
  153.2 0.8 collective-permute-done.9
  154.0 8.8 %collective-permute-start.10 = (f32[2,16,128]{2,1,0:T(8,128)S(1)}, f32[2,16,128]{2,1,0:T(8,128)S(1)}, u32[]{:S(2)}, u32[]{:S(2)}) collective-permute-start(f32[2,16,128]{2,1,0:T(8,128)S(1)} %select_bitcast_fusion.1), channel_id=1, source_target_pairs={{0,64},{64,0},{1,65},{65,1},{2,66},{66,2},{3,67},{67,3},{4,68},{68... | collective-permute-start | bytes 49160 | tf_op jit(solution)/shard_map/ppermute | solution.py:40
  162.9 4.3 %collective-permute-done.10 = f32[2,16,128]{2,1,0:T(8,128)S(1)} collective-permute-done((f32[2,16,128]{2,1,0:T(8,128)S(1)}, f32[2,16,128]{2,1,0:T(8,128)S(1)}, u32[]{:S(2)}, u32[]{:S(2)}) %collective-permute-start.10) | collective-permute-done | bytes 16416 | tf_op jit(solution)/shard_map/ppermute | solution.py:40
  167.2 0.6 fusion.45
  (56 shorter events, 0.8 us)
Async XLA Ops:
  0.0 100.3 %copy-start = (f32[2,128,256]{2,1,0:T(8,128)S(1)}, f32[2,128,256]{2,1,0:T(8,128)}, u32[]{:S(2)}) copy-start(f32[2,128,256]{2,1,0:T(8,128)} %param.8) | copy-start | bytes 786436
  0.0 8.3 %slice-start = ((f32[2,128,256]{2,1,0:T(8,128)}), f32[1,128,256]{2,1,0:T(8,128)S(1)}, s32[]{:S(2)}) async-start(f32[2,128,256]{2,1,0:T(8,128)} %param.10), calls=%async_computation.6 | async-start | bytes 262144 | tf_op jit(solution)/shard_map/slice | solution.py:72
  0.0 8.4 %copy-start.1 = (f32[2,256,256]{2,1,0:T(8,128)S(1)}, f32[2,256,256]{2,1,0:T(8,128)}, u32[]{:S(2)}) copy-start(f32[2,256,256]{2,1,0:T(8,128)} %param.9) | copy-start | bytes 1572868
  2.1 9.7 %all-to-all-start = ((f32[4,64,128]{2,1,0:T(8,128)}), f32[4,64,128]{2,1,0:T(8,128)S(1)}, u32[]{:S(2)}, u32[]{:S(2)}) async-start(f32[4,64,128]{2,1,0:T(8,128)} %bitcast.3), calls=%async_computation | async-start | bytes 262144 | tf_op jit(solution)/shard_map/all_to_all | solution.py:44
  7.0 1.8 %copy-start.5 = (f32[256,128]{1,0:T(8,128)S(1)}, f32[256,128]{1,0:T(8,128)}, u32[]{:S(2)}) copy-start(f32[256,128]{1,0:T(8,128)} %param.11) | copy-start | bytes 393220
  11.8 32.1 %copy-start.2 = (f32[512,256]{1,0:T(8,128)S(1)}, f32[512,256]{1,0:T(8,128)}, u32[]{:S(2)}) copy-start(f32[512,256]{1,0:T(8,128)} %param.6) | copy-start | bytes 1572868
  11.8 26.3 %all-to-all-start.1 = ((f32[4,704,128]{2,1,0:T(8,128)}), f32[4,704,128]{2,1,0:T(8,128)S(1)}, u32[]{:S(2)}, u32[]{:S(2)}) async-start(f32[4,704,128]{2,1,0:T(8,128)} %pad_maximum_fusion.1), calls=%async_computation.1 | async-start | bytes 2883584 | tf_op jit(solution)/shard_map/all_to_all | solution.py:44
  15.5 9.2 %collective-permute-start = (f32[64,128]{1,0:T(8,128)S(1)}, f32[64,128]{1,0:T(8,128)S(1)}, u32[]{:S(2)}, u32[]{:S(2)}) collective-permute-start(f32[64,128]{1,0:T(8,128)S(1)} %reduce_sum.27), channel_id=1, source_target_pairs={{0,32},{32,0},{1,33},{33,1},{2,34},{34,2},{3,35},{35,3},{4,36},{36... | collective-permute-start | bytes 98312 | tf_op jit(solution)/shard_map/ppermute | solution.py:40
  24.7 13.4 %collective-permute-start.1 = (f32[64,128]{1,0:T(8,128)S(1)}, f32[64,128]{1,0:T(8,128)S(1)}, u32[]{:S(2)}, u32[]{:S(2)}) collective-permute-start(f32[64,128]{1,0:T(8,128)S(1)} %add.82), channel_id=1, source_target_pairs={{0,64},{64,0},{1,65},{65,1},{2,66},{66,2},{3,67},{67,3},{4,68},{68... | collective-permute-start | bytes 98312 | tf_op jit(solution)/shard_map/ppermute | solution.py:40
  38.1 1.1 copy-start.3
  39.2 13.5 %all-to-all-start.2 = ((f32[16,16,256]{2,1,0:T(8,128)}), f32[16,16,256]{2,1,0:T(8,128)S(1)}, u32[]{:S(2)}, u32[]{:S(2)}) async-start(f32[16,16,256]{2,1,0:T(8,128)} %bitcast.17), calls=%async_computation.2 | async-start | bytes 524288 | tf_op jit(solution)/shard_map/all_to_all | solution.py:44
  43.9 18.9 %collective-permute-start.4 = (f32[512,256]{1,0:T(8,128)S(1)}, f32[512,256]{1,0:T(8,128)S(1)}, u32[]{:S(2)}, u32[]{:S(2)}) collective-permute-start(f32[512,256]{1,0:T(8,128)S(1)} %copy-done.2), channel_id=1, source_target_pairs={{0,384},{128,256},{256,128},{384,0},{1,385},{129,257},{257,129},{3... | collective-permute-start | bytes 1572872 | tf_op jit(solution)/shard_map/ppermute | solution.py:83
  48.7 14.1 %collective-permute-start.3 = (f32[512,256]{1,0:T(8,128)S(1)}, f32[512,256]{1,0:T(8,128)S(1)}, u32[]{:S(2)}, u32[]{:S(2)}) collective-permute-start(f32[512,256]{1,0:T(8,128)S(1)} %copy-done.2), channel_id=1, source_target_pairs={{0,128},{128,0},{256,384},{384,256},{1,129},{129,1},{257,385},{385... | collective-permute-start | bytes 1572872 | tf_op jit(solution)/shard_map/ppermute | solution.py:83
  52.7 10.0 %collective-permute-start.2 = (f32[16,256]{1,0:T(8,128)S(1)}, f32[16,256]{1,0:T(8,128)S(1)}, u32[]{:S(2)}, u32[]{:S(2)}) collective-permute-start(f32[16,256]{1,0:T(8,128)S(1)} %reduce_sum.28), channel_id=1, source_target_pairs={{0,16},{16,0},{1,17},{17,1},{2,18},{18,2},{3,19},{19,3},{4,20},{20... | collective-permute-start | bytes 49160 | tf_op jit(solution)/shard_map/ppermute | solution.py:40
  63.5 15.1 %all-to-all-start.3 = ((f32[16,16,256]{2,1,0:T(8,128)}), f32[16,16,256]{2,1,0:T(8,128)S(1)}, u32[]{:S(2)}, u32[]{:S(2)}) async-start(f32[16,16,256]{2,1,0:T(8,128)} %broadcast_in_dim.13), calls=%async_computation.3 | async-start | bytes 524288 | tf_op jit(solution)/shard_map/all_to_all | solution.py:44
  69.6 17.1 %collective-permute-start.6 = (f32[512,256]{1,0:T(8,128)S(1)}, f32[512,256]{1,0:T(8,128)}, u32[]{:S(2)}, u32[]{:S(2)}) collective-permute-start(f32[512,256]{1,0:T(8,128)S(1)} %copy-done.2), channel_id=1, source_target_pairs={{0,256},{128,384},{256,0},{384,128},{1,257},{129,385},{257,1},{385... | collective-permute-start | bytes 1572872 | tf_op jit(solution)/shard_map/ppermute | solution.py:83
  79.1 7.6 %collective-permute-start.5 = (f32[64,128]{1,0:T(8,128)S(1)}, f32[64,128]{1,0:T(8,128)S(1)}, u32[]{:S(2)}, u32[]{:S(2)}) collective-permute-start(f32[64,128]{1,0:T(8,128)S(1)} %fusion.13), channel_id=1, source_target_pairs={{0,32},{32,0},{1,33},{33,1},{2,34},{34,2},{3,35},{35,3},{4,36},{36... | collective-permute-start | bytes 98312 | tf_op jit(solution)/shard_map/ppermute | solution.py:40
  86.7 14.8 %collective-permute-start.7 = (f32[64,128]{1,0:T(8,128)S(1)}, f32[64,128]{1,0:T(8,128)S(1)}, u32[]{:S(2)}, u32[]{:S(2)}) collective-permute-start(f32[64,128]{1,0:T(8,128)S(1)} %add.87), channel_id=1, source_target_pairs={{0,64},{64,0},{1,65},{65,1},{2,66},{66,2},{3,67},{67,3},{4,68},{68... | collective-permute-start | bytes 98312 | tf_op jit(solution)/shard_map/ppermute | solution.py:40
  100.3 1.3 copy-start.4
  102.1 24.4 %copy-start.6 = (f32[4,2,8,128]{3,2,0,1:T(8,128)S(1)}, f32[4,2,8,128]{3,2,0,1:T(8,128)}, u32[]{:S(2)}) copy-start(f32[4,2,8,128]{3,2,0,1:T(8,128)} %copy.37) | copy-start | bytes 98308
  116.4 10.0 %collective-permute-start.8 = (f32[16,512]{1,0:T(8,128)S(1)}, f32[16,512]{1,0:T(8,128)S(1)}, u32[]{:S(2)}, u32[]{:S(2)}) collective-permute-start(f32[16,512]{1,0:T(8,128)S(1)} %reduce_sum.29), channel_id=1, source_target_pairs={{0,16},{16,0},{1,17},{17,1},{2,18},{18,2},{3,19},{19,3},{4,20},{20... | collective-permute-start | bytes 98312 | tf_op jit(solution)/shard_map/ppermute | solution.py:40
  142.3 11.7 %collective-permute-start.9 = (f32[2,2,16,128]{3,2,1,0:T(8,128)S(1)}, f32[2,2,16,128]{3,2,1,0:T(8,128)S(1)}, u32[]{:S(2)}, u32[]{:S(2)}) collective-permute-start(f32[2,2,16,128]{3,2,1,0:T(8,128)S(1)} %select_bitcast_fusion), channel_id=1, source_target_pairs={{0,32},{32,0},{1,33},{33,1},{2,34},{34,2},{3,35},{35,3},{4,36},{36... | collective-permute-start | bytes 98312 | tf_op jit(solution)/shard_map/ppermute | solution.py:40
  154.0 13.2 %collective-permute-start.10 = (f32[2,16,128]{2,1,0:T(8,128)S(1)}, f32[2,16,128]{2,1,0:T(8,128)S(1)}, u32[]{:S(2)}, u32[]{:S(2)}) collective-permute-start(f32[2,16,128]{2,1,0:T(8,128)S(1)} %select_bitcast_fusion.1), channel_id=1, source_target_pairs={{0,64},{64,0},{1,65},{65,1},{2,66},{66,2},{3,67},{67,3},{4,68},{68... | collective-permute-start | bytes 49160 | tf_op jit(solution)/shard_map/ppermute | solution.py:40

commit v17 on v16

--- a/solution.py
+++ b/solution.py
@@ -81,8 +81,6 @@
     carried = dot(second, blocks[:, :256], 1, 2).transpose(1, 0, 2)
     carried, flat = lax.optimization_barrier((carried, points))
     near, far, wrap = (lax.ppermute(flat, "x", [(i, i ^ k) for i in range(4)]) for k in (1, 2, 3))
-    target = lax.dynamic_index_in_dim(blocks[:, 640:], z, 0, keepdims=False)
-    target = target.reshape(4, 16, 128).transpose(1, 0, 2).reshape(16, 512)
     carried = jnp.sum(exchange(carried.reshape(16, 16, 256), zy), 0)
     coeff = blocks[:, 512:640].reshape(4, 2, 64, 128)
     coeff = lax.dynamic_slice(coeff, (z, 0, y * 16, 0), (1, 2, 16, 128))
@@ -102,7 +100,9 @@
 
     first = solve(0) + solve(1)
     first = first + swap(first, "c")
-    first, far = lax.optimization_barrier((first, far))
+    first, flat, near, wrap, blocks = lax.optimization_barrier((first, flat, near, wrap, blocks))
+    target = lax.dynamic_slice(blocks, (z, 640, 0), (1, 64, 128))
+    target = target.reshape(4, 16, 128).transpose(1, 0, 2).reshape(16, 512)
     others = jnp.stack([flat, near, far, wrap])
     points_x = [lax.dynamic_index_in_dim(others, x ^ k, 0, keepdims=False) for k in range(4)]
     score = dot(jnp.concatenate(points_x, 0), centres.reshape(256, 256), 1, 1)

time: 169 us -> 170 us (level)
  starting transfers between devices: 105 us -> 100 us
  blocking collectives: 28.7 us -> 33.3 us
  local copies, waits for them, and re-layouts: 5.81 us -> 3.78 us
  matrix products: 6.98 us -> 8.8 us
    ppermute x8, starting transfers between devices: 75.1 us -> 70.3 us  [swap(): return lax.ppermute(a, axis, [(0, 1), (1, 0)])]
    all_to_all x2, blocking collectives: 28.7 us -> 33.3 us  [exchange(): return lax.all_to_all(a, axes, 0, 0, tiled=True)]
  transfers between devices with their start and end apart: 15 -> 15, of which waited for: 9 -> 10; matrix products, arithmetic and copies ran while one was open for 6% -> 5% of each run, Pallas kernels for 0% -> 0%
where the time goes in v17:
time: 170 us; the launch traced here: 169 us
  starting transfers between devices  100 us (59%)
  blocking collectives  33.3 us (20%)
  waiting for transfers between devices  18.2 us (11%)
  matrix products  8.8 us (5%)
  other arithmetic  4.04 us (2%)
  local copies, waits for them, and re-layouts  3.78 us (2%)
    ppermute x8, starting transfers between devices, swap(): return lax.ppermute(a, axis, [(0, 1), (1, 0)])  70.3 us
    all_to_all x2, blocking collectives, exchange(): return lax.all_to_all(a, axes, 0, 0, tiled=True)  33.3 us
    all_to_all x4, starting transfers between devices, exchange(): return lax.all_to_all(a, axes, 0, 0, tiled=True)  19.3 us
    ppermute x3, starting transfers between devices, local(): lax.ppermute(flat, 'x', [(i, i ^ k) for i in range(4)])  10.5 us
    ppermute x8, waiting for transfers between devices, swap(): return lax.ppermute(a, axis, [(0, 1), (1, 0)])  10 us
    all_to_all x4, waiting for transfers between devices, exchange(): return lax.all_to_all(a, axes, 0, 0, tiled=True)  8.23 us
    dot_general x3, matrix products, dot(): lax.dot_general(a, b, (((ca,), (cb,)), ((), ())), precision=HIGH, preferr...  3.7 us
  transfers between devices with their start and end apart: 15, of which 10 were waited for; matrix products, arithmetic and copies ran while one was open for 5% of the time, Pallas kernels for 0%

profile of v17, /device:TPU:1, one launch (start us, length us, event | category | flops | bytes accessed | tf_op | source)
XLA Modules:
  0.0 168.8 jit_solution(6384417717283614806)
XLA Ops:
  0.0 1.3 fusion.19
  1.3 0.8 copy.19
  2.1 4.8 %all-to-all-start = ((f32[4,64,128]{2,1,0:T(8,128)}), f32[4,64,128]{2,1,0:T(8,128)S(1)}, u32[]{:S(2)}, u32[]{:S(2)}) async-start(f32[4,64,128]{2,1,0:T(8,128)} %bitcast.3), calls=%async_computation | async-start | bytes 262144 | tf_op jit(solution)/shard_map/all_to_all | solution.py:44
  7.0 1.2 fusion.33
  8.4 0.1 copy.21
  8.6 0.1 reshape.71
  8.8 1.2 pad_maximum_fusion.1
  10.0 1.7 %all-to-all-done = f32[4,64,128]{2,1,0:T(8,128)S(1)} async-done(((f32[4,64,128]{2,1,0:T(8,128)}), f32[4,64,128]{2,1,0:T(8,128)S(1)}, u32[]{:S(2)}, u32[]{:S(2)}) %all-to-all-start) | async-done | bytes 131104 | tf_op jit(solution)/shard_map/all_to_all | solution.py:44
  11.8 3.7 %all-to-all-start.1 = ((f32[4,704,128]{2,1,0:T(8,128)}), f32[4,704,128]{2,1,0:T(8,128)S(1)}, u32[]{:S(2)}, u32[]{:S(2)}) async-start(f32[4,704,128]{2,1,0:T(8,128)} %pad_maximum_fusion.1), calls=%async_computation.1 | async-start | bytes 2883584 | tf_op jit(solution)/shard_map/all_to_all | solution.py:44
  15.5 8.4 %collective-permute-start = (f32[64,128]{1,0:T(8,128)S(1)}, f32[64,128]{1,0:T(8,128)S(1)}, u32[]{:S(2)}, u32[]{:S(2)}) collective-permute-start(f32[64,128]{1,0:T(8,128)S(1)} %reduce_sum.27), channel_id=1, source_target_pairs={{0,32},{32,0},{1,33},{33,1},{2,34},{34,2},{3,35},{35,3},{4,36},{36... | collective-permute-start | bytes 98312 | tf_op jit(solution)/shard_map/ppermute | solution.py:40
  23.9 0.8 collective-permute-done
  24.7 11.1 %collective-permute-start.1 = (f32[64,128]{1,0:T(8,128)S(1)}, f32[64,128]{1,0:T(8,128)S(1)}, u32[]{:S(2)}, u32[]{:S(2)}) collective-permute-start(f32[64,128]{1,0:T(8,128)S(1)} %add.81), channel_id=1, source_target_pairs={{0,64},{64,0},{1,65},{65,1},{2,66},{66,2},{3,67},{67,3},{4,68},{68... | collective-permute-start | bytes 98312 | tf_op jit(solution)/shard_map/ppermute | solution.py:40
  35.8 2.3 %collective-permute-done.1 = f32[64,128]{1,0:T(8,128)S(1)} collective-permute-done((f32[64,128]{1,0:T(8,128)S(1)}, f32[64,128]{1,0:T(8,128)S(1)}, u32[]{:S(2)}, u32[]{:S(2)}) %collective-permute-start.1) | collective-permute-done | bytes 32800 | tf_op jit(solution)/shard_map/ppermute | solution.py:40
  38.1 1.1 convolution_bitcast_fusion
  39.2 4.7 %all-to-all-start.2 = ((f32[16,16,256]{2,1,0:T(8,128)}), f32[16,16,256]{2,1,0:T(8,128)S(1)}, u32[]{:S(2)}, u32[]{:S(2)}) async-start(f32[16,16,256]{2,1,0:T(8,128)} %bitcast.17), calls=%async_computation.2 | async-start | bytes 524288 | tf_op jit(solution)/shard_map/all_to_all | solution.py:44
  43.9 4.8 %collective-permute-start.4 = (f32[512,256]{1,0:T(8,128)S(1)}, f32[512,256]{1,0:T(8,128)S(1)}, u32[]{:S(2)}, u32[]{:S(2)}) collective-permute-start(f32[512,256]{1,0:T(8,128)S(1)} %copy-done.3), channel_id=1, source_target_pairs={{0,384},{128,256},{256,128},{384,0},{1,385},{129,257},{257,129},{3... | collective-permute-start | bytes 1572872 | tf_op jit(solution)/shard_map/ppermute | solution.py:83
  48.7 1.9 %collective-permute-start.3 = (f32[512,256]{1,0:T(8,128)S(1)}, f32[512,256]{1,0:T(8,128)S(1)}, u32[]{:S(2)}, u32[]{:S(2)}) collective-permute-start(f32[512,256]{1,0:T(8,128)S(1)} %copy-done.3), channel_id=1, source_target_pairs={{0,128},{128,0},{256,384},{384,256},{1,129},{129,1},{257,385},{385... | collective-permute-start | bytes 1572872 | tf_op jit(solution)/shard_map/ppermute | solution.py:83
  50.7 0.7 slice.62
  51.4 1.4 all-to-all-done.2
  52.7 8.9 %collective-permute-start.2 = (f32[16,256]{1,0:T(8,128)S(1)}, f32[16,256]{1,0:T(8,128)S(1)}, u32[]{:S(2)}, u32[]{:S(2)}) collective-permute-start(f32[16,256]{1,0:T(8,128)S(1)} %reduce_sum.28), channel_id=1, source_target_pairs={{0,16},{16,0},{1,17},{17,1},{2,18},{18,2},{3,19},{19,3},{4,20},{20... | collective-permute-start | bytes 49160 | tf_op jit(solution)/shard_map/ppermute | solution.py:40
  61.7 0.7 constant_dynamic-slice_fusion.1
  62.4 0.4 collective-permute-done.2
  62.8 0.7 broadcast_in_dim.13
  63.5 6.1 %all-to-all-start.3 = ((f32[16,16,256]{2,1,0:T(8,128)}), f32[16,16,256]{2,1,0:T(8,128)S(1)}, u32[]{:S(2)}, u32[]{:S(2)}) async-start(f32[16,16,256]{2,1,0:T(8,128)} %broadcast_in_dim.13), calls=%async_computation.3 | async-start | bytes 524288 | tf_op jit(solution)/shard_map/all_to_all | solution.py:44
  69.6 3.8 %collective-permute-start.7 = (f32[512,256]{1,0:T(8,128)S(1)}, f32[512,256]{1,0:T(8,128)}, u32[]{:S(2)}, u32[]{:S(2)}) collective-permute-start(f32[512,256]{1,0:T(8,128)S(1)} %copy-done.3), channel_id=1, source_target_pairs={{0,256},{128,384},{256,0},{384,128},{1,257},{129,385},{257,1},{385... | collective-permute-start | bytes 1572872 | tf_op jit(solution)/shard_map/ppermute | solution.py:83
  73.4 5.1 %all-to-all-done.3 = f32[16,16,256]{2,1,0:T(8,128)S(1)} async-done(((f32[16,16,256]{2,1,0:T(8,128)}), f32[16,16,256]{2,1,0:T(8,128)S(1)}, u32[]{:S(2)}, u32[]{:S(2)}) %all-to-all-start.3) | async-done | bytes 262176 | tf_op jit(solution)/shard_map/all_to_all | solution.py:44
  78.6 0.3 convolution_bitcast_fusion.4
  78.8 0.9 fusion.13
  79.7 6.2 %collective-permute-start.5 = (f32[64,128]{1,0:T(8,128)}, f32[64,128]{1,0:T(8,128)S(1)}, u32[]{:S(2)}, u32[]{:S(2)}) collective-permute-start(f32[64,128]{1,0:T(8,128)} %fusion.13), channel_id=1, source_target_pairs={{0,32},{32,0},{1,33},{33,1},{2,34},{34,2},{3,35},{35,3},{4,36},{36... | collective-permute-start | bytes 98312 | tf_op jit(solution)/shard_map/ppermute | solution.py:40
  86.0 1.0 collective-permute-done.5
  87.0 0.8 add.86
  87.7 12.2 %collective-permute-start.6 = (f32[64,128]{1,0:T(8,128)S(1)}, f32[64,128]{1,0:T(8,128)S(1)}, u32[]{:S(2)}, u32[]{:S(2)}) collective-permute-start(f32[64,128]{1,0:T(8,128)S(1)} %add.86), channel_id=1, source_target_pairs={{0,64},{64,0},{1,65},{65,1},{2,66},{66,2},{3,67},{67,3},{4,68},{68... | collective-permute-start | bytes 98312 | tf_op jit(solution)/shard_map/ppermute | solution.py:40
  99.9 1.2 pad_maximum_fusion
  101.1 0.1 dynamic-slice_bitcast_fusion.3
  101.3 1.3 fusion.1
  102.7 0.5 fusion.29
  103.2 0.4 fusion
  103.7 16.5 %all_to_all.30 = f32[16,16,512]{2,1,0:T(8,128)S(1)} all-to-all(f32[16,16,512]{2,1,0:T(8,128)S(1)} %bitcast.110), channel_id=1, replica_groups=mesh['x'=4,'h'=2,'c'=2,'w'=2,'z'=4,'y'=4] {'z','y'}, dimensions={0} | all-to-all | bytes 1048576 | tf_op jit(solution)/shard_map/all_to_all | solution.py:44
  120.2 6.8 %collective-permute-start.8 = (f32[16,512]{1,0:T(8,128)S(1)}, f32[16,512]{1,0:T(8,128)S(1)}, u32[]{:S(2)}, u32[]{:S(2)}) collective-permute-start(f32[16,512]{1,0:T(8,128)S(1)} %reduce_sum.29), channel_id=1, source_target_pairs={{0,16},{16,0},{1,17},{17,1},{2,18},{18,2},{3,19},{19,3},{4,20},{20... | collective-permute-start | bytes 98312 | tf_op jit(solution)/shard_map/ppermute | solution.py:40
  127.0 1.8 %collective-permute-done.8 = f32[16,512]{1,0:T(8,128)S(1)} collective-permute-done((f32[16,512]{1,0:T(8,128)S(1)}, f32[16,512]{1,0:T(8,128)S(1)}, u32[]{:S(2)}, u32[]{:S(2)}) %collective-permute-start.8) | collective-permute-done | bytes 32800 | tf_op jit(solution)/shard_map/ppermute | solution.py:40
  128.8 16.8 %all_to_all.31 = f32[16,16,512]{2,1,0:T(8,128)S(1)} all-to-all(f32[16,16,512]{2,1,0:T(8,128)S(1)} %broadcast_in_dim.14), channel_id=1, replica_groups=mesh['x'=4,'h'=2,'c'=2,'w'=2,'z'=4,'y'=4] {'z','y'}, dimensions={0} | all-to-all | bytes 1048576 | tf_op jit(solution)/shard_map/all_to_all | solution.py:44
  145.7 1.5 convolution_bitcast_fusion.1
  147.3 0.3 fusion.12
  147.7 6.5 %collective-permute-start.9 = (f32[2,2,16,128]{3,2,1,0:T(8,128)S(1)}, f32[2,2,16,128]{3,2,1,0:T(8,128)S(1)}, u32[]{:S(2)}, u32[]{:S(2)}) collective-permute-start(f32[2,2,16,128]{3,2,1,0:T(8,128)S(1)} %select_bitcast_fusion), channel_id=1, source_target_pairs={{0,32},{32,0},{1,33},{33,1},{2,34},{34,2},{3,35},{35,3},{4,36},{36... | collective-permute-start | bytes 98312 | tf_op jit(solution)/shard_map/ppermute | solution.py:40
  154.2 0.8 collective-permute-done.9
  155.0 10.3 %collective-permute-start.10 = (f32[2,16,128]{2,1,0:T(8,128)S(1)}, f32[2,16,128]{2,1,0:T(8,128)S(1)}, u32[]{:S(2)}, u32[]{:S(2)}) collective-permute-start(f32[2,16,128]{2,1,0:T(8,128)S(1)} %select_bitcast_fusion.1), channel_id=1, source_target_pairs={{0,64},{64,0},{1,65},{65,1},{2,66},{66,2},{3,67},{67,3},{4,68},{68... | collective-permute-start | bytes 49160 | tf_op jit(solution)/shard_map/ppermute | solution.py:40
  165.3 2.9 %collective-permute-done.10 = f32[2,16,128]{2,1,0:T(8,128)S(1)} collective-permute-done((f32[2,16,128]{2,1,0:T(8,128)S(1)}, f32[2,16,128]{2,1,0:T(8,128)S(1)}, u32[]{:S(2)}, u32[]{:S(2)}) %collective-permute-start.10) | collective-permute-done | bytes 16416 | tf_op jit(solution)/shard_map/ppermute | solution.py:40
  168.2 0.6 fusion.45
  (55 shorter events, 0.7 us)
Async XLA Ops:
  0.0 101.3 %copy-start = (f32[2,128,256]{2,1,0:T(8,128)S(1)}, f32[2,128,256]{2,1,0:T(8,128)}, u32[]{:S(2)}) copy-start(f32[2,128,256]{2,1,0:T(8,128)} %param.8) | copy-start | bytes 786436
  0.0 8.3 %slice-start = ((f32[2,128,256]{2,1,0:T(8,128)}), f32[1,128,256]{2,1,0:T(8,128)S(1)}, s32[]{:S(2)}) async-start(f32[2,128,256]{2,1,0:T(8,128)} %param.10), calls=%async_computation.6 | async-start | bytes 262144 | tf_op jit(solution)/shard_map/slice | solution.py:72
  0.0 8.4 %copy-start.2 = (f32[2,256,256]{2,1,0:T(8,128)S(1)}, f32[2,256,256]{2,1,0:T(8,128)}, u32[]{:S(2)}) copy-start(f32[2,256,256]{2,1,0:T(8,128)} %param.9) | copy-start | bytes 1572868
  2.1 9.7 %all-to-all-start = ((f32[4,64,128]{2,1,0:T(8,128)}), f32[4,64,128]{2,1,0:T(8,128)S(1)}, u32[]{:S(2)}, u32[]{:S(2)}) async-start(f32[4,64,128]{2,1,0:T(8,128)} %bitcast.3), calls=%async_computation | async-start | bytes 262144 | tf_op jit(solution)/shard_map/all_to_all | solution.py:44
  7.0 1.8 %copy-start.6 = (f32[256,128]{1,0:T(8,128)S(1)}, f32[256,128]{1,0:T(8,128)}, u32[]{:S(2)}) copy-start(f32[256,128]{1,0:T(8,128)} %param.11) | copy-start | bytes 393220
  11.8 32.1 %copy-start.3 = (f32[512,256]{1,0:T(8,128)S(1)}, f32[512,256]{1,0:T(8,128)}, u32[]{:S(2)}) copy-start(f32[512,256]{1,0:T(8,128)} %param.6) | copy-start | bytes 1572868
  11.8 26.3 %all-to-all-start.1 = ((f32[4,704,128]{2,1,0:T(8,128)}), f32[4,704,128]{2,1,0:T(8,128)S(1)}, u32[]{:S(2)}, u32[]{:S(2)}) async-start(f32[4,704,128]{2,1,0:T(8,128)} %pad_maximum_fusion.1), calls=%async_computation.1 | async-start | bytes 2883584 | tf_op jit(solution)/shard_map/all_to_all | solution.py:44
  15.5 9.2 %collective-permute-start = (f32[64,128]{1,0:T(8,128)S(1)}, f32[64,128]{1,0:T(8,128)S(1)}, u32[]{:S(2)}, u32[]{:S(2)}) collective-permute-start(f32[64,128]{1,0:T(8,128)S(1)} %reduce_sum.27), channel_id=1, source_target_pairs={{0,32},{32,0},{1,33},{33,1},{2,34},{34,2},{3,35},{35,3},{4,36},{36... | collective-permute-start | bytes 98312 | tf_op jit(solution)/shard_map/ppermute | solution.py:40
  24.7 13.4 %collective-permute-start.1 = (f32[64,128]{1,0:T(8,128)S(1)}, f32[64,128]{1,0:T(8,128)S(1)}, u32[]{:S(2)}, u32[]{:S(2)}) collective-permute-start(f32[64,128]{1,0:T(8,128)S(1)} %add.81), channel_id=1, source_target_pairs={{0,64},{64,0},{1,65},{65,1},{2,66},{66,2},{3,67},{67,3},{4,68},{68... | collective-permute-start | bytes 98312 | tf_op jit(solution)/shard_map/ppermute | solution.py:40
  38.1 1.1 copy-start.4
  39.2 13.5 %all-to-all-start.2 = ((f32[16,16,256]{2,1,0:T(8,128)}), f32[16,16,256]{2,1,0:T(8,128)S(1)}, u32[]{:S(2)}, u32[]{:S(2)}) async-start(f32[16,16,256]{2,1,0:T(8,128)} %bitcast.17), calls=%async_computation.2 | async-start | bytes 524288 | tf_op jit(solution)/shard_map/all_to_all | solution.py:44
  43.9 18.9 %collective-permute-start.4 = (f32[512,256]{1,0:T(8,128)S(1)}, f32[512,256]{1,0:T(8,128)S(1)}, u32[]{:S(2)}, u32[]{:S(2)}) collective-permute-start(f32[512,256]{1,0:T(8,128)S(1)} %copy-done.3), channel_id=1, source_target_pairs={{0,384},{128,256},{256,128},{384,0},{1,385},{129,257},{257,129},{3... | collective-permute-start | bytes 1572872 | tf_op jit(solution)/shard_map/ppermute | solution.py:83
  48.7 14.1 %collective-permute-start.3 = (f32[512,256]{1,0:T(8,128)S(1)}, f32[512,256]{1,0:T(8,128)S(1)}, u32[]{:S(2)}, u32[]{:S(2)}) collective-permute-start(f32[512,256]{1,0:T(8,128)S(1)} %copy-done.3), channel_id=1, source_target_pairs={{0,128},{128,0},{256,384},{384,256},{1,129},{129,1},{257,385},{385... | collective-permute-start | bytes 1572872 | tf_op jit(solution)/shard_map/ppermute | solution.py:83
  52.7 10.0 %collective-permute-start.2 = (f32[16,256]{1,0:T(8,128)S(1)}, f32[16,256]{1,0:T(8,128)S(1)}, u32[]{:S(2)}, u32[]{:S(2)}) collective-permute-start(f32[16,256]{1,0:T(8,128)S(1)} %reduce_sum.28), channel_id=1, source_target_pairs={{0,16},{16,0},{1,17},{17,1},{2,18},{18,2},{3,19},{19,3},{4,20},{20... | collective-permute-start | bytes 49160 | tf_op jit(solution)/shard_map/ppermute | solution.py:40
  63.5 15.1 %all-to-all-start.3 = ((f32[16,16,256]{2,1,0:T(8,128)}), f32[16,16,256]{2,1,0:T(8,128)S(1)}, u32[]{:S(2)}, u32[]{:S(2)}) async-start(f32[16,16,256]{2,1,0:T(8,128)} %broadcast_in_dim.13), calls=%async_computation.3 | async-start | bytes 524288 | tf_op jit(solution)/shard_map/all_to_all | solution.py:44
  69.6 30.3 %collective-permute-start.7 = (f32[512,256]{1,0:T(8,128)S(1)}, f32[512,256]{1,0:T(8,128)}, u32[]{:S(2)}, u32[]{:S(2)}) collective-permute-start(f32[512,256]{1,0:T(8,128)S(1)} %copy-done.3), channel_id=1, source_target_pairs={{0,256},{128,384},{256,0},{384,128},{1,257},{129,385},{257,1},{385... | collective-permute-start | bytes 1572872 | tf_op jit(solution)/shard_map/ppermute | solution.py:83
  79.7 7.3 %collective-permute-start.5 = (f32[64,128]{1,0:T(8,128)}, f32[64,128]{1,0:T(8,128)S(1)}, u32[]{:S(2)}, u32[]{:S(2)}) collective-permute-start(f32[64,128]{1,0:T(8,128)} %fusion.13), channel_id=1, source_target_pairs={{0,32},{32,0},{1,33},{33,1},{2,34},{34,2},{3,35},{35,3},{4,36},{36... | collective-permute-start | bytes 98312 | tf_op jit(solution)/shard_map/ppermute | solution.py:40
  87.7 14.9 %collective-permute-start.6 = (f32[64,128]{1,0:T(8,128)S(1)}, f32[64,128]{1,0:T(8,128)S(1)}, u32[]{:S(2)}, u32[]{:S(2)}) collective-permute-start(f32[64,128]{1,0:T(8,128)S(1)} %add.86), channel_id=1, source_target_pairs={{0,64},{64,0},{1,65},{65,1},{2,66},{66,2},{3,67},{67,3},{4,68},{68... | collective-permute-start | bytes 98312 | tf_op jit(solution)/shard_map/ppermute | solution.py:40
  101.3 1.4 copy-start.5
  102.6 1.0 copy-start.1
  120.2 8.6 %collective-permute-start.8 = (f32[16,512]{1,0:T(8,128)S(1)}, f32[16,512]{1,0:T(8,128)S(1)}, u32[]{:S(2)}, u32[]{:S(2)}) collective-permute-start(f32[16,512]{1,0:T(8,128)S(1)} %reduce_sum.29), channel_id=1, source_target_pairs={{0,16},{16,0},{1,17},{17,1},{2,18},{18,2},{3,19},{19,3},{4,20},{20... | collective-permute-start | bytes 98312 | tf_op jit(solution)/shard_map/ppermute | solution.py:40
  147.7 7.3 %collective-permute-start.9 = (f32[2,2,16,128]{3,2,1,0:T(8,128)S(1)}, f32[2,2,16,128]{3,2,1,0:T(8,128)S(1)}, u32[]{:S(2)}, u32[]{:S(2)}) collective-permute-start(f32[2,2,16,128]{3,2,1,0:T(8,128)S(1)} %select_bitcast_fusion), channel_id=1, source_target_pairs={{0,32},{32,0},{1,33},{33,1},{2,34},{34,2},{3,35},{35,3},{4,36},{36... | collective-permute-start | bytes 98312 | tf_op jit(solution)/shard_map/ppermute | solution.py:40
  155.0 13.2 %collective-permute-start.10 = (f32[2,16,128]{2,1,0:T(8,128)S(1)}, f32[2,16,128]{2,1,0:T(8,128)S(1)}, u32[]{:S(2)}, u32[]{:S(2)}) collective-permute-start(f32[2,16,128]{2,1,0:T(8,128)S(1)} %select_bitcast_fusion.1), channel_id=1, source_target_pairs={{0,64},{64,0},{1,65},{65,1},{2,66},{66,2},{3,67},{67,3},{4,68},{68... | collective-permute-start | bytes 49160 | tf_op jit(solution)/shard_map/ppermute | solution.py:40

commit v18 on v16

--- a/solution.py
+++ b/solution.py
@@ -102,7 +102,7 @@
 
     first = solve(0) + solve(1)
     first = first + swap(first, "c")
-    first, far = lax.optimization_barrier((first, far))
+    first, flat, near, wrap = lax.optimization_barrier((first, flat, near, wrap))
     others = jnp.stack([flat, near, far, wrap])
     points_x = [lax.dynamic_index_in_dim(others, x ^ k, 0, keepdims=False) for k in range(4)]
     score = dot(jnp.concatenate(points_x, 0), centres.reshape(256, 256), 1, 1)

time: 169 us -> 168 us (level)
  starting transfers between devices: 105 us -> 100 us
  blocking collectives: 28.7 us -> 33.4 us
    ppermute x8, starting transfers between devices: 75.1 us -> 70.2 us  [swap(): return lax.ppermute(a, axis, [(0, 1), (1, 0)])]
    all_to_all x2, blocking collectives: 28.7 us -> 33.4 us  [exchange(): return lax.all_to_all(a, axes, 0, 0, tiled=True)]
where the time goes in v18:
time: 168 us; the launch traced here: 167 us
  starting transfers between devices  100 us (60%)
  blocking collectives  33.4 us (20%)
  waiting for transfers between devices  16.6 us (10%)
  matrix products  6.98 us (4%)
  local copies, waits for them, and re-layouts  5.81 us (3%)
  other arithmetic  3.28 us (2%)
    ppermute x8, starting transfers between devices, swap(): return lax.ppermute(a, axis, [(0, 1), (1, 0)])  70.2 us
    all_to_all x2, blocking collectives, exchange(): return lax.all_to_all(a, axes, 0, 0, tiled=True)  33.4 us
    all_to_all x4, starting transfers between devices, exchange(): return lax.all_to_all(a, axes, 0, 0, tiled=True)  19.3 us
    ppermute x3, starting transfers between devices, local(): lax.ppermute(flat, 'x', [(i, i ^ k) for i in range(4)])  10.5 us
    ppermute x8, waiting for transfers between devices, swap(): return lax.ppermute(a, axis, [(0, 1), (1, 0)])  9.07 us
    all_to_all x4, waiting for transfers between devices, exchange(): return lax.all_to_all(a, axes, 0, 0, tiled=True)  7.54 us
    dot_general x3, matrix products, dot(): lax.dot_general(a, b, (((ca,), (cb,)), ((), ())), precision=HIGH, preferr...  3.7 us
  transfers between devices with their start and end apart: 15, of which 9 were waited for; matrix products, arithmetic and copies ran while one was open for 6% of the time, Pallas kernels for 0%

profile of v18, /device:TPU:1, one launch (start us, length us, event | category | flops | bytes accessed | tf_op | source)
XLA Modules:
  0.0 166.6 jit_solution(6951135889437210240)
XLA Ops:
  0.0 1.3 fusion.19
  1.3 0.8 copy.19
  2.1 4.8 %all-to-all-start = ((f32[4,64,128]{2,1,0:T(8,128)}), f32[4,64,128]{2,1,0:T(8,128)S(1)}, u32[]{:S(2)}, u32[]{:S(2)}) async-start(f32[4,64,128]{2,1,0:T(8,128)} %bitcast.3), calls=%async_computation | async-start | bytes 262144 | tf_op jit(solution)/shard_map/all_to_all | solution.py:44
  7.0 1.2 fusion.33
  8.6 0.1 reshape.72
  8.8 1.2 pad_maximum_fusion.1
  10.0 1.7 %all-to-all-done = f32[4,64,128]{2,1,0:T(8,128)S(1)} async-done(((f32[4,64,128]{2,1,0:T(8,128)}), f32[4,64,128]{2,1,0:T(8,128)S(1)}, u32[]{:S(2)}, u32[]{:S(2)}) %all-to-all-start) | async-done | bytes 131104 | tf_op jit(solution)/shard_map/all_to_all | solution.py:44
  11.8 3.7 %all-to-all-start.1 = ((f32[4,704,128]{2,1,0:T(8,128)}), f32[4,704,128]{2,1,0:T(8,128)S(1)}, u32[]{:S(2)}, u32[]{:S(2)}) async-start(f32[4,704,128]{2,1,0:T(8,128)} %pad_maximum_fusion.1), calls=%async_computation.1 | async-start | bytes 2883584 | tf_op jit(solution)/shard_map/all_to_all | solution.py:44
  15.5 8.4 %collective-permute-start = (f32[64,128]{1,0:T(8,128)S(1)}, f32[64,128]{1,0:T(8,128)S(1)}, u32[]{:S(2)}, u32[]{:S(2)}) collective-permute-start(f32[64,128]{1,0:T(8,128)S(1)} %reduce_sum.27), channel_id=1, source_target_pairs={{0,32},{32,0},{1,33},{33,1},{2,34},{34,2},{3,35},{35,3},{4,36},{36... | collective-permute-start | bytes 98312 | tf_op jit(solution)/shard_map/ppermute | solution.py:40
  23.9 0.8 collective-permute-done
  24.7 11.1 %collective-permute-start.1 = (f32[64,128]{1,0:T(8,128)S(1)}, f32[64,128]{1,0:T(8,128)S(1)}, u32[]{:S(2)}, u32[]{:S(2)}) collective-permute-start(f32[64,128]{1,0:T(8,128)S(1)} %add.82), channel_id=1, source_target_pairs={{0,64},{64,0},{1,65},{65,1},{2,66},{66,2},{3,67},{67,3},{4,68},{68... | collective-permute-start | bytes 98312 | tf_op jit(solution)/shard_map/ppermute | solution.py:40
  35.8 2.3 %collective-permute-done.1 = f32[64,128]{1,0:T(8,128)S(1)} collective-permute-done((f32[64,128]{1,0:T(8,128)S(1)}, f32[64,128]{1,0:T(8,128)S(1)}, u32[]{:S(2)}, u32[]{:S(2)}) %collective-permute-start.1) | collective-permute-done | bytes 32800 | tf_op jit(solution)/shard_map/ppermute | solution.py:40
  38.1 1.1 convolution_bitcast_fusion
  39.2 4.7 %all-to-all-start.2 = ((f32[16,16,256]{2,1,0:T(8,128)}), f32[16,16,256]{2,1,0:T(8,128)S(1)}, u32[]{:S(2)}, u32[]{:S(2)}) async-start(f32[16,16,256]{2,1,0:T(8,128)} %bitcast.17), calls=%async_computation.2 | async-start | bytes 524288 | tf_op jit(solution)/shard_map/all_to_all | solution.py:44
  43.9 4.8 %collective-permute-start.4 = (f32[512,256]{1,0:T(8,128)S(1)}, f32[512,256]{1,0:T(8,128)S(1)}, u32[]{:S(2)}, u32[]{:S(2)}) collective-permute-start(f32[512,256]{1,0:T(8,128)S(1)} %copy-done.2), channel_id=1, source_target_pairs={{0,384},{128,256},{256,128},{384,0},{1,385},{129,257},{257,129},{3... | collective-permute-start | bytes 1572872 | tf_op jit(solution)/shard_map/ppermute | solution.py:83
  48.7 1.9 %collective-permute-start.3 = (f32[512,256]{1,0:T(8,128)S(1)}, f32[512,256]{1,0:T(8,128)S(1)}, u32[]{:S(2)}, u32[]{:S(2)}) collective-permute-start(f32[512,256]{1,0:T(8,128)S(1)} %copy-done.2), channel_id=1, source_target_pairs={{0,128},{128,0},{256,384},{384,256},{1,129},{129,1},{257,385},{385... | collective-permute-start | bytes 1572872 | tf_op jit(solution)/shard_map/ppermute | solution.py:83
  50.7 0.7 slice.65
  51.4 1.4 all-to-all-done.2
  52.7 8.9 %collective-permute-start.2 = (f32[16,256]{1,0:T(8,128)S(1)}, f32[16,256]{1,0:T(8,128)S(1)}, u32[]{:S(2)}, u32[]{:S(2)}) collective-permute-start(f32[16,256]{1,0:T(8,128)S(1)} %reduce_sum.28), channel_id=1, source_target_pairs={{0,16},{16,0},{1,17},{17,1},{2,18},{18,2},{3,19},{19,3},{4,20},{20... | collective-permute-start | bytes 49160 | tf_op jit(solution)/shard_map/ppermute | solution.py:40
  61.7 0.7 constant_dynamic-slice_fusion.1
  62.4 0.4 collective-permute-done.2
  62.8 0.7 broadcast_in_dim.13
  63.5 6.1 %all-to-all-start.3 = ((f32[16,16,256]{2,1,0:T(8,128)}), f32[16,16,256]{2,1,0:T(8,128)S(1)}, u32[]{:S(2)}, u32[]{:S(2)}) async-start(f32[16,16,256]{2,1,0:T(8,128)} %broadcast_in_dim.13), calls=%async_computation.3 | async-start | bytes 524288 | tf_op jit(solution)/shard_map/all_to_all | solution.py:44
  69.6 3.8 %collective-permute-start.7 = (f32[512,256]{1,0:T(8,128)S(1)}, f32[512,256]{1,0:T(8,128)}, u32[]{:S(2)}, u32[]{:S(2)}) collective-permute-start(f32[512,256]{1,0:T(8,128)S(1)} %copy-done.2), channel_id=1, source_target_pairs={{0,256},{128,384},{256,0},{384,128},{1,257},{129,385},{257,1},{385... | collective-permute-start | bytes 1572872 | tf_op jit(solution)/shard_map/ppermute | solution.py:83
  73.5 0.7 slice.71
  74.1 4.5 %all-to-all-done.3 = f32[16,16,256]{2,1,0:T(8,128)S(1)} async-done(((f32[16,16,256]{2,1,0:T(8,128)}), f32[16,16,256]{2,1,0:T(8,128)S(1)}, u32[]{:S(2)}, u32[]{:S(2)}) %all-to-all-start.3) | async-done | bytes 262176 | tf_op jit(solution)/shard_map/all_to_all | solution.py:44
  78.6 0.3 convolution_bitcast_fusion.4
  78.8 0.3 fusion.13
  79.1 6.2 %collective-permute-start.5 = (f32[64,128]{1,0:T(8,128)S(1)}, f32[64,128]{1,0:T(8,128)S(1)}, u32[]{:S(2)}, u32[]{:S(2)}) collective-permute-start(f32[64,128]{1,0:T(8,128)S(1)} %fusion.13), channel_id=1, source_target_pairs={{0,32},{32,0},{1,33},{33,1},{2,34},{34,2},{3,35},{35,3},{4,36},{36... | collective-permute-start | bytes 98312 | tf_op jit(solution)/shard_map/ppermute | solution.py:40
  85.3 0.8 constant_dynamic-slice_fusion
  86.1 0.6 copy.37
  86.7 12.2 %collective-permute-start.6 = (f32[64,128]{1,0:T(8,128)S(1)}, f32[64,128]{1,0:T(8,128)S(1)}, u32[]{:S(2)}, u32[]{:S(2)}) collective-permute-start(f32[64,128]{1,0:T(8,128)S(1)} %add.87), channel_id=1, source_target_pairs={{0,64},{64,0},{1,65},{65,1},{2,66},{66,2},{3,67},{67,3},{4,68},{68... | collective-permute-start | bytes 98312 | tf_op jit(solution)/shard_map/ppermute | solution.py:40
  98.9 1.2 pad_maximum_fusion
  100.1 0.1 dynamic-slice_bitcast_fusion.3
  100.3 1.3 fusion.1
  101.6 0.5 fusion.29
  102.1 0.4 fusion
  102.6 16.8 %all_to_all.30 = f32[16,16,512]{2,1,0:T(8,128)S(1)} all-to-all(f32[16,16,512]{2,1,0:T(8,128)S(1)} %bitcast.110), channel_id=1, replica_groups=mesh['x'=4,'h'=2,'c'=2,'w'=2,'z'=4,'y'=4] {'z','y'}, dimensions={0} | all-to-all | bytes 1048576 | tf_op jit(solution)/shard_map/all_to_all | solution.py:44
  119.5 6.6 %collective-permute-start.8 = (f32[16,512]{1,0:T(8,128)S(1)}, f32[16,512]{1,0:T(8,128)S(1)}, u32[]{:S(2)}, u32[]{:S(2)}) collective-permute-start(f32[16,512]{1,0:T(8,128)S(1)} %reduce_sum.29), channel_id=1, source_target_pairs={{0,16},{16,0},{1,17},{17,1},{2,18},{18,2},{3,19},{19,3},{4,20},{20... | collective-permute-start | bytes 98312 | tf_op jit(solution)/shard_map/ppermute | solution.py:40
  126.1 2.0 %collective-permute-done.8 = f32[16,512]{1,0:T(8,128)S(1)} collective-permute-done((f32[16,512]{1,0:T(8,128)S(1)}, f32[16,512]{1,0:T(8,128)S(1)}, u32[]{:S(2)}, u32[]{:S(2)}) %collective-permute-start.8) | collective-permute-done | bytes 32800 | tf_op jit(solution)/shard_map/ppermute | solution.py:40
  128.2 16.5 %all_to_all.31 = f32[16,16,512]{2,1,0:T(8,128)S(1)} all-to-all(f32[16,16,512]{2,1,0:T(8,128)S(1)} %broadcast_in_dim.14), channel_id=1, replica_groups=mesh['x'=4,'h'=2,'c'=2,'w'=2,'z'=4,'y'=4] {'z','y'}, dimensions={0} | all-to-all | bytes 1048576 | tf_op jit(solution)/shard_map/all_to_all | solution.py:44
  144.8 0.3 convolution_bitcast_fusion.1
  145.1 0.3 fusion.12
  145.5 6.4 %collective-permute-start.9 = (f32[2,2,16,128]{3,2,1,0:T(8,128)S(1)}, f32[2,2,16,128]{3,2,1,0:T(8,128)S(1)}, u32[]{:S(2)}, u32[]{:S(2)}) collective-permute-start(f32[2,2,16,128]{3,2,1,0:T(8,128)S(1)} %select_bitcast_fusion), channel_id=1, source_target_pairs={{0,32},{32,0},{1,33},{33,1},{2,34},{34,2},{3,35},{35,3},{4,36},{36... | collective-permute-start | bytes 98312 | tf_op jit(solution)/shard_map/ppermute | solution.py:40
  152.0 0.8 collective-permute-done.9
  152.8 10.4 %collective-permute-start.10 = (f32[2,16,128]{2,1,0:T(8,128)S(1)}, f32[2,16,128]{2,1,0:T(8,128)S(1)}, u32[]{:S(2)}, u32[]{:S(2)}) collective-permute-start(f32[2,16,128]{2,1,0:T(8,128)S(1)} %select_bitcast_fusion.1), channel_id=1, source_target_pairs={{0,64},{64,0},{1,65},{65,1},{2,66},{66,2},{3,67},{67,3},{4,68},{68... | collective-permute-start | bytes 49160 | tf_op jit(solution)/shard_map/ppermute | solution.py:40
  163.3 2.8 %collective-permute-done.10 = f32[2,16,128]{2,1,0:T(8,128)S(1)} collective-permute-done((f32[2,16,128]{2,1,0:T(8,128)S(1)}, f32[2,16,128]{2,1,0:T(8,128)S(1)}, u32[]{:S(2)}, u32[]{:S(2)}) %collective-permute-start.10) | collective-permute-done | bytes 16416 | tf_op jit(solution)/shard_map/ppermute | solution.py:40
  166.0 0.6 fusion.45
  (56 shorter events, 0.8 us)
Async XLA Ops:
  0.0 100.3 %copy-start = (f32[2,128,256]{2,1,0:T(8,128)S(1)}, f32[2,128,256]{2,1,0:T(8,128)}, u32[]{:S(2)}) copy-start(f32[2,128,256]{2,1,0:T(8,128)} %param.8) | copy-start | bytes 786436
  0.0 8.3 %slice-start = ((f32[2,128,256]{2,1,0:T(8,128)}), f32[1,128,256]{2,1,0:T(8,128)S(1)}, s32[]{:S(2)}) async-start(f32[2,128,256]{2,1,0:T(8,128)} %param.10), calls=%async_computation.6 | async-start | bytes 262144 | tf_op jit(solution)/shard_map/slice | solution.py:72
  0.0 8.4 %copy-start.1 = (f32[2,256,256]{2,1,0:T(8,128)S(1)}, f32[2,256,256]{2,1,0:T(8,128)}, u32[]{:S(2)}) copy-start(f32[2,256,256]{2,1,0:T(8,128)} %param.9) | copy-start | bytes 1572868
  2.1 9.7 %all-to-all-start = ((f32[4,64,128]{2,1,0:T(8,128)}), f32[4,64,128]{2,1,0:T(8,128)S(1)}, u32[]{:S(2)}, u32[]{:S(2)}) async-start(f32[4,64,128]{2,1,0:T(8,128)} %bitcast.3), calls=%async_computation | async-start | bytes 262144 | tf_op jit(solution)/shard_map/all_to_all | solution.py:44
  7.0 1.8 %copy-start.5 = (f32[256,128]{1,0:T(8,128)S(1)}, f32[256,128]{1,0:T(8,128)}, u32[]{:S(2)}) copy-start(f32[256,128]{1,0:T(8,128)} %param.11) | copy-start | bytes 393220
  11.8 32.1 %copy-start.2 = (f32[512,256]{1,0:T(8,128)S(1)}, f32[512,256]{1,0:T(8,128)}, u32[]{:S(2)}) copy-start(f32[512,256]{1,0:T(8,128)} %param.6) | copy-start | bytes 1572868
  11.8 26.3 %all-to-all-start.1 = ((f32[4,704,128]{2,1,0:T(8,128)}), f32[4,704,128]{2,1,0:T(8,128)S(1)}, u32[]{:S(2)}, u32[]{:S(2)}) async-start(f32[4,704,128]{2,1,0:T(8,128)} %pad_maximum_fusion.1), calls=%async_computation.1 | async-start | bytes 2883584 | tf_op jit(solution)/shard_map/all_to_all | solution.py:44
  15.5 9.2 %collective-permute-start = (f32[64,128]{1,0:T(8,128)S(1)}, f32[64,128]{1,0:T(8,128)S(1)}, u32[]{:S(2)}, u32[]{:S(2)}) collective-permute-start(f32[64,128]{1,0:T(8,128)S(1)} %reduce_sum.27), channel_id=1, source_target_pairs={{0,32},{32,0},{1,33},{33,1},{2,34},{34,2},{3,35},{35,3},{4,36},{36... | collective-permute-start | bytes 98312 | tf_op jit(solution)/shard_map/ppermute | solution.py:40
  24.7 13.4 %collective-permute-start.1 = (f32[64,128]{1,0:T(8,128)S(1)}, f32[64,128]{1,0:T(8,128)S(1)}, u32[]{:S(2)}, u32[]{:S(2)}) collective-permute-start(f32[64,128]{1,0:T(8,128)S(1)} %add.82), channel_id=1, source_target_pairs={{0,64},{64,0},{1,65},{65,1},{2,66},{66,2},{3,67},{67,3},{4,68},{68... | collective-permute-start | bytes 98312 | tf_op jit(solution)/shard_map/ppermute | solution.py:40
  38.1 1.1 copy-start.3
  39.2 13.5 %all-to-all-start.2 = ((f32[16,16,256]{2,1,0:T(8,128)}), f32[16,16,256]{2,1,0:T(8,128)S(1)}, u32[]{:S(2)}, u32[]{:S(2)}) async-start(f32[16,16,256]{2,1,0:T(8,128)} %bitcast.17), calls=%async_computation.2 | async-start | bytes 524288 | tf_op jit(solution)/shard_map/all_to_all | solution.py:44
  43.9 18.9 %collective-permute-start.4 = (f32[512,256]{1,0:T(8,128)S(1)}, f32[512,256]{1,0:T(8,128)S(1)}, u32[]{:S(2)}, u32[]{:S(2)}) collective-permute-start(f32[512,256]{1,0:T(8,128)S(1)} %copy-done.2), channel_id=1, source_target_pairs={{0,384},{128,256},{256,128},{384,0},{1,385},{129,257},{257,129},{3... | collective-permute-start | bytes 1572872 | tf_op jit(solution)/shard_map/ppermute | solution.py:83
  48.7 14.1 %collective-permute-start.3 = (f32[512,256]{1,0:T(8,128)S(1)}, f32[512,256]{1,0:T(8,128)S(1)}, u32[]{:S(2)}, u32[]{:S(2)}) collective-permute-start(f32[512,256]{1,0:T(8,128)S(1)} %copy-done.2), channel_id=1, source_target_pairs={{0,128},{128,0},{256,384},{384,256},{1,129},{129,1},{257,385},{385... | collective-permute-start | bytes 1572872 | tf_op jit(solution)/shard_map/ppermute | solution.py:83
  52.7 10.0 %collective-permute-start.2 = (f32[16,256]{1,0:T(8,128)S(1)}, f32[16,256]{1,0:T(8,128)S(1)}, u32[]{:S(2)}, u32[]{:S(2)}) collective-permute-start(f32[16,256]{1,0:T(8,128)S(1)} %reduce_sum.28), channel_id=1, source_target_pairs={{0,16},{16,0},{1,17},{17,1},{2,18},{18,2},{3,19},{19,3},{4,20},{20... | collective-permute-start | bytes 49160 | tf_op jit(solution)/shard_map/ppermute | solution.py:40
  63.5 15.1 %all-to-all-start.3 = ((f32[16,16,256]{2,1,0:T(8,128)}), f32[16,16,256]{2,1,0:T(8,128)S(1)}, u32[]{:S(2)}, u32[]{:S(2)}) async-start(f32[16,16,256]{2,1,0:T(8,128)} %broadcast_in_dim.13), calls=%async_computation.3 | async-start | bytes 524288 | tf_op jit(solution)/shard_map/all_to_all | solution.py:44
  69.6 29.3 %collective-permute-start.7 = (f32[512,256]{1,0:T(8,128)S(1)}, f32[512,256]{1,0:T(8,128)}, u32[]{:S(2)}, u32[]{:S(2)}) collective-permute-start(f32[512,256]{1,0:T(8,128)S(1)} %copy-done.2), channel_id=1, source_target_pairs={{0,256},{128,384},{256,0},{384,128},{1,257},{129,385},{257,1},{385... | collective-permute-start | bytes 1572872 | tf_op jit(solution)/shard_map/ppermute | solution.py:83
  79.1 7.6 %collective-permute-start.5 = (f32[64,128]{1,0:T(8,128)S(1)}, f32[64,128]{1,0:T(8,128)S(1)}, u32[]{:S(2)}, u32[]{:S(2)}) collective-permute-start(f32[64,128]{1,0:T(8,128)S(1)} %fusion.13), channel_id=1, source_target_pairs={{0,32},{32,0},{1,33},{33,1},{2,34},{34,2},{3,35},{35,3},{4,36},{36... | collective-permute-start | bytes 98312 | tf_op jit(solution)/shard_map/ppermute | solution.py:40
  86.7 14.8 %collective-permute-start.6 = (f32[64,128]{1,0:T(8,128)S(1)}, f32[64,128]{1,0:T(8,128)S(1)}, u32[]{:S(2)}, u32[]{:S(2)}) collective-permute-start(f32[64,128]{1,0:T(8,128)S(1)} %add.87), channel_id=1, source_target_pairs={{0,64},{64,0},{1,65},{65,1},{2,66},{66,2},{3,67},{67,3},{4,68},{68... | collective-permute-start | bytes 98312 | tf_op jit(solution)/shard_map/ppermute | solution.py:40
  100.3 1.3 copy-start.4
  102.1 26.0 %copy-start.6 = (f32[4,2,8,128]{3,2,0,1:T(8,128)S(1)}, f32[4,2,8,128]{3,2,0,1:T(8,128)}, u32[]{:S(2)}) copy-start(f32[4,2,8,128]{3,2,0,1:T(8,128)} %copy.37) | copy-start | bytes 98308
  119.5 8.6 %collective-permute-start.8 = (f32[16,512]{1,0:T(8,128)S(1)}, f32[16,512]{1,0:T(8,128)S(1)}, u32[]{:S(2)}, u32[]{:S(2)}) collective-permute-start(f32[16,512]{1,0:T(8,128)S(1)} %reduce_sum.29), channel_id=1, source_target_pairs={{0,16},{16,0},{1,17},{17,1},{2,18},{18,2},{3,19},{19,3},{4,20},{20... | collective-permute-start | bytes 98312 | tf_op jit(solution)/shard_map/ppermute | solution.py:40
  145.5 7.3 %collective-permute-start.9 = (f32[2,2,16,128]{3,2,1,0:T(8,128)S(1)}, f32[2,2,16,128]{3,2,1,0:T(8,128)S(1)}, u32[]{:S(2)}, u32[]{:S(2)}) collective-permute-start(f32[2,2,16,128]{3,2,1,0:T(8,128)S(1)} %select_bitcast_fusion), channel_id=1, source_target_pairs={{0,32},{32,0},{1,33},{33,1},{2,34},{34,2},{3,35},{35,3},{4,36},{36... | collective-permute-start | bytes 98312 | tf_op jit(solution)/shard_map/ppermute | solution.py:40
  152.8 13.2 %collective-permute-start.10 = (f32[2,16,128]{2,1,0:T(8,128)S(1)}, f32[2,16,128]{2,1,0:T(8,128)S(1)}, u32[]{:S(2)}, u32[]{:S(2)}) collective-permute-start(f32[2,16,128]{2,1,0:T(8,128)S(1)} %select_bitcast_fusion.1), channel_id=1, source_target_pairs={{0,64},{64,0},{1,65},{65,1},{2,66},{66,2},{3,67},{67,3},{4,68},{68... | collective-permute-start | bytes 49160 | tf_op jit(solution)/shard_map/ppermute | solution.py:40

commit v19 on v18

--- a/solution.py
+++ b/solution.py
@@ -88,7 +88,7 @@
     coeff = lax.dynamic_slice(coeff, (z, 0, y * 16, 0), (1, 2, 16, 128))
     coeff = coeff.reshape(2, 16, 128).transpose(1, 0, 2).reshape(16, 256)
     rest = (coeff - carried) - swap(carried, "w")
-    rest, near, wrap = lax.optimization_barrier((rest, near, wrap))
+    rest, near, wrap, target = lax.optimization_barrier((rest, near, wrap, target))
     rest = exchange(copies(rest, 16), zy).reshape(4, 64, 256)
 
     def solve(side):

time: 168 us -> 170 us (1.012)
  no operation moved by 1% of the time
where the time goes in v19:
time: 170 us; the launch traced here: 169 us
  starting transfers between devices  100 us (59%)
  blocking collectives  34 us (20%)
  waiting for transfers between devices  16.9 us (10%)
  matrix products  7.59 us (4%)
  local copies, waits for them, and re-layouts  5.77 us (3%)
  other arithmetic  4.04 us (2%)
    ppermute x8, starting transfers between devices, swap(): return lax.ppermute(a, axis, [(0, 1), (1, 0)])  69.6 us
    all_to_all x2, blocking collectives, exchange(): return lax.all_to_all(a, axes, 0, 0, tiled=True)  34 us
    all_to_all x4, starting transfers between devices, exchange(): return lax.all_to_all(a, axes, 0, 0, tiled=True)  19.9 us
    ppermute x3, starting transfers between devices, local(): lax.ppermute(flat, 'x', [(i, i ^ k) for i in range(4)])  10.4 us
    ppermute x8, waiting for transfers between devices, swap(): return lax.ppermute(a, axis, [(0, 1), (1, 0)])  9.32 us
    all_to_all x4, waiting for transfers between devices, exchange(): return lax.all_to_all(a, axes, 0, 0, tiled=True)  7.57 us
    dot_general x3, matrix products, dot(): lax.dot_general(a, b, (((ca,), (cb,)), ((), ())), precision=HIGH, preferr...  3.7 us
  transfers between devices with their start and end apart: 15, of which 9 were waited for; matrix products, arithmetic and copies ran while one was open for 6% of the time, Pallas kernels for 0%

profile of v19, /device:TPU:1, one launch (start us, length us, event | category | flops | bytes accessed | tf_op | source)
XLA Modules:
  0.0 168.8 jit_solution(15683181986239582524)
XLA Ops:
  0.0 1.3 fusion.19
  1.3 0.8 copy.19
  2.1 4.8 %all-to-all-start = ((f32[4,64,128]{2,1,0:T(8,128)}), f32[4,64,128]{2,1,0:T(8,128)S(1)}, u32[]{:S(2)}, u32[]{:S(2)}) async-start(f32[4,64,128]{2,1,0:T(8,128)} %bitcast.3), calls=%async_computation | async-start | bytes 262144 | tf_op jit(solution)/shard_map/all_to_all | solution.py:44
  7.0 1.2 fusion.33
  8.4 0.1 reshape.72
  8.8 1.2 pad_maximum_fusion.1
  10.0 1.7 %all-to-all-done = f32[4,64,128]{2,1,0:T(8,128)S(1)} async-done(((f32[4,64,128]{2,1,0:T(8,128)}), f32[4,64,128]{2,1,0:T(8,128)S(1)}, u32[]{:S(2)}, u32[]{:S(2)}) %all-to-all-start) | async-done | bytes 131104 | tf_op jit(solution)/shard_map/all_to_all | solution.py:44
  11.8 3.7 %all-to-all-start.1 = ((f32[4,704,128]{2,1,0:T(8,128)}), f32[4,704,128]{2,1,0:T(8,128)S(1)}, u32[]{:S(2)}, u32[]{:S(2)}) async-start(f32[4,704,128]{2,1,0:T(8,128)} %pad_maximum_fusion.1), calls=%async_computation.1 | async-start | bytes 2883584 | tf_op jit(solution)/shard_map/all_to_all | solution.py:44
  15.5 8.4 %collective-permute-start = (f32[64,128]{1,0:T(8,128)S(1)}, f32[64,128]{1,0:T(8,128)S(1)}, u32[]{:S(2)}, u32[]{:S(2)}) collective-permute-start(f32[64,128]{1,0:T(8,128)S(1)} %reduce_sum.27), channel_id=1, source_target_pairs={{0,32},{32,0},{1,33},{33,1},{2,34},{34,2},{3,35},{35,3},{4,36},{36... | collective-permute-start | bytes 98312 | tf_op jit(solution)/shard_map/ppermute | solution.py:40
  23.9 0.8 collective-permute-done
  24.7 11.1 %collective-permute-start.1 = (f32[64,128]{1,0:T(8,128)S(1)}, f32[64,128]{1,0:T(8,128)S(1)}, u32[]{:S(2)}, u32[]{:S(2)}) collective-permute-start(f32[64,128]{1,0:T(8,128)S(1)} %add.82), channel_id=1, source_target_pairs={{0,64},{64,0},{1,65},{65,1},{2,66},{66,2},{3,67},{67,3},{4,68},{68... | collective-permute-start | bytes 98312 | tf_op jit(solution)/shard_map/ppermute | solution.py:40
  35.8 2.3 %collective-permute-done.1 = f32[64,128]{1,0:T(8,128)S(1)} collective-permute-done((f32[64,128]{1,0:T(8,128)S(1)}, f32[64,128]{1,0:T(8,128)S(1)}, u32[]{:S(2)}, u32[]{:S(2)}) %collective-permute-start.1) | collective-permute-done | bytes 32800 | tf_op jit(solution)/shard_map/ppermute | solution.py:40
  38.1 1.1 convolution_bitcast_fusion
  39.2 4.7 %all-to-all-start.2 = ((f32[16,16,256]{2,1,0:T(8,128)}), f32[16,16,256]{2,1,0:T(8,128)S(1)}, u32[]{:S(2)}, u32[]{:S(2)}) async-start(f32[16,16,256]{2,1,0:T(8,128)} %bitcast.17), calls=%async_computation.2 | async-start | bytes 524288 | tf_op jit(solution)/shard_map/all_to_all | solution.py:44
  43.9 3.6 %collective-permute-start.3 = (f32[512,256]{1,0:T(8,128)S(1)}, f32[512,256]{1,0:T(8,128)S(1)}, u32[]{:S(2)}, u32[]{:S(2)}) collective-permute-start(f32[512,256]{1,0:T(8,128)S(1)} %copy-done.2), channel_id=1, source_target_pairs={{0,128},{128,0},{256,384},{384,256},{1,129},{129,1},{257,385},{385... | collective-permute-start | bytes 1572872 | tf_op jit(solution)/shard_map/ppermute | solution.py:83
  47.5 3.7 %collective-permute-start.4 = (f32[512,256]{1,0:T(8,128)S(1)}, f32[512,256]{1,0:T(8,128)S(1)}, u32[]{:S(2)}, u32[]{:S(2)}) collective-permute-start(f32[512,256]{1,0:T(8,128)S(1)} %copy-done.2), channel_id=1, source_target_pairs={{0,384},{128,256},{256,128},{384,0},{1,385},{129,257},{257,129},{3... | collective-permute-start | bytes 1572872 | tf_op jit(solution)/shard_map/ppermute | solution.py:83
  51.2 0.7 slice.65
  51.9 0.6 constant_dynamic-slice_fusion
  52.6 0.2 all-to-all-done.2
  52.7 8.9 %collective-permute-start.2 = (f32[16,256]{1,0:T(8,128)S(1)}, f32[16,256]{1,0:T(8,128)S(1)}, u32[]{:S(2)}, u32[]{:S(2)}) collective-permute-start(f32[16,256]{1,0:T(8,128)S(1)} %reduce_sum.28), channel_id=1, source_target_pairs={{0,16},{16,0},{1,17},{17,1},{2,18},{18,2},{3,19},{19,3},{4,20},{20... | collective-permute-start | bytes 49160 | tf_op jit(solution)/shard_map/ppermute | solution.py:40
  61.7 0.7 constant_dynamic-slice_fusion.1
  62.4 1.4 copy.37
  63.8 0.7 broadcast_in_dim.13
  64.5 6.7 %all-to-all-start.3 = ((f32[16,16,256]{2,1,0:T(8,128)}), f32[16,16,256]{2,1,0:T(8,128)S(1)}, u32[]{:S(2)}, u32[]{:S(2)}) async-start(f32[16,16,256]{2,1,0:T(8,128)} %broadcast_in_dim.13), calls=%async_computation.3 | async-start | bytes 524288 | tf_op jit(solution)/shard_map/all_to_all | solution.py:44
  71.3 3.1 %collective-permute-start.7 = (f32[512,256]{1,0:T(8,128)S(1)}, f32[512,256]{1,0:T(8,128)}, u32[]{:S(2)}, u32[]{:S(2)}) collective-permute-start(f32[512,256]{1,0:T(8,128)S(1)} %copy-done.2), channel_id=1, source_target_pairs={{0,256},{128,384},{256,0},{384,128},{1,257},{129,385},{257,1},{385... | collective-permute-start | bytes 1572872 | tf_op jit(solution)/shard_map/ppermute | solution.py:83
  74.5 5.7 %all-to-all-done.3 = f32[16,16,256]{2,1,0:T(8,128)S(1)} async-done(((f32[16,16,256]{2,1,0:T(8,128)}), f32[16,16,256]{2,1,0:T(8,128)S(1)}, u32[]{:S(2)}, u32[]{:S(2)}) %all-to-all-start.3) | async-done | bytes 262176 | tf_op jit(solution)/shard_map/all_to_all | solution.py:44
  80.1 0.3 convolution_bitcast_fusion.4
  80.4 0.9 fusion.13
  81.3 5.5 %collective-permute-start.5 = (f32[64,128]{1,0:T(8,128)}, f32[64,128]{1,0:T(8,128)S(1)}, u32[]{:S(2)}, u32[]{:S(2)}) collective-permute-start(f32[64,128]{1,0:T(8,128)} %fusion.13), channel_id=1, source_target_pairs={{0,32},{32,0},{1,33},{33,1},{2,34},{34,2},{3,35},{35,3},{4,36},{36... | collective-permute-start | bytes 98312 | tf_op jit(solution)/shard_map/ppermute | solution.py:40
  86.8 1.0 collective-permute-done.5
  87.8 0.8 add.87
  88.6 12.1 %collective-permute-start.6 = (f32[64,128]{1,0:T(8,128)S(1)}, f32[64,128]{1,0:T(8,128)S(1)}, u32[]{:S(2)}, u32[]{:S(2)}) collective-permute-start(f32[64,128]{1,0:T(8,128)S(1)} %add.87), channel_id=1, source_target_pairs={{0,64},{64,0},{1,65},{65,1},{2,66},{66,2},{3,67},{67,3},{4,68},{68... | collective-permute-start | bytes 98312 | tf_op jit(solution)/shard_map/ppermute | solution.py:40
  100.7 1.2 pad_maximum_fusion
  101.9 0.1 dynamic-slice_bitcast_fusion.3
  102.0 1.3 fusion.1
  103.4 0.5 fusion.29
  103.9 0.4 fusion
  104.4 16.5 %all_to_all.30 = f32[16,16,512]{2,1,0:T(8,128)S(1)} all-to-all(f32[16,16,512]{2,1,0:T(8,128)S(1)} %bitcast.110), channel_id=1, replica_groups=mesh['x'=4,'h'=2,'c'=2,'w'=2,'z'=4,'y'=4] {'z','y'}, dimensions={0} | all-to-all | bytes 1048576 | tf_op jit(solution)/shard_map/all_to_all | solution.py:44
  120.9 7.4 %collective-permute-start.8 = (f32[16,512]{1,0:T(8,128)S(1)}, f32[16,512]{1,0:T(8,128)S(1)}, u32[]{:S(2)}, u32[]{:S(2)}) collective-permute-start(f32[16,512]{1,0:T(8,128)S(1)} %reduce_sum.29), channel_id=1, source_target_pairs={{0,16},{16,0},{1,17},{17,1},{2,18},{18,2},{3,19},{19,3},{4,20},{20... | collective-permute-start | bytes 98312 | tf_op jit(solution)/shard_map/ppermute | solution.py:40
  128.3 1.3 collective-permute-done.8
  129.6 17.5 %all_to_all.31 = f32[16,16,512]{2,1,0:T(8,128)S(1)} all-to-all(f32[16,16,512]{2,1,0:T(8,128)S(1)} %broadcast_in_dim.14), channel_id=1, replica_groups=mesh['x'=4,'h'=2,'c'=2,'w'=2,'z'=4,'y'=4] {'z','y'}, dimensions={0} | all-to-all | bytes 1048576 | tf_op jit(solution)/shard_map/all_to_all | solution.py:44
  147.2 0.3 convolution_bitcast_fusion.1
  147.6 0.3 fusion.12
  148.0 6.2 %collective-permute-start.9 = (f32[2,2,16,128]{3,2,1,0:T(8,128)S(1)}, f32[2,2,16,128]{3,2,1,0:T(8,128)S(1)}, u32[]{:S(2)}, u32[]{:S(2)}) collective-permute-start(f32[2,2,16,128]{3,2,1,0:T(8,128)S(1)} %select_bitcast_fusion), channel_id=1, source_target_pairs={{0,32},{32,0},{1,33},{33,1},{2,34},{34,2},{3,35},{35,3},{4,36},{36... | collective-permute-start | bytes 98312 | tf_op jit(solution)/shard_map/ppermute | solution.py:40
  154.1 0.8 collective-permute-done.9
  155.0 10.2 %collective-permute-start.10 = (f32[2,16,128]{2,1,0:T(8,128)S(1)}, f32[2,16,128]{2,1,0:T(8,128)S(1)}, u32[]{:S(2)}, u32[]{:S(2)}) collective-permute-start(f32[2,16,128]{2,1,0:T(8,128)S(1)} %select_bitcast_fusion.1), channel_id=1, source_target_pairs={{0,64},{64,0},{1,65},{65,1},{2,66},{66,2},{3,67},{67,3},{4,68},{68... | collective-permute-start | bytes 49160 | tf_op jit(solution)/shard_map/ppermute | solution.py:40
  165.2 3.0 %collective-permute-done.10 = f32[2,16,128]{2,1,0:T(8,128)S(1)} collective-permute-done((f32[2,16,128]{2,1,0:T(8,128)S(1)}, f32[2,16,128]{2,1,0:T(8,128)S(1)}, u32[]{:S(2)}, u32[]{:S(2)}) %collective-permute-start.10) | collective-permute-done | bytes 16416 | tf_op jit(solution)/shard_map/ppermute | solution.py:40
  168.2 0.6 fusion.45
  (56 shorter events, 0.9 us)
Async XLA Ops:
  0.0 102.0 %copy-start = (f32[2,128,256]{2,1,0:T(8,128)S(1)}, f32[2,128,256]{2,1,0:T(8,128)}, u32[]{:S(2)}) copy-start(f32[2,128,256]{2,1,0:T(8,128)} %param.8) | copy-start | bytes 786436
  0.0 8.3 %copy-start.1 = (f32[2,256,256]{2,1,0:T(8,128)S(1)}, f32[2,256,256]{2,1,0:T(8,128)}, u32[]{:S(2)}) copy-start(f32[2,256,256]{2,1,0:T(8,128)} %param.9) | copy-start | bytes 1572868
  0.0 8.6 %slice-start = ((f32[2,128,256]{2,1,0:T(8,128)}), f32[1,128,256]{2,1,0:T(8,128)S(1)}, s32[]{:S(2)}) async-start(f32[2,128,256]{2,1,0:T(8,128)} %param.10), calls=%async_computation.6 | async-start | bytes 262144 | tf_op jit(solution)/shard_map/slice | solution.py:72
  2.1 9.7 %all-to-all-start = ((f32[4,64,128]{2,1,0:T(8,128)}), f32[4,64,128]{2,1,0:T(8,128)S(1)}, u32[]{:S(2)}, u32[]{:S(2)}) async-start(f32[4,64,128]{2,1,0:T(8,128)} %bitcast.3), calls=%async_computation | async-start | bytes 262144 | tf_op jit(solution)/shard_map/all_to_all | solution.py:44
  7.0 1.8 %copy-start.5 = (f32[256,128]{1,0:T(8,128)S(1)}, f32[256,128]{1,0:T(8,128)}, u32[]{:S(2)}) copy-start(f32[256,128]{1,0:T(8,128)} %param.11) | copy-start | bytes 393220
  11.8 32.1 %copy-start.2 = (f32[512,256]{1,0:T(8,128)S(1)}, f32[512,256]{1,0:T(8,128)}, u32[]{:S(2)}) copy-start(f32[512,256]{1,0:T(8,128)} %param.6) | copy-start | bytes 1572868
  11.8 26.3 %all-to-all-start.1 = ((f32[4,704,128]{2,1,0:T(8,128)}), f32[4,704,128]{2,1,0:T(8,128)S(1)}, u32[]{:S(2)}, u32[]{:S(2)}) async-start(f32[4,704,128]{2,1,0:T(8,128)} %pad_maximum_fusion.1), calls=%async_computation.1 | async-start | bytes 2883584 | tf_op jit(solution)/shard_map/all_to_all | solution.py:44
  15.5 9.2 %collective-permute-start = (f32[64,128]{1,0:T(8,128)S(1)}, f32[64,128]{1,0:T(8,128)S(1)}, u32[]{:S(2)}, u32[]{:S(2)}) collective-permute-start(f32[64,128]{1,0:T(8,128)S(1)} %reduce_sum.27), channel_id=1, source_target_pairs={{0,32},{32,0},{1,33},{33,1},{2,34},{34,2},{3,35},{35,3},{4,36},{36... | collective-permute-start | bytes 98312 | tf_op jit(solution)/shard_map/ppermute | solution.py:40
  24.7 13.4 %collective-permute-start.1 = (f32[64,128]{1,0:T(8,128)S(1)}, f32[64,128]{1,0:T(8,128)S(1)}, u32[]{:S(2)}, u32[]{:S(2)}) collective-permute-start(f32[64,128]{1,0:T(8,128)S(1)} %add.82), channel_id=1, source_target_pairs={{0,64},{64,0},{1,65},{65,1},{2,66},{66,2},{3,67},{67,3},{4,68},{68... | collective-permute-start | bytes 98312 | tf_op jit(solution)/shard_map/ppermute | solution.py:40
  38.1 1.1 copy-start.3
  39.2 13.5 %all-to-all-start.2 = ((f32[16,16,256]{2,1,0:T(8,128)}), f32[16,16,256]{2,1,0:T(8,128)S(1)}, u32[]{:S(2)}, u32[]{:S(2)}) async-start(f32[16,16,256]{2,1,0:T(8,128)} %bitcast.17), calls=%async_computation.2 | async-start | bytes 524288 | tf_op jit(solution)/shard_map/all_to_all | solution.py:44
  43.9 19.9 %collective-permute-start.3 = (f32[512,256]{1,0:T(8,128)S(1)}, f32[512,256]{1,0:T(8,128)S(1)}, u32[]{:S(2)}, u32[]{:S(2)}) collective-permute-start(f32[512,256]{1,0:T(8,128)S(1)} %copy-done.2), channel_id=1, source_target_pairs={{0,128},{128,0},{256,384},{384,256},{1,129},{129,1},{257,385},{385... | collective-permute-start | bytes 1572872 | tf_op jit(solution)/shard_map/ppermute | solution.py:83
  47.5 16.3 %collective-permute-start.4 = (f32[512,256]{1,0:T(8,128)S(1)}, f32[512,256]{1,0:T(8,128)S(1)}, u32[]{:S(2)}, u32[]{:S(2)}) collective-permute-start(f32[512,256]{1,0:T(8,128)S(1)} %copy-done.2), channel_id=1, source_target_pairs={{0,384},{128,256},{256,128},{384,0},{1,385},{129,257},{257,129},{3... | collective-permute-start | bytes 1572872 | tf_op jit(solution)/shard_map/ppermute | solution.py:83
  52.7 11.0 %collective-permute-start.2 = (f32[16,256]{1,0:T(8,128)S(1)}, f32[16,256]{1,0:T(8,128)S(1)}, u32[]{:S(2)}, u32[]{:S(2)}) collective-permute-start(f32[16,256]{1,0:T(8,128)S(1)} %reduce_sum.28), channel_id=1, source_target_pairs={{0,16},{16,0},{1,17},{17,1},{2,18},{18,2},{3,19},{19,3},{4,20},{20... | collective-permute-start | bytes 49160 | tf_op jit(solution)/shard_map/ppermute | solution.py:40
  64.5 15.6 %all-to-all-start.3 = ((f32[16,16,256]{2,1,0:T(8,128)}), f32[16,16,256]{2,1,0:T(8,128)S(1)}, u32[]{:S(2)}, u32[]{:S(2)}) async-start(f32[16,16,256]{2,1,0:T(8,128)} %broadcast_in_dim.13), calls=%async_computation.3 | async-start | bytes 524288 | tf_op jit(solution)/shard_map/all_to_all | solution.py:44
  71.3 29.4 %collective-permute-start.7 = (f32[512,256]{1,0:T(8,128)S(1)}, f32[512,256]{1,0:T(8,128)}, u32[]{:S(2)}, u32[]{:S(2)}) collective-permute-start(f32[512,256]{1,0:T(8,128)S(1)} %copy-done.2), channel_id=1, source_target_pairs={{0,256},{128,384},{256,0},{384,128},{1,257},{129,385},{257,1},{385... | collective-permute-start | bytes 1572872 | tf_op jit(solution)/shard_map/ppermute | solution.py:83
  81.3 6.5 %collective-permute-start.5 = (f32[64,128]{1,0:T(8,128)}, f32[64,128]{1,0:T(8,128)S(1)}, u32[]{:S(2)}, u32[]{:S(2)}) collective-permute-start(f32[64,128]{1,0:T(8,128)} %fusion.13), channel_id=1, source_target_pairs={{0,32},{32,0},{1,33},{33,1},{2,34},{34,2},{3,35},{35,3},{4,36},{36... | collective-permute-start | bytes 98312 | tf_op jit(solution)/shard_map/ppermute | solution.py:40
  88.6 14.7 %collective-permute-start.6 = (f32[64,128]{1,0:T(8,128)S(1)}, f32[64,128]{1,0:T(8,128)S(1)}, u32[]{:S(2)}, u32[]{:S(2)}) collective-permute-start(f32[64,128]{1,0:T(8,128)S(1)} %add.87), channel_id=1, source_target_pairs={{0,64},{64,0},{1,65},{65,1},{2,66},{66,2},{3,67},{67,3},{4,68},{68... | collective-permute-start | bytes 98312 | tf_op jit(solution)/shard_map/ppermute | solution.py:40
  102.0 1.3 copy-start.4
  103.9 25.7 %copy-start.6 = (f32[4,2,8,128]{3,2,0,1:T(8,128)S(1)}, f32[4,2,8,128]{3,2,0,1:T(8,128)}, u32[]{:S(2)}) copy-start(f32[4,2,8,128]{3,2,0,1:T(8,128)} %copy.37) | copy-start | bytes 98308
  120.9 8.7 %collective-permute-start.8 = (f32[16,512]{1,0:T(8,128)S(1)}, f32[16,512]{1,0:T(8,128)S(1)}, u32[]{:S(2)}, u32[]{:S(2)}) collective-permute-start(f32[16,512]{1,0:T(8,128)S(1)} %reduce_sum.29), channel_id=1, source_target_pairs={{0,16},{16,0},{1,17},{17,1},{2,18},{18,2},{3,19},{19,3},{4,20},{20... | collective-permute-start | bytes 98312 | tf_op jit(solution)/shard_map/ppermute | solution.py:40
  148.0 7.0 %collective-permute-start.9 = (f32[2,2,16,128]{3,2,1,0:T(8,128)S(1)}, f32[2,2,16,128]{3,2,1,0:T(8,128)S(1)}, u32[]{:S(2)}, u32[]{:S(2)}) collective-permute-start(f32[2,2,16,128]{3,2,1,0:T(8,128)S(1)} %select_bitcast_fusion), channel_id=1, source_target_pairs={{0,32},{32,0},{1,33},{33,1},{2,34},{34,2},{3,35},{35,3},{4,36},{36... | collective-permute-start | bytes 98312 | tf_op jit(solution)/shard_map/ppermute | solution.py:40
  155.0 13.2 %collective-permute-start.10 = (f32[2,16,128]{2,1,0:T(8,128)S(1)}, f32[2,16,128]{2,1,0:T(8,128)S(1)}, u32[]{:S(2)}, u32[]{:S(2)}) collective-permute-start(f32[2,16,128]{2,1,0:T(8,128)S(1)} %select_bitcast_fusion.1), channel_id=1, source_target_pairs={{0,64},{64,0},{1,65},{65,1},{2,66},{66,2},{3,67},{67,3},{4,68},{68... | collective-permute-start | bytes 49160 | tf_op jit(solution)/shard_map/ppermute | solution.py:40
